TPU v7x, 32 devices: a whole 2x2x4 slice. The times are simulated.
32 devices in a mesh: node: 4 (over y, x), rows: 8 (over z, core).
Axes of the slice: x: 2, y: 2, z: 4, core: 2. Of those that a mesh axis runs over, the one named last changes fastest.
Arguments:
- subspace: bfloat16 [6144, 256], P('rows'), may hold values from -6 to 6
- inverse: bfloat16 [4, 2, 6144, 768], P('node', None, 'rows')
- weights: float32 [4, 2], P('node'), may hold values from 0.25 to 1
- diag_tiles: float32 [6144, 128], P('rows'), may hold values from -0.5 to 0.5
- upper_tiles: float32 [6144, 128], P('rows'), may hold values from -0.5 to 0.5
Outputs:
- subspace_out: float32 [6144, 256], P('rows')
- projected: float32 [2, 256, 256], replicated
All inputs are finite; a program needn't handle non-finite values.
Results may differ from a plain program's by a relative error of at most 0.0025.
Values may be sent and summed in bfloat16 or wider, within the bound.
No kernel may reach another device: no remote copies, remote signals or barrier semaphores. Data moves between devices by JAX's collectives and lax.ppermute only.
A program may use at most 64 MiB of HBM per device.

v0:
```python
import jax
import jax.numpy as jnp
from jax import lax
from jax.sharding import PartitionSpec as P

ITERS = 2


precise = lax.Precision.HIGHEST


def padded_2(cells, sides, width):
    for axis, dim in sides:
        count = lax.axis_size(axis)
        ends = count - 1
        head = lax.slice_in_dim(cells, 0, width, axis=dim)
        tail = lax.slice_in_dim(cells, cells.shape[dim] - width, cells.shape[dim], axis=dim)
        cells = jnp.concatenate(
            [
                lax.ppermute(tail, axis, [(i, (i + 1) % count) for i in range(ends)]),
                cells,
                lax.ppermute(head, axis, [((i + 1) % count, i) for i in range(ends)]),
            ],
            axis=dim,
        )
    return cells


def passed_along(block, axis, distance):
    devices = range(lax.axis_size(axis))
    route = [(i - distance, i) for i in devices if i - distance in devices]
    return lax.ppermute(block, axis, route)


def inner(left, right):
    return jnp.dot(left.T, right, precision=precise)


def right_solve(values, factor):
    return jax.scipy.linalg.solve_triangular(factor, values.T, lower=True).T


def both_sides(matrix, factor):
    halfway = jax.scipy.linalg.solve_triangular(factor, matrix, lower=True)
    return jax.scipy.linalg.solve_triangular(factor, halfway.T, lower=True).T


def band_product(field, diag_tiles, upper_tiles, prior_coupling):
    band_width = diag_tiles.shape[1]
    number = field.shape[0] // band_width
    edge_rows = jnp.concatenate([field[:band_width], field[-band_width:]], 0)
    padded = padded_2(edge_rows, (("rows", 0),), band_width)
    from_prior = padded[:band_width]
    from_next = padded[-band_width:]
    field_tiles = field.reshape(number, band_width, field.shape[1])
    diagonal = diag_tiles.reshape(number, band_width, band_width)
    diagonal = 0.5 * (diagonal + jnp.swapaxes(diagonal, 1, 2))
    upper_part = upper_tiles.reshape(number, band_width, band_width)
    next_tiles = jnp.concatenate([field_tiles[1:], from_next[None]], 0)
    prior_tiles = jnp.concatenate([from_prior[None], field_tiles[:-1]], 0)
    prior_upper = jnp.concatenate([prior_coupling[None], upper_part[:-1]], 0)
    result = jnp.einsum("tij,tjm->tim", diagonal, field_tiles, precision=precise)
    result = result + jnp.einsum("tij,tjm->tim", upper_part, next_tiles, precision=precise)
    result = result + jnp.einsum("tji,tjm->tim", prior_upper, prior_tiles, precision=precise)
    return result.reshape(field.shape)


def filter_term(current, inverse, weights, coupling_here, prior_coupling):
    band_width = coupling_here.shape[0]
    columns = current.shape[1]
    blocks = inverse[0]
    solved = jnp.einsum("cij,jm->cim", blocks, current, preferred_element_type=jnp.float32)
    first_rows = jnp.concatenate([solved[0, :band_width], solved[1, :band_width]], 1)
    last_rows = jnp.concatenate([solved[0, -band_width:], solved[1, -band_width:]], 1)
    edge_rows = jnp.concatenate([first_rows, last_rows], 0).astype(jnp.bfloat16)
    padded = padded_2(edge_rows, (("rows", 0),), band_width)
    from_prior = padded[:band_width].astype(jnp.float32)
    from_next = padded[-band_width:].astype(jnp.float32)
    edge_top = jnp.dot(prior_coupling.T, from_prior, precision=precise)
    edge_bottom = jnp.dot(coupling_here, from_next, precision=precise)
    edge_terms = jnp.concatenate([edge_top, edge_bottom], 0).astype(jnp.bfloat16)
    corner = jnp.concatenate([blocks[:, :, :band_width], blocks[:, :, -band_width:]], 2)
    real_side = jnp.dot(corner[0], edge_terms, preferred_element_type=jnp.float32)
    imag_side = jnp.dot(corner[1], edge_terms, preferred_element_type=jnp.float32)
    real_part = solved[0] + real_side[:, :columns] - imag_side[:, columns:]
    imag_part = solved[1] + real_side[:, columns:] + imag_side[:, :columns]
    return weights[0, 0] * real_part - weights[0, 1] * imag_part


def per_device(subspace, inverse, weights, diag_tiles, upper_tiles):
    band_width = diag_tiles.shape[1]
    coupling_here = upper_tiles[-band_width:]
    prior_coupling = passed_along(coupling_here, "rows", 1)
    order = subspace.shape[0] * lax.axis_size("rows")
    current = subspace
    history = []
    orthonormal = jnp.zeros(subspace.shape, jnp.float32)
    for iteration in range(ITERS):
        node_term = filter_term(current, inverse, weights, coupling_here, prior_coupling)
        filtered = lax.psum(node_term, "node")
        imaged = band_product(filtered, diag_tiles, upper_tiles, prior_coupling)
        gram_matrix, reduced = lax.psum(
            (inner(filtered, filtered), inner(filtered, imaged)), "rows"
        )
        factor = jnp.linalg.cholesky(gram_matrix / order)
        orthonormal = right_solve(filtered, factor)
        history.append(both_sides(reduced / order, factor))
        current = orthonormal.astype(jnp.bfloat16)
    return (orthonormal, jnp.stack(history))


def solution(mesh):
    placed = (
        P("rows", None),
        P("node", None, "rows", None),
        P("node", None),
        P("rows", None),
        P("rows", None),
    )
    return jax.shard_map(
        per_device, mesh=mesh, in_specs=placed, out_specs=(P("rows", None), P()), check_vma=False
    )
```

profile of v0, /device:TPU:0, one launch (start us, length us, event | category | flops | bytes accessed | tf_op | source)
XLA Modules:
  0.0 449.3 jit_solution(18409366254475777658)
XLA Ops:
  8.2 3.8 fusion.107
  14.0 3.7 collective-permute-start
  18.4 3.9 collective-permute-start.1
  27.5 2.4 fusion.12
  31.8 1.9 copy.50
  33.7 47.5 %all-reduce.7.cloned.1.call-done = f32[768,256]{0,1:T(8,128)} async-done(((f32[768,256]{0,1:T(8,128)}), f32[768,256]{0,1:T(8,128)}) %all-reduce.7.cloned.1.call-update) | async-done | bytes 786448 | tf_op jit(solution)/shard_map/psum | solution.py:100
  81.2 3.0 fusion.109
  85.0 2.3 collective-permute-start.6
  87.3 1.7 collective-permute-start.5
  90.2 49.6 %all-reduce.9.cloned.1.call-done = f32[256,256]{0,1:T(8,128)} async-done(((f32[256,256]{0,1:T(8,128)}), f32[256,256]{0,1:T(8,128)}) %all-reduce.9.cloned.1.call-update) | async-done | bytes 262160 | tf_op jit(solution)/shard_map/psum | solution.py:102
  139.9 1.7 broadcast_multiply_fusion.3
  141.6 1.8 copy.43
  145.7 13.2 %cholesky.130 = f32[128,128]{1,0:T(8,128)} custom-call(f32[128,128]{1,0:T(8,128)} %cholesky.194), custom_call_target="Cholesky" | custom-call | tf_op jit(solution)/shard_map/jit(cholesky)/cholesky | solution.py:105
  158.9 1.5 fusion.66
  160.4 1.6 cholesky.155
  162.0 11.3 %custom-call.19 = f32[1,128,128]{1,2,0:T(8,128)} custom-call(f32[1,128,128]{2,1,0:T(8,128)} %get-tuple-element.103), custom_call_target="InvertDiagBlocksLowerTriangular" | custom-call | tf_op jit(solution)/shard_map/jit(cholesky)/cholesky | solution.py:105
  173.2 1.7 constant_dynamic-update-slice_fusion.3
  174.9 1.7 convolution_subtract_fusion.7
  176.7 13.2 %cholesky.147 = f32[128,128]{1,0:T(8,128)} custom-call(f32[128,128]{1,0:T(8,128)} %convolution_subtract_fusion.7), custom_call_target="Cholesky" | custom-call | tf_op jit(solution)/shard_map/jit(cholesky)/cholesky | solution.py:105
  189.9 1.5 fusion.67
  193.2 1.7 select_select_fusion.1
  195.6 7.0 %while.12 = (s32[]{:T(128)}, f32[256,256]{1,0:T(8,128)}, s32[2,2]{1,0:T(2,128)S(1)}, f32[2,128,128]{2,1,0:T(8,128)}, s32[]{:T(128)}) while((s32[]{:T(128)}, f32[256,256]{1,0:T(8,128)}, s32[2,2]{1,0:T(2,128)S(1)}, f32[2,128,128]{2,1,0:T(8,128)}, s32[]{:T(128)}) %tuple.77), condition=%wide.while_cond, body=%wide.while_body.sunk | while | flops 2 | bytes 132205 | solution.py:40
  196.4 2.9 bitcast_dynamic-update-slice_fusion.4
  199.9 2.8 bitcast_dynamic-update-slice_fusion.4
  202.7 21.1 %custom-call.20 = f32[2,128,128]{1,2,0:T(8,128)} custom-call(f32[2,128,128]{2,1,0:T(8,128)} %get-tuple-element.45), custom_call_target="InvertDiagBlocksLowerTriangular" | custom-call | tf_op jit(solution)/shard_map/jit(_solve_triangular)/triangular_solve | solution.py:40
  223.8 1.4 fusion.34
  230.3 3.0 collective-permute-start.3
  235.5 2.4 fusion.9
  241.4 1.7 copy.56
  244.1 1.9 fusion.17
  246.8 2.1 fusion.111
  249.0 39.7 %all-reduce.11.cloned.1.call-done = f32[768,256]{0,1:T(8,128)} async-done(((f32[768,256]{0,1:T(8,128)}), f32[768,256]{0,1:T(8,128)}) %all-reduce.11.cloned.1.call-update) | async-done | bytes 786448 | tf_op jit(solution)/shard_map/psum | solution.py:100
  288.7 1.7 fusion.105
  290.4 2.3 collective-permute-start.8
  292.7 2.3 copy.58
  295.0 2.0 fusion.46
  297.0 1.5 collective-permute-start.7
  299.5 1.5 fusion.110
  301.0 2.2 copy.61
  304.2 1.7 copy.62
  306.6 2.0 fusion.24
  309.5 2.1 fusion.112
  311.6 60.0 %all-reduce.13.cloned.1.call-done = (f32[256,256]{0,1:T(8,128)}, f32[256,256]{0,1:T(8,128)}, f32[256,256]{0,1:T(8,128)}) async-done(((f32[256,256]{0,1:T(8,128)}, f32[256,256]{0,1:T(8,128)}, f32[256,256]{0,1:T(8,128)}), (f32[256,256]{0,1:T(8,128)}, f32[256,256]{0,1:T(8,128)}, f32[256,256]{0,1:T(8,128)})) %all-reduce.13.cloned.1.call-update) | async-done | bytes 786448 | tf_op jit(solution)/shard_map/psum | solution.py:102
  373.8 11.7 %cholesky.164 = f32[128,128]{1,0:T(8,128)S(1)} custom-call(f32[128,128]{1,0:T(8,128)S(1)} %cholesky.197), custom_call_target="Cholesky" | custom-call | tf_op jit(solution)/shard_map/jit(cholesky)/cholesky | solution.py:105
  385.6 9.8 %custom-call.21 = f32[1,128,128]{1,2,0:T(8,128)S(1)} custom-call(f32[1,128,128]{2,1,0:T(8,128)S(1)} %get-tuple-element.99), custom_call_target="InvertDiagBlocksLowerTriangular" | custom-call | tf_op jit(solution)/shard_map/jit(cholesky)/cholesky | solution.py:105
  395.9 11.9 %cholesky.181 = f32[128,128]{1,0:T(8,128)S(1)} custom-call(f32[128,128]{1,0:T(8,128)S(1)} %convolution_subtract_fusion.6), custom_call_target="Cholesky" | custom-call | tf_op jit(solution)/shard_map/jit(cholesky)/cholesky | solution.py:105
  410.5 4.0 while.13
  414.5 19.7 %custom-call.22 = f32[2,128,128]{1,2,0:T(8,128)S(1)} custom-call(f32[2,128,128]{2,1,0:T(8,128)S(1)} %get-tuple-element.46), custom_call_target="InvertDiagBlocksLowerTriangular" | custom-call | tf_op jit(solution)/shard_map/jit(_solve_triangular)/triangular_solve | solution.py:40
  (166 shorter events, 49.3 us)
Async XLA Ops:
  7.2 1.0 copy-start
  7.2 10.5 %slice-start = ((f32[768,128]{1,0:T(8,128)}), f32[128,128]{1,0:T(8,128)S(1)}, s32[]{:S(2)}) async-start(f32[768,128]{1,0:T(8,128)} %param.14), calls=%async_computation.4 | async-start | bytes 131072
  7.2 74.0 %all-reduce.7.cloned.1.call-start = ((), (), s32[]{:S(2)}) async-start(), calls=%async_computation | async-start | bytes 1572864 | tf_op jit(solution)/shard_map/psum | solution.py:100
  8.2 14.2 %copy-start.3 = (bf16[1,2,768,768]{3,2,1,0:T(8,128)(2,1)S(1)}, bf16[1,2,768,768]{3,2,1,0:T(8,128)(2,1)}, u32[]{:S(2)}) copy-start(bf16[1,2,768,768]{3,2,1,0:T(8,128)(2,1)} %param.11) | copy-start | bytes 7077892
  12.0 10.5 %copy-start.27 = (f32[1,2]{1,0:T(1,128)S(1)}, f32[1,2]{1,0:T(1,128)}, u32[]{:S(2)}) copy-start(f32[1,2]{1,0:T(1,128)} %param.12) | copy-start | bytes 28
  12.0 11.2 %copy-start.9 = (f32[768,128]{1,0:T(8,128)S(1)}, f32[768,128]{1,0:T(8,128)}, u32[]{:S(2)}) copy-start(f32[768,128]{1,0:T(8,128)} %param.14) | copy-start | bytes 1179652
  12.7 10.5 %collective-permute-start.2 = (bf16[128,512]{0,1:T(8,128)(2,1)}, bf16[128,512]{0,1:T(8,128)(2,1)}, u32[]{:S(2)}, u32[]{:S(2)}) collective-permute-start(bf16[128,512]{0,1:T(8,128)(2,1)} %pad_maximum_fusion.12), channel_id=1, source_target_pairs={{1,0},{2,1},{3,2},{4,3},{5,4},{6,5},{7,6},{9,8},{10,9},{11,10},{12... | collective-permute-start | bytes 393224 | tf_op jit(solution)/shard_map/ppermute | solution.py:22
  14.0 10.4 %collective-permute-start = (bf16[128,512]{0,1:T(8,128)(2,1)S(1)}, bf16[128,512]{0,1:T(8,128)(2,1)}, u32[]{:S(2)}, u32[]{:S(2)}) collective-permute-start(bf16[128,512]{0,1:T(8,128)(2,1)S(1)} %pad_maximum_fusion.11), channel_id=1, source_target_pairs={{0,1},{1,2},{2,3},{3,4},{4,5},{5,6},{6,7},{8,9},{9,10},{10,11},{11... | collective-permute-start | bytes 393224 | tf_op jit(solution)/shard_map/ppermute | solution.py:20
  18.4 6.0 %collective-permute-start.1 = (f32[128,128]{0,1:T(8,128)}, f32[128,128]{0,1:T(8,128)S(1)}, u32[]{:S(2)}, u32[]{:S(2)}) collective-permute-start(f32[128,128]{0,1:T(8,128)} %copy.76), channel_id=1, source_target_pairs={{0,1},{1,2},{2,3},{3,4},{4,5},{5,6},{6,7},{8,9},{9,10},{10,11},{11... | collective-permute-start | bytes 196616 | tf_op jit(solution)/shard_map/ppermute | solution.py:32
  22.5 3.5 copy-start.4
  22.5 3.5 copy-start.6
  24.4 2.1 copy-start.21
  26.1 1.4 copy-start.8
  29.9 1.0 slice-start.1
  29.9 109.9 %all-reduce.9.cloned.1.call-start = ((), (), s32[]{:S(2)}) async-start(), calls=%async_computation.1 | async-start | bytes 524288 | tf_op jit(solution)/shard_map/psum | solution.py:102
  81.2 3.1 copy-start.1
  84.3 204.4 %all-reduce.11.cloned.1.call-start = ((), (), s32[]{:S(2)}) async-start(), calls=%async_computation.2 | async-start | bytes 1572864 | tf_op jit(solution)/shard_map/psum | solution.py:100
  85.0 156.3 %collective-permute-start.6 = (f32[128,256]{0,1:T(8,128)}, f32[128,256]{0,1:T(8,128)}, u32[]{:S(2)}, u32[]{:S(2)}) collective-permute-start(f32[128,256]{0,1:T(8,128)} %get-tuple-element.83), channel_id=1, source_target_pairs={{0,1},{1,2},{2,3},{3,4},{4,5},{5,6},{6,7},{8,9},{9,10},{10,11},{11... | collective-permute-start | bytes 393224 | tf_op jit(solution)/shard_map/ppermute | solution.py:20
  87.3 155.7 %collective-permute-start.5 = (f32[128,256]{0,1:T(8,128)}, f32[128,256]{0,1:T(8,128)}, u32[]{:S(2)}, u32[]{:S(2)}) collective-permute-start(f32[128,256]{0,1:T(8,128)} %get-tuple-element.82), channel_id=1, source_target_pairs={{1,0},{2,1},{3,2},{4,3},{5,4},{6,5},{7,6},{9,8},{10,9},{11,10},{12... | collective-permute-start | bytes 393224 | tf_op jit(solution)/shard_map/ppermute | solution.py:22
  144.4 0.7 copy-start.23
  223.8 2.8 copy-start.19
  227.1 2.4 copy-start.11
  227.1 2.4 copy-start.13
  227.1 2.4 copy-start.15
  228.0 5.4 %copy-start.10 = (f32[768,128]{1,0:T(8,128)S(1)}, f32[768,128]{1,0:T(8,128)}, u32[]{:S(2)}) copy-start(f32[768,128]{1,0:T(8,128)} %param.14) | copy-start | bytes 1179652
  228.0 6.4 %copy-start.22 = (f32[128,128]{0,1:T(8,128)S(1)}, f32[128,128]{0,1:T(8,128)}, u32[]{:S(2)}) copy-start(f32[128,128]{0,1:T(8,128)} %copy-done.21) | copy-start | bytes 196612
  228.0 5.4 %collective-permute-start.4 = (bf16[128,512]{0,1:T(8,128)(2,1)S(1)}, bf16[128,512]{0,1:T(8,128)(2,1)S(1)}, u32[]{:S(2)}, u32[]{:S(2)}) collective-permute-start(bf16[128,512]{0,1:T(8,128)(2,1)S(1)} %pad_maximum_fusion.14), channel_id=1, source_target_pairs={{1,0},{2,1},{3,2},{4,3},{5,4},{6,5},{7,6},{9,8},{10,9},{11,10},{12... | collective-permute-start | bytes 393224 | tf_op jit(solution)/shard_map/ppermute | solution.py:22
  229.5 5.2 %copy-start.5 = (bf16[2,768,128]{2,1,0:T(8,128)(2,1)S(1)}, bf16[2,768,128]{2,1,0:T(8,128)(2,1)}, u32[]{:S(2)}) copy-start(bf16[2,768,128]{2,1,0:T(8,128)(2,1)} %copy-done.4) | copy-start | bytes 1179652
  229.5 5.2 %copy-start.7 = (bf16[2,768,128]{2,1,0:T(8,128)(2,1)S(1)}, bf16[2,768,128]{2,1,0:T(8,128)(2,1)}, u32[]{:S(2)}) copy-start(bf16[2,768,128]{2,1,0:T(8,128)(2,1)} %copy-done.6) | copy-start | bytes 1179652
  230.3 4.0 collective-permute-start.3
  238.0 133.7 %all-reduce.13.cloned.1.call-start = ((), (), s32[]{:S(2)}) async-start(), calls=%async_computation.3 | async-start | bytes 1572864 | tf_op jit(solution)/shard_map/psum | solution.py:102
  238.9 5.1 %copy-start.16 = (f32[5,128,128]{1,2,0:T(8,128)S(1)}, f32[5,128,128]{1,2,0:T(8,128)}, u32[]{:S(2)}) copy-start(f32[5,128,128]{1,2,0:T(8,128)} %copy.54) | copy-start | bytes 983044
  246.8 48.1 %copy-start.12 = (f32[768,128]{1,0:T(8,128)S(1)}, f32[768,128]{1,0:T(8,128)}, u32[]{:S(2)}) copy-start(f32[768,128]{1,0:T(8,128)} %param.13) | copy-start | bytes 1179652
  246.8 48.1 %copy-start.14 = (f32[6,128,128]{1,2,0:T(8,128)S(1)}, f32[6,128,128]{1,2,0:T(8,128)}, u32[]{:S(2)}) copy-start(f32[6,128,128]{1,2,0:T(8,128)} %copy.50) | copy-start | bytes 1179652
  290.4 13.8 %collective-permute-start.8 = (f32[128,256]{0,1:T(8,128)}, f32[128,256]{0,1:T(8,128)}, u32[]{:S(2)}, u32[]{:S(2)}) collective-permute-start(f32[128,256]{0,1:T(8,128)} %get-tuple-element.87), channel_id=1, source_target_pairs={{0,1},{1,2},{2,3},{3,4},{4,5},{5,6},{6,7},{8,9},{9,10},{10,11},{11... | collective-permute-start | bytes 393224 | tf_op jit(solution)/shard_map/ppermute | solution.py:20
  295.0 3.6 copy-start.2
  297.0 8.9 %collective-permute-start.7 = (f32[128,256]{0,1:T(8,128)}, f32[128,256]{0,1:T(8,128)S(1)}, u32[]{:S(2)}, u32[]{:S(2)}) collective-permute-start(f32[128,256]{0,1:T(8,128)} %get-tuple-element.86), channel_id=1, source_target_pairs={{1,0},{2,1},{3,2},{4,3},{5,4},{6,5},{7,6},{9,8},{10,9},{11,10},{12... | collective-permute-start | bytes 393224 | tf_op jit(solution)/shard_map/ppermute | solution.py:22
  306.6 2.0 copy-start.17
  306.6 2.0 copy-start.24
  435.7 1.2 copy-start.26
  436.9 2.2 copy-start.25
  437.7 1.5 copy-start.20
  438.0 1.5 copy-start.18
Sparse Core Ops, SparseCore 0:
  30.1 51.1 all-reduce.6
  84.4 55.4 all-reduce.8
  238.1 50.5 all-reduce.10
  311.7 59.8 all-reduce.12
where the time goes:
time: 454 us; the launch traced here: 449 us
  waiting for transfers between devices  198 us (44%)
  other arithmetic  129 us (28%)
  local copies, waits for them, and re-layouts  44.3 us (10%)
  matrix products  39.1 us (9%)
  starting transfers between devices  21.3 us (5%)
  between operations  17.6 us (4%)
    psum x2, waiting for transfers between devices, per_device(): lax.psum((inner(filtered, filtered), inner(filtered, imaged)), 'rows')  110 us
    psum x2, waiting for transfers between devices, per_device(): filtered = lax.psum(node_term, 'node')  87.3 us
    another operation x13, other arithmetic, per_device(): factor = jnp.linalg.cholesky(gram_matrix / order)  76.1 us
    another operation x5, other arithmetic, right_solve(): return jax.scipy.linalg.solve_triangular(factor, values.T, lower=True).T  42.5 us
    another operation x15, local copies, waits for them, and re-layouts, right_solve(): return jax.scipy.linalg.solve_triangular(factor, values.T, lower=True).T  11.6 us
    ppermute x4, starting transfers between devices, padded_2(): lax.ppermute(tail, axis, [(i, (i + 1) % count) for i in range(ends)])  11.3 us
  transfers between devices with their start and end apart: 13, of which 5 were waited for; matrix products, arithmetic and copies ran while one was open for 27% of the time, Pallas kernels for 0%

commit v1 on v0

v1 whole, which is shorter than its diff:
```python
import functools

import jax
import jax.numpy as jnp
from jax import lax
from jax.experimental import pallas as pl
from jax.experimental.pallas import tpu as pltpu
from jax.sharding import PartitionSpec as P

ITERS = 2
GROUP = 8
SEND_TYPES = (jnp.float32, jnp.bfloat16)

precise = lax.Precision.HIGHEST
F32 = jnp.float32
BF16 = jnp.bfloat16


def dot(left, right):
    return jnp.dot(left, right, precision=precise, preferred_element_type=F32)


def dot_tn(left, right):
    dims = (((0,), (0,)), ((), ()))
    return lax.dot_general(left, right, dims, precision=precise, preferred_element_type=F32)


def dot_nt(left, right):
    dims = (((1,), (1,)), ((), ()))
    return lax.dot_general(left, right, dims, precision=precise, preferred_element_type=F32)


def like(shape, dtype=F32):
    return jax.ShapeDtypeStruct(shape, dtype)


def whole(kernel, out_shape, *operands, scratch=(), flops=10**8, specs=None, name=None):
    size = sum(x.size * x.dtype.itemsize for x in operands)
    return pl.pallas_call(
        kernel,
        out_shape=out_shape,
        in_specs=specs or [pl.BlockSpec(memory_space=pltpu.VMEM) for _ in operands],
        scratch_shapes=list(scratch),
        cost_estimate=pl.CostEstimate(flops=flops, bytes_accessed=size, transcendentals=0),
        name=name,
    )(*operands)


def node_swap(block, step):
    count = lax.axis_size("node")
    return lax.ppermute(block, "node", [(i, i ^ step) for i in range(count)])


def core_swap(block):
    count = lax.axis_size("rows")
    return lax.ppermute(block, "rows", [(i, i ^ 1) for i in range(count)])


def link_swap(block):
    count = lax.axis_size("rows")
    pairs = [(i, i + 1) for i in range(1, count - 1, 2)]
    return lax.ppermute(block, "rows", pairs + [(b, a) for a, b in pairs])


def node_spread(blocks):
    return [node_swap(block, step + 1) for step, block in enumerate(blocks)]


def tree_sum(blocks):
    while len(blocks) > 1:
        blocks = [a + b for a, b in zip(blocks[::2], blocks[1::2])]
    return blocks[0]


def chip_sum(block):
    count = lax.axis_size("rows")
    chips = count // 2
    if chips <= 4:
        steps = range(1, chips)
        routes = [[(i, i ^ (2 * s)) for i in range(count)] for s in steps]
        return tree_sum([block] + [lax.ppermute(block, "rows", route) for route in routes])
    step = 2
    while step < count:
        block = block + lax.ppermute(block, "rows", [(i, i ^ step) for i in range(count)])
        step *= 2
    return block


def emit_messages(is_even, first, last, out_a, out_b):
    out_a[...] = jnp.where(is_even, last, first)
    out_b[...] = jnp.where(is_even, first, last)


def solve_kernel(pieces, weights, *refs):
    count = lax.axis_size("node")
    node = lax.axis_index("node")
    is_even = lax.rem(lax.axis_index("rows"), 2) == 0
    step = pl.program_id(0)
    steps = pl.num_programs(0)
    if pieces:
        blocks, (factor, coupling, inverse, base, out_a, out_b, full, head, tip, current) = (
            refs[:count],
            refs[count:],
        )

        @pl.when(step == 0)
        def _():
            size = blocks[0].shape[0]
            for s, block in enumerate(blocks):
                where = pl.multiple_of((node ^ s) * size, 8)
                full[pl.ds(where, size), :] = block[...]
            result = dot_nt(full[...], factor[...])
            full[...] = result
            head[...] = result[: coupling.shape[0]]
            current[...] = result.astype(BF16)

        vectors = current[...]
    else:
        subspace, coupling, inverse, base, out_a, out_b, tip = refs
        vectors = subspace[...]
    band = coupling.shape[0]
    real = jnp.dot(inverse[0, 0], vectors, preferred_element_type=F32)
    imag = jnp.dot(inverse[0, 1], vectors, preferred_element_type=F32)
    base[...] = weights[0, 0] * real - weights[0, 1] * imag

    @pl.when(step == 0)
    def _():
        tip[...] = jnp.concatenate([real[:band], imag[:band]], 1).astype(BF16)

    @pl.when(step == steps - 1)
    def _():
        last = jnp.concatenate([real[-band:], imag[-band:]], 1).astype(BF16)
        last = dot_tn(coupling[...], last.astype(F32)).astype(BF16)
        emit_messages(is_even, tip[...], last, out_a, out_b)


def solve(vectors, factor, weights, upper_tiles, inverse):
    _, _, rows, _ = inverse.shape
    band = upper_tiles.shape[1]
    tile = 2 * band if rows % (2 * band) == 0 else band
    pieces = factor is not None
    vectors = vectors if pieces else [vectors]
    columns = vectors[0].shape[1]
    operands = [weights] + vectors + ([factor] if pieces else []) + [upper_tiles, inverse]
    constant = lambda x: pl.BlockSpec(x.shape, lambda t: (0,) * x.ndim)
    in_specs = (
        [pl.BlockSpec(memory_space=pltpu.SMEM)]
        + [constant(x) for x in vectors]
        + ([constant(factor)] if pieces else [])
        + [
            pl.BlockSpec((band, band), lambda t: (rows // band - 1, 0)),
            pl.BlockSpec((1, 2, tile, rows), lambda t: (0, 0, t, 0)),
        ]
    )
    message = like((band, 2 * columns), BF16)
    outs = [like((rows, columns)), message, message]
    out_specs = [pl.BlockSpec((tile, columns), lambda t: (t, 0)), constant(message), constant(message)]
    scratch = [pltpu.VMEM((band, 2 * columns), BF16)]
    if pieces:
        outs += [like((rows, columns)), like((band, columns))]
        out_specs += [constant(outs[3]), constant(outs[4])]
        scratch += [pltpu.VMEM((rows, columns), BF16)]
    return pl.pallas_call(
        functools.partial(solve_kernel, pieces),
        grid=(rows // tile,),
        in_specs=in_specs,
        out_specs=out_specs,
        out_shape=outs,
        scratch_shapes=scratch,
        cost_estimate=pl.CostEstimate(
            flops=4 * rows * rows * columns, bytes_accessed=inverse.size * 2, transcendentals=0
        ),
        name="solve",
    )(*operands)


def correct_kernel(weights, base, got_a, got_b, coupling, left, right, own, *refs):
    sends, term = refs[:-1], refs[-1]
    node = lax.axis_index("node")
    is_even = lax.rem(lax.axis_index("rows"), 2) == 0
    from_prior = jnp.where(is_even, got_b[...], got_a[...])
    from_next = jnp.where(is_even, got_a[...], got_b[...])
    below = dot(coupling[...], from_next.astype(F32)).astype(BF16)
    product = lambda c: jnp.dot(left[0, c], from_prior, preferred_element_type=F32) + jnp.dot(
        right[0, c], below, preferred_element_type=F32
    )
    real_side, imag_side = product(0), product(1)
    columns = base.shape[1]
    real = real_side[:, :columns] - imag_side[:, columns:]
    imag = real_side[:, columns:] + imag_side[:, :columns]
    term[...] = base[...] + (weights[0, 0] * real - weights[0, 1] * imag)
    size = own.shape[0]
    for s, out in enumerate((own,) + sends):
        where = pl.multiple_of((node ^ s) * size, 8)
        out[...] = term[pl.ds(where, size), :].astype(out.dtype)


def correct(weights, base, got_a, got_b, upper_tiles, inverse, kind):
    rows, columns = base.shape
    band = upper_tiles.shape[1]
    count = lax.axis_size("node")
    size = rows // count
    vmem = pl.BlockSpec(memory_space=pltpu.VMEM)
    outs = [like((size, columns))] + [like((size, columns), kind)] * (count - 1)
    constant = lambda x: pl.BlockSpec(x.shape, lambda t: (0,) * x.ndim)
    return pl.pallas_call(
        correct_kernel,
        grid=(1,),
        in_specs=[
            pl.BlockSpec(memory_space=pltpu.SMEM),
            constant(base),
            constant(got_a),
            constant(got_b),
            pl.BlockSpec((band, band), lambda t: (rows // band - 1, 0)),
            pl.BlockSpec((1, 2, rows, band), lambda t: (0, 0, 0, 0)),
            pl.BlockSpec((1, 2, rows, band), lambda t: (0, 0, 0, rows // band - 1)),
        ],
        out_specs=[constant(x) for x in outs],
        out_shape=outs,
        scratch_shapes=[pltpu.VMEM((rows, columns), F32)],
        cost_estimate=pl.CostEstimate(
            flops=16 * rows * band * columns, bytes_accessed=4 * rows * band * 2, transcendentals=0
        ),
        name="correct",
    )(weights, base, got_a, got_b, upper_tiles, inverse, inverse)


def core_halves(matrix, keep, send):
    half = keep.shape[0]
    core = lax.rem(lax.axis_index("rows"), 2)
    keep[...] = matrix[pl.ds(pl.multiple_of(core * half, 8), half), :]
    send[...] = matrix[pl.ds(pl.multiple_of((1 - core) * half, 8), half), :]


def piece_kernel(*refs):
    *blocks, piece, keep, send, matrix = refs
    total = blocks[0][...]
    for block in blocks[1:]:
        total = total + block[...].astype(F32)
    piece[...] = total
    matrix[...] = dot_tn(total, total)
    core_halves(matrix, keep, send)


def gram_piece(blocks):
    rows, columns = blocks[0].shape
    half = like((columns // 2, columns))
    outs = [like((rows, columns)), half, half]
    scratch = [pltpu.VMEM((columns, columns), F32)]
    return whole(piece_kernel, outs, *blocks, scratch=scratch, name="gram")


def node_slices_kernel(keep, got, own, *refs):
    sends, total = refs[:-1], refs[-1]
    node = lax.axis_index("node")
    total[...] = keep[...] + got[...]
    size = own.shape[0]
    for s, out in enumerate((own,) + sends):
        out[...] = total[pl.ds(pl.multiple_of((node ^ s) * size, 8), size), :]


def node_slices(keep, got):
    rows, columns = keep.shape
    count = lax.axis_size("node")
    outs = [like((rows // count, columns))] * count
    return whole(node_slices_kernel, outs, keep, got, scratch=[pltpu.VMEM(keep.shape, F32)], name="slices")


def join_kernel(*refs):
    *blocks, out = refs
    node = lax.axis_index("node")
    size = blocks[0].shape[0]
    for s, block in enumerate(blocks):
        out[pl.ds(pl.multiple_of((node ^ s) * size, 8), size), :] = block[...]


def node_join(blocks):
    rows, columns = blocks[0].shape
    return whole(join_kernel, like((rows * len(blocks), columns)), *blocks, name="join")


def join_cores(first, second, out):
    half = first.shape[0]
    core = lax.rem(lax.axis_index("rows"), 2)
    out[pl.ds(pl.multiple_of(core * half, 8), half), :] = first[...]
    out[pl.ds(pl.multiple_of((1 - core) * half, 8), half), :] = second[...]


def eliminate(block, out, base):
    count = block.shape[0]
    full = (GROUP, count)
    lane = lax.broadcasted_iota(jnp.int32, full, 1)
    span = range(GROUP)
    tiles = [block[t * GROUP : (t + 1) * GROUP] for t in range(count // GROUP)]
    for t, tile in enumerate(tiles):
        k = t * GROUP
        tile = tiles[t]
        rows = [jnp.broadcast_to(tile[i : i + 1], full) for i in span]
        pivot = [[jnp.broadcast_to(rows[i][:, k + j : k + j + 1], full) for j in range(i + 1)] for i in span]
        scale = []
        low = [[None] * GROUP for _ in span]
        for j in span:
            scale.append(lax.rsqrt(pivot[j][j]))
            for i in range(j + 1, GROUP):
                low[i][j] = pivot[i][j] * scale[j]
            for i in range(j + 1, GROUP):
                for m in range(j + 1, i + 1):
                    pivot[i][m] = pivot[i][m] - low[i][j] * low[m][j]
        inv = [[None] * GROUP for _ in span]
        for j in span:
            inv[j][j] = scale[j]
            for i in range(j + 1, GROUP):
                total = low[i][j] * inv[j][j]
                for m in range(j + 1, i):
                    total = total + low[i][m] * inv[m][j]
                inv[i][j] = -total * scale[i]
        inside = (lane >= k) & (lane < k + GROUP)
        rows = [jnp.where(inside, jnp.where(lane == k + i, 1.0, 0.0), rows[i]) for i in span]
        done = []
        for i in span:
            total = inv[i][0] * rows[0]
            for j in range(1, i + 1):
                total = total + inv[i][j] * rows[j]
            done.append(total)
            at = base + k + i
            out[at : at + 1, base : base + count] = jnp.where(lane < k + GROUP, total, 0.0)[:1]
        if t + 1 < len(tiles):
            back = []
            for j in span:
                total = inv[j][j] * done[j]
                for i in range(j + 1, GROUP):
                    total = total + inv[i][j] * done[i]
                back.append(total)
            for u in range(t + 1, len(tiles)):
                old = tiles[u]
                new = jnp.where(inside, 0.0, old)
                for j in span:
                    new = new - old[:, k + j : k + j + 1] * back[j]
                tiles[u] = new


def factor_kernel(order, first, second, out, matrix):
    join_cores(first, second, matrix)
    count = matrix.shape[0]
    half = count // 2
    values = matrix[...] * (1.0 / order)
    eye = lax.broadcasted_iota(jnp.int32, (count, count), 0) == lax.broadcasted_iota(
        jnp.int32, (count, count), 1
    )
    diagonal = jnp.where(eye, values, 0.0)
    across = lax.rsqrt(jnp.sum(diagonal, 0, keepdims=True))
    down = lax.rsqrt(jnp.sum(diagonal, 1, keepdims=True))
    values = values * across * down
    out[:half, half:] = jnp.zeros((half, count - half), F32)
    eliminate(values[:half, :half], out, 0)
    top = out[:half, :half]
    beside = dot(top, values[:half, half:])
    corner = dot_tn(beside, top)
    eliminate(values[half:, half:] - dot_tn(beside, beside), out, half)
    out[half:, :half] = -dot(out[half:, half:], corner)
    out[...] = out[...] * across


def inverse_factor(halves, order):
    columns = halves[0].shape[1]
    return whole(
        functools.partial(factor_kernel, order),
        like((columns, columns)),
        *halves,
        scratch=[pltpu.VMEM((columns, columns), F32)],
        name="factor",
    )


def sum_halves(keep, send):
    slices = node_slices(keep, core_swap(send))
    total = tree_sum([slices[0]] + node_spread(slices[1:]))
    return gather_halves(chip_sum(total))


def gather_halves(block):
    half = node_join([block] + node_spread([block] * (lax.axis_size("node") - 1)))
    return half, core_swap(half)


def next_head(head):
    count = lax.axis_size("rows")
    return lax.ppermute(head, "rows", [(i + 1, i) for i in range(count - 1)])


def band_kernel(field, after, diag_tiles, upper_tiles, keep, send, image, matrix):
    band = after.shape[0]
    tiles = field.shape[0] // band
    for t in range(tiles):
        at = slice(t * band, (t + 1) * band)
        following = after[...] if t == tiles - 1 else field[(t + 1) * band : (t + 2) * band]
        image[at] = 0.5 * dot(diag_tiles[at], field[at]) + dot(upper_tiles[at], following)
    matrix[...] = dot_tn(field[...], image[...])
    size = keep.shape[0]
    half = matrix.shape[0] // 2
    node = lax.axis_index("node")
    core = lax.rem(lax.axis_index("rows"), 2)
    keep[...] = matrix[pl.ds(pl.multiple_of(core * half + node * size, 8), size), :]
    send[...] = matrix[pl.ds(pl.multiple_of((1 - core) * half + node * size, 8), size), :]


def band_slices(field, after, diag_tiles, upper_tiles):
    rows, columns = field.shape
    part = like((columns // 2 // lax.axis_size("node"), columns))
    return whole(
        band_kernel,
        [part, part],
        field,
        after,
        diag_tiles,
        upper_tiles,
        scratch=[pltpu.VMEM((rows, columns), F32), pltpu.VMEM((columns, columns), F32)],
        name="band",
    )


def last_kernel(field, factor, out):
    out[...] = dot_nt(field[...], factor[...])


def projected_kernel(order, first, second, factor, out, matrix):
    columns = factor.shape[0]
    half = columns // 2
    core = lax.rem(lax.axis_index("rows"), 2)
    size = first.shape[0] // lax.axis_size("node") // ITERS
    for ref, place in ((first, core), (second, 1 - core)):
        for j in range(half // size):
            for k in range(ITERS):
                at = pl.multiple_of(place * half + j * size, 8)
                start = (j * ITERS + k) * size
                matrix[k, pl.ds(at, size), :] = ref[start : start + size]
    scale = 1.0 / order
    for k in range(ITERS):
        value = matrix[k]
        if k == ITERS - 1:
            value = dot_nt(dot(factor[...], value), factor[...])
        out[k] = (value + value.T) * scale


def per_device(subspace, inverse, weights, diag_tiles, upper_tiles):
    order = float(subspace.shape[0] * lax.axis_size("rows"))
    factor, blocks = None, subspace
    kept, sent = [], []
    for iteration in range(ITERS):
        base, out_a, out_b, *rest = solve(blocks, factor, weights, upper_tiles, inverse)
        if iteration > 0:
            field, head = rest
            keep, send = band_slices(field, next_head(head), diag_tiles, upper_tiles)
            kept.append(keep)
            sent.append(send)
        got_a, got_b = core_swap(out_a), link_swap(out_b)
        own, *others = correct(
            weights, base, got_a, got_b, upper_tiles, inverse, SEND_TYPES[iteration]
        )
        piece, keep, send = gram_piece([own] + node_spread(others))
        blocks = [piece] + node_spread([piece] * len(others))
        factor = inverse_factor(sum_halves(keep, send), order)
    field = node_join(blocks)
    head = field[: diag_tiles.shape[1]]
    keep, send = band_slices(field, next_head(head), diag_tiles, upper_tiles)
    kept.append(keep)
    sent.append(send)
    part = jnp.concatenate(kept, 0) + core_swap(jnp.concatenate(sent, 0))
    halves = gather_halves(chip_sum(part))
    columns = subspace.shape[1]
    orthonormal = whole(last_kernel, like(subspace.shape), field, factor, name="last")
    projected = whole(
        functools.partial(projected_kernel, order),
        like((ITERS, columns, columns)),
        *halves,
        factor,
        scratch=[pltpu.VMEM((ITERS, columns, columns), F32)],
        name="projected",
    )
    return orthonormal, projected


def solution(mesh):
    placed = (
        P("rows", None),
        P("node", None, "rows", None),
        P("node", None),
        P("rows", None),
        P("rows", None),
    )
    return jax.shard_map(
        per_device, mesh=mesh, in_specs=placed, out_specs=(P("rows", None), P()), check_vma=False
    )
```

time: 454 us -> 194 us (0.43)
  waiting for transfers between devices: 198 us -> 40.1 us
  other arithmetic: 129 us -> 3.14 us
  Pallas kernels: 0 us -> 72.7 us
  starting transfers between devices: 21.3 us -> 62.2 us
  matrix products: 39.1 us -> 0 us
  local copies, waits for them, and re-layouts: 44.3 us -> 14.1 us
  between operations: 17.6 us -> 0.86 us
    psum x4 -> x0, waiting for transfers between devices: 197 us -> none  [the longest x2 110 us: per_device(): lax.psum((inner(filtered, filtered), inner(filtered, imaged)), 'rows')]
    another operation x21 -> x0, other arithmetic: 119 us -> none  [the longest x13 76.1 us: per_device(): factor = jnp.linalg.cholesky(gram_matrix / order)]
    pallas_call x0 -> x18, Pallas kernels: none -> 72.7 us  [the longest x14 54.9 us: whole(): pl.pallas_call(kernel, out_shape=out_shape, in_specs=specs or [pl.BlockSp...]
    ppermute x9 -> x48, starting transfers between devices: 21.2 us -> 62.2 us  [the longest x27 32.5 us: node_swap(): return lax.ppermute(block, 'node', [(i, i ^ step) for i in range(count)])]
    ppermute x9 -> x48, waiting for transfers between devices: 0.68 us -> 40.1 us  [the longest x27 29.1 us: node_swap(): return lax.ppermute(block, 'node', [(i, i ^ step) for i in range(count)])]
    dot_general x20 -> x0, matrix products: 26.4 us -> none  [the longest x4 8.76 us: inner(): return jnp.dot(left.T, right, precision=precise)]
    another operation x19 -> x0, local copies, waits for them, and re-layouts: 13.8 us -> none  [the longest x15 11.6 us: right_solve(): return jax.scipy.linalg.solve_triangular(factor, values.T, lower=True).T]
    another operation x22 -> x0, matrix products: 12.7 us -> none  [the longest x6 4.74 us: right_solve(): return jax.scipy.linalg.solve_triangular(factor, values.T, lower=True).T]
  transfers between devices with their start and end apart: 13 -> 48, of which waited for: 5 -> 26; matrix products, arithmetic and copies ran while one was open for 27% -> 1% of each run, Pallas kernels for 0% -> 21%
where the time goes in v1:
time: 194 us; the launch traced here: 193 us
  Pallas kernels  72.7 us (37%)
  starting transfers between devices  62.2 us (32%)
  waiting for transfers between devices  40.1 us (21%)
  local copies, waits for them, and re-layouts  14.1 us (7%)
  other arithmetic  3.14 us (2%)
    pallas_call x14, Pallas kernels, whole(): pl.pallas_call(kernel, out_shape=out_shape, in_specs=specs or [pl.BlockSp...  54.9 us
    ppermute x27, starting transfers between devices, node_swap(): return lax.ppermute(block, 'node', [(i, i ^ step) for i in range(count)])  32.5 us
    ppermute x27, waiting for transfers between devices, node_swap(): return lax.ppermute(block, 'node', [(i, i ^ step) for i in range(count)])  29.1 us
    ppermute x9, starting transfers between devices, chip_sum(): lax.ppermute(block, 'rows', route)  16.8 us
    unnamed x74, local copies, waits for them, and re-layouts  13.2 us
    pallas_call x2, Pallas kernels, solve(): pl.pallas_call(functools.partial(solve_kernel, pieces), grid=(rows // til...  10.3 us
    ppermute x8, starting transfers between devices, core_swap(): return lax.ppermute(block, 'rows', [(i, i ^ 1) for i in range(count)])  8.73 us
    pallas_call x2, Pallas kernels, correct(): pl.pallas_call(correct_kernel, grid=(1,), in_specs=[pl.BlockSpec(memory_s...  7.54 us
  transfers between devices with their start and end apart: 48, of which 26 were waited for; matrix products, arithmetic and copies ran while one was open for 1% of the time, Pallas kernels for 21%

profile of v1, /device:TPU:0, one launch (start us, length us, event | category | flops | bytes accessed | tf_op | source)
XLA Modules:
  0.0 193.0 jit_solution(11886532935921631514)
XLA Ops:
  0.6 4.5 %solve.2 = (f32[768,256]{1,0:T(8,128)}, bf16[128,512]{1,0:T(8,128)(2,1)}, bf16[128,512]{1,0:T(8,128)(2,1)}) custom-call(f32[1,2]{1,0:T(1,128)} %weights.7, bf16[768,256]{1,0:T(8,128)(2,1)} %refs_0_.1, f32[768,128]{1,0:T(8,128)} %upper_tiles.3, bf16[1,2,768,768]{3,2,1,0:T(8,128)(2,1)} %right.3), custom_call_target="tpu_custom_call" | custom-call | flops 603979776 | bytes 2359296 | tf_op jit(solution)/shard_map/solve/pallas_call | solution.py:163
  7.5 3.8 %correct.2 = (f32[192,256]{1,0:T(8,128)}, f32[192,256]{1,0:T(8,128)}, f32[192,256]{1,0:T(8,128)}, f32[192,256]{1,0:T(8,128)}) custom-call(f32[1,2]{1,0:T(1,128)} %weights.7, f32[768,256]{1,0:T(8,128)} %get-tuple-element.36.base, bf16[128,512]{1,0:T(8,128)(2,1)} %copy-done.11, bf16[128,512]{1,0:T(8,128)(2,1)} %copy-done.13, f32[768,128]{1,0:T(8,128)} %upper_tiles.3, ...), custom_call_target="tpu_custom_call" | custom-call | flops 402653184 | bytes 786432 | tf_op jit(solution)/shard_map/correct/pallas_call | solution.py:206
  11.3 2.8 %collective-permute-start.2 = (f32[192,256]{1,0:T(8,128)}, f32[192,256]{1,0:T(8,128)S(1)}, u32[]{:S(2)}, u32[]{:S(2)}) collective-permute-start(f32[192,256]{1,0:T(8,128)} %get-tuple-element.40), channel_id=1, source_target_pairs={{0,8},{8,0},{16,24},{24,16},{1,9},{9,1},{17,25},{25,17},{2,10},{10... | collective-permute-start | bytes 589832 | tf_op jit(solution)/shard_map/ppermute | solution.py:51
  14.2 1.5 collective-permute-start.3
  15.7 2.3 %collective-permute-done.2.refs_1_ = f32[192,256]{1,0:T(8,128)S(1)} collective-permute-done((f32[192,256]{1,0:T(8,128)}, f32[192,256]{1,0:T(8,128)S(1)}, u32[]{:S(2)}, u32[]{:S(2)}) %collective-permute-start.2) | collective-permute-done | bytes 196640 | tf_op jit(solution)/shard_map/ppermute | solution.py:51
  18.0 2.8 %collective-permute-done.3.refs_2_ = f32[192,256]{1,0:T(8,128)S(1)} collective-permute-done((f32[192,256]{1,0:T(8,128)}, f32[192,256]{1,0:T(8,128)S(1)}, u32[]{:S(2)}, u32[]{:S(2)}) %collective-permute-start.3) | collective-permute-done | bytes 196640 | tf_op jit(solution)/shard_map/ppermute | solution.py:51
  20.9 2.3 %collective-permute-done.4.refs_3_ = f32[192,256]{1,0:T(8,128)S(1)} collective-permute-done((f32[192,256]{1,0:T(8,128)}, f32[192,256]{1,0:T(8,128)S(1)}, u32[]{:S(2)}, u32[]{:S(2)}) %collective-permute-start.4) | collective-permute-done | bytes 196640 | tf_op jit(solution)/shard_map/ppermute | solution.py:51
  23.8 2.4 %gram.2 = (f32[192,256]{1,0:T(8,128)}, f32[128,256]{1,0:T(8,128)}, f32[128,256]{1,0:T(8,128)}) custom-call(f32[192,256]{1,0:T(8,128)} %get-tuple-element.39.refs_0_, f32[192,256]{1,0:T(8,128)} %copy-done.8, f32[192,256]{1,0:T(8,128)} %copy-done.9, f32[192,256]{1,0:T(8,128)} %copy-done.10), custom_call_target="tpu_custom_call" | custom-call | flops 100000000 | bytes 786432 | tf_op jit(solution)/shard_map/gram/pallas_call | solution.py:39
  26.2 3.6 %collective-permute-start.8 = (f32[128,256]{1,0:T(8,128)}, f32[128,256]{1,0:T(8,128)S(1)}, u32[]{:S(2)}, u32[]{:S(2)}) collective-permute-start(f32[128,256]{1,0:T(8,128)} %get-tuple-element.45), channel_id=1, source_target_pairs={{0,1},{1,0},{2,3},{3,2},{4,5},{5,4},{6,7},{7,6},{8,9},{9,8},{10,11... | collective-permute-start | bytes 393224 | tf_op jit(solution)/shard_map/ppermute | solution.py:56
  31.6 1.6 slices.2
  34.9 1.9 collective-permute-start.11
  38.0 1.9 collective-permute-done.11
  40.7 4.9 %collective-permute-start.14 = (f32[32,256]{1,0:T(8,128)S(1)}, f32[32,256]{1,0:T(8,128)S(1)}, u32[]{:S(2)}, u32[]{:S(2)}) collective-permute-start(f32[32,256]{1,0:T(8,128)S(1)} %add_add_fusion.4), channel_id=1, source_target_pairs={{0,6},{1,7},{2,4},{3,5},{4,2},{5,3},{6,0},{7,1},{8,14},{9,15},{10,... | collective-permute-start | bytes 98312 | tf_op jit(solution)/shard_map/ppermute | solution.py:81
  45.5 2.9 %collective-permute-start.13 = (f32[32,256]{1,0:T(8,128)S(1)}, f32[32,256]{1,0:T(8,128)S(1)}, u32[]{:S(2)}, u32[]{:S(2)}) collective-permute-start(f32[32,256]{1,0:T(8,128)S(1)} %add_add_fusion.4), channel_id=1, source_target_pairs={{0,4},{1,5},{2,6},{3,7},{4,0},{5,1},{6,2},{7,3},{8,12},{9,13},{10,... | collective-permute-start | bytes 98312 | tf_op jit(solution)/shard_map/ppermute | solution.py:81
  48.6 2.1 %collective-permute-done.13 = f32[32,256]{1,0:T(8,128)S(1)} collective-permute-done((f32[32,256]{1,0:T(8,128)S(1)}, f32[32,256]{1,0:T(8,128)S(1)}, u32[]{:S(2)}, u32[]{:S(2)}) %collective-permute-start.13) | collective-permute-done | bytes 32800 | tf_op jit(solution)/shard_map/ppermute | solution.py:81
  50.7 1.7 collective-permute-done.12
  52.4 1.5 collective-permute-start.17
  53.9 1.5 collective-permute-start.7
  57.4 1.5 collective-permute-start.16
  59.4 4.2 %collective-permute-done.16.refs_2_ = f32[32,256]{1,0:T(8,128)S(1)} collective-permute-done((f32[32,256]{1,0:T(8,128)S(1)}, f32[32,256]{1,0:T(8,128)S(1)}, u32[]{:S(2)}, u32[]{:S(2)}) %collective-permute-start.16) | collective-permute-done | bytes 32800 | tf_op jit(solution)/shard_map/ppermute | solution.py:51
  64.8 1.5 join.4.first
  66.3 1.6 collective-permute-done.18.second
  68.5 12.9 %factor.2.refs_4_ = f32[256,256]{1,0:T(8,128)} custom-call(f32[128,256]{1,0:T(8,128)} %join.4.first, f32[128,256]{1,0:T(8,128)} %copy-done.15), custom_call_target="tpu_custom_call" | custom-call | flops 100000000 | bytes 262144 | tf_op jit(solution)/shard_map/factor/pallas_call | solution.py:39
  82.8 5.8 %solve.3 = (f32[768,256]{1,0:T(8,128)}, bf16[128,512]{1,0:T(8,128)(2,1)}, bf16[128,512]{1,0:T(8,128)(2,1)}, f32[768,256]{1,0:T(8,128)}, f32[128,256]{1,0:T(8,128)}) custom-call(f32[1,2]{1,0:T(1,128)} %weights.7, f32[192,256]{1,0:T(8,128)} %get-tuple-element.43.refs_0_, f32[192,256]{1,0:T(8,128)} %copy-done.4, f32[192,256]{1,0:T(8,128)} %copy-done.3, ...), custom_call_target="tpu_custom_call" | custom-call | flops 603979776 | bytes 2359296 | tf_op jit(solution)/shard_map/solve/pallas_call | solution.py:163
  91.0 3.7 %correct.3 = (f32[192,256]{1,0:T(8,128)}, bf16[192,256]{1,0:T(8,128)(2,1)}, bf16[192,256]{1,0:T(8,128)(2,1)}, bf16[192,256]{1,0:T(8,128)(2,1)}) custom-call(f32[1,2]{1,0:T(1,128)} %weights.7, f32[768,256]{1,0:T(8,128)} %get-tuple-element.50.base, bf16[128,512]{1,0:T(8,128)(2,1)} %copy-done.12, bf16[128,512]{1,0:T(8,128)(2,1)} %copy-done.14, ...), custom_call_target="tpu_custom_call" | custom-call | flops 402653184 | bytes 786432 | tf_op jit(solution)/shard_map/correct/pallas_call | solution.py:206
  96.7 1.5 collective-permute-start.23
  100.6 1.8 collective-permute-done.23.refs_3_
  103.1 2.2 %gram.3 = (f32[192,256]{1,0:T(8,128)}, f32[128,256]{1,0:T(8,128)}, f32[128,256]{1,0:T(8,128)}) custom-call(f32[192,256]{1,0:T(8,128)} %get-tuple-element.53.refs_0_, bf16[192,256]{1,0:T(8,128)(2,1)} %copy-done.19, bf16[192,256]{1,0:T(8,128)(2,1)} %copy-done.20, bf16[192,256]{1,0:T(8,128)(2,1)} %copy-done.21), custom_call_target="tpu_custom_call" | custom-call | flops 100000000 | bytes 491520 | tf_op jit(solution)/shard_map/gram/pallas_call | solution.py:39
  105.3 1.5 collective-permute-start.26
  110.2 2.0 %collective-permute-done.26.refs_3_ = f32[192,256]{1,0:T(8,128)S(1)} collective-permute-done((f32[192,256]{1,0:T(8,128)}, f32[192,256]{1,0:T(8,128)S(1)}, u32[]{:S(2)}, u32[]{:S(2)}) %collective-permute-start.26) | collective-permute-done | bytes 196640 | tf_op jit(solution)/shard_map/ppermute | solution.py:51
  112.2 5.4 %collective-permute-done.25.refs_2_ = f32[192,256]{1,0:T(8,128)S(1)} collective-permute-done((f32[192,256]{1,0:T(8,128)}, f32[192,256]{1,0:T(8,128)S(1)}, u32[]{:S(2)}, u32[]{:S(2)}) %collective-permute-start.25) | collective-permute-done | bytes 196640 | tf_op jit(solution)/shard_map/ppermute | solution.py:51
  119.0 2.2 %join.5.field = f32[768,256]{1,0:T(8,128)} custom-call(f32[192,256]{1,0:T(8,128)} %get-tuple-element.57.refs_0_, f32[192,256]{1,0:T(8,128)} %copy-done.7, f32[192,256]{1,0:T(8,128)} %copy-done.6, f32[192,256]{1,0:T(8,128)} %copy-done.5), custom_call_target="tpu_custom_call" | custom-call | flops 100000000 | bytes 786432 | tf_op jit(solution)/shard_map/join/pallas_call | solution.py:39
  124.0 4.1 %band.2 = (f32[32,256]{1,0:T(8,128)}, f32[32,256]{1,0:T(8,128)}) custom-call(f32[768,256]{1,0:T(8,128)} %get-tuple-element.64.field, f32[128,256]{1,0:T(8,128)} %copy-done.17, f32[768,128]{1,0:T(8,128)} %diag_tiles.3, f32[768,128]{1,0:T(8,128)} %upper_tiles.3), custom_call_target="tpu_custom_call" | custom-call | flops 100000000 | bytes 1703936 | tf_op jit(solution)/shard_map/band/pallas_call | solution.py:39
  128.8 4.1 %band.3 = (f32[32,256]{1,0:T(8,128)}, f32[32,256]{1,0:T(8,128)}) custom-call(f32[768,256]{1,0:T(8,128)} %join.5.field, f32[128,256]{1,0:T(8,128)} %copy-done.18, f32[768,128]{1,0:T(8,128)} %diag_tiles.3, f32[768,128]{1,0:T(8,128)} %upper_tiles.3), custom_call_target="tpu_custom_call" | custom-call | flops 100000000 | bytes 1703936 | tf_op jit(solution)/shard_map/band/pallas_call | solution.py:39
  133.7 4.4 %collective-permute-start.40 = (f32[64,256]{1,0:T(8,128)S(1)}, f32[64,256]{1,0:T(8,128)S(1)}, u32[]{:S(2)}, u32[]{:S(2)}) collective-permute-start(f32[64,256]{1,0:T(8,128)S(1)} %pad_maximum_fusion), channel_id=1, source_target_pairs={{0,1},{1,0},{2,3},{3,2},{4,5},{5,4},{6,7},{7,6},{8,9},{9,8},{10,11... | collective-permute-start | bytes 196616 | tf_op jit(solution)/shard_map/ppermute | solution.py:56
  139.8 3.5 %collective-permute-start.43 = (f32[64,256]{1,0:T(8,128)S(1)}, f32[64,256]{1,0:T(8,128)S(1)}, u32[]{:S(2)}, u32[]{:S(2)}) collective-permute-start(f32[64,256]{1,0:T(8,128)S(1)} %maximum_add_fusion), channel_id=1, source_target_pairs={{0,6},{1,7},{2,4},{3,5},{4,2},{5,3},{6,0},{7,1},{8,14},{9,15},{10,... | collective-permute-start | bytes 196616 | tf_op jit(solution)/shard_map/ppermute | solution.py:81
  144.9 1.6 slices.3
  148.3 1.7 collective-permute-start.30
  152.3 1.5 collective-permute-start.44
  154.6 3.3 %collective-permute-start.33 = (f32[32,256]{1,0:T(8,128)S(1)}, f32[32,256]{1,0:T(8,128)S(1)}, u32[]{:S(2)}, u32[]{:S(2)}) collective-permute-start(f32[32,256]{1,0:T(8,128)S(1)} %add_add_fusion.2), channel_id=1, source_target_pairs={{0,6},{1,7},{2,4},{3,5},{4,2},{5,3},{6,0},{7,1},{8,14},{9,15},{10,... | collective-permute-start | bytes 98312 | tf_op jit(solution)/shard_map/ppermute | solution.py:81
  160.3 1.7 join.7.first
  162.8 1.5 collective-permute-start.36
  166.3 1.6 collective-permute-done.36.refs_3_
  169.6 1.5 join.6.first
  171.0 1.6 collective-permute-done.37.second
  173.3 13.1 %factor.3 = f32[256,256]{1,0:T(8,128)} custom-call(f32[128,256]{1,0:T(8,128)} %join.6.first, f32[128,256]{1,0:T(8,128)} %copy-done.16), custom_call_target="tpu_custom_call" | custom-call | flops 100000000 | bytes 262144 | tf_op jit(solution)/shard_map/factor/pallas_call | solution.py:39
  186.4 2.9 %last.1 = f32[768,256]{1,0:T(8,128)} custom-call(f32[768,256]{1,0:T(8,128)} %join.5.field, f32[256,256]{1,0:T(8,128)} %factor.3), custom_call_target="tpu_custom_call" | custom-call | flops 100000000 | bytes 1048576 | tf_op jit(solution)/shard_map/last/pallas_call | solution.py:39
  190.0 3.0 %projected.1 = f32[2,256,256]{2,1,0:T(8,128)} custom-call(f32[256,256]{1,0:T(8,128)} %join.7.first, f32[256,256]{1,0:T(8,128)} %copy-done, f32[256,256]{1,0:T(8,128)} %factor.3), custom_call_target="tpu_custom_call" | custom-call | flops 100000000 | bytes 786432 | tf_op jit(solution)/shard_map/projected/pallas_call | solution.py:39
  (148 shorter events, 47.1 us)
Async XLA Ops:
  5.1 1.7 collective-permute-start
  5.6 1.2 collective-permute-start.1
  11.3 6.7 %collective-permute-start.2 = (f32[192,256]{1,0:T(8,128)}, f32[192,256]{1,0:T(8,128)S(1)}, u32[]{:S(2)}, u32[]{:S(2)}) collective-permute-start(f32[192,256]{1,0:T(8,128)} %get-tuple-element.40), channel_id=1, source_target_pairs={{0,8},{8,0},{16,24},{24,16},{1,9},{9,1},{17,25},{25,17},{2,10},{10... | collective-permute-start | bytes 589832 | tf_op jit(solution)/shard_map/ppermute | solution.py:51
  14.2 6.7 %collective-permute-start.3 = (f32[192,256]{1,0:T(8,128)}, f32[192,256]{1,0:T(8,128)S(1)}, u32[]{:S(2)}, u32[]{:S(2)}) collective-permute-start(f32[192,256]{1,0:T(8,128)} %get-tuple-element.41), channel_id=1, source_target_pairs={{0,16},{8,24},{16,0},{24,8},{1,17},{9,25},{17,1},{25,9},{2,18},{10... | collective-permute-start | bytes 589832 | tf_op jit(solution)/shard_map/ppermute | solution.py:51
  15.7 7.4 %collective-permute-start.4 = (f32[192,256]{1,0:T(8,128)}, f32[192,256]{1,0:T(8,128)S(1)}, u32[]{:S(2)}, u32[]{:S(2)}) collective-permute-start(f32[192,256]{1,0:T(8,128)} %get-tuple-element.42), channel_id=1, source_target_pairs={{0,24},{8,16},{16,8},{24,0},{1,25},{9,17},{17,9},{25,1},{2,26},{10... | collective-permute-start | bytes 589832 | tf_op jit(solution)/shard_map/ppermute | solution.py:51
  26.2 4.8 %collective-permute-start.8 = (f32[128,256]{1,0:T(8,128)}, f32[128,256]{1,0:T(8,128)S(1)}, u32[]{:S(2)}, u32[]{:S(2)}) collective-permute-start(f32[128,256]{1,0:T(8,128)} %get-tuple-element.45), channel_id=1, source_target_pairs={{0,1},{1,0},{2,3},{3,2},{4,5},{5,4},{6,7},{7,6},{8,9},{9,8},{10,11... | collective-permute-start | bytes 393224 | tf_op jit(solution)/shard_map/ppermute | solution.py:56
  33.3 4.1 %collective-permute-start.9 = (f32[32,256]{1,0:T(8,128)}, f32[32,256]{1,0:T(8,128)S(1)}, u32[]{:S(2)}, u32[]{:S(2)}) collective-permute-start(f32[32,256]{1,0:T(8,128)} %get-tuple-element.47), channel_id=1, source_target_pairs={{0,8},{8,0},{16,24},{24,16},{1,9},{9,1},{17,25},{25,17},{2,10},{10... | collective-permute-start | bytes 98312 | tf_op jit(solution)/shard_map/ppermute | solution.py:51
  33.9 4.1 %collective-permute-start.10 = (f32[32,256]{1,0:T(8,128)}, f32[32,256]{1,0:T(8,128)S(1)}, u32[]{:S(2)}, u32[]{:S(2)}) collective-permute-start(f32[32,256]{1,0:T(8,128)} %get-tuple-element.48), channel_id=1, source_target_pairs={{0,16},{8,24},{16,0},{24,8},{1,17},{9,25},{17,1},{25,9},{2,18},{10... | collective-permute-start | bytes 98312 | tf_op jit(solution)/shard_map/ppermute | solution.py:51
  34.9 5.0 %collective-permute-start.11 = (f32[32,256]{1,0:T(8,128)}, f32[32,256]{1,0:T(8,128)S(1)}, u32[]{:S(2)}, u32[]{:S(2)}) collective-permute-start(f32[32,256]{1,0:T(8,128)} %get-tuple-element.49), channel_id=1, source_target_pairs={{0,24},{8,16},{16,8},{24,0},{1,25},{9,17},{17,9},{25,1},{2,26},{10... | collective-permute-start | bytes 98312 | tf_op jit(solution)/shard_map/ppermute | solution.py:51
  40.7 7.9 %collective-permute-start.14 = (f32[32,256]{1,0:T(8,128)S(1)}, f32[32,256]{1,0:T(8,128)S(1)}, u32[]{:S(2)}, u32[]{:S(2)}) collective-permute-start(f32[32,256]{1,0:T(8,128)S(1)} %add_add_fusion.4), channel_id=1, source_target_pairs={{0,6},{1,7},{2,4},{3,5},{4,2},{5,3},{6,0},{7,1},{8,14},{9,15},{10,... | collective-permute-start | bytes 98312 | tf_op jit(solution)/shard_map/ppermute | solution.py:81
  45.5 5.1 %collective-permute-start.13 = (f32[32,256]{1,0:T(8,128)S(1)}, f32[32,256]{1,0:T(8,128)S(1)}, u32[]{:S(2)}, u32[]{:S(2)}) collective-permute-start(f32[32,256]{1,0:T(8,128)S(1)} %add_add_fusion.4), channel_id=1, source_target_pairs={{0,4},{1,5},{2,6},{3,7},{4,0},{5,1},{6,2},{7,3},{8,12},{9,13},{10,... | collective-permute-start | bytes 98312 | tf_op jit(solution)/shard_map/ppermute | solution.py:81
  48.4 3.9 %collective-permute-start.12 = (f32[32,256]{1,0:T(8,128)S(1)}, f32[32,256]{1,0:T(8,128)S(1)}, u32[]{:S(2)}, u32[]{:S(2)}) collective-permute-start(f32[32,256]{1,0:T(8,128)S(1)} %add_add_fusion.4), channel_id=1, source_target_pairs={{0,2},{1,3},{2,0},{3,1},{4,6},{5,7},{6,4},{7,5},{8,10},{9,11},{10,... | collective-permute-start | bytes 98312 | tf_op jit(solution)/shard_map/ppermute | solution.py:81
  52.4 6.5 %collective-permute-start.17 = (f32[32,256]{1,0:T(8,128)S(1)}, f32[32,256]{1,0:T(8,128)S(1)}, u32[]{:S(2)}, u32[]{:S(2)}) collective-permute-start(f32[32,256]{1,0:T(8,128)S(1)} %add_add_fusion.3.refs_0_), channel_id=1, source_target_pairs={{0,24},{8,16},{16,8},{24,0},{1,25},{9,17},{17,9},{25,1},{2,26},{10... | collective-permute-start | bytes 98312 | tf_op jit(solution)/shard_map/ppermute | solution.py:51
  53.9 27.5 %collective-permute-start.7 = (f32[192,256]{1,0:T(8,128)}, f32[192,256]{1,0:T(8,128)S(1)}, u32[]{:S(2)}, u32[]{:S(2)}) collective-permute-start(f32[192,256]{1,0:T(8,128)} %get-tuple-element.43.refs_0_), channel_id=1, source_target_pairs={{0,24},{8,16},{16,8},{24,0},{1,25},{9,17},{17,9},{25,1},{2,26},{10... | collective-permute-start | bytes 589832 | tf_op jit(solution)/shard_map/ppermute | solution.py:51
  55.4 26.0 %collective-permute-start.6 = (f32[192,256]{1,0:T(8,128)}, f32[192,256]{1,0:T(8,128)S(1)}, u32[]{:S(2)}, u32[]{:S(2)}) collective-permute-start(f32[192,256]{1,0:T(8,128)} %get-tuple-element.43.refs_0_), channel_id=1, source_target_pairs={{0,16},{8,24},{16,0},{24,8},{1,17},{9,25},{17,1},{25,9},{2,18},{10... | collective-permute-start | bytes 589832 | tf_op jit(solution)/shard_map/ppermute | solution.py:51
  56.5 24.9 %collective-permute-start.5 = (f32[192,256]{1,0:T(8,128)}, f32[192,256]{1,0:T(8,128)S(1)}, u32[]{:S(2)}, u32[]{:S(2)}) collective-permute-start(f32[192,256]{1,0:T(8,128)} %get-tuple-element.43.refs_0_), channel_id=1, source_target_pairs={{0,8},{8,0},{16,24},{24,16},{1,9},{9,1},{17,25},{25,17},{2,10},{10... | collective-permute-start | bytes 589832 | tf_op jit(solution)/shard_map/ppermute | solution.py:51
  57.4 6.2 %collective-permute-start.16 = (f32[32,256]{1,0:T(8,128)S(1)}, f32[32,256]{1,0:T(8,128)S(1)}, u32[]{:S(2)}, u32[]{:S(2)}) collective-permute-start(f32[32,256]{1,0:T(8,128)S(1)} %add_add_fusion.3.refs_0_), channel_id=1, source_target_pairs={{0,16},{8,24},{16,0},{24,8},{1,17},{9,25},{17,1},{25,9},{2,18},{10... | collective-permute-start | bytes 98312 | tf_op jit(solution)/shard_map/ppermute | solution.py:51
  58.9 4.8 %collective-permute-start.15 = (f32[32,256]{1,0:T(8,128)S(1)}, f32[32,256]{1,0:T(8,128)S(1)}, u32[]{:S(2)}, u32[]{:S(2)}) collective-permute-start(f32[32,256]{1,0:T(8,128)S(1)} %add_add_fusion.3.refs_0_), channel_id=1, source_target_pairs={{0,8},{8,0},{16,24},{24,16},{1,9},{9,1},{17,25},{25,17},{2,10},{10... | collective-permute-start | bytes 98312 | tf_op jit(solution)/shard_map/ppermute | solution.py:51
  66.3 1.6 collective-permute-start.18
  88.7 1.6 collective-permute-start.19
  88.9 1.4 collective-permute-start.20
  94.7 4.8 %collective-permute-start.21 = (bf16[192,256]{1,0:T(8,128)(2,1)}, bf16[192,256]{1,0:T(8,128)(2,1)S(1)}, u32[]{:S(2)}, u32[]{:S(2)}) collective-permute-start(bf16[192,256]{1,0:T(8,128)(2,1)} %get-tuple-element.54), channel_id=1, source_target_pairs={{0,8},{8,0},{16,24},{24,16},{1,9},{9,1},{17,25},{25,17},{2,10},{10... | collective-permute-start | bytes 294920 | tf_op jit(solution)/shard_map/ppermute | solution.py:51
  95.8 4.8 %collective-permute-start.22 = (bf16[192,256]{1,0:T(8,128)(2,1)}, bf16[192,256]{1,0:T(8,128)(2,1)S(1)}, u32[]{:S(2)}, u32[]{:S(2)}) collective-permute-start(bf16[192,256]{1,0:T(8,128)(2,1)} %get-tuple-element.55), channel_id=1, source_target_pairs={{0,16},{8,24},{16,0},{24,8},{1,17},{9,25},{17,1},{25,9},{2,18},{10... | collective-permute-start | bytes 294920 | tf_op jit(solution)/shard_map/ppermute | solution.py:51
  96.7 5.7 %collective-permute-start.23 = (bf16[192,256]{1,0:T(8,128)(2,1)}, bf16[192,256]{1,0:T(8,128)(2,1)S(1)}, u32[]{:S(2)}, u32[]{:S(2)}) collective-permute-start(bf16[192,256]{1,0:T(8,128)(2,1)} %get-tuple-element.56), channel_id=1, source_target_pairs={{0,24},{8,16},{16,8},{24,0},{1,25},{9,17},{17,9},{25,1},{2,26},{10... | collective-permute-start | bytes 294920 | tf_op jit(solution)/shard_map/ppermute | solution.py:51
  105.3 6.9 %collective-permute-start.26 = (f32[192,256]{1,0:T(8,128)}, f32[192,256]{1,0:T(8,128)S(1)}, u32[]{:S(2)}, u32[]{:S(2)}) collective-permute-start(f32[192,256]{1,0:T(8,128)} %get-tuple-element.57.refs_0_), channel_id=1, source_target_pairs={{0,24},{8,16},{16,8},{24,0},{1,25},{9,17},{17,9},{25,1},{2,26},{10... | collective-permute-start | bytes 589832 | tf_op jit(solution)/shard_map/ppermute | solution.py:51
  106.8 10.8 %collective-permute-start.25 = (f32[192,256]{1,0:T(8,128)}, f32[192,256]{1,0:T(8,128)S(1)}, u32[]{:S(2)}, u32[]{:S(2)}) collective-permute-start(f32[192,256]{1,0:T(8,128)} %get-tuple-element.57.refs_0_), channel_id=1, source_target_pairs={{0,16},{8,24},{16,0},{24,8},{1,17},{9,25},{17,1},{25,9},{2,18},{10... | collective-permute-start | bytes 589832 | tf_op jit(solution)/shard_map/ppermute | solution.py:51
  108.2 9.4 %collective-permute-start.24 = (f32[192,256]{1,0:T(8,128)}, f32[192,256]{1,0:T(8,128)S(1)}, u32[]{:S(2)}, u32[]{:S(2)}) collective-permute-start(f32[192,256]{1,0:T(8,128)} %get-tuple-element.57.refs_0_), channel_id=1, source_target_pairs={{0,8},{8,0},{16,24},{24,16},{1,9},{9,1},{17,25},{25,17},{2,10},{10... | collective-permute-start | bytes 589832 | tf_op jit(solution)/shard_map/ppermute | solution.py:51
  108.8 14.6 %collective-permute-start.38 = (f32[128,256]{1,0:T(8,128)S(1)}, f32[128,256]{1,0:T(8,128)S(1)}, u32[]{:S(2)}, u32[]{:S(2)}) collective-permute-start(f32[128,256]{1,0:T(8,128)S(1)} %copy-done.27), channel_id=1, source_target_pairs={{1,0},{2,1},{3,2},{4,3},{5,4},{6,5},{7,6},{9,8},{10,9},{11,10},{12... | collective-permute-start | bytes 393224 | tf_op jit(solution)/shard_map/ppermute | solution.py:388
  122.1 6.1 %collective-permute-start.39 = (f32[128,256]{1,0:T(8,128)S(1)}, f32[128,256]{1,0:T(8,128)S(1)}, u32[]{:S(2)}, u32[]{:S(2)}) collective-permute-start(f32[128,256]{1,0:T(8,128)S(1)} %slice.4), channel_id=1, source_target_pairs={{1,0},{2,1},{3,2},{4,3},{5,4},{6,5},{7,6},{9,8},{10,9},{11,10},{12... | collective-permute-start | bytes 393224 | tf_op jit(solution)/shard_map/ppermute | solution.py:388
  133.7 5.3 %collective-permute-start.40 = (f32[64,256]{1,0:T(8,128)S(1)}, f32[64,256]{1,0:T(8,128)S(1)}, u32[]{:S(2)}, u32[]{:S(2)}) collective-permute-start(f32[64,256]{1,0:T(8,128)S(1)} %pad_maximum_fusion), channel_id=1, source_target_pairs={{0,1},{1,0},{2,3},{3,2},{4,5},{5,4},{6,7},{7,6},{8,9},{9,8},{10,11... | collective-permute-start | bytes 196616 | tf_op jit(solution)/shard_map/ppermute | solution.py:56
  138.1 6.1 %collective-permute-start.27 = (f32[128,256]{1,0:T(8,128)S(1)}, f32[128,256]{1,0:T(8,128)S(1)}, u32[]{:S(2)}, u32[]{:S(2)}) collective-permute-start(f32[128,256]{1,0:T(8,128)S(1)} %copy-done.28), channel_id=1, source_target_pairs={{0,1},{1,0},{2,3},{3,2},{4,5},{5,4},{6,7},{7,6},{8,9},{9,8},{10,11... | collective-permute-start | bytes 393224 | tf_op jit(solution)/shard_map/ppermute | solution.py:56
  139.8 8.5 %collective-permute-start.43 = (f32[64,256]{1,0:T(8,128)S(1)}, f32[64,256]{1,0:T(8,128)S(1)}, u32[]{:S(2)}, u32[]{:S(2)}) collective-permute-start(f32[64,256]{1,0:T(8,128)S(1)} %maximum_add_fusion), channel_id=1, source_target_pairs={{0,6},{1,7},{2,4},{3,5},{4,2},{5,3},{6,0},{7,1},{8,14},{9,15},{10,... | collective-permute-start | bytes 196616 | tf_op jit(solution)/shard_map/ppermute | solution.py:81
  143.3 6.9 %collective-permute-start.42 = (f32[64,256]{1,0:T(8,128)S(1)}, f32[64,256]{1,0:T(8,128)S(1)}, u32[]{:S(2)}, u32[]{:S(2)}) collective-permute-start(f32[64,256]{1,0:T(8,128)S(1)} %maximum_add_fusion), channel_id=1, source_target_pairs={{0,4},{1,5},{2,6},{3,7},{4,0},{5,1},{6,2},{7,3},{8,12},{9,13},{10,... | collective-permute-start | bytes 196616 | tf_op jit(solution)/shard_map/ppermute | solution.py:81
  143.8 6.4 %collective-permute-start.41 = (f32[64,256]{1,0:T(8,128)S(1)}, f32[64,256]{1,0:T(8,128)S(1)}, u32[]{:S(2)}, u32[]{:S(2)}) collective-permute-start(f32[64,256]{1,0:T(8,128)S(1)} %maximum_add_fusion), channel_id=1, source_target_pairs={{0,2},{1,3},{2,0},{3,1},{4,6},{5,7},{6,4},{7,5},{8,10},{9,11},{10,... | collective-permute-start | bytes 196616 | tf_op jit(solution)/shard_map/ppermute | solution.py:81
  146.5 5.8 %collective-permute-start.28 = (f32[32,256]{1,0:T(8,128)}, f32[32,256]{1,0:T(8,128)S(1)}, u32[]{:S(2)}, u32[]{:S(2)}) collective-permute-start(f32[32,256]{1,0:T(8,128)} %get-tuple-element.61), channel_id=1, source_target_pairs={{0,8},{8,0},{16,24},{24,16},{1,9},{9,1},{17,25},{25,17},{2,10},{10... | collective-permute-start | bytes 98312 | tf_op jit(solution)/shard_map/ppermute | solution.py:51
  147.0 6.8 %collective-permute-start.29 = (f32[32,256]{1,0:T(8,128)}, f32[32,256]{1,0:T(8,128)S(1)}, u32[]{:S(2)}, u32[]{:S(2)}) collective-permute-start(f32[32,256]{1,0:T(8,128)} %get-tuple-element.62), channel_id=1, source_target_pairs={{0,16},{8,24},{16,0},{24,8},{1,17},{9,25},{17,1},{25,9},{2,18},{10... | collective-permute-start | bytes 98312 | tf_op jit(solution)/shard_map/ppermute | solution.py:51
  148.3 5.5 %collective-permute-start.30 = (f32[32,256]{1,0:T(8,128)}, f32[32,256]{1,0:T(8,128)S(1)}, u32[]{:S(2)}, u32[]{:S(2)}) collective-permute-start(f32[32,256]{1,0:T(8,128)} %get-tuple-element.63), channel_id=1, source_target_pairs={{0,24},{8,16},{16,8},{24,0},{1,25},{9,17},{17,9},{25,1},{2,26},{10... | collective-permute-start | bytes 98312 | tf_op jit(solution)/shard_map/ppermute | solution.py:51
  150.2 7.7 %collective-permute-start.46 = (f32[64,256]{1,0:T(8,128)S(1)}, f32[64,256]{1,0:T(8,128)S(1)}, u32[]{:S(2)}, u32[]{:S(2)}) collective-permute-start(f32[64,256]{1,0:T(8,128)S(1)} %add_add_fusion.refs_0_), channel_id=1, source_target_pairs={{0,24},{8,16},{16,8},{24,0},{1,25},{9,17},{17,9},{25,1},{2,26},{10... | collective-permute-start | bytes 196616 | tf_op jit(solution)/shard_map/ppermute | solution.py:51
  151.5 7.6 %collective-permute-start.45 = (f32[64,256]{1,0:T(8,128)S(1)}, f32[64,256]{1,0:T(8,128)S(1)}, u32[]{:S(2)}, u32[]{:S(2)}) collective-permute-start(f32[64,256]{1,0:T(8,128)S(1)} %add_add_fusion.refs_0_), channel_id=1, source_target_pairs={{0,16},{8,24},{16,0},{24,8},{1,17},{9,25},{17,1},{25,9},{2,18},{10... | collective-permute-start | bytes 196616 | tf_op jit(solution)/shard_map/ppermute | solution.py:51
  152.3 6.8 %collective-permute-start.44 = (f32[64,256]{1,0:T(8,128)S(1)}, f32[64,256]{1,0:T(8,128)S(1)}, u32[]{:S(2)}, u32[]{:S(2)}) collective-permute-start(f32[64,256]{1,0:T(8,128)S(1)} %add_add_fusion.refs_0_), channel_id=1, source_target_pairs={{0,8},{8,0},{16,24},{24,16},{1,9},{9,1},{17,25},{25,17},{2,10},{10... | collective-permute-start | bytes 196616 | tf_op jit(solution)/shard_map/ppermute | solution.py:51
  154.6 7.4 %collective-permute-start.33 = (f32[32,256]{1,0:T(8,128)S(1)}, f32[32,256]{1,0:T(8,128)S(1)}, u32[]{:S(2)}, u32[]{:S(2)}) collective-permute-start(f32[32,256]{1,0:T(8,128)S(1)} %add_add_fusion.2), channel_id=1, source_target_pairs={{0,6},{1,7},{2,4},{3,5},{4,2},{5,3},{6,0},{7,1},{8,14},{9,15},{10,... | collective-permute-start | bytes 98312 | tf_op jit(solution)/shard_map/ppermute | solution.py:81
  157.9 4.8 %collective-permute-start.32 = (f32[32,256]{1,0:T(8,128)S(1)}, f32[32,256]{1,0:T(8,128)S(1)}, u32[]{:S(2)}, u32[]{:S(2)}) collective-permute-start(f32[32,256]{1,0:T(8,128)S(1)} %add_add_fusion.2), channel_id=1, source_target_pairs={{0,4},{1,5},{2,6},{3,7},{4,0},{5,1},{6,2},{7,3},{8,12},{9,13},{10,... | collective-permute-start | bytes 98312 | tf_op jit(solution)/shard_map/ppermute | solution.py:81
  157.9 4.8 %collective-permute-start.31 = (f32[32,256]{1,0:T(8,128)S(1)}, f32[32,256]{1,0:T(8,128)S(1)}, u32[]{:S(2)}, u32[]{:S(2)}) collective-permute-start(f32[32,256]{1,0:T(8,128)S(1)} %add_add_fusion.2), channel_id=1, source_target_pairs={{0,2},{1,3},{2,0},{3,1},{4,6},{5,7},{6,4},{7,5},{8,10},{9,11},{10,... | collective-permute-start | bytes 98312 | tf_op jit(solution)/shard_map/ppermute | solution.py:81
  162.0 27.3 %collective-permute-start.47 = (f32[256,256]{1,0:T(8,128)}, f32[256,256]{1,0:T(8,128)S(1)}, u32[]{:S(2)}, u32[]{:S(2)}) collective-permute-start(f32[256,256]{1,0:T(8,128)} %join.7.first), channel_id=1, source_target_pairs={{0,1},{1,0},{2,3},{3,2},{4,5},{5,4},{6,7},{7,6},{8,9},{9,8},{10,11... | collective-permute-start | bytes 786440 | tf_op jit(solution)/shard_map/ppermute | solution.py:56
  162.8 5.2 %collective-permute-start.36 = (f32[32,256]{1,0:T(8,128)S(1)}, f32[32,256]{1,0:T(8,128)S(1)}, u32[]{:S(2)}, u32[]{:S(2)}) collective-permute-start(f32[32,256]{1,0:T(8,128)S(1)} %add_add_fusion.1.refs_0_), channel_id=1, source_target_pairs={{0,24},{8,16},{16,8},{24,0},{1,25},{9,17},{17,9},{25,1},{2,26},{10... | collective-permute-start | bytes 98312 | tf_op jit(solution)/shard_map/ppermute | solution.py:51
  164.3 4.0 %collective-permute-start.35 = (f32[32,256]{1,0:T(8,128)S(1)}, f32[32,256]{1,0:T(8,128)S(1)}, u32[]{:S(2)}, u32[]{:S(2)}) collective-permute-start(f32[32,256]{1,0:T(8,128)S(1)} %add_add_fusion.1.refs_0_), channel_id=1, source_target_pairs={{0,16},{8,24},{16,0},{24,8},{1,17},{9,25},{17,1},{25,9},{2,18},{10... | collective-permute-start | bytes 98312 | tf_op jit(solution)/shard_map/ppermute | solution.py:51
  165.0 3.9 %collective-permute-start.34 = (f32[32,256]{1,0:T(8,128)S(1)}, f32[32,256]{1,0:T(8,128)S(1)}, u32[]{:S(2)}, u32[]{:S(2)}) collective-permute-start(f32[32,256]{1,0:T(8,128)S(1)} %add_add_fusion.1.refs_0_), channel_id=1, source_target_pairs={{0,8},{8,0},{16,24},{24,16},{1,9},{9,1},{17,25},{25,17},{2,10},{10... | collective-permute-start | bytes 98312 | tf_op jit(solution)/shard_map/ppermute | solution.py:51
  171.0 1.6 collective-permute-start.37
  (37 other events, 113.8 us)

commit v2 on v1

v2 whole, which is shorter than its diff:
```python
import functools

import jax
import jax.numpy as jnp
from jax import lax
from jax.experimental import pallas as pl
from jax.experimental.pallas import tpu as pltpu
from jax.sharding import PartitionSpec as P


ITERS = 2
GROUP = 8
SEND_TYPES = (jnp.float32, jnp.bfloat16)

precise = lax.Precision.HIGHEST
F32 = jnp.float32
BF16 = jnp.bfloat16


def dot(left, right):
    return jnp.dot(left, right, precision=precise, preferred_element_type=F32)


def dot_tn(left, right):
    dims = (((0,), (0,)), ((), ()))
    return lax.dot_general(left, right, dims, precision=precise, preferred_element_type=F32)


def dot_nt(left, right):
    dims = (((1,), (1,)), ((), ()))
    return lax.dot_general(left, right, dims, precision=precise, preferred_element_type=F32)


def like(shape, dtype=F32):
    return jax.ShapeDtypeStruct(shape, dtype)


def whole(kernel, out_shape, *operands, scratch=(), flops=10**8, specs=None):
    size = sum(x.size * x.dtype.itemsize for x in operands)
    return pl.pallas_call(
        kernel,
        out_shape=out_shape,
        in_specs=specs or [pl.BlockSpec(memory_space=pltpu.VMEM) for _ in operands],
        scratch_shapes=list(scratch),
        cost_estimate=pl.CostEstimate(flops=flops, bytes_accessed=size, transcendentals=0),
    )(*operands)


def node_swap(block, step):
    count = lax.axis_size("node")
    return lax.ppermute(block, "node", [(i, i ^ step) for i in range(count)])


def core_swap(block):
    count = lax.axis_size("rows")
    return lax.ppermute(block, "rows", [(i, i ^ 1) for i in range(count)])


def link_swap(block):
    count = lax.axis_size("rows")
    pairs = [(i, i + 1) for i in range(1, count - 1, 2)]
    return lax.ppermute(block, "rows", pairs + [(b, a) for a, b in pairs])


def node_spread(blocks):
    return [node_swap(block, step + 1) for step, block in enumerate(blocks)]


def tree_sum(blocks):
    while len(blocks) > 1:
        odd = blocks[len(blocks) // 2 * 2 :]
        blocks = [a + b for a, b in zip(blocks[::2], blocks[1::2])] + odd
    return blocks[0]


def chip_sum(block):
    count = lax.axis_size("rows")
    chips = count // 2
    if chips <= 4:
        steps = range(1, chips)
        routes = [[(i, i ^ (2 * s)) for i in range(count)] for s in steps]
        return tree_sum([block] + [lax.ppermute(block, "rows", route) for route in routes])
    step = 2
    while step < count:
        block = block + lax.ppermute(block, "rows", [(i, i ^ step) for i in range(count)])
        step *= 2
    return block


def solve_kernel(refine, weights, vectors, *refs):
    is_even = lax.rem(lax.axis_index("rows"), 2) == 0
    step = pl.program_id(0)
    steps = pl.num_programs(0)
    if refine:
        factor, coupling, inverse, base, out_a, out_b, tip, current = refs

        @pl.when(step == 0)
        def _():
            current[...] = dot_nt(vectors[...], factor[...]).astype(BF16)

    else:
        coupling, inverse, base, out_a, out_b, tip = refs
        current = vectors
    band = coupling.shape[0]
    real = jnp.dot(inverse[0, 0], current[...], preferred_element_type=F32)
    imag = jnp.dot(inverse[0, 1], current[...], preferred_element_type=F32)
    base[...] = weights[0, 0] * real - weights[0, 1] * imag

    @pl.when(step == 0)
    def _():
        tip[...] = jnp.concatenate([real[:band], imag[:band]], 1).astype(BF16)

    @pl.when(step == steps - 1)
    def _():
        last = jnp.concatenate([real[-band:], imag[-band:]], 1).astype(BF16)
        last = dot_tn(coupling[...], last.astype(F32)).astype(BF16)
        out_a[...] = jnp.where(is_even, last, tip[...])
        out_b[...] = jnp.where(is_even, tip[...], last)


def solve(vectors, factor, weights, upper_tiles, inverse):
    rows, columns = vectors.shape
    band = upper_tiles.shape[1]
    tile = 2 * band if rows % (2 * band) == 0 else band
    refine = factor is not None
    constant = lambda x: pl.BlockSpec(x.shape, lambda t: (0,) * x.ndim)
    in_specs = [pl.BlockSpec(memory_space=pltpu.SMEM), constant(vectors)]
    operands = [weights, vectors]
    if refine:
        in_specs.append(constant(factor))
        operands.append(factor)
    in_specs += [
        pl.BlockSpec((band, band), lambda t: (rows // band - 1, 0)),
        pl.BlockSpec((1, 2, tile, rows), lambda t: (0, 0, t, 0)),
    ]
    message = like((band, 2 * columns), BF16)
    outs = [like((rows, columns)), message, message]
    out_specs = [pl.BlockSpec((tile, columns), lambda t: (t, 0)), constant(message), constant(message)]
    scratch = [pltpu.VMEM((band, 2 * columns), BF16)]
    if refine:
        scratch += [pltpu.VMEM((rows, columns), BF16)]
    return pl.pallas_call(
        functools.partial(solve_kernel, refine),
        grid=(rows // tile,),
        in_specs=in_specs,
        out_specs=out_specs,
        out_shape=outs,
        scratch_shapes=scratch,
        cost_estimate=pl.CostEstimate(
            flops=4 * rows * rows * columns, bytes_accessed=inverse.size * 2, transcendentals=0
        ),
        name="solve",
    )(*operands, upper_tiles, inverse)


def correct_kernel(weights, base, got_a, got_b, coupling, left, right, own, *refs):
    sends, term = refs[:-1], refs[-1]
    node = lax.axis_index("node")
    is_even = lax.rem(lax.axis_index("rows"), 2) == 0
    from_prior = jnp.where(is_even, got_b[...], got_a[...])
    from_next = jnp.where(is_even, got_a[...], got_b[...])
    below = dot(coupling[...], from_next.astype(F32)).astype(BF16)
    product = lambda c: jnp.dot(left[0, c], from_prior, preferred_element_type=F32) + jnp.dot(
        right[0, c], below, preferred_element_type=F32
    )
    real_side, imag_side = product(0), product(1)
    columns = base.shape[1]
    real = real_side[:, :columns] - imag_side[:, columns:]
    imag = real_side[:, columns:] + imag_side[:, :columns]
    term[...] = base[...] + (weights[0, 0] * real - weights[0, 1] * imag)
    size = own.shape[0]
    for s, out in enumerate((own,) + sends):
        where = pl.multiple_of((node ^ s) * size, 8)
        out[...] = term[pl.ds(where, size), :].astype(out.dtype)


def correct(weights, base, got_a, got_b, upper_tiles, inverse, kind):
    rows, columns = base.shape
    band = upper_tiles.shape[1]
    count = lax.axis_size("node")
    size = rows // count
    vmem = pl.BlockSpec(memory_space=pltpu.VMEM)
    outs = [like((size, columns))] + [like((size, columns), kind)] * (count - 1)
    constant = lambda x: pl.BlockSpec(x.shape, lambda t: (0,) * x.ndim)
    return pl.pallas_call(
        correct_kernel,
        grid=(1,),
        in_specs=[
            pl.BlockSpec(memory_space=pltpu.SMEM),
            constant(base),
            constant(got_a),
            constant(got_b),
            pl.BlockSpec((band, band), lambda t: (rows // band - 1, 0)),
            pl.BlockSpec((1, 2, rows, band), lambda t: (0, 0, 0, 0)),
            pl.BlockSpec((1, 2, rows, band), lambda t: (0, 0, 0, rows // band - 1)),
        ],
        out_specs=[constant(x) for x in outs],
        out_shape=outs,
        scratch_shapes=[pltpu.VMEM((rows, columns), F32)],
        cost_estimate=pl.CostEstimate(
            flops=16 * rows * band * columns, bytes_accessed=4 * rows * band * 2, transcendentals=0
        ),
        name="correct",
    )(weights, base, got_a, got_b, upper_tiles, inverse, inverse)


def place(blocks, out):
    node = lax.axis_index("node")
    size = blocks[0].shape[0]
    for step, block in enumerate(blocks):
        out[pl.ds(pl.multiple_of((node ^ step) * size, 8), size), :] = block[...]


def gram_kernel(*refs):
    *blocks, field, head, part, matrix = refs
    place(blocks, field)
    head[...] = field[: head.shape[0]]
    matrix[...] = dot_tn(field[...], field[...])
    size = part.shape[0]
    part[...] = matrix[pl.ds(pl.multiple_of(lax.axis_index("node") * size, 8), size), :]


def gram_slice(blocks, band):
    rows, columns = blocks[0].shape
    count = len(blocks)
    outs = [like((rows * count, columns)), like((band, columns)), like((columns // count, columns))]
    scratch = [pltpu.VMEM((columns, columns), F32)]
    return whole(gram_kernel, outs, *blocks, scratch=scratch)


def eliminate(block, out, base):
    count = block.shape[0]
    full = (GROUP, count)
    lane = lax.broadcasted_iota(jnp.int32, full, 1)
    span = range(GROUP)
    tiles = [block[t * GROUP : (t + 1) * GROUP] for t in range(count // GROUP)]
    for t, tile in enumerate(tiles):
        k = t * GROUP
        tile = tiles[t]
        rows = [jnp.broadcast_to(tile[i : i + 1], full) for i in span]
        pivot = [[jnp.broadcast_to(rows[i][:, k + j : k + j + 1], full) for j in range(i + 1)] for i in span]
        scale = []
        low = [[None] * GROUP for _ in span]
        for j in span:
            scale.append(lax.rsqrt(pivot[j][j]))
            for i in range(j + 1, GROUP):
                low[i][j] = pivot[i][j] * scale[j]
            for i in range(j + 1, GROUP):
                for m in range(j + 1, i + 1):
                    pivot[i][m] = pivot[i][m] - low[i][j] * low[m][j]
        inv = [[None] * GROUP for _ in span]
        for j in span:
            inv[j][j] = scale[j]
            for i in range(j + 1, GROUP):
                total = low[i][j] * inv[j][j]
                for m in range(j + 1, i):
                    total = total + low[i][m] * inv[m][j]
                inv[i][j] = -total * scale[i]
        inside = (lane >= k) & (lane < k + GROUP)
        rows = [jnp.where(inside, jnp.where(lane == k + i, 1.0, 0.0), rows[i]) for i in span]
        done = []
        for i in span:
            total = inv[i][0] * rows[0]
            for j in range(1, i + 1):
                total = total + inv[i][j] * rows[j]
            done.append(total)
            at = base + k + i
            out[at : at + 1, base : base + count] = jnp.where(lane < k + GROUP, total, 0.0)[:1]
        if t + 1 < len(tiles):
            back = []
            for j in span:
                total = inv[j][j] * done[j]
                for i in range(j + 1, GROUP):
                    total = total + inv[i][j] * done[i]
                back.append(total)
            for u in range(t + 1, len(tiles)):
                old = tiles[u]
                new = jnp.where(inside, 0.0, old)
                for j in span:
                    new = new - old[:, k + j : k + j + 1] * back[j]
                tiles[u] = new


def first_factor_kernel(order, *refs):
    *blocks, top, corner, rest, across, matrix = refs
    place(blocks, matrix)
    count = matrix.shape[0]
    half = count // 2
    values = matrix[...] * (1.0 / order)
    eye = lax.broadcasted_iota(jnp.int32, (count, count), 0) == lax.broadcasted_iota(
        jnp.int32, (count, count), 1
    )
    diagonal = jnp.where(eye, values, 0.0)
    scale = lax.rsqrt(jnp.sum(diagonal, 0, keepdims=True))
    down = lax.rsqrt(jnp.sum(diagonal, 1, keepdims=True))
    across[...] = scale
    values = values * scale * down
    eliminate(values[:half, :half], top, 0)
    beside = dot(top[...], values[:half, half:])
    corner[...] = dot_tn(beside, top[...])
    rest[...] = values[half:, half:] - dot_tn(beside, beside)


def second_factor_kernel(top, corner, rest, across, out):
    half = top.shape[0]
    out[:half, :half] = top[...]
    out[:half, half:] = jnp.zeros((half, half), F32)
    eliminate(rest[...], out, half)
    out[half:, :half] = -dot(out[half:, half:], corner[...])
    out[...] = out[...] * across[...]


def first_factor(blocks, order):
    columns = blocks[0].shape[1]
    half = like((columns // 2, columns // 2))
    return whole(
        functools.partial(first_factor_kernel, order),
        [half, half, half, like((1, columns))],
        *blocks,
        scratch=[pltpu.VMEM((columns, columns), F32)],
        flops=6 * 10**9,
    )


def second_factor(halves):
    columns = halves[3].shape[1]
    return whole(second_factor_kernel, like((columns, columns)), *halves, flops=6 * 10**9)


def next_head(head):
    count = lax.axis_size("rows")
    return lax.ppermute(head, "rows", [(i + 1, i) for i in range(count - 1)])


def band_kernel(field, after, diag_tiles, upper_tiles, part, image, matrix):
    band = after.shape[0]
    tiles = field.shape[0] // band
    for t in range(tiles):
        at = slice(t * band, (t + 1) * band)
        following = after[...] if t == tiles - 1 else field[(t + 1) * band : (t + 2) * band]
        image[at] = 0.5 * dot(diag_tiles[at], field[at]) + dot(upper_tiles[at], following)
    matrix[...] = dot_tn(field[...], image[...])
    size = part.shape[0]
    part[...] = matrix[pl.ds(pl.multiple_of(lax.axis_index("node") * size, 8), size), :]


def band_slice(field, after, diag_tiles, upper_tiles):
    rows, columns = field.shape
    return whole(
        band_kernel,
        like((columns // lax.axis_size("node"), columns)),
        field,
        after,
        diag_tiles,
        upper_tiles,
        scratch=[pltpu.VMEM((rows, columns), F32), pltpu.VMEM((columns, columns), F32)],
    )


def last_kernel(field, factor, out):
    out[...] = dot_nt(field[...], factor[...])


def projected_kernel(order, *refs):
    blocks, factors, (out, matrix) = refs[: -2 - ITERS], refs[-2 - ITERS : -2], refs[-2:]
    node = lax.axis_index("node")
    size = blocks[0].shape[0] // ITERS
    for k, factor in enumerate(factors):
        for step, block in enumerate(blocks):
            at = pl.multiple_of((node ^ step) * size, 8)
            matrix[pl.ds(at, size), :] = block[k * size : (k + 1) * size]
        value = dot_nt(dot(factor[...], matrix[...]), factor[...])
        out[k] = (value + value.T) * (1.0 / order)


def after(value, *others):
    return lax.optimization_barrier((value,) + others)[0]


def per_device(subspace, inverse, weights, diag_tiles, upper_tiles):
    order = float(subspace.shape[0] * lax.axis_size("rows"))
    band = upper_tiles.shape[1]
    partners = lax.axis_size("node") - 1
    columns = subspace.shape[1]
    factor, field = None, subspace
    factors, parts = [], []
    for iteration in range(ITERS):
        base, out_a, out_b = solve(field, factor, weights, upper_tiles, inverse)
        got_a, got_b = core_swap(out_a), link_swap(out_b)
        own, *others = correct(
            weights, base, got_a, got_b, upper_tiles, inverse, SEND_TYPES[iteration]
        )
        piece = tree_sum([own] + [x.astype(F32) for x in node_spread(others)])
        field, head, part = gram_slice([piece] + node_spread([piece] * partners), band)
        part = part + core_swap(part)
        following = next_head(after(head, part))
        total = chip_sum(part)
        gathered = [total] + node_spread([total] * partners)
        parts.append(band_slice(field, after(following, total), diag_tiles, upper_tiles))
        halves = first_factor(gathered, order)
        if iteration == ITERS - 1:
            pair = jnp.concatenate(parts, 0)
            pair = after(pair + core_swap(pair), *gathered)
            pair = chip_sum(pair)
            pair = after(pair, *halves)
            spread = [pair] + node_spread([pair] * partners)
        factor = second_factor(halves)
        factors.append(factor)
    orthonormal = whole(last_kernel, like(subspace.shape), field, factor)
    projected = whole(
        functools.partial(projected_kernel, order),
        like((ITERS, columns, columns)),
        *spread,
        *factors,
        scratch=[pltpu.VMEM((columns, columns), F32)],
    )
    return orthonormal, projected


def solution(mesh):
    placed = (
        P("rows", None),
        P("node", None, "rows", None),
        P("node", None),
        P("rows", None),
        P("rows", None),
    )
    return jax.shard_map(
        per_device, mesh=mesh, in_specs=placed, out_specs=(P("rows", None), P()), check_vma=False
    )
```

time: 194 us -> 182 us (0.938)
  starting transfers between devices: 62.2 us -> 55 us
  Pallas kernels: 72.7 us -> 65.8 us
  local copies, waits for them, and re-layouts: 14.1 us -> 7.44 us
  waiting for transfers between devices: 40.1 us -> 46.5 us
  other arithmetic: 3.14 us -> 5.46 us
    ppermute x27 -> x21, starting transfers between devices: 32.5 us -> 25.6 us  [node_swap(): return lax.ppermute(block, 'node', [(i, i ^ step) for i in range(count)])]
    pallas_call x14 -> x10, Pallas kernels: 54.9 us -> 48.3 us  [whole(): pl.pallas_call(kernel, out_shape=out_shape, in_specs=specs or [pl.BlockSp...]
    unnamed x74 -> x56, local copies, waits for them, and re-layouts: 13.2 us -> 7.44 us
    ppermute x27 -> x21, waiting for transfers between devices: 29.1 us -> 34.2 us  [node_swap(): return lax.ppermute(block, 'node', [(i, i ^ step) for i in range(count)])]
    ppermute x8 -> x5, starting transfers between devices: 8.73 us -> 4.97 us  [core_swap(): return lax.ppermute(block, 'rows', [(i, i ^ 1) for i in range(count)])]
    ppermute x9, starting transfers between devices: 16.8 us -> 20.3 us  [chip_sum(): lax.ppermute(block, 'rows', route)]
    ppermute x8 -> x5, waiting for transfers between devices: 6.24 us -> 3.45 us  [core_swap(): return lax.ppermute(block, 'rows', [(i, i ^ 1) for i in range(count)])]
    add x6 -> x8, other arithmetic: 2.36 us -> 4.58 us  [the longest x5 2.02 us: tree_sum(): blocks = [a + b for a, b in zip(blocks[::2], blocks[1::2])] + odd]
  transfers between devices with their start and end apart: 48 -> 39, of which waited for: 26 -> 24; matrix products, arithmetic and copies ran while one was open for 1% -> 1% of each run, Pallas kernels for 21% -> 13%
where the time goes in v2:
time: 182 us; the launch traced here: 181 us
  Pallas kernels  65.8 us (36%)
  starting transfers between devices  55 us (30%)
  waiting for transfers between devices  46.5 us (26%)
  local copies, waits for them, and re-layouts  7.44 us (4%)
  other arithmetic  5.46 us (3%)
    pallas_call x10, Pallas kernels, whole(): pl.pallas_call(kernel, out_shape=out_shape, in_specs=specs or [pl.BlockSp...  48.3 us
    ppermute x21, waiting for transfers between devices, node_swap(): return lax.ppermute(block, 'node', [(i, i ^ step) for i in range(count)])  34.2 us
    ppermute x21, starting transfers between devices, node_swap(): return lax.ppermute(block, 'node', [(i, i ^ step) for i in range(count)])  25.6 us
    ppermute x9, starting transfers between devices, chip_sum(): lax.ppermute(block, 'rows', route)  20.3 us
    pallas_call x2, Pallas kernels, solve(): pl.pallas_call(functools.partial(solve_kernel, refine), grid=(rows // til...  10 us
    pallas_call x2, Pallas kernels, correct(): pl.pallas_call(correct_kernel, grid=(1,), in_specs=[pl.BlockSpec(memory_s...  7.55 us
    unnamed x56, local copies, waits for them, and re-layouts  7.44 us
    ppermute x9, waiting for transfers between devices, chip_sum(): lax.ppermute(block, 'rows', route)  6.68 us
  transfers between devices with their start and end apart: 39, of which 24 were waited for; matrix products, arithmetic and copies ran while one was open for 1% of the time, Pallas kernels for 13%

profile of v2, /device:TPU:0, one launch (start us, length us, event | category | flops | bytes accessed | tf_op | source)
XLA Modules:
  0.0 181.1 jit_solution(51292448578946590)
XLA Ops:
  0.6 4.5 %solve.2 = (f32[768,256]{1,0:T(8,128)}, bf16[128,512]{1,0:T(8,128)(2,1)}, bf16[128,512]{1,0:T(8,128)(2,1)}) custom-call(f32[1,2]{1,0:T(1,128)} %weights.7, bf16[768,256]{1,0:T(8,128)(2,1)} %vectors.1, f32[768,128]{1,0:T(8,128)} %upper_tiles.3, bf16[1,2,768,768]{3,2,1,0:T(8,128)(2,1)} %right.3), custom_call_target="tpu_custom_call" | custom-call | flops 603979776 | bytes 2359296 | tf_op jit(solution)/shard_map/solve/pallas_call | solution.py:142
  7.5 3.8 %correct.2 = (f32[192,256]{1,0:T(8,128)}, f32[192,256]{1,0:T(8,128)}, f32[192,256]{1,0:T(8,128)}, f32[192,256]{1,0:T(8,128)}) custom-call(f32[1,2]{1,0:T(1,128)} %weights.7, f32[768,256]{1,0:T(8,128)} %get-tuple-element.36.base, bf16[128,512]{1,0:T(8,128)(2,1)} %copy-done.15, bf16[128,512]{1,0:T(8,128)(2,1)} %copy-done.17, f32[768,128]{1,0:T(8,128)} %upper_tiles.3, ...), custom_call_target="tpu_custom_call" | custom-call | flops 402653184 | bytes 786432 | tf_op jit(solution)/shard_map/correct/pallas_call | solution.py:185
  11.3 2.8 %collective-permute-start.2 = (f32[192,256]{1,0:T(8,128)}, f32[192,256]{1,0:T(8,128)S(1)}, u32[]{:S(2)}, u32[]{:S(2)}) collective-permute-start(f32[192,256]{1,0:T(8,128)} %get-tuple-element.40), channel_id=1, source_target_pairs={{0,8},{8,0},{16,24},{24,16},{1,9},{9,1},{17,25},{25,17},{2,10},{10... | collective-permute-start | bytes 589832 | tf_op jit(solution)/shard_map/ppermute | solution.py:51
  14.2 1.5 collective-permute-start.3
  15.7 2.3 %collective-permute-done.2 = f32[192,256]{1,0:T(8,128)S(1)} collective-permute-done((f32[192,256]{1,0:T(8,128)}, f32[192,256]{1,0:T(8,128)S(1)}, u32[]{:S(2)}, u32[]{:S(2)}) %collective-permute-start.2) | collective-permute-done | bytes 196640 | tf_op jit(solution)/shard_map/ppermute | solution.py:51
  18.0 2.9 %collective-permute-done.3 = f32[192,256]{1,0:T(8,128)S(1)} collective-permute-done((f32[192,256]{1,0:T(8,128)}, f32[192,256]{1,0:T(8,128)S(1)}, u32[]{:S(2)}, u32[]{:S(2)}) %collective-permute-start.3) | collective-permute-done | bytes 196640 | tf_op jit(solution)/shard_map/ppermute | solution.py:51
  20.9 2.2 %collective-permute-done.4 = f32[192,256]{1,0:T(8,128)S(1)} collective-permute-done((f32[192,256]{1,0:T(8,128)}, f32[192,256]{1,0:T(8,128)S(1)}, u32[]{:S(2)}, u32[]{:S(2)}) %collective-permute-start.4) | collective-permute-done | bytes 196640 | tf_op jit(solution)/shard_map/ppermute | solution.py:51
  25.7 1.9 %collective-permute-start.5 = (f32[192,256]{1,0:T(8,128)S(1)}, f32[192,256]{1,0:T(8,128)S(1)}, u32[]{:S(2)}, u32[]{:S(2)}) collective-permute-start(f32[192,256]{1,0:T(8,128)S(1)} %add_add_fusion.1.refs_0_), channel_id=1, source_target_pairs={{0,8},{8,0},{16,24},{24,16},{1,9},{9,1},{17,25},{25,17},{2,10},{10... | collective-permute-start | bytes 589832 | tf_op jit(solution)/shard_map/ppermute | solution.py:51
  27.7 3.2 %collective-permute-done.7.refs_3_ = f32[192,256]{1,0:T(8,128)S(1)} collective-permute-done((f32[192,256]{1,0:T(8,128)S(1)}, f32[192,256]{1,0:T(8,128)S(1)}, u32[]{:S(2)}, u32[]{:S(2)}) %collective-permute-start.7) | collective-permute-done | bytes 196640 | tf_op jit(solution)/shard_map/ppermute | solution.py:51
  30.9 5.3 %collective-permute-done.6.refs_2_ = f32[192,256]{1,0:T(8,128)S(1)} collective-permute-done((f32[192,256]{1,0:T(8,128)S(1)}, f32[192,256]{1,0:T(8,128)S(1)}, u32[]{:S(2)}, u32[]{:S(2)}) %collective-permute-start.6) | collective-permute-done | bytes 196640 | tf_op jit(solution)/shard_map/ppermute | solution.py:51
  37.5 2.8 %shard_map.68 = (f32[768,256]{1,0:T(8,128)}, f32[128,256]{1,0:T(8,128)}, f32[64,256]{1,0:T(8,128)}) custom-call(f32[192,256]{1,0:T(8,128)} %copy-done.1, f32[192,256]{1,0:T(8,128)} %copy-done.9, f32[192,256]{1,0:T(8,128)} %copy-done.8, f32[192,256]{1,0:T(8,128)} %copy-done.6), custom_call_target="tpu_custom_call" | custom-call | flops 100000000 | bytes 786432 | tf_op jit(solution)/shard_map/pallas_call | solution.py:40
  42.8 6.5 %collective-permute-start.11 = (f32[64,256]{1,0:T(8,128)S(1)}, f32[64,256]{1,0:T(8,128)S(1)}, u32[]{:S(2)}, u32[]{:S(2)}) collective-permute-start(f32[64,256]{1,0:T(8,128)S(1)} %add.57), channel_id=1, source_target_pairs={{0,6},{1,7},{2,4},{3,5},{4,2},{5,3},{6,0},{7,1},{8,14},{9,15},{10,... | collective-permute-start | bytes 196616 | tf_op jit(solution)/shard_map/ppermute | solution.py:82
  49.3 3.2 %collective-permute-start.10 = (f32[64,256]{1,0:T(8,128)S(1)}, f32[64,256]{1,0:T(8,128)S(1)}, u32[]{:S(2)}, u32[]{:S(2)}) collective-permute-start(f32[64,256]{1,0:T(8,128)S(1)} %add.57), channel_id=1, source_target_pairs={{0,4},{1,5},{2,6},{3,7},{4,0},{5,1},{6,2},{7,3},{8,12},{9,13},{10,... | collective-permute-start | bytes 196616 | tf_op jit(solution)/shard_map/ppermute | solution.py:82
  52.7 4.3 %collective-permute-done.10 = f32[64,256]{1,0:T(8,128)S(1)} collective-permute-done((f32[64,256]{1,0:T(8,128)S(1)}, f32[64,256]{1,0:T(8,128)S(1)}, u32[]{:S(2)}, u32[]{:S(2)}) %collective-permute-start.10) | collective-permute-done | bytes 65568 | tf_op jit(solution)/shard_map/ppermute | solution.py:82
  57.3 1.5 collective-permute-start.14
  58.8 1.5 collective-permute-start.13
  60.9 1.7 collective-permute-done.14.refs_3_
  63.3 1.3 collective-permute-done.12.refs_1_
  65.2 7.3 %shard_map.69 = (f32[128,128]{1,0:T(8,128)}, f32[128,128]{1,0:T(8,128)}, f32[128,128]{1,0:T(8,128)}, f32[1,256]{1,0:T(1,128)}) custom-call(f32[64,256]{1,0:T(8,128)} %copy-done.20, f32[64,256]{1,0:T(8,128)} %copy-done.27, f32[64,256]{1,0:T(8,128)} %copy-done.26, f32[64,256]{1,0:T(8,128)} %copy-done.25), custom_call_target="tpu_custom_call" | custom-call | flops 6000000000 | bytes 262144 | tf_op jit(solution)/shard_map/pallas_call | solution.py:40
  72.6 6.6 %shard_map.70.refs_0_.refs_4_ = f32[256,256]{1,0:T(8,128)} custom-call(f32[128,128]{1,0:T(8,128)} %get-tuple-element.45.top, f32[128,128]{1,0:T(8,128)} %get-tuple-element.46.corner, f32[128,128]{1,0:T(8,128)} %get-tuple-element.47.rest, f32[1,256]{1,0:T(1,128)} %get-tuple-element.48.across), custom_call_target="tpu_custom_call" | custom-call | flops 6000000000 | bytes 197632 | tf_op jit(solution)/shard_map/pallas_call | solution.py:40
  79.2 5.5 %solve.3 = (f32[768,256]{1,0:T(8,128)}, bf16[128,512]{1,0:T(8,128)(2,1)}, bf16[128,512]{1,0:T(8,128)(2,1)}) custom-call(f32[1,2]{1,0:T(1,128)} %weights.7, f32[768,256]{1,0:T(8,128)} %get-tuple-element.43.vectors.field, f32[256,256]{1,0:T(8,128)} %shard_map.70.refs_0_.refs_4_, f32[768,128]{1,0:T(8,128)} %upper_tiles.3, bf16[1,2,768,768]{3,2,1,0:T(8,128)(2,1)} %right.3), custom_call_target="tpu_custom_call" | custom-call | flops 603979776 | bytes 2359296 | tf_op jit(solution)/shard_map/solve/pallas_call | solution.py:142
  87.0 3.7 %correct.3 = (f32[192,256]{1,0:T(8,128)}, bf16[192,256]{1,0:T(8,128)(2,1)}, bf16[192,256]{1,0:T(8,128)(2,1)}, bf16[192,256]{1,0:T(8,128)(2,1)}) custom-call(f32[1,2]{1,0:T(1,128)} %weights.7, f32[768,256]{1,0:T(8,128)} %get-tuple-element.49.base, bf16[128,512]{1,0:T(8,128)(2,1)} %copy-done.16, bf16[128,512]{1,0:T(8,128)(2,1)} %copy-done.18, ...), custom_call_target="tpu_custom_call" | custom-call | flops 402653184 | bytes 786432 | tf_op jit(solution)/shard_map/correct/pallas_call | solution.py:185
  91.4 1.3 collective-permute-start.18
  92.7 1.4 collective-permute-start.19
  94.2 1.3 collective-permute-done.17
  96.3 2.2 %collective-permute-done.19 = bf16[192,256]{1,0:T(8,128)(2,1)S(1)} collective-permute-done((bf16[192,256]{1,0:T(8,128)(2,1)}, bf16[192,256]{1,0:T(8,128)(2,1)S(1)}, u32[]{:S(2)}, u32[]{:S(2)}) %collective-permute-start.19) | collective-permute-done | bytes 98336 | tf_op jit(solution)/shard_map/ppermute | solution.py:51
  99.4 1.5 collective-permute-start.22
  101.7 1.3 collective-permute-start.20
  103.0 1.3 collective-permute-start.30
  104.3 1.9 %collective-permute-done.22.refs_3_ = f32[192,256]{1,0:T(8,128)S(1)} collective-permute-done((f32[192,256]{1,0:T(8,128)S(1)}, f32[192,256]{1,0:T(8,128)S(1)}, u32[]{:S(2)}, u32[]{:S(2)}) %collective-permute-start.22) | collective-permute-done | bytes 196640 | tf_op jit(solution)/shard_map/ppermute | solution.py:51
  106.2 5.5 %collective-permute-done.21.refs_2_ = f32[192,256]{1,0:T(8,128)S(1)} collective-permute-done((f32[192,256]{1,0:T(8,128)S(1)}, f32[192,256]{1,0:T(8,128)S(1)}, u32[]{:S(2)}, u32[]{:S(2)}) %collective-permute-start.21) | collective-permute-done | bytes 196640 | tf_op jit(solution)/shard_map/ppermute | solution.py:51
  113.0 2.8 %shard_map.71 = (f32[768,256]{1,0:T(8,128)}, f32[128,256]{1,0:T(8,128)}, f32[64,256]{1,0:T(8,128)}) custom-call(f32[192,256]{1,0:T(8,128)} %copy-done, f32[192,256]{1,0:T(8,128)} %copy-done.7, f32[192,256]{1,0:T(8,128)} %copy-done.5, f32[192,256]{1,0:T(8,128)} %copy-done.4), custom_call_target="tpu_custom_call" | custom-call | flops 100000000 | bytes 786432 | tf_op jit(solution)/shard_map/pallas_call | solution.py:40
  118.4 5.2 %collective-permute-start.26 = (f32[64,256]{1,0:T(8,128)S(1)}, f32[64,256]{1,0:T(8,128)S(1)}, u32[]{:S(2)}, u32[]{:S(2)}) collective-permute-start(f32[64,256]{1,0:T(8,128)S(1)} %add.64), channel_id=1, source_target_pairs={{0,6},{1,7},{2,4},{3,5},{4,2},{5,3},{6,0},{7,1},{8,14},{9,15},{10,... | collective-permute-start | bytes 196616 | tf_op jit(solution)/shard_map/ppermute | solution.py:82
  125.0 4.1 %shard_map.75 = f32[64,256]{1,0:T(8,128)} custom-call(f32[768,256]{1,0:T(8,128)} %get-tuple-element.43.vectors.field, f32[128,256]{1,0:T(8,128)} %copy-done.10, f32[768,128]{1,0:T(8,128)} %diag_tiles.3, f32[768,128]{1,0:T(8,128)} %upper_tiles.3), custom_call_target="tpu_custom_call" | custom-call | flops 100000000 | bytes 1703936 | tf_op jit(solution)/shard_map/pallas_call | solution.py:40
  129.2 1.4 collective-permute-start.31
  130.6 2.1 %collective-permute-done.31.after = f32[128,256]{1,0:T(8,128)S(1)} collective-permute-done((f32[128,256]{1,0:T(8,128)}, f32[128,256]{1,0:T(8,128)S(1)}, u32[]{:S(2)}, u32[]{:S(2)}) %collective-permute-start.31) | collective-permute-done | bytes 131104 | tf_op jit(solution)/shard_map/ppermute | solution.py:332
  133.4 4.1 %shard_map.76 = f32[64,256]{1,0:T(8,128)} custom-call(f32[768,256]{1,0:T(8,128)} %get-tuple-element.56.field, f32[128,256]{1,0:T(8,128)} %copy-done.14, f32[768,128]{1,0:T(8,128)} %diag_tiles.3, f32[768,128]{1,0:T(8,128)} %upper_tiles.3), custom_call_target="tpu_custom_call" | custom-call | flops 100000000 | bytes 1703936 | tf_op jit(solution)/shard_map/pallas_call | solution.py:40
  138.4 3.5 %collective-permute-start.32 = (f32[128,256]{1,0:T(8,128)S(1)}, f32[128,256]{1,0:T(8,128)S(1)}, u32[]{:S(2)}, u32[]{:S(2)}) collective-permute-start(f32[128,256]{1,0:T(8,128)S(1)} %pad_maximum_fusion), channel_id=1, source_target_pairs={{0,1},{1,0},{2,3},{3,2},{4,5},{5,4},{6,7},{7,6},{8,9},{9,8},{10,11... | collective-permute-start | bytes 393224 | tf_op jit(solution)/shard_map/ppermute | solution.py:56
  141.9 1.5 collective-permute-start.29
  143.4 1.6 collective-permute-start.28
  150.3 1.4 collective-permute-start.34
  151.7 1.9 %collective-permute-start.33 = (f32[128,256]{1,0:T(8,128)S(1)}, f32[128,256]{1,0:T(8,128)S(1)}, u32[]{:S(2)}, u32[]{:S(2)}) collective-permute-start(f32[128,256]{1,0:T(8,128)S(1)} %fusion), channel_id=1, source_target_pairs={{0,2},{1,3},{2,0},{3,1},{4,6},{5,7},{6,4},{7,5},{8,10},{9,11},{10,... | collective-permute-start | bytes 393224 | tf_op jit(solution)/shard_map/ppermute | solution.py:82
  153.6 7.4 %shard_map.72 = (f32[128,128]{1,0:T(8,128)}, f32[128,128]{1,0:T(8,128)}, f32[128,128]{1,0:T(8,128)}, f32[1,256]{1,0:T(1,128)}) custom-call(f32[64,256]{1,0:T(8,128)} %copy-done.19, f32[64,256]{1,0:T(8,128)} %copy-done.24, f32[64,256]{1,0:T(8,128)} %copy-done.23, f32[64,256]{1,0:T(8,128)} %copy-done.22), custom_call_target="tpu_custom_call" | custom-call | flops 6000000000 | bytes 262144 | tf_op jit(solution)/shard_map/pallas_call | solution.py:40
  161.0 2.0 %collective-permute-done.34 = f32[128,256]{1,0:T(8,128)S(1)} collective-permute-done((f32[128,256]{1,0:T(8,128)S(1)}, f32[128,256]{1,0:T(8,128)S(1)}, u32[]{:S(2)}, u32[]{:S(2)}) %collective-permute-start.34) | collective-permute-done | bytes 131104 | tf_op jit(solution)/shard_map/ppermute | solution.py:82
  163.0 1.6 collective-permute-start.38
  166.6 6.6 %shard_map.73.factor.refs_5_ = f32[256,256]{1,0:T(8,128)} custom-call(f32[128,128]{1,0:T(8,128)} %get-tuple-element.58.top, f32[128,128]{1,0:T(8,128)} %get-tuple-element.59.corner, f32[128,128]{1,0:T(8,128)} %get-tuple-element.60.rest, f32[1,256]{1,0:T(1,128)} %get-tuple-element.61.across), custom_call_target="tpu_custom_call" | custom-call | flops 6000000000 | bytes 197632 | tf_op jit(solution)/shard_map/pallas_call | solution.py:40
  173.2 2.9 %shard_map.74 = f32[768,256]{1,0:T(8,128)} custom-call(f32[768,256]{1,0:T(8,128)} %get-tuple-element.56.field, f32[256,256]{1,0:T(8,128)} %shard_map.73.factor.refs_5_), custom_call_target="tpu_custom_call" | custom-call | flops 100000000 | bytes 1048576 | tf_op jit(solution)/shard_map/pallas_call | solution.py:40
  177.5 3.6 %shard_map.77 = f32[2,256,256]{2,1,0:T(8,128)} custom-call(f32[128,256]{1,0:T(8,128)} %copy-done.3, f32[128,256]{1,0:T(8,128)} %copy-done.13, f32[128,256]{1,0:T(8,128)} %copy-done.12, f32[128,256]{1,0:T(8,128)} %copy-done.11, f32[256,256]{1,0:T(8,128)} %shard_map.70.refs_0_.refs_4_, f32[256,256]{1,0:T(8,128)} %shard_map.73.factor.refs_5_), custom_call_target="tpu_custom_call" | custom-call | flops 100000000 | bytes 1048576 | tf_op jit(solution)/shard_map/pallas_call | solution.py:40
  (109 shorter events, 32.2 us)
Async XLA Ops:
  5.1 1.7 collective-permute-start
  5.6 1.2 collective-permute-start.1
  11.3 6.7 %collective-permute-start.2 = (f32[192,256]{1,0:T(8,128)}, f32[192,256]{1,0:T(8,128)S(1)}, u32[]{:S(2)}, u32[]{:S(2)}) collective-permute-start(f32[192,256]{1,0:T(8,128)} %get-tuple-element.40), channel_id=1, source_target_pairs={{0,8},{8,0},{16,24},{24,16},{1,9},{9,1},{17,25},{25,17},{2,10},{10... | collective-permute-start | bytes 589832 | tf_op jit(solution)/shard_map/ppermute | solution.py:51
  14.2 6.7 %collective-permute-start.3 = (f32[192,256]{1,0:T(8,128)}, f32[192,256]{1,0:T(8,128)S(1)}, u32[]{:S(2)}, u32[]{:S(2)}) collective-permute-start(f32[192,256]{1,0:T(8,128)} %get-tuple-element.41), channel_id=1, source_target_pairs={{0,16},{8,24},{16,0},{24,8},{1,17},{9,25},{17,1},{25,9},{2,18},{10... | collective-permute-start | bytes 589832 | tf_op jit(solution)/shard_map/ppermute | solution.py:51
  15.7 7.4 %collective-permute-start.4 = (f32[192,256]{1,0:T(8,128)}, f32[192,256]{1,0:T(8,128)S(1)}, u32[]{:S(2)}, u32[]{:S(2)}) collective-permute-start(f32[192,256]{1,0:T(8,128)} %get-tuple-element.42), channel_id=1, source_target_pairs={{0,24},{8,16},{16,8},{24,0},{1,25},{9,17},{17,9},{25,1},{2,26},{10... | collective-permute-start | bytes 589832 | tf_op jit(solution)/shard_map/ppermute | solution.py:51
  24.1 12.1 %copy-start.1 = (f32[192,256]{1,0:T(8,128)}, f32[192,256]{1,0:T(8,128)S(1)}, u32[]{:S(2)}) copy-start(f32[192,256]{1,0:T(8,128)S(1)} %add_add_fusion.1.refs_0_) | copy-start | bytes 589828
  24.1 6.7 %collective-permute-start.7 = (f32[192,256]{1,0:T(8,128)S(1)}, f32[192,256]{1,0:T(8,128)S(1)}, u32[]{:S(2)}, u32[]{:S(2)}) collective-permute-start(f32[192,256]{1,0:T(8,128)S(1)} %add_add_fusion.1.refs_0_), channel_id=1, source_target_pairs={{0,24},{8,16},{16,8},{24,0},{1,25},{9,17},{17,9},{25,1},{2,26},{10... | collective-permute-start | bytes 589832 | tf_op jit(solution)/shard_map/ppermute | solution.py:51
  24.8 11.4 %collective-permute-start.6 = (f32[192,256]{1,0:T(8,128)S(1)}, f32[192,256]{1,0:T(8,128)S(1)}, u32[]{:S(2)}, u32[]{:S(2)}) collective-permute-start(f32[192,256]{1,0:T(8,128)S(1)} %add_add_fusion.1.refs_0_), channel_id=1, source_target_pairs={{0,16},{8,24},{16,0},{24,8},{1,17},{9,25},{17,1},{25,9},{2,18},{10... | collective-permute-start | bytes 589832 | tf_op jit(solution)/shard_map/ppermute | solution.py:51
  25.7 10.5 %collective-permute-start.5 = (f32[192,256]{1,0:T(8,128)S(1)}, f32[192,256]{1,0:T(8,128)S(1)}, u32[]{:S(2)}, u32[]{:S(2)}) collective-permute-start(f32[192,256]{1,0:T(8,128)S(1)} %add_add_fusion.1.refs_0_), channel_id=1, source_target_pairs={{0,8},{8,0},{16,24},{24,16},{1,9},{9,1},{17,25},{25,17},{2,10},{10... | collective-permute-start | bytes 589832 | tf_op jit(solution)/shard_map/ppermute | solution.py:51
  40.4 1.5 collective-permute-start.8
  42.8 9.9 %collective-permute-start.11 = (f32[64,256]{1,0:T(8,128)S(1)}, f32[64,256]{1,0:T(8,128)S(1)}, u32[]{:S(2)}, u32[]{:S(2)}) collective-permute-start(f32[64,256]{1,0:T(8,128)S(1)} %add.57), channel_id=1, source_target_pairs={{0,6},{1,7},{2,4},{3,5},{4,2},{5,3},{6,0},{7,1},{8,14},{9,15},{10,... | collective-permute-start | bytes 196616 | tf_op jit(solution)/shard_map/ppermute | solution.py:82
  49.3 7.7 %collective-permute-start.10 = (f32[64,256]{1,0:T(8,128)S(1)}, f32[64,256]{1,0:T(8,128)S(1)}, u32[]{:S(2)}, u32[]{:S(2)}) collective-permute-start(f32[64,256]{1,0:T(8,128)S(1)} %add.57), channel_id=1, source_target_pairs={{0,4},{1,5},{2,6},{3,7},{4,0},{5,1},{6,2},{7,3},{8,12},{9,13},{10,... | collective-permute-start | bytes 196616 | tf_op jit(solution)/shard_map/ppermute | solution.py:82
  52.5 4.8 %collective-permute-start.9 = (f32[64,256]{1,0:T(8,128)S(1)}, f32[64,256]{1,0:T(8,128)S(1)}, u32[]{:S(2)}, u32[]{:S(2)}) collective-permute-start(f32[64,256]{1,0:T(8,128)S(1)} %add.57), channel_id=1, source_target_pairs={{0,2},{1,3},{2,0},{3,1},{4,6},{5,7},{6,4},{7,5},{8,10},{9,11},{10,... | collective-permute-start | bytes 196616 | tf_op jit(solution)/shard_map/ppermute | solution.py:82
  57.3 7.2 %copy-start.20 = (f32[64,256]{1,0:T(8,128)}, f32[64,256]{1,0:T(8,128)S(1)}, u32[]{:S(2)}) copy-start(f32[64,256]{1,0:T(8,128)S(1)} %add_add_fusion.4.refs_0_) | copy-start | bytes 196612
  57.3 5.2 %collective-permute-start.14 = (f32[64,256]{1,0:T(8,128)S(1)}, f32[64,256]{1,0:T(8,128)S(1)}, u32[]{:S(2)}, u32[]{:S(2)}) collective-permute-start(f32[64,256]{1,0:T(8,128)S(1)} %add_add_fusion.4.refs_0_), channel_id=1, source_target_pairs={{0,24},{8,16},{16,8},{24,0},{1,25},{9,17},{17,9},{25,1},{2,26},{10... | collective-permute-start | bytes 196616 | tf_op jit(solution)/shard_map/ppermute | solution.py:51
  58.8 4.4 %collective-permute-start.13 = (f32[64,256]{1,0:T(8,128)S(1)}, f32[64,256]{1,0:T(8,128)S(1)}, u32[]{:S(2)}, u32[]{:S(2)}) collective-permute-start(f32[64,256]{1,0:T(8,128)S(1)} %add_add_fusion.4.refs_0_), channel_id=1, source_target_pairs={{0,16},{8,24},{16,0},{24,8},{1,17},{9,25},{17,1},{25,9},{2,18},{10... | collective-permute-start | bytes 196616 | tf_op jit(solution)/shard_map/ppermute | solution.py:51
  60.3 4.3 %collective-permute-start.12 = (f32[64,256]{1,0:T(8,128)S(1)}, f32[64,256]{1,0:T(8,128)S(1)}, u32[]{:S(2)}, u32[]{:S(2)}) collective-permute-start(f32[64,256]{1,0:T(8,128)S(1)} %add_add_fusion.4.refs_0_), channel_id=1, source_target_pairs={{0,8},{8,0},{16,24},{24,16},{1,9},{9,1},{17,25},{25,17},{2,10},{10... | collective-permute-start | bytes 196616 | tf_op jit(solution)/shard_map/ppermute | solution.py:51
  84.7 1.6 collective-permute-start.15
  84.7 1.6 collective-permute-start.16
  87.0 16.0 %copy-start.21 = (f32[128,256]{1,0:T(8,128)S(1)}, f32[128,256]{1,0:T(8,128)}, u32[]{:S(2)}) copy-start(f32[128,256]{1,0:T(8,128)} %get-tuple-element.63) | copy-start | bytes 393220
  90.7 4.8 %collective-permute-start.17 = (bf16[192,256]{1,0:T(8,128)(2,1)}, bf16[192,256]{1,0:T(8,128)(2,1)S(1)}, u32[]{:S(2)}, u32[]{:S(2)}) collective-permute-start(bf16[192,256]{1,0:T(8,128)(2,1)} %get-tuple-element.53), channel_id=1, source_target_pairs={{0,8},{8,0},{16,24},{24,16},{1,9},{9,1},{17,25},{25,17},{2,10},{10... | collective-permute-start | bytes 294920 | tf_op jit(solution)/shard_map/ppermute | solution.py:51
  91.4 4.8 %collective-permute-start.18 = (bf16[192,256]{1,0:T(8,128)(2,1)}, bf16[192,256]{1,0:T(8,128)(2,1)S(1)}, u32[]{:S(2)}, u32[]{:S(2)}) collective-permute-start(bf16[192,256]{1,0:T(8,128)(2,1)} %get-tuple-element.54), channel_id=1, source_target_pairs={{0,16},{8,24},{16,0},{24,8},{1,17},{9,25},{17,1},{25,9},{2,18},{10... | collective-permute-start | bytes 294920 | tf_op jit(solution)/shard_map/ppermute | solution.py:51
  92.7 5.7 %collective-permute-start.19 = (bf16[192,256]{1,0:T(8,128)(2,1)}, bf16[192,256]{1,0:T(8,128)(2,1)S(1)}, u32[]{:S(2)}, u32[]{:S(2)}) collective-permute-start(bf16[192,256]{1,0:T(8,128)(2,1)} %get-tuple-element.55), channel_id=1, source_target_pairs={{0,24},{8,16},{16,8},{24,0},{1,25},{9,17},{17,9},{25,1},{2,26},{10... | collective-permute-start | bytes 294920 | tf_op jit(solution)/shard_map/ppermute | solution.py:51
  99.4 12.2 %copy-start = (f32[192,256]{1,0:T(8,128)}, f32[192,256]{1,0:T(8,128)S(1)}, u32[]{:S(2)}) copy-start(f32[192,256]{1,0:T(8,128)S(1)} %add_add_fusion.refs_0_) | copy-start | bytes 589828
  99.4 6.7 %collective-permute-start.22 = (f32[192,256]{1,0:T(8,128)S(1)}, f32[192,256]{1,0:T(8,128)S(1)}, u32[]{:S(2)}, u32[]{:S(2)}) collective-permute-start(f32[192,256]{1,0:T(8,128)S(1)} %add_add_fusion.refs_0_), channel_id=1, source_target_pairs={{0,24},{8,16},{16,8},{24,0},{1,25},{9,17},{17,9},{25,1},{2,26},{10... | collective-permute-start | bytes 589832 | tf_op jit(solution)/shard_map/ppermute | solution.py:51
  101.0 10.7 %collective-permute-start.21 = (f32[192,256]{1,0:T(8,128)S(1)}, f32[192,256]{1,0:T(8,128)S(1)}, u32[]{:S(2)}, u32[]{:S(2)}) collective-permute-start(f32[192,256]{1,0:T(8,128)S(1)} %add_add_fusion.refs_0_), channel_id=1, source_target_pairs={{0,16},{8,24},{16,0},{24,8},{1,17},{9,25},{17,1},{25,9},{2,18},{10... | collective-permute-start | bytes 589832 | tf_op jit(solution)/shard_map/ppermute | solution.py:51
  101.7 10.0 %collective-permute-start.20 = (f32[192,256]{1,0:T(8,128)S(1)}, f32[192,256]{1,0:T(8,128)S(1)}, u32[]{:S(2)}, u32[]{:S(2)}) collective-permute-start(f32[192,256]{1,0:T(8,128)S(1)} %add_add_fusion.refs_0_), channel_id=1, source_target_pairs={{0,8},{8,0},{16,24},{24,16},{1,9},{9,1},{17,25},{25,17},{2,10},{10... | collective-permute-start | bytes 589832 | tf_op jit(solution)/shard_map/ppermute | solution.py:51
  103.0 21.4 %collective-permute-start.30 = (f32[128,256]{1,0:T(8,128)S(1)}, f32[128,256]{1,0:T(8,128)S(1)}, u32[]{:S(2)}, u32[]{:S(2)}) collective-permute-start(f32[128,256]{1,0:T(8,128)S(1)} %copy-done.21), channel_id=1, source_target_pairs={{1,0},{2,1},{3,2},{4,3},{5,4},{6,5},{7,6},{9,8},{10,9},{11,10},{12... | collective-permute-start | bytes 393224 | tf_op jit(solution)/shard_map/ppermute | solution.py:332
  106.2 5.5 %copy-start.4 = (f32[192,256]{1,0:T(8,128)}, f32[192,256]{1,0:T(8,128)S(1)}, u32[]{:S(2)}) copy-start(f32[192,256]{1,0:T(8,128)S(1)} %collective-permute-done.22.refs_3_) | copy-start | bytes 589828
  115.8 1.7 collective-permute-start.23
  118.4 12.2 %collective-permute-start.26 = (f32[64,256]{1,0:T(8,128)S(1)}, f32[64,256]{1,0:T(8,128)S(1)}, u32[]{:S(2)}, u32[]{:S(2)}) collective-permute-start(f32[64,256]{1,0:T(8,128)S(1)} %add.64), channel_id=1, source_target_pairs={{0,6},{1,7},{2,4},{3,5},{4,2},{5,3},{6,0},{7,1},{8,14},{9,15},{10,... | collective-permute-start | bytes 196616 | tf_op jit(solution)/shard_map/ppermute | solution.py:82
  123.6 7.0 %collective-permute-start.25 = (f32[64,256]{1,0:T(8,128)S(1)}, f32[64,256]{1,0:T(8,128)S(1)}, u32[]{:S(2)}, u32[]{:S(2)}) collective-permute-start(f32[64,256]{1,0:T(8,128)S(1)} %add.64), channel_id=1, source_target_pairs={{0,4},{1,5},{2,6},{3,7},{4,0},{5,1},{6,2},{7,3},{8,12},{9,13},{10,... | collective-permute-start | bytes 196616 | tf_op jit(solution)/shard_map/ppermute | solution.py:82
  124.3 6.3 %collective-permute-start.24 = (f32[64,256]{1,0:T(8,128)S(1)}, f32[64,256]{1,0:T(8,128)S(1)}, u32[]{:S(2)}, u32[]{:S(2)}) collective-permute-start(f32[64,256]{1,0:T(8,128)S(1)} %add.64), channel_id=1, source_target_pairs={{0,2},{1,3},{2,0},{3,1},{4,6},{5,7},{6,4},{7,5},{8,10},{9,11},{10,... | collective-permute-start | bytes 196616 | tf_op jit(solution)/shard_map/ppermute | solution.py:82
  129.2 16.2 %copy-start.2 = (f32[64,256]{1,0:T(8,128)S(1)}, f32[64,256]{1,0:T(8,128)}, u32[]{:S(2)}) copy-start(f32[64,256]{1,0:T(8,128)} %shard_map.75) | copy-start | bytes 196612
  129.2 3.6 %collective-permute-start.31 = (f32[128,256]{1,0:T(8,128)}, f32[128,256]{1,0:T(8,128)S(1)}, u32[]{:S(2)}, u32[]{:S(2)}) collective-permute-start(f32[128,256]{1,0:T(8,128)} %get-tuple-element.66), channel_id=1, source_target_pairs={{1,0},{2,1},{3,2},{4,3},{5,4},{6,5},{7,6},{9,8},{10,9},{11,10},{12... | collective-permute-start | bytes 393224 | tf_op jit(solution)/shard_map/ppermute | solution.py:332
  130.6 23.0 %copy-start.19 = (f32[64,256]{1,0:T(8,128)}, f32[64,256]{1,0:T(8,128)S(1)}, u32[]{:S(2)}) copy-start(f32[64,256]{1,0:T(8,128)S(1)} %add_add_fusion.3.refs_0_) | copy-start | bytes 196612
  138.4 7.0 %collective-permute-start.32 = (f32[128,256]{1,0:T(8,128)S(1)}, f32[128,256]{1,0:T(8,128)S(1)}, u32[]{:S(2)}, u32[]{:S(2)}) collective-permute-start(f32[128,256]{1,0:T(8,128)S(1)} %pad_maximum_fusion), channel_id=1, source_target_pairs={{0,1},{1,0},{2,3},{3,2},{4,5},{5,4},{6,7},{7,6},{8,9},{9,8},{10,11... | collective-permute-start | bytes 393224 | tf_op jit(solution)/shard_map/ppermute | solution.py:56
  141.9 5.3 %collective-permute-start.29 = (f32[64,256]{1,0:T(8,128)S(1)}, f32[64,256]{1,0:T(8,128)S(1)}, u32[]{:S(2)}, u32[]{:S(2)}) collective-permute-start(f32[64,256]{1,0:T(8,128)S(1)} %add_add_fusion.3.refs_0_), channel_id=1, source_target_pairs={{0,24},{8,16},{16,8},{24,0},{1,25},{9,17},{17,9},{25,1},{2,26},{10... | collective-permute-start | bytes 196616 | tf_op jit(solution)/shard_map/ppermute | solution.py:51
  143.4 4.9 %collective-permute-start.28 = (f32[64,256]{1,0:T(8,128)S(1)}, f32[64,256]{1,0:T(8,128)S(1)}, u32[]{:S(2)}, u32[]{:S(2)}) collective-permute-start(f32[64,256]{1,0:T(8,128)S(1)} %add_add_fusion.3.refs_0_), channel_id=1, source_target_pairs={{0,16},{8,24},{16,0},{24,8},{1,17},{9,25},{17,1},{25,9},{2,18},{10... | collective-permute-start | bytes 196616 | tf_op jit(solution)/shard_map/ppermute | solution.py:51
  144.9 4.3 %collective-permute-start.27 = (f32[64,256]{1,0:T(8,128)S(1)}, f32[64,256]{1,0:T(8,128)S(1)}, u32[]{:S(2)}, u32[]{:S(2)}) collective-permute-start(f32[64,256]{1,0:T(8,128)S(1)} %add_add_fusion.3.refs_0_), channel_id=1, source_target_pairs={{0,8},{8,0},{16,24},{24,16},{1,9},{9,1},{17,25},{25,17},{2,10},{10... | collective-permute-start | bytes 196616 | tf_op jit(solution)/shard_map/ppermute | solution.py:51
  147.2 6.5 %copy-start.22 = (f32[64,256]{1,0:T(8,128)}, f32[64,256]{1,0:T(8,128)S(1)}, u32[]{:S(2)}) copy-start(f32[64,256]{1,0:T(8,128)S(1)} %collective-permute-done.29.refs_3_) | copy-start | bytes 196612
  149.2 11.8 %collective-permute-start.35 = (f32[128,256]{1,0:T(8,128)S(1)}, f32[128,256]{1,0:T(8,128)S(1)}, u32[]{:S(2)}, u32[]{:S(2)}) collective-permute-start(f32[128,256]{1,0:T(8,128)S(1)} %fusion), channel_id=1, source_target_pairs={{0,6},{1,7},{2,4},{3,5},{4,2},{5,3},{6,0},{7,1},{8,14},{9,15},{10,... | collective-permute-start | bytes 393224 | tf_op jit(solution)/shard_map/ppermute | solution.py:82
  150.3 12.7 %collective-permute-start.34 = (f32[128,256]{1,0:T(8,128)S(1)}, f32[128,256]{1,0:T(8,128)S(1)}, u32[]{:S(2)}, u32[]{:S(2)}) collective-permute-start(f32[128,256]{1,0:T(8,128)S(1)} %fusion), channel_id=1, source_target_pairs={{0,4},{1,5},{2,6},{3,7},{4,0},{5,1},{6,2},{7,3},{8,12},{9,13},{10,... | collective-permute-start | bytes 393224 | tf_op jit(solution)/shard_map/ppermute | solution.py:82
  151.7 11.3 %collective-permute-start.33 = (f32[128,256]{1,0:T(8,128)S(1)}, f32[128,256]{1,0:T(8,128)S(1)}, u32[]{:S(2)}, u32[]{:S(2)}) collective-permute-start(f32[128,256]{1,0:T(8,128)S(1)} %fusion), channel_id=1, source_target_pairs={{0,2},{1,3},{2,0},{3,1},{4,6},{5,7},{6,4},{7,5},{8,10},{9,11},{10,... | collective-permute-start | bytes 393224 | tf_op jit(solution)/shard_map/ppermute | solution.py:82
  163.0 10.2 %copy-start.3 = (f32[128,256]{1,0:T(8,128)}, f32[128,256]{1,0:T(8,128)S(1)}, u32[]{:S(2)}) copy-start(f32[128,256]{1,0:T(8,128)S(1)} %add_add_fusion.2.refs_0_) | copy-start | bytes 393220
  163.0 13.0 %collective-permute-start.38 = (f32[128,256]{1,0:T(8,128)S(1)}, f32[128,256]{1,0:T(8,128)S(1)}, u32[]{:S(2)}, u32[]{:S(2)}) collective-permute-start(f32[128,256]{1,0:T(8,128)S(1)} %add_add_fusion.2.refs_0_), channel_id=1, source_target_pairs={{0,24},{8,16},{16,8},{24,0},{1,25},{9,17},{17,9},{25,1},{2,26},{10... | collective-permute-start | bytes 393224 | tf_op jit(solution)/shard_map/ppermute | solution.py:51
  164.6 11.4 %collective-permute-start.37 = (f32[128,256]{1,0:T(8,128)S(1)}, f32[128,256]{1,0:T(8,128)S(1)}, u32[]{:S(2)}, u32[]{:S(2)}) collective-permute-start(f32[128,256]{1,0:T(8,128)S(1)} %add_add_fusion.2.refs_0_), channel_id=1, source_target_pairs={{0,16},{8,24},{16,0},{24,8},{1,17},{9,25},{17,1},{25,9},{2,18},{10... | collective-permute-start | bytes 393224 | tf_op jit(solution)/shard_map/ppermute | solution.py:51
  165.7 10.4 %collective-permute-start.36 = (f32[128,256]{1,0:T(8,128)S(1)}, f32[128,256]{1,0:T(8,128)S(1)}, u32[]{:S(2)}, u32[]{:S(2)}) collective-permute-start(f32[128,256]{1,0:T(8,128)S(1)} %add_add_fusion.2.refs_0_), channel_id=1, source_target_pairs={{0,8},{8,0},{16,24},{24,16},{1,9},{9,1},{17,25},{25,17},{2,10},{10... | collective-permute-start | bytes 393224 | tf_op jit(solution)/shard_map/ppermute | solution.py:51
  (19 other events, 27.8 us)

commit v3 on v2

--- a/solution.py
+++ b/solution.py
@@ -10,7 +10,8 @@
 
 ITERS = 2
 GROUP = 8
-SEND_TYPES = (jnp.float32, jnp.bfloat16)
+TERM_TYPES = (jnp.float32, jnp.bfloat16)
+FIELD_TYPES = (jnp.float32, jnp.bfloat16)
 
 precise = lax.Precision.HIGHEST
 F32 = jnp.float32
@@ -26,21 +27,39 @@
     return lax.dot_general(left, right, dims, precision=precise, preferred_element_type=F32)
 
 
-def dot_nt(left, right):
-    dims = (((1,), (1,)), ((), ()))
-    return lax.dot_general(left, right, dims, precision=precise, preferred_element_type=F32)
+def halves_of(value):
+    high = value.astype(BF16)
+    return high, (value - high.astype(F32)).astype(BF16)
+
+
+def dot_three(left, right, dims=(((1,), (0,)), ((), ()))):
+    times = lambda a, b: lax.dot_general(a, b, dims, preferred_element_type=F32)
+    (a, b), (c, d) = halves_of(left), halves_of(right)
+    return times(a, c) + (times(a, d) + times(b, c))
+
+
+def dot_two(left, right, dims=(((1,), (0,)), ((), ()))):
+    times = lambda a, b: lax.dot_general(a, b, dims, preferred_element_type=F32)
+    c, d = halves_of(right)
+    return times(left, c) + times(left, d)
+
+
+NT = (((1,), (1,)), ((), ()))
+TN = (((0,), (0,)), ((), ()))
 
 
 def like(shape, dtype=F32):
     return jax.ShapeDtypeStruct(shape, dtype)
 
 
-def whole(kernel, out_shape, *operands, scratch=(), flops=10**8, specs=None):
+def whole(kernel, out_shape, *operands, scratch=(), flops=10**8):
     size = sum(x.size * x.dtype.itemsize for x in operands)
     return pl.pallas_call(
         kernel,
         out_shape=out_shape,
-        in_specs=specs or [pl.BlockSpec(memory_space=pltpu.VMEM) for _ in operands],
+        in_specs=[
+            pl.BlockSpec(memory_space=pltpu.SMEM if x.size < 64 else pltpu.VMEM) for x in operands
+        ],
         scratch_shapes=list(scratch),
         cost_estimate=pl.CostEstimate(flops=flops, bytes_accessed=size, transcendentals=0),
     )(*operands)
@@ -87,87 +106,115 @@
     return block
 
 
-def solve_kernel(refine, weights, vectors, *refs):
+def emit_messages(is_even, first, last, out_a, out_b):
+    out_a[...] = jnp.where(is_even, last, first)
+    out_b[...] = jnp.where(is_even, first, last)
+
+
+def emit_messages(real, imag, coupling, tip, out_a, out_b):
+    band = coupling.shape[0]
     is_even = lax.rem(lax.axis_index("rows"), 2) == 0
+    last = jnp.concatenate([real[-band:], imag[-band:]], 1).astype(BF16)
+    last = dot_tn(coupling, last.astype(F32)).astype(BF16)
+    out_a[...] = jnp.where(is_even, last, tip)
+    out_b[...] = jnp.where(is_even, tip, last)
+
+
+def tip_of(real, imag, band):
+    return jnp.concatenate([real[:band], imag[:band]], 1).astype(BF16)
+
+
+def start_kernel(weights, vectors, coupling, inverse, base, out_a, out_b, tip):
     step = pl.program_id(0)
-    steps = pl.num_programs(0)
-    if refine:
-        factor, coupling, inverse, base, out_a, out_b, tip, current = refs
-
-        @pl.when(step == 0)
-        def _():
-            current[...] = dot_nt(vectors[...], factor[...]).astype(BF16)
-
-    else:
-        coupling, inverse, base, out_a, out_b, tip = refs
-        current = vectors
-    band = coupling.shape[0]
-    real = jnp.dot(inverse[0, 0], current[...], preferred_element_type=F32)
-    imag = jnp.dot(inverse[0, 1], current[...], preferred_element_type=F32)
+    real = jnp.dot(inverse[0, 0], vectors[...], preferred_element_type=F32)
+    imag = jnp.dot(inverse[0, 1], vectors[...], preferred_element_type=F32)
     base[...] = weights[0, 0] * real - weights[0, 1] * imag
 
     @pl.when(step == 0)
     def _():
-        tip[...] = jnp.concatenate([real[:band], imag[:band]], 1).astype(BF16)
-
-    @pl.when(step == steps - 1)
+        tip[...] = tip_of(real, imag, coupling.shape[0])
+
+    @pl.when(step == pl.num_programs(0) - 1)
     def _():
-        last = jnp.concatenate([real[-band:], imag[-band:]], 1).astype(BF16)
-        last = dot_tn(coupling[...], last.astype(F32)).astype(BF16)
-        out_a[...] = jnp.where(is_even, last, tip[...])
-        out_b[...] = jnp.where(is_even, tip[...], last)
-
-
-def solve(vectors, factor, weights, upper_tiles, inverse):
+        emit_messages(real, imag, coupling[...], tip[...], out_a, out_b)
+
+
+def start(vectors, weights, upper_tiles, inverse):
     rows, columns = vectors.shape
     band = upper_tiles.shape[1]
     tile = 2 * band if rows % (2 * band) == 0 else band
-    refine = factor is not None
     constant = lambda x: pl.BlockSpec(x.shape, lambda t: (0,) * x.ndim)
-    in_specs = [pl.BlockSpec(memory_space=pltpu.SMEM), constant(vectors)]
-    operands = [weights, vectors]
-    if refine:
-        in_specs.append(constant(factor))
-        operands.append(factor)
-    in_specs += [
-        pl.BlockSpec((band, band), lambda t: (rows // band - 1, 0)),
-        pl.BlockSpec((1, 2, tile, rows), lambda t: (0, 0, t, 0)),
-    ]
     message = like((band, 2 * columns), BF16)
-    outs = [like((rows, columns)), message, message]
-    out_specs = [pl.BlockSpec((tile, columns), lambda t: (t, 0)), constant(message), constant(message)]
-    scratch = [pltpu.VMEM((band, 2 * columns), BF16)]
-    if refine:
-        scratch += [pltpu.VMEM((rows, columns), BF16)]
     return pl.pallas_call(
-        functools.partial(solve_kernel, refine),
+        start_kernel,
         grid=(rows // tile,),
-        in_specs=in_specs,
-        out_specs=out_specs,
-        out_shape=outs,
-        scratch_shapes=scratch,
+        in_specs=[
+            pl.BlockSpec(memory_space=pltpu.SMEM),
+            constant(vectors),
+            pl.BlockSpec((band, band), lambda t: (rows // band - 1, 0)),
+            pl.BlockSpec((1, 2, tile, rows), lambda t: (0, 0, t, 0)),
+        ],
+        out_specs=[
+            pl.BlockSpec((tile, columns), lambda t: (t, 0)),
+            constant(message),
+            constant(message),
+        ],
+        out_shape=[like((rows, columns)), message, message],
+        scratch_shapes=[pltpu.VMEM((band, 2 * columns), BF16)],
         cost_estimate=pl.CostEstimate(
             flops=4 * rows * rows * columns, bytes_accessed=inverse.size * 2, transcendentals=0
         ),
-        name="solve",
-    )(*operands, upper_tiles, inverse)
-
-
-def correct_kernel(weights, base, got_a, got_b, coupling, left, right, own, *refs):
+        name="start",
+    )(weights, vectors, upper_tiles, inverse)
+
+
+def solve_kernel(weights, field, factor, upper_tiles, inverse, base, out_a, out_b, tip, current):
+    band = upper_tiles.shape[1]
+    rows = field.shape[0]
+    current[...] = dot_three(field[...], factor[...], NT).astype(BF16)
+    tile = 2 * band if rows % (2 * band) == 0 else band
+    for at in range(0, rows, tile):
+        real = jnp.dot(inverse[0, 0, at : at + tile], current[...], preferred_element_type=F32)
+        imag = jnp.dot(inverse[0, 1, at : at + tile], current[...], preferred_element_type=F32)
+        base[at : at + tile] = weights[0, 0] * real - weights[0, 1] * imag
+        if at == 0:
+            tip[...] = tip_of(real, imag, band)
+    emit_messages(real, imag, upper_tiles[-band:], tip[...], out_a, out_b)
+
+
+def solve(field, factor, weights, upper_tiles, inverse):
+    rows, columns = field.shape
+    band = upper_tiles.shape[1]
+    message = like((band, 2 * columns), BF16)
+    return whole(
+        solve_kernel,
+        [like((rows, columns)), message, message],
+        weights,
+        field,
+        factor,
+        upper_tiles,
+        inverse,
+        scratch=[pltpu.VMEM((band, 2 * columns), BF16), pltpu.VMEM((rows, columns), BF16)],
+        flops=4 * rows * rows * columns,
+    )
+
+
+def correct_kernel(weights, base, got_a, got_b, upper_tiles, inverse, own, *refs):
     sends, term = refs[:-1], refs[-1]
+    band = upper_tiles.shape[1]
+    rows, columns = base.shape
     node = lax.axis_index("node")
     is_even = lax.rem(lax.axis_index("rows"), 2) == 0
-    from_prior = jnp.where(is_even, got_b[...], got_a[...])
+    above = jnp.where(is_even, got_b[...], got_a[...])
     from_next = jnp.where(is_even, got_a[...], got_b[...])
-    below = dot(coupling[...], from_next.astype(F32)).astype(BF16)
-    product = lambda c: jnp.dot(left[0, c], from_prior, preferred_element_type=F32) + jnp.dot(
-        right[0, c], below, preferred_element_type=F32
-    )
-    real_side, imag_side = product(0), product(1)
-    columns = base.shape[1]
-    real = real_side[:, :columns] - imag_side[:, columns:]
-    imag = real_side[:, columns:] + imag_side[:, :columns]
-    term[...] = base[...] + (weights[0, 0] * real - weights[0, 1] * imag)
+    below = dot(upper_tiles[-band:], from_next.astype(F32)).astype(BF16)
+    total = base[...]
+    for edge, columns_at in ((above, 0), (below, rows - band)):
+        real, imag = edge[:, :columns].astype(F32), edge[:, columns:].astype(F32)
+        part = slice(columns_at, columns_at + band)
+        total = total + dot_two(inverse[0, 0, :, part], weights[0, 0] * real - weights[0, 1] * imag)
+        total = total - dot_two(inverse[0, 1, :, part], weights[0, 0] * imag + weights[0, 1] * real)
+    term[...] = total
     size = own.shape[0]
     for s, out in enumerate((own,) + sends):
         where = pl.multiple_of((node ^ s) * size, 8)
@@ -179,29 +226,19 @@
     band = upper_tiles.shape[1]
     count = lax.axis_size("node")
     size = rows // count
-    vmem = pl.BlockSpec(memory_space=pltpu.VMEM)
     outs = [like((size, columns))] + [like((size, columns), kind)] * (count - 1)
-    constant = lambda x: pl.BlockSpec(x.shape, lambda t: (0,) * x.ndim)
-    return pl.pallas_call(
+    return whole(
         correct_kernel,
-        grid=(1,),
-        in_specs=[
-            pl.BlockSpec(memory_space=pltpu.SMEM),
-            constant(base),
-            constant(got_a),
-            constant(got_b),
-            pl.BlockSpec((band, band), lambda t: (rows // band - 1, 0)),
-            pl.BlockSpec((1, 2, rows, band), lambda t: (0, 0, 0, 0)),
-            pl.BlockSpec((1, 2, rows, band), lambda t: (0, 0, 0, rows // band - 1)),
-        ],
-        out_specs=[constant(x) for x in outs],
-        out_shape=outs,
-        scratch_shapes=[pltpu.VMEM((rows, columns), F32)],
-        cost_estimate=pl.CostEstimate(
-            flops=16 * rows * band * columns, bytes_accessed=4 * rows * band * 2, transcendentals=0
-        ),
-        name="correct",
-    )(weights, base, got_a, got_b, upper_tiles, inverse, inverse)
+        outs,
+        weights,
+        base,
+        got_a,
+        got_b,
+        upper_tiles,
+        inverse,
+        scratch=[pltpu.VMEM((rows, columns), F32)],
+        flops=16 * rows * band * columns,
+    )
 
 
 def place(blocks, out):
@@ -215,7 +252,10 @@
     *blocks, field, head, part, matrix = refs
     place(blocks, field)
     head[...] = field[: head.shape[0]]
-    matrix[...] = dot_tn(field[...], field[...])
+    if field.dtype == BF16:
+        matrix[...] = lax.dot_general(field[...], field[...], TN, preferred_element_type=F32)
+    else:
+        matrix[...] = dot_tn(field[...], field[...])
     size = part.shape[0]
     part[...] = matrix[pl.ds(pl.multiple_of(lax.axis_index("node") * size, 8), size), :]
 
@@ -223,7 +263,12 @@
 def gram_slice(blocks, band):
     rows, columns = blocks[0].shape
     count = len(blocks)
-    outs = [like((rows * count, columns)), like((band, columns)), like((columns // count, columns))]
+    kind = blocks[0].dtype
+    outs = [
+        like((rows * count, columns), kind),
+        like((band, columns), kind),
+        like((columns // count, columns)),
+    ]
     scratch = [pltpu.VMEM((columns, columns), F32)]
     return whole(gram_kernel, outs, *blocks, scratch=scratch)
 
@@ -332,33 +377,47 @@
     return lax.ppermute(head, "rows", [(i + 1, i) for i in range(count - 1)])
 
 
-def band_kernel(field, after, diag_tiles, upper_tiles, part, image, matrix):
+def band_kernel(field, after, diag_tiles, upper_tiles, *refs):
+    earlier, (part, image, matrix) = refs[:-3], refs[-3:]
     band = after.shape[0]
     tiles = field.shape[0] // band
+    values = lambda x: x.astype(F32)
     for t in range(tiles):
         at = slice(t * band, (t + 1) * band)
         following = after[...] if t == tiles - 1 else field[(t + 1) * band : (t + 2) * band]
-        image[at] = 0.5 * dot(diag_tiles[at], field[at]) + dot(upper_tiles[at], following)
-    matrix[...] = dot_tn(field[...], image[...])
-    size = part.shape[0]
-    part[...] = matrix[pl.ds(pl.multiple_of(lax.axis_index("node") * size, 8), size), :]
-
-
-def band_slice(field, after, diag_tiles, upper_tiles):
+        image[at] = 0.5 * dot_three(diag_tiles[at], values(field[at])) + dot_three(
+            upper_tiles[at], values(following)
+        )
+    if field.dtype == BF16:
+        matrix[...] = dot_two(field[...], image[...], TN)
+    else:
+        matrix[...] = dot_three(field[...], image[...], TN)
+    size = matrix.shape[0] // lax.axis_size("node")
+    for ref in earlier:
+        part[:-size] = ref[...]
+    part[-size:] = matrix[pl.ds(pl.multiple_of(lax.axis_index("node") * size, 8), size), :]
+
+
+def band_slice(field, after, diag_tiles, upper_tiles, *earlier):
     rows, columns = field.shape
+    size = columns // lax.axis_size("node")
     return whole(
         band_kernel,
-        like((columns // lax.axis_size("node"), columns)),
+        like((size * (1 + sum(x.shape[0] // size for x in earlier)), columns)),
         field,
         after,
         diag_tiles,
         upper_tiles,
+        *earlier,
         scratch=[pltpu.VMEM((rows, columns), F32), pltpu.VMEM((columns, columns), F32)],
     )
 
 
 def last_kernel(field, factor, out):
-    out[...] = dot_nt(field[...], factor[...])
+    if field.dtype == BF16:
+        out[...] = dot_two(field[...], factor[...], NT)
+    else:
+        out[...] = dot_three(field[...], factor[...], NT)
 
 
 def projected_kernel(order, *refs):
@@ -369,7 +428,7 @@
         for step, block in enumerate(blocks):
             at = pl.multiple_of((node ^ step) * size, 8)
             matrix[pl.ds(at, size), :] = block[k * size : (k + 1) * size]
-        value = dot_nt(dot(factor[...], matrix[...]), factor[...])
+        value = dot_three(dot_three(factor[...], matrix[...]), factor[...], NT)
         out[k] = (value + value.T) * (1.0 / order)
 
 
@@ -382,30 +441,34 @@
     band = upper_tiles.shape[1]
     partners = lax.axis_size("node") - 1
     columns = subspace.shape[1]
-    factor, field = None, subspace
-    factors, parts = [], []
+    factors, parts = [], ()
     for iteration in range(ITERS):
-        base, out_a, out_b = solve(field, factor, weights, upper_tiles, inverse)
+        if iteration == 0:
+            base, out_a, out_b = start(subspace, weights, upper_tiles, inverse)
+        else:
+            base, out_a, out_b = solve(field, factor, weights, upper_tiles, inverse)
         got_a, got_b = core_swap(out_a), link_swap(out_b)
         own, *others = correct(
-            weights, base, got_a, got_b, upper_tiles, inverse, SEND_TYPES[iteration]
+            weights, base, got_a, got_b, upper_tiles, inverse, TERM_TYPES[iteration]
         )
         piece = tree_sum([own] + [x.astype(F32) for x in node_spread(others)])
+        piece = piece.astype(FIELD_TYPES[iteration])
         field, head, part = gram_slice([piece] + node_spread([piece] * partners), band)
         part = part + core_swap(part)
         following = next_head(after(head, part))
         total = chip_sum(part)
         gathered = [total] + node_spread([total] * partners)
-        parts.append(band_slice(field, after(following, total), diag_tiles, upper_tiles))
+        pair = band_slice(field, after(following, total), diag_tiles, upper_tiles, *parts)
+        parts = (pair,)
         halves = first_factor(gathered, order)
         if iteration == ITERS - 1:
-            pair = jnp.concatenate(parts, 0)
-            pair = after(pair + core_swap(pair), *gathered)
+            pair = pair + core_swap(after(pair, *gathered))
+            pair = after(pair, *halves)
             pair = chip_sum(pair)
-            pair = after(pair, *halves)
-            spread = [pair] + node_spread([pair] * partners)
         factor = second_factor(halves)
         factors.append(factor)
+    pair = after(pair, factor)
+    spread = [pair] + node_spread([pair] * partners)
     orthonormal = whole(last_kernel, like(subspace.shape), field, factor)
     projected = whole(
         functools.partial(projected_kernel, order),

time: 182 us -> 173 us (0.951)
  Pallas kernels: 65.8 us -> 62.1 us
  waiting for transfers between devices: 46.5 us -> 44.3 us
    ppermute x21, waiting for transfers between devices: 34.2 us -> 30 us  [node_swap(): return lax.ppermute(block, 'node', [(i, i ^ step) for i in range(count)])]
    ppermute x9, waiting for transfers between devices: 6.68 us -> 10.7 us  [chip_sum(): lax.ppermute(block, 'rows', route)]
    pallas_call x14, Pallas kernels: 65.8 us -> 62.1 us  [the longest x13 57.6 us: whole(): pl.pallas_call(kernel, out_shape=out_shape, in_specs=[pl.BlockSpec(memory...]
    ppermute x2, waiting for transfers between devices: 2.09 us -> 0.01 us  [next_head(): return lax.ppermute(head, 'rows', [(i + 1, i) for i in range(count - 1)])]
  transfers between devices with their start and end apart: 39 -> 39, of which waited for: 24 -> 24; matrix products, arithmetic and copies ran while one was open for 1% -> 0% of each run, Pallas kernels for 13% -> 13%
where the time goes in v3:
time: 173 us
  Pallas kernels  62.1 us (36%)
  starting transfers between devices  54.4 us (31%)
  waiting for transfers between devices  44.3 us (26%)
  local copies, waits for them, and re-layouts  7.19 us (4%)
  other arithmetic  3.75 us (2%)
    pallas_call x13, Pallas kernels, whole(): pl.pallas_call(kernel, out_shape=out_shape, in_specs=[pl.BlockSpec(memory...  57.6 us
    ppermute x21, waiting for transfers between devices, node_swap(): return lax.ppermute(block, 'node', [(i, i ^ step) for i in range(count)])  30 us
    ppermute x21, starting transfers between devices, node_swap(): return lax.ppermute(block, 'node', [(i, i ^ step) for i in range(count)])  25.6 us
    ppermute x9, starting transfers between devices, chip_sum(): lax.ppermute(block, 'rows', route)  21.3 us
    ppermute x9, waiting for transfers between devices, chip_sum(): lax.ppermute(block, 'rows', route)  10.7 us
    unnamed x56, local copies, waits for them, and re-layouts  7.19 us
    pallas_call x1, Pallas kernels, start(): pl.pallas_call(start_kernel, grid=(rows // tile,), in_specs=[pl.BlockSpec...  4.49 us
    ppermute x5, waiting for transfers between devices, core_swap(): return lax.ppermute(block, 'rows', [(i, i ^ 1) for i in range(count)])  3.65 us
  transfers between devices with their start and end apart: 39, of which 24 were waited for; matrix products, arithmetic and copies ran while one was open for 0% of the time, Pallas kernels for 13%

profile of v3, /device:TPU:0, one launch (start us, length us, event | category | flops | bytes accessed | tf_op | source)
XLA Modules:
  0.0 172.7 jit_solution(12560380134012373777)
XLA Ops:
  0.6 4.5 %start.1 = (f32[768,256]{1,0:T(8,128)}, bf16[128,512]{1,0:T(8,128)(2,1)}, bf16[128,512]{1,0:T(8,128)(2,1)}) custom-call(f32[1,2]{1,0:T(1,128)} %weights.7, bf16[768,256]{1,0:T(8,128)(2,1)} %vectors.1, f32[768,128]{1,0:T(8,128)} %upper_tiles.9, bf16[1,2,768,768]{3,2,1,0:T(8,128)(2,1)} %inverse.7), custom_call_target="tpu_custom_call" | custom-call | flops 603979776 | bytes 2359296 | tf_op jit(solution)/shard_map/start/pallas_call | solution.py:148
  7.5 4.3 %shard_map.68 = (f32[192,256]{1,0:T(8,128)}, f32[192,256]{1,0:T(8,128)}, f32[192,256]{1,0:T(8,128)}, f32[192,256]{1,0:T(8,128)}) custom-call(f32[1,2]{1,0:T(1,128)} %weights.7, f32[768,256]{1,0:T(8,128)} %get-tuple-element.37.base, bf16[128,512]{1,0:T(8,128)(2,1)} %copy-done.10, bf16[128,512]{1,0:T(8,128)(2,1)} %copy-done.13, f32[768,128]{1,0:T(8,128)} %upper_tiles.9, ...), custom_call_target="tpu_custom_call" | custom-call | flops 402653184 | bytes 3801096 | tf_op jit(solution)/shard_map/pallas_call | solution.py:57
  11.8 2.8 %collective-permute-start.2 = (f32[192,256]{1,0:T(8,128)}, f32[192,256]{1,0:T(8,128)S(1)}, u32[]{:S(2)}, u32[]{:S(2)}) collective-permute-start(f32[192,256]{1,0:T(8,128)} %get-tuple-element.41), channel_id=1, source_target_pairs={{0,8},{8,0},{16,24},{24,16},{1,9},{9,1},{17,25},{25,17},{2,10},{10... | collective-permute-start | bytes 589832 | tf_op jit(solution)/shard_map/ppermute | solution.py:70
  14.6 1.5 collective-permute-start.3
  16.2 2.3 %collective-permute-done.2 = f32[192,256]{1,0:T(8,128)S(1)} collective-permute-done((f32[192,256]{1,0:T(8,128)}, f32[192,256]{1,0:T(8,128)S(1)}, u32[]{:S(2)}, u32[]{:S(2)}) %collective-permute-start.2) | collective-permute-done | bytes 196640 | tf_op jit(solution)/shard_map/ppermute | solution.py:70
  18.5 2.9 %collective-permute-done.3 = f32[192,256]{1,0:T(8,128)S(1)} collective-permute-done((f32[192,256]{1,0:T(8,128)}, f32[192,256]{1,0:T(8,128)S(1)}, u32[]{:S(2)}, u32[]{:S(2)}) %collective-permute-start.3) | collective-permute-done | bytes 196640 | tf_op jit(solution)/shard_map/ppermute | solution.py:70
  21.4 2.2 %collective-permute-done.4 = f32[192,256]{1,0:T(8,128)S(1)} collective-permute-done((f32[192,256]{1,0:T(8,128)}, f32[192,256]{1,0:T(8,128)S(1)}, u32[]{:S(2)}, u32[]{:S(2)}) %collective-permute-start.4) | collective-permute-done | bytes 196640 | tf_op jit(solution)/shard_map/ppermute | solution.py:70
  26.2 2.0 %collective-permute-start.5 = (f32[192,256]{1,0:T(8,128)S(1)}, f32[192,256]{1,0:T(8,128)S(1)}, u32[]{:S(2)}, u32[]{:S(2)}) collective-permute-start(f32[192,256]{1,0:T(8,128)S(1)} %add_add_fusion.refs_0_), channel_id=1, source_target_pairs={{0,8},{8,0},{16,24},{24,16},{1,9},{9,1},{17,25},{25,17},{2,10},{10... | collective-permute-start | bytes 589832 | tf_op jit(solution)/shard_map/ppermute | solution.py:70
  28.2 3.2 %collective-permute-done.7.refs_3_ = f32[192,256]{1,0:T(8,128)S(1)} collective-permute-done((f32[192,256]{1,0:T(8,128)S(1)}, f32[192,256]{1,0:T(8,128)S(1)}, u32[]{:S(2)}, u32[]{:S(2)}) %collective-permute-start.7) | collective-permute-done | bytes 196640 | tf_op jit(solution)/shard_map/ppermute | solution.py:70
  31.3 5.3 %collective-permute-done.6.refs_2_ = f32[192,256]{1,0:T(8,128)S(1)} collective-permute-done((f32[192,256]{1,0:T(8,128)S(1)}, f32[192,256]{1,0:T(8,128)S(1)}, u32[]{:S(2)}, u32[]{:S(2)}) %collective-permute-start.6) | collective-permute-done | bytes 196640 | tf_op jit(solution)/shard_map/ppermute | solution.py:70
  38.0 2.8 %shard_map.69 = (f32[768,256]{1,0:T(8,128)}, f32[128,256]{1,0:T(8,128)}, f32[64,256]{1,0:T(8,128)}) custom-call(f32[192,256]{1,0:T(8,128)} %copy-done, f32[192,256]{1,0:T(8,128)} %copy-done.6, f32[192,256]{1,0:T(8,128)} %copy-done.5, f32[192,256]{1,0:T(8,128)} %copy-done.4), custom_call_target="tpu_custom_call" | custom-call | flops 100000000 | bytes 786432 | tf_op jit(solution)/shard_map/pallas_call | solution.py:57
  43.2 6.6 %collective-permute-start.11 = (f32[64,256]{1,0:T(8,128)S(1)}, f32[64,256]{1,0:T(8,128)S(1)}, u32[]{:S(2)}, u32[]{:S(2)}) collective-permute-start(f32[64,256]{1,0:T(8,128)S(1)} %add.57), channel_id=1, source_target_pairs={{0,6},{1,7},{2,4},{3,5},{4,2},{5,3},{6,0},{7,1},{8,14},{9,15},{10,... | collective-permute-start | bytes 196616 | tf_op jit(solution)/shard_map/ppermute | solution.py:101
  49.8 3.2 %collective-permute-start.10 = (f32[64,256]{1,0:T(8,128)S(1)}, f32[64,256]{1,0:T(8,128)S(1)}, u32[]{:S(2)}, u32[]{:S(2)}) collective-permute-start(f32[64,256]{1,0:T(8,128)S(1)} %add.57), channel_id=1, source_target_pairs={{0,4},{1,5},{2,6},{3,7},{4,0},{5,1},{6,2},{7,3},{8,12},{9,13},{10,... | collective-permute-start | bytes 196616 | tf_op jit(solution)/shard_map/ppermute | solution.py:101
  53.1 4.3 %collective-permute-done.10 = f32[64,256]{1,0:T(8,128)S(1)} collective-permute-done((f32[64,256]{1,0:T(8,128)S(1)}, f32[64,256]{1,0:T(8,128)S(1)}, u32[]{:S(2)}, u32[]{:S(2)}) %collective-permute-start.10) | collective-permute-done | bytes 65568 | tf_op jit(solution)/shard_map/ppermute | solution.py:101
  57.8 1.5 collective-permute-start.14
  59.3 1.5 collective-permute-start.13
  61.3 1.7 collective-permute-done.14.refs_3_
  63.7 1.3 collective-permute-done.12.refs_1_
  65.7 7.3 %shard_map.70 = (f32[128,128]{1,0:T(8,128)}, f32[128,128]{1,0:T(8,128)}, f32[128,128]{1,0:T(8,128)}, f32[1,256]{1,0:T(1,128)}) custom-call(f32[64,256]{1,0:T(8,128)} %copy-done.20, f32[64,256]{1,0:T(8,128)} %copy-done.27, f32[64,256]{1,0:T(8,128)} %copy-done.26, f32[64,256]{1,0:T(8,128)} %copy-done.25), custom_call_target="tpu_custom_call" | custom-call | flops 6000000000 | bytes 262144 | tf_op jit(solution)/shard_map/pallas_call | solution.py:57
  73.0 6.6 %shard_map.71.factor.refs_4_ = f32[256,256]{1,0:T(8,128)} custom-call(f32[128,128]{1,0:T(8,128)} %get-tuple-element.46.top, f32[128,128]{1,0:T(8,128)} %get-tuple-element.47.corner, f32[128,128]{1,0:T(8,128)} %get-tuple-element.48.rest, f32[1,256]{1,0:T(1,128)} %get-tuple-element.49.across), custom_call_target="tpu_custom_call" | custom-call | flops 6000000000 | bytes 197632 | tf_op jit(solution)/shard_map/pallas_call | solution.py:57
  79.6 4.9 %shard_map.72 = (f32[768,256]{1,0:T(8,128)}, bf16[128,512]{1,0:T(8,128)(2,1)}, bf16[128,512]{1,0:T(8,128)(2,1)}) custom-call(f32[1,2]{1,0:T(1,128)} %weights.7, f32[768,256]{1,0:T(8,128)} %get-tuple-element.44.field, f32[256,256]{1,0:T(8,128)} %shard_map.71.factor.refs_4_, f32[768,128]{1,0:T(8,128)} %upper_tiles.9, bf16[1,2,768,768]{3,2,1,0:T(8,128)(2,1)} %inverse.7), custom_call_target="tpu_custom_call" | custom-call | flops 603979776 | bytes 3801096 | tf_op jit(solution)/shard_map/pallas_call | solution.py:57
  86.8 4.2 %shard_map.73 = (f32[192,256]{1,0:T(8,128)}, bf16[192,256]{1,0:T(8,128)(2,1)}, bf16[192,256]{1,0:T(8,128)(2,1)}, bf16[192,256]{1,0:T(8,128)(2,1)}) custom-call(f32[1,2]{1,0:T(1,128)} %weights.7, f32[768,256]{1,0:T(8,128)} %get-tuple-element.50.base, bf16[128,512]{1,0:T(8,128)(2,1)} %copy-done.11, bf16[128,512]{1,0:T(8,128)(2,1)} %copy-done.14, ...), custom_call_target="tpu_custom_call" | custom-call | flops 402653184 | bytes 3801096 | tf_op jit(solution)/shard_map/pallas_call | solution.py:57
  91.8 1.3 collective-permute-start.18
  93.1 1.4 collective-permute-start.19
  94.5 1.3 collective-permute-done.17
  96.6 2.2 %collective-permute-done.19 = bf16[192,256]{1,0:T(8,128)(2,1)S(1)} collective-permute-done((bf16[192,256]{1,0:T(8,128)(2,1)}, bf16[192,256]{1,0:T(8,128)(2,1)S(1)}, u32[]{:S(2)}, u32[]{:S(2)}) %collective-permute-start.19) | collective-permute-done | bytes 98336 | tf_op jit(solution)/shard_map/ppermute | solution.py:70
  99.8 1.5 collective-permute-start.22
  102.1 1.3 collective-permute-start.20
  103.3 2.1 %collective-permute-done.22.refs_3_ = bf16[192,256]{1,0:T(8,128)(2,1)S(1)} collective-permute-done((bf16[192,256]{1,0:T(8,128)(2,1)S(1)}, bf16[192,256]{1,0:T(8,128)(2,1)S(1)}, u32[]{:S(2)}, u32[]{:S(2)}) %collective-permute-start.22) | collective-permute-done | bytes 98336 | tf_op jit(solution)/shard_map/ppermute | solution.py:70
  107.7 2.0 %shard_map.74 = (bf16[768,256]{1,0:T(8,128)(2,1)}, bf16[128,256]{1,0:T(8,128)(2,1)}, f32[64,256]{1,0:T(8,128)}) custom-call(bf16[192,256]{1,0:T(8,128)(2,1)} %copy-done.3, bf16[192,256]{1,0:T(8,128)(2,1)} %copy-done.17, bf16[192,256]{1,0:T(8,128)(2,1)} %copy-done.16, bf16[192,256]{1,0:T(8,128)(2,1)} %copy-done.15), custom_call_target="tpu_custom_call" | custom-call | flops 100000000 | bytes 393216 | tf_op jit(solution)/shard_map/pallas_call | solution.py:57
  109.7 2.6 %collective-permute-start.23 = (f32[64,256]{1,0:T(8,128)}, f32[64,256]{1,0:T(8,128)S(1)}, u32[]{:S(2)}, u32[]{:S(2)}) collective-permute-start(f32[64,256]{1,0:T(8,128)} %get-tuple-element.58), channel_id=1, source_target_pairs={{0,1},{1,0},{2,3},{3,2},{4,5},{5,4},{6,7},{7,6},{8,9},{9,8},{10,11... | collective-permute-start | bytes 196616 | tf_op jit(solution)/shard_map/ppermute | solution.py:75
  114.3 6.3 %collective-permute-start.26 = (f32[64,256]{1,0:T(8,128)S(1)}, f32[64,256]{1,0:T(8,128)S(1)}, u32[]{:S(2)}, u32[]{:S(2)}) collective-permute-start(f32[64,256]{1,0:T(8,128)S(1)} %add.64), channel_id=1, source_target_pairs={{0,6},{1,7},{2,4},{3,5},{4,2},{5,3},{6,0},{7,1},{8,14},{9,15},{10,... | collective-permute-start | bytes 196616 | tf_op jit(solution)/shard_map/ppermute | solution.py:101
  121.3 1.3 collective-permute-start.31
  122.6 1.3 collective-permute-start.30
  123.9 2.5 %collective-permute-done.25 = f32[64,256]{1,0:T(8,128)S(1)} collective-permute-done((f32[64,256]{1,0:T(8,128)S(1)}, f32[64,256]{1,0:T(8,128)S(1)}, u32[]{:S(2)}, u32[]{:S(2)}) %collective-permute-start.25) | collective-permute-done | bytes 65568 | tf_op jit(solution)/shard_map/ppermute | solution.py:101
  126.3 1.5 collective-permute-start.29
  127.8 1.4 collective-permute-start.28
  130.6 3.3 %shard_map.78.refs_0_ = f32[64,256]{1,0:T(8,128)} custom-call(f32[768,256]{1,0:T(8,128)} %get-tuple-element.44.field, f32[128,256]{1,0:T(8,128)} %copy-done.7, f32[768,128]{1,0:T(8,128)} %diag_tiles.3, f32[768,128]{1,0:T(8,128)} %upper_tiles.9), custom_call_target="tpu_custom_call" | custom-call | flops 100000000 | bytes 1703936 | tf_op jit(solution)/shard_map/pallas_call | solution.py:57
  134.5 2.9 %shard_map.79 = f32[128,256]{1,0:T(8,128)} custom-call(bf16[768,256]{1,0:T(8,128)(2,1)} %get-tuple-element.57.field, bf16[128,256]{1,0:T(8,128)(2,1)} %copy-done.19, f32[768,128]{1,0:T(8,128)} %diag_tiles.3, f32[768,128]{1,0:T(8,128)} %upper_tiles.9, f32[64,256]{1,0:T(8,128)} %shard_map.78.refs_0_), custom_call_target="tpu_custom_call" | custom-call | flops 100000000 | bytes 1310720 | tf_op jit(solution)/shard_map/pallas_call | solution.py:57
  138.1 7.3 %shard_map.75 = (f32[128,128]{1,0:T(8,128)}, f32[128,128]{1,0:T(8,128)}, f32[128,128]{1,0:T(8,128)}, f32[1,256]{1,0:T(1,128)}) custom-call(f32[64,256]{1,0:T(8,128)} %copy-done.18, f32[64,256]{1,0:T(8,128)} %copy-done.24, f32[64,256]{1,0:T(8,128)} %copy-done.23, f32[64,256]{1,0:T(8,128)} %copy-done.22), custom_call_target="tpu_custom_call" | custom-call | flops 6000000000 | bytes 262144 | tf_op jit(solution)/shard_map/pallas_call | solution.py:57
  145.4 2.7 %collective-permute-start.35 = (f32[128,256]{1,0:T(8,128)S(1)}, f32[128,256]{1,0:T(8,128)S(1)}, u32[]{:S(2)}, u32[]{:S(2)}) collective-permute-start(f32[128,256]{1,0:T(8,128)S(1)} %add.68), channel_id=1, source_target_pairs={{0,6},{1,7},{2,4},{3,5},{4,2},{5,3},{6,0},{7,1},{8,14},{9,15},{10,... | collective-permute-start | bytes 393224 | tf_op jit(solution)/shard_map/ppermute | solution.py:101
  148.3 1.6 collective-permute-start.33
  149.9 6.6 %shard_map.76.factor.refs_5_ = f32[256,256]{1,0:T(8,128)} custom-call(f32[128,128]{1,0:T(8,128)} %get-tuple-element.59.top, f32[128,128]{1,0:T(8,128)} %get-tuple-element.60.corner, f32[128,128]{1,0:T(8,128)} %get-tuple-element.61.rest, f32[1,256]{1,0:T(1,128)} %get-tuple-element.62.across), custom_call_target="tpu_custom_call" | custom-call | flops 6000000000 | bytes 197632 | tf_op jit(solution)/shard_map/pallas_call | solution.py:57
  156.5 3.5 %collective-permute-done.34 = f32[128,256]{1,0:T(8,128)S(1)} collective-permute-done((f32[128,256]{1,0:T(8,128)S(1)}, f32[128,256]{1,0:T(8,128)S(1)}, u32[]{:S(2)}, u32[]{:S(2)}) %collective-permute-start.34) | collective-permute-done | bytes 131104 | tf_op jit(solution)/shard_map/ppermute | solution.py:101
  160.1 1.5 collective-permute-start.38
  163.7 2.4 %shard_map.77 = f32[768,256]{1,0:T(8,128)} custom-call(bf16[768,256]{1,0:T(8,128)(2,1)} %get-tuple-element.57.field, f32[256,256]{1,0:T(8,128)} %shard_map.76.factor.refs_5_), custom_call_target="tpu_custom_call" | custom-call | flops 100000000 | bytes 655360 | tf_op jit(solution)/shard_map/pallas_call | solution.py:57
  167.0 1.4 collective-permute-done.37.refs_2_
  169.7 3.0 %shard_map.80 = f32[2,256,256]{2,1,0:T(8,128)} custom-call(f32[128,256]{1,0:T(8,128)} %copy-done.1, f32[128,256]{1,0:T(8,128)} %copy-done.12, f32[128,256]{1,0:T(8,128)} %copy-done.9, f32[128,256]{1,0:T(8,128)} %copy-done.8, f32[256,256]{1,0:T(8,128)} %shard_map.71.factor.refs_4_, f32[256,256]{1,0:T(8,128)} %shard_map.76.factor.refs_5_), custom_call_target="tpu_custom_call" | custom-call | flops 100000000 | bytes 1048576 | tf_op jit(solution)/shard_map/pallas_call | solution.py:57
  (108 shorter events, 28.7 us)
Async XLA Ops:
  5.1 1.7 collective-permute-start
  5.6 1.2 collective-permute-start.1
  11.8 6.7 %collective-permute-start.2 = (f32[192,256]{1,0:T(8,128)}, f32[192,256]{1,0:T(8,128)S(1)}, u32[]{:S(2)}, u32[]{:S(2)}) collective-permute-start(f32[192,256]{1,0:T(8,128)} %get-tuple-element.41), channel_id=1, source_target_pairs={{0,8},{8,0},{16,24},{24,16},{1,9},{9,1},{17,25},{25,17},{2,10},{10... | collective-permute-start | bytes 589832 | tf_op jit(solution)/shard_map/ppermute | solution.py:70
  14.6 6.7 %collective-permute-start.3 = (f32[192,256]{1,0:T(8,128)}, f32[192,256]{1,0:T(8,128)S(1)}, u32[]{:S(2)}, u32[]{:S(2)}) collective-permute-start(f32[192,256]{1,0:T(8,128)} %get-tuple-element.42), channel_id=1, source_target_pairs={{0,16},{8,24},{16,0},{24,8},{1,17},{9,25},{17,1},{25,9},{2,18},{10... | collective-permute-start | bytes 589832 | tf_op jit(solution)/shard_map/ppermute | solution.py:70
  16.2 7.4 %collective-permute-start.4 = (f32[192,256]{1,0:T(8,128)}, f32[192,256]{1,0:T(8,128)S(1)}, u32[]{:S(2)}, u32[]{:S(2)}) collective-permute-start(f32[192,256]{1,0:T(8,128)} %get-tuple-element.43), channel_id=1, source_target_pairs={{0,24},{8,16},{16,8},{24,0},{1,25},{9,17},{17,9},{25,1},{2,26},{10... | collective-permute-start | bytes 589832 | tf_op jit(solution)/shard_map/ppermute | solution.py:70
  24.6 12.0 %copy-start = (f32[192,256]{1,0:T(8,128)}, f32[192,256]{1,0:T(8,128)S(1)}, u32[]{:S(2)}) copy-start(f32[192,256]{1,0:T(8,128)S(1)} %add_add_fusion.refs_0_) | copy-start | bytes 589828
  24.6 6.7 %collective-permute-start.7 = (f32[192,256]{1,0:T(8,128)S(1)}, f32[192,256]{1,0:T(8,128)S(1)}, u32[]{:S(2)}, u32[]{:S(2)}) collective-permute-start(f32[192,256]{1,0:T(8,128)S(1)} %add_add_fusion.refs_0_), channel_id=1, source_target_pairs={{0,24},{8,16},{16,8},{24,0},{1,25},{9,17},{17,9},{25,1},{2,26},{10... | collective-permute-start | bytes 589832 | tf_op jit(solution)/shard_map/ppermute | solution.py:70
  25.2 11.4 %collective-permute-start.6 = (f32[192,256]{1,0:T(8,128)S(1)}, f32[192,256]{1,0:T(8,128)S(1)}, u32[]{:S(2)}, u32[]{:S(2)}) collective-permute-start(f32[192,256]{1,0:T(8,128)S(1)} %add_add_fusion.refs_0_), channel_id=1, source_target_pairs={{0,16},{8,24},{16,0},{24,8},{1,17},{9,25},{17,1},{25,9},{2,18},{10... | collective-permute-start | bytes 589832 | tf_op jit(solution)/shard_map/ppermute | solution.py:70
  26.2 10.4 %collective-permute-start.5 = (f32[192,256]{1,0:T(8,128)S(1)}, f32[192,256]{1,0:T(8,128)S(1)}, u32[]{:S(2)}, u32[]{:S(2)}) collective-permute-start(f32[192,256]{1,0:T(8,128)S(1)} %add_add_fusion.refs_0_), channel_id=1, source_target_pairs={{0,8},{8,0},{16,24},{24,16},{1,9},{9,1},{17,25},{25,17},{2,10},{10... | collective-permute-start | bytes 589832 | tf_op jit(solution)/shard_map/ppermute | solution.py:70
  31.3 5.3 %copy-start.4 = (f32[192,256]{1,0:T(8,128)}, f32[192,256]{1,0:T(8,128)S(1)}, u32[]{:S(2)}) copy-start(f32[192,256]{1,0:T(8,128)S(1)} %collective-permute-done.7.refs_3_) | copy-start | bytes 589828
  40.8 1.5 collective-permute-start.8
  43.2 9.9 %collective-permute-start.11 = (f32[64,256]{1,0:T(8,128)S(1)}, f32[64,256]{1,0:T(8,128)S(1)}, u32[]{:S(2)}, u32[]{:S(2)}) collective-permute-start(f32[64,256]{1,0:T(8,128)S(1)} %add.57), channel_id=1, source_target_pairs={{0,6},{1,7},{2,4},{3,5},{4,2},{5,3},{6,0},{7,1},{8,14},{9,15},{10,... | collective-permute-start | bytes 196616 | tf_op jit(solution)/shard_map/ppermute | solution.py:101
  49.8 7.7 %collective-permute-start.10 = (f32[64,256]{1,0:T(8,128)S(1)}, f32[64,256]{1,0:T(8,128)S(1)}, u32[]{:S(2)}, u32[]{:S(2)}) collective-permute-start(f32[64,256]{1,0:T(8,128)S(1)} %add.57), channel_id=1, source_target_pairs={{0,4},{1,5},{2,6},{3,7},{4,0},{5,1},{6,2},{7,3},{8,12},{9,13},{10,... | collective-permute-start | bytes 196616 | tf_op jit(solution)/shard_map/ppermute | solution.py:101
  53.0 4.8 %collective-permute-start.9 = (f32[64,256]{1,0:T(8,128)S(1)}, f32[64,256]{1,0:T(8,128)S(1)}, u32[]{:S(2)}, u32[]{:S(2)}) collective-permute-start(f32[64,256]{1,0:T(8,128)S(1)} %add.57), channel_id=1, source_target_pairs={{0,2},{1,3},{2,0},{3,1},{4,6},{5,7},{6,4},{7,5},{8,10},{9,11},{10,... | collective-permute-start | bytes 196616 | tf_op jit(solution)/shard_map/ppermute | solution.py:101
  57.8 7.3 %copy-start.20 = (f32[64,256]{1,0:T(8,128)}, f32[64,256]{1,0:T(8,128)S(1)}, u32[]{:S(2)}) copy-start(f32[64,256]{1,0:T(8,128)S(1)} %add_add_fusion.3.refs_0_) | copy-start | bytes 196612
  57.8 5.2 %collective-permute-start.14 = (f32[64,256]{1,0:T(8,128)S(1)}, f32[64,256]{1,0:T(8,128)S(1)}, u32[]{:S(2)}, u32[]{:S(2)}) collective-permute-start(f32[64,256]{1,0:T(8,128)S(1)} %add_add_fusion.3.refs_0_), channel_id=1, source_target_pairs={{0,24},{8,16},{16,8},{24,0},{1,25},{9,17},{17,9},{25,1},{2,26},{10... | collective-permute-start | bytes 196616 | tf_op jit(solution)/shard_map/ppermute | solution.py:70
  59.3 4.4 %collective-permute-start.13 = (f32[64,256]{1,0:T(8,128)S(1)}, f32[64,256]{1,0:T(8,128)S(1)}, u32[]{:S(2)}, u32[]{:S(2)}) collective-permute-start(f32[64,256]{1,0:T(8,128)S(1)} %add_add_fusion.3.refs_0_), channel_id=1, source_target_pairs={{0,16},{8,24},{16,0},{24,8},{1,17},{9,25},{17,1},{25,9},{2,18},{10... | collective-permute-start | bytes 196616 | tf_op jit(solution)/shard_map/ppermute | solution.py:70
  60.8 4.3 %collective-permute-start.12 = (f32[64,256]{1,0:T(8,128)S(1)}, f32[64,256]{1,0:T(8,128)S(1)}, u32[]{:S(2)}, u32[]{:S(2)}) collective-permute-start(f32[64,256]{1,0:T(8,128)S(1)} %add_add_fusion.3.refs_0_), channel_id=1, source_target_pairs={{0,8},{8,0},{16,24},{24,16},{1,9},{9,1},{17,25},{25,17},{2,10},{10... | collective-permute-start | bytes 196616 | tf_op jit(solution)/shard_map/ppermute | solution.py:70
  63.0 2.0 %copy-start.25 = (f32[64,256]{1,0:T(8,128)}, f32[64,256]{1,0:T(8,128)S(1)}, u32[]{:S(2)}) copy-start(f32[64,256]{1,0:T(8,128)S(1)} %collective-permute-done.14.refs_3_) | copy-start | bytes 196612
  84.6 1.6 collective-permute-start.15
  84.6 1.6 collective-permute-start.16
  86.8 34.4 %copy-start.21 = (f32[128,256]{1,0:T(8,128)S(1)}, f32[128,256]{1,0:T(8,128)}, u32[]{:S(2)}) copy-start(f32[128,256]{1,0:T(8,128)} %get-tuple-element.67) | copy-start | bytes 393220
  91.0 4.8 %collective-permute-start.17 = (bf16[192,256]{1,0:T(8,128)(2,1)}, bf16[192,256]{1,0:T(8,128)(2,1)S(1)}, u32[]{:S(2)}, u32[]{:S(2)}) collective-permute-start(bf16[192,256]{1,0:T(8,128)(2,1)} %get-tuple-element.54), channel_id=1, source_target_pairs={{0,8},{8,0},{16,24},{24,16},{1,9},{9,1},{17,25},{25,17},{2,10},{10... | collective-permute-start | bytes 294920 | tf_op jit(solution)/shard_map/ppermute | solution.py:70
  91.8 4.8 %collective-permute-start.18 = (bf16[192,256]{1,0:T(8,128)(2,1)}, bf16[192,256]{1,0:T(8,128)(2,1)S(1)}, u32[]{:S(2)}, u32[]{:S(2)}) collective-permute-start(bf16[192,256]{1,0:T(8,128)(2,1)} %get-tuple-element.55), channel_id=1, source_target_pairs={{0,16},{8,24},{16,0},{24,8},{1,17},{9,25},{17,1},{25,9},{2,18},{10... | collective-permute-start | bytes 294920 | tf_op jit(solution)/shard_map/ppermute | solution.py:70
  93.1 5.7 %collective-permute-start.19 = (bf16[192,256]{1,0:T(8,128)(2,1)}, bf16[192,256]{1,0:T(8,128)(2,1)S(1)}, u32[]{:S(2)}, u32[]{:S(2)}) collective-permute-start(bf16[192,256]{1,0:T(8,128)(2,1)} %get-tuple-element.56), channel_id=1, source_target_pairs={{0,24},{8,16},{16,8},{24,0},{1,25},{9,17},{17,9},{25,1},{2,26},{10... | collective-permute-start | bytes 294920 | tf_op jit(solution)/shard_map/ppermute | solution.py:70
  99.8 7.3 %copy-start.3 = (bf16[192,256]{1,0:T(8,128)(2,1)}, bf16[192,256]{1,0:T(8,128)(2,1)S(1)}, u32[]{:S(2)}) copy-start(bf16[192,256]{1,0:T(8,128)(2,1)S(1)} %add_convert_fusion.refs_0_) | copy-start | bytes 294916
  99.8 5.6 %collective-permute-start.22 = (bf16[192,256]{1,0:T(8,128)(2,1)S(1)}, bf16[192,256]{1,0:T(8,128)(2,1)S(1)}, u32[]{:S(2)}, u32[]{:S(2)}) collective-permute-start(bf16[192,256]{1,0:T(8,128)(2,1)S(1)} %add_convert_fusion.refs_0_), channel_id=1, source_target_pairs={{0,24},{8,16},{16,8},{24,0},{1,25},{9,17},{17,9},{25,1},{2,26},{10... | collective-permute-start | bytes 294920 | tf_op jit(solution)/shard_map/ppermute | solution.py:70
  101.3 5.1 %collective-permute-start.21 = (bf16[192,256]{1,0:T(8,128)(2,1)S(1)}, bf16[192,256]{1,0:T(8,128)(2,1)S(1)}, u32[]{:S(2)}, u32[]{:S(2)}) collective-permute-start(bf16[192,256]{1,0:T(8,128)(2,1)S(1)} %add_convert_fusion.refs_0_), channel_id=1, source_target_pairs={{0,16},{8,24},{16,0},{24,8},{1,17},{9,25},{17,1},{25,9},{2,18},{10... | collective-permute-start | bytes 294920 | tf_op jit(solution)/shard_map/ppermute | solution.py:70
  102.1 5.0 %collective-permute-start.20 = (bf16[192,256]{1,0:T(8,128)(2,1)S(1)}, bf16[192,256]{1,0:T(8,128)(2,1)S(1)}, u32[]{:S(2)}, u32[]{:S(2)}) collective-permute-start(bf16[192,256]{1,0:T(8,128)(2,1)S(1)} %add_convert_fusion.refs_0_), channel_id=1, source_target_pairs={{0,8},{8,0},{16,24},{24,16},{1,9},{9,1},{17,25},{25,17},{2,10},{10... | collective-permute-start | bytes 294920 | tf_op jit(solution)/shard_map/ppermute | solution.py:70
  109.7 3.7 %collective-permute-start.23 = (f32[64,256]{1,0:T(8,128)}, f32[64,256]{1,0:T(8,128)S(1)}, u32[]{:S(2)}, u32[]{:S(2)}) collective-permute-start(f32[64,256]{1,0:T(8,128)} %get-tuple-element.58), channel_id=1, source_target_pairs={{0,1},{1,0},{2,3},{3,2},{4,5},{5,4},{6,7},{7,6},{8,9},{9,8},{10,11... | collective-permute-start | bytes 196616 | tf_op jit(solution)/shard_map/ppermute | solution.py:75
  114.3 9.5 %collective-permute-start.26 = (f32[64,256]{1,0:T(8,128)S(1)}, f32[64,256]{1,0:T(8,128)S(1)}, u32[]{:S(2)}, u32[]{:S(2)}) collective-permute-start(f32[64,256]{1,0:T(8,128)S(1)} %add.64), channel_id=1, source_target_pairs={{0,6},{1,7},{2,4},{3,5},{4,2},{5,3},{6,0},{7,1},{8,14},{9,15},{10,... | collective-permute-start | bytes 196616 | tf_op jit(solution)/shard_map/ppermute | solution.py:101
  120.6 5.7 %collective-permute-start.25 = (f32[64,256]{1,0:T(8,128)S(1)}, f32[64,256]{1,0:T(8,128)S(1)}, u32[]{:S(2)}, u32[]{:S(2)}) collective-permute-start(f32[64,256]{1,0:T(8,128)S(1)} %add.64), channel_id=1, source_target_pairs={{0,4},{1,5},{2,6},{3,7},{4,0},{5,1},{6,2},{7,3},{8,12},{9,13},{10,... | collective-permute-start | bytes 196616 | tf_op jit(solution)/shard_map/ppermute | solution.py:101
  120.6 5.7 %collective-permute-start.24 = (f32[64,256]{1,0:T(8,128)S(1)}, f32[64,256]{1,0:T(8,128)S(1)}, u32[]{:S(2)}, u32[]{:S(2)}) collective-permute-start(f32[64,256]{1,0:T(8,128)S(1)} %add.64), channel_id=1, source_target_pairs={{0,2},{1,3},{2,0},{3,1},{4,6},{5,7},{6,4},{7,5},{8,10},{9,11},{10,... | collective-permute-start | bytes 196616 | tf_op jit(solution)/shard_map/ppermute | solution.py:101
  121.3 8.6 %collective-permute-start.31 = (f32[128,256]{1,0:T(8,128)S(1)}, f32[128,256]{1,0:T(8,128)S(1)}, u32[]{:S(2)}, u32[]{:S(2)}) collective-permute-start(f32[128,256]{1,0:T(8,128)S(1)} %copy-done.21), channel_id=1, source_target_pairs={{1,0},{2,1},{3,2},{4,3},{5,4},{6,5},{7,6},{9,8},{10,9},{11,10},{12... | collective-permute-start | bytes 393224 | tf_op jit(solution)/shard_map/ppermute | solution.py:377
  122.6 11.3 %collective-permute-start.30 = (bf16[128,256]{1,0:T(8,128)(2,1)}, bf16[128,256]{1,0:T(8,128)(2,1)S(1)}, u32[]{:S(2)}, u32[]{:S(2)}) collective-permute-start(bf16[128,256]{1,0:T(8,128)(2,1)} %get-tuple-element.64), channel_id=1, source_target_pairs={{1,0},{2,1},{3,2},{4,3},{5,4},{6,5},{7,6},{9,8},{10,9},{11,10},{12... | collective-permute-start | bytes 196616 | tf_op jit(solution)/shard_map/ppermute | solution.py:377
  126.3 11.2 %copy-start.18 = (f32[64,256]{1,0:T(8,128)}, f32[64,256]{1,0:T(8,128)S(1)}, u32[]{:S(2)}) copy-start(f32[64,256]{1,0:T(8,128)S(1)} %add_add_fusion.2.refs_0_) | copy-start | bytes 196612
  126.3 11.0 %collective-permute-start.29 = (f32[64,256]{1,0:T(8,128)S(1)}, f32[64,256]{1,0:T(8,128)S(1)}, u32[]{:S(2)}, u32[]{:S(2)}) collective-permute-start(f32[64,256]{1,0:T(8,128)S(1)} %add_add_fusion.2.refs_0_), channel_id=1, source_target_pairs={{0,24},{8,16},{16,8},{24,0},{1,25},{9,17},{17,9},{25,1},{2,26},{10... | collective-permute-start | bytes 196616 | tf_op jit(solution)/shard_map/ppermute | solution.py:70
  127.8 9.6 %collective-permute-start.28 = (f32[64,256]{1,0:T(8,128)S(1)}, f32[64,256]{1,0:T(8,128)S(1)}, u32[]{:S(2)}, u32[]{:S(2)}) collective-permute-start(f32[64,256]{1,0:T(8,128)S(1)} %add_add_fusion.2.refs_0_), channel_id=1, source_target_pairs={{0,16},{8,24},{16,0},{24,8},{1,17},{9,25},{17,1},{25,9},{2,18},{10... | collective-permute-start | bytes 196616 | tf_op jit(solution)/shard_map/ppermute | solution.py:70
  129.2 8.2 %collective-permute-start.27 = (f32[64,256]{1,0:T(8,128)S(1)}, f32[64,256]{1,0:T(8,128)S(1)}, u32[]{:S(2)}, u32[]{:S(2)}) collective-permute-start(f32[64,256]{1,0:T(8,128)S(1)} %add_add_fusion.2.refs_0_), channel_id=1, source_target_pairs={{0,8},{8,0},{16,24},{24,16},{1,9},{9,1},{17,25},{25,17},{2,10},{10... | collective-permute-start | bytes 196616 | tf_op jit(solution)/shard_map/ppermute | solution.py:70
  137.4 8.0 %copy-start.2 = (f32[128,256]{1,0:T(8,128)S(1)}, f32[128,256]{1,0:T(8,128)}, u32[]{:S(2)}) copy-start(f32[128,256]{1,0:T(8,128)} %shard_map.79) | copy-start | bytes 393220
  137.4 8.0 %collective-permute-start.32 = (f32[128,256]{1,0:T(8,128)}, f32[128,256]{1,0:T(8,128)S(1)}, u32[]{:S(2)}, u32[]{:S(2)}) collective-permute-start(f32[128,256]{1,0:T(8,128)} %shard_map.79), channel_id=1, source_target_pairs={{0,1},{1,0},{2,3},{3,2},{4,5},{5,4},{6,7},{7,6},{8,9},{9,8},{10,11... | collective-permute-start | bytes 393224 | tf_op jit(solution)/shard_map/ppermute | solution.py:75
  145.4 11.1 %collective-permute-start.35 = (f32[128,256]{1,0:T(8,128)S(1)}, f32[128,256]{1,0:T(8,128)S(1)}, u32[]{:S(2)}, u32[]{:S(2)}) collective-permute-start(f32[128,256]{1,0:T(8,128)S(1)} %add.68), channel_id=1, source_target_pairs={{0,6},{1,7},{2,4},{3,5},{4,2},{5,3},{6,0},{7,1},{8,14},{9,15},{10,... | collective-permute-start | bytes 393224 | tf_op jit(solution)/shard_map/ppermute | solution.py:101
  148.2 11.9 %collective-permute-start.34 = (f32[128,256]{1,0:T(8,128)S(1)}, f32[128,256]{1,0:T(8,128)S(1)}, u32[]{:S(2)}, u32[]{:S(2)}) collective-permute-start(f32[128,256]{1,0:T(8,128)S(1)} %add.68), channel_id=1, source_target_pairs={{0,4},{1,5},{2,6},{3,7},{4,0},{5,1},{6,2},{7,3},{8,12},{9,13},{10,... | collective-permute-start | bytes 393224 | tf_op jit(solution)/shard_map/ppermute | solution.py:101
  148.3 11.8 %collective-permute-start.33 = (f32[128,256]{1,0:T(8,128)S(1)}, f32[128,256]{1,0:T(8,128)S(1)}, u32[]{:S(2)}, u32[]{:S(2)}) collective-permute-start(f32[128,256]{1,0:T(8,128)S(1)} %add.68), channel_id=1, source_target_pairs={{0,2},{1,3},{2,0},{3,1},{4,6},{5,7},{6,4},{7,5},{8,10},{9,11},{10,... | collective-permute-start | bytes 393224 | tf_op jit(solution)/shard_map/ppermute | solution.py:101
  160.1 8.3 %copy-start.1 = (f32[128,256]{1,0:T(8,128)}, f32[128,256]{1,0:T(8,128)S(1)}, u32[]{:S(2)}) copy-start(f32[128,256]{1,0:T(8,128)S(1)} %add_add_fusion.1.refs_0_) | copy-start | bytes 393220
  160.1 6.9 %collective-permute-start.38 = (f32[128,256]{1,0:T(8,128)S(1)}, f32[128,256]{1,0:T(8,128)S(1)}, u32[]{:S(2)}, u32[]{:S(2)}) collective-permute-start(f32[128,256]{1,0:T(8,128)S(1)} %add_add_fusion.1.refs_0_), channel_id=1, source_target_pairs={{0,24},{8,16},{16,8},{24,0},{1,25},{9,17},{17,9},{25,1},{2,26},{10... | collective-permute-start | bytes 393224 | tf_op jit(solution)/shard_map/ppermute | solution.py:70
  161.6 6.8 %collective-permute-start.37 = (f32[128,256]{1,0:T(8,128)S(1)}, f32[128,256]{1,0:T(8,128)S(1)}, u32[]{:S(2)}, u32[]{:S(2)}) collective-permute-start(f32[128,256]{1,0:T(8,128)S(1)} %add_add_fusion.1.refs_0_), channel_id=1, source_target_pairs={{0,16},{8,24},{16,0},{24,8},{1,17},{9,25},{17,1},{25,9},{2,18},{10... | collective-permute-start | bytes 393224 | tf_op jit(solution)/shard_map/ppermute | solution.py:70
  162.5 5.8 %collective-permute-start.36 = (f32[128,256]{1,0:T(8,128)S(1)}, f32[128,256]{1,0:T(8,128)S(1)}, u32[]{:S(2)}, u32[]{:S(2)}) collective-permute-start(f32[128,256]{1,0:T(8,128)S(1)} %add_add_fusion.1.refs_0_), channel_id=1, source_target_pairs={{0,8},{8,0},{16,24},{24,16},{1,9},{9,1},{17,25},{25,17},{2,10},{10... | collective-permute-start | bytes 393224 | tf_op jit(solution)/shard_map/ppermute | solution.py:70
  (19 other events, 14.8 us)

commit v4 on v3

--- a/solution.py
+++ b/solution.py
@@ -49,20 +49,49 @@
 
 
 def like(shape, dtype=F32):
+    return pltpu.VMEM(shape, dtype)
+
+
+def halves_of(value):
+    high = value.astype(BF16)
+    return high, (value - high.astype(F32)).astype(BF16)
+
+
+def dot_three(left, right, dims=(((1,), (0,)), ((), ()))):
+    times = lambda a, b: lax.dot_general(a, b, dims, preferred_element_type=F32)
+    (a, b), (c, d) = halves_of(left), halves_of(right)
+    return times(a, c) + (times(a, d) + times(b, c))
+
+
+def dot_two(left, right, dims=(((1,), (0,)), ((), ()))):
+    times = lambda a, b: lax.dot_general(a, b, dims, preferred_element_type=F32)
+    c, d = halves_of(right)
+    return times(left, c) + times(left, d)
+
+
+NT = (((1,), (1,)), ((), ()))
+TN = (((0,), (0,)), ((), ()))
+
+
+def like(shape, dtype=F32):
     return jax.ShapeDtypeStruct(shape, dtype)
+
+
+def local(value):
+    return pltpu.with_memory_space_constraint(value, pltpu.VMEM)
 
 
 def whole(kernel, out_shape, *operands, scratch=(), flops=10**8):
     size = sum(x.size * x.dtype.itemsize for x in operands)
+    vmem = pl.BlockSpec(memory_space=pltpu.VMEM)
     return pl.pallas_call(
         kernel,
         out_shape=out_shape,
-        in_specs=[
-            pl.BlockSpec(memory_space=pltpu.SMEM if x.size < 64 else pltpu.VMEM) for x in operands
-        ],
+        in_specs=[vmem for _ in operands],
+        out_specs=jax.tree.map(lambda _: vmem, out_shape),
         scratch_shapes=list(scratch),
         cost_estimate=pl.CostEstimate(flops=flops, bytes_accessed=size, transcendentals=0),
-    )(*operands)
+    )(*[local(x) for x in operands])
 
 
 def node_swap(block, step):
@@ -124,67 +153,69 @@
     return jnp.concatenate([real[:band], imag[:band]], 1).astype(BF16)
 
 
-def start_kernel(weights, vectors, coupling, inverse, base, out_a, out_b, tip):
-    step = pl.program_id(0)
-    real = jnp.dot(inverse[0, 0], vectors[...], preferred_element_type=F32)
-    imag = jnp.dot(inverse[0, 1], vectors[...], preferred_element_type=F32)
-    base[...] = weights[0, 0] * real - weights[0, 1] * imag
-
-    @pl.when(step == 0)
-    def _():
-        tip[...] = tip_of(real, imag, coupling.shape[0])
-
-    @pl.when(step == pl.num_programs(0) - 1)
-    def _():
-        emit_messages(real, imag, coupling[...], tip[...], out_a, out_b)
-
-
-def start(vectors, weights, upper_tiles, inverse):
+def combine(weights, real, imag):
+    return weights[:, 0:1] * real - weights[:, 1:2] * imag
+
+
+def start_kernel(weights, source, vectors, coupling, base, out_a, out_b, inverse, tip, arrived):
+    rows = vectors.shape[0]
+    band = coupling.shape[0]
+    tile = 2 * band if rows % (2 * band) == 0 else band
+    spans = [pl.ds(at, tile) for at in range(0, rows, tile)]
+    copies = [
+        pltpu.make_async_copy(source.at[:, :, span], inverse.at[:, :, span], arrived.at[i])
+        for i, span in enumerate(spans)
+    ]
+    for copy in copies:
+        copy.start()
+    for i, span in enumerate(spans):
+        copies[i].wait()
+        real = jnp.dot(inverse[0, 0, span], vectors[...], preferred_element_type=F32)
+        imag = jnp.dot(inverse[0, 1, span], vectors[...], preferred_element_type=F32)
+        base[span] = combine(weights, real, imag)
+        if i == 0:
+            tip[...] = tip_of(real, imag, band)
+    emit_messages(real, imag, coupling[...], tip[...], out_a, out_b)
+
+
+def start(vectors, weights, coupling, inverse):
     rows, columns = vectors.shape
-    band = upper_tiles.shape[1]
-    tile = 2 * band if rows % (2 * band) == 0 else band
-    constant = lambda x: pl.BlockSpec(x.shape, lambda t: (0,) * x.ndim)
+    band = coupling.shape[1]
     message = like((band, 2 * columns), BF16)
+    vmem = pl.BlockSpec(memory_space=pltpu.VMEM)
     return pl.pallas_call(
         start_kernel,
-        grid=(rows // tile,),
-        in_specs=[
-            pl.BlockSpec(memory_space=pltpu.SMEM),
-            constant(vectors),
-            pl.BlockSpec((band, band), lambda t: (rows // band - 1, 0)),
-            pl.BlockSpec((1, 2, tile, rows), lambda t: (0, 0, t, 0)),
+        in_specs=[vmem, pl.BlockSpec(memory_space=pltpu.HBM), vmem, vmem],
+        out_specs=[vmem] * 4,
+        out_shape=[like((rows, columns)), message, message, like(inverse.shape, BF16)],
+        scratch_shapes=[
+            pltpu.VMEM((band, 2 * columns), BF16),
+            pltpu.SemaphoreType.DMA((rows // band,)),
         ],
-        out_specs=[
-            pl.BlockSpec((tile, columns), lambda t: (t, 0)),
-            constant(message),
-            constant(message),
-        ],
-        out_shape=[like((rows, columns)), message, message],
-        scratch_shapes=[pltpu.VMEM((band, 2 * columns), BF16)],
         cost_estimate=pl.CostEstimate(
             flops=4 * rows * rows * columns, bytes_accessed=inverse.size * 2, transcendentals=0
         ),
         name="start",
-    )(weights, vectors, upper_tiles, inverse)
-
-
-def solve_kernel(weights, field, factor, upper_tiles, inverse, base, out_a, out_b, tip, current):
-    band = upper_tiles.shape[1]
+    )(local(weights), inverse, local(vectors), local(coupling))
+
+
+def solve_kernel(weights, field, factor, coupling, inverse, base, out_a, out_b, tip, current):
+    band = coupling.shape[0]
     rows = field.shape[0]
     current[...] = dot_three(field[...], factor[...], NT).astype(BF16)
     tile = 2 * band if rows % (2 * band) == 0 else band
     for at in range(0, rows, tile):
         real = jnp.dot(inverse[0, 0, at : at + tile], current[...], preferred_element_type=F32)
         imag = jnp.dot(inverse[0, 1, at : at + tile], current[...], preferred_element_type=F32)
-        base[at : at + tile] = weights[0, 0] * real - weights[0, 1] * imag
+        base[at : at + tile] = combine(weights, real, imag)
         if at == 0:
             tip[...] = tip_of(real, imag, band)
-    emit_messages(real, imag, upper_tiles[-band:], tip[...], out_a, out_b)
-
-
-def solve(field, factor, weights, upper_tiles, inverse):
+    emit_messages(real, imag, coupling[...], tip[...], out_a, out_b)
+
+
+def solve(field, factor, weights, coupling, inverse):
     rows, columns = field.shape
-    band = upper_tiles.shape[1]
+    band = coupling.shape[1]
     message = like((band, 2 * columns), BF16)
     return whole(
         solve_kernel,
@@ -192,28 +223,28 @@
         weights,
         field,
         factor,
-        upper_tiles,
+        coupling,
         inverse,
         scratch=[pltpu.VMEM((band, 2 * columns), BF16), pltpu.VMEM((rows, columns), BF16)],
         flops=4 * rows * rows * columns,
     )
 
 
-def correct_kernel(weights, base, got_a, got_b, upper_tiles, inverse, own, *refs):
+def correct_kernel(weights, base, got_a, got_b, coupling, inverse, own, *refs):
     sends, term = refs[:-1], refs[-1]
-    band = upper_tiles.shape[1]
+    band = coupling.shape[1]
     rows, columns = base.shape
     node = lax.axis_index("node")
     is_even = lax.rem(lax.axis_index("rows"), 2) == 0
     above = jnp.where(is_even, got_b[...], got_a[...])
     from_next = jnp.where(is_even, got_a[...], got_b[...])
-    below = dot(upper_tiles[-band:], from_next.astype(F32)).astype(BF16)
+    below = dot(coupling[...], from_next.astype(F32)).astype(BF16)
     total = base[...]
     for edge, columns_at in ((above, 0), (below, rows - band)):
         real, imag = edge[:, :columns].astype(F32), edge[:, columns:].astype(F32)
         part = slice(columns_at, columns_at + band)
-        total = total + dot_two(inverse[0, 0, :, part], weights[0, 0] * real - weights[0, 1] * imag)
-        total = total - dot_two(inverse[0, 1, :, part], weights[0, 0] * imag + weights[0, 1] * real)
+        total = total + dot_two(inverse[0, 0, :, part], combine(weights, real, imag))
+        total = total - dot_two(inverse[0, 1, :, part], weights[:, 0:1] * imag + weights[:, 1:2] * real)
     term[...] = total
     size = own.shape[0]
     for s, out in enumerate((own,) + sends):
@@ -221,9 +252,9 @@
         out[...] = term[pl.ds(where, size), :].astype(out.dtype)
 
 
-def correct(weights, base, got_a, got_b, upper_tiles, inverse, kind):
+def correct(weights, base, got_a, got_b, coupling, inverse, kind):
     rows, columns = base.shape
-    band = upper_tiles.shape[1]
+    band = coupling.shape[1]
     count = lax.axis_size("node")
     size = rows // count
     outs = [like((size, columns))] + [like((size, columns), kind)] * (count - 1)
@@ -234,7 +265,7 @@
         base,
         got_a,
         got_b,
-        upper_tiles,
+        coupling,
         inverse,
         scratch=[pltpu.VMEM((rows, columns), F32)],
         flops=16 * rows * band * columns,
@@ -439,17 +470,18 @@
 def per_device(subspace, inverse, weights, diag_tiles, upper_tiles):
     order = float(subspace.shape[0] * lax.axis_size("rows"))
     band = upper_tiles.shape[1]
+    coupling = upper_tiles[-band:]
     partners = lax.axis_size("node") - 1
     columns = subspace.shape[1]
     factors, parts = [], ()
     for iteration in range(ITERS):
         if iteration == 0:
-            base, out_a, out_b = start(subspace, weights, upper_tiles, inverse)
+            base, out_a, out_b, inverse = start(subspace, weights, coupling, inverse)
         else:
-            base, out_a, out_b = solve(field, factor, weights, upper_tiles, inverse)
+            base, out_a, out_b = solve(field, factor, weights, coupling, inverse)
         got_a, got_b = core_swap(out_a), link_swap(out_b)
         own, *others = correct(
-            weights, base, got_a, got_b, upper_tiles, inverse, TERM_TYPES[iteration]
+            weights, base, got_a, got_b, coupling, inverse, TERM_TYPES[iteration]
         )
         piece = tree_sum([own] + [x.astype(F32) for x in node_spread(others)])
         piece = piece.astype(FIELD_TYPES[iteration])
@@ -469,10 +501,10 @@
         factors.append(factor)
     pair = after(pair, factor)
     spread = [pair] + node_spread([pair] * partners)
-    orthonormal = whole(last_kernel, like(subspace.shape), field, factor)
+    orthonormal = whole(last_kernel, jax.ShapeDtypeStruct(subspace.shape, F32), field, factor)
     projected = whole(
         functools.partial(projected_kernel, order),
-        like((ITERS, columns, columns)),
+        jax.ShapeDtypeStruct((ITERS, columns, columns), F32),
         *spread,
         *factors,
         scratch=[pltpu.VMEM((columns, columns), F32)],

time: 173 us -> 172 us (level)
  local copies, waits for them, and re-layouts: 7.19 us -> 26.6 us
  Pallas kernels: 62.1 us -> 43.9 us
  starting transfers between devices: 54.4 us -> 52.3 us
    unnamed x56 -> x68, local copies, waits for them, and re-layouts: 7.19 us -> 25.7 us
    pallas_call x14, Pallas kernels: 62.1 us -> 43.9 us  [the longest x13 40.2 us: whole(): pl.pallas_call(kernel, out_shape=out_shape, in_specs=[vmem for _ in opera...]
    ppermute x9, waiting for transfers between devices: 10.7 us -> 8.92 us  [chip_sum(): lax.ppermute(block, 'rows', route)]
  transfers between devices with their start and end apart: 39 -> 39, of which waited for: 24 -> 24; matrix products, arithmetic and copies ran while one was open for 0% -> 0% of each run, Pallas kernels for 13% -> 10%
where the time goes in v4:
time: 172 us; the launch traced here: 171 us
  starting transfers between devices  52.3 us (30%)
  Pallas kernels  43.9 us (26%)
  waiting for transfers between devices  43.8 us (25%)
  local copies, waits for them, and re-layouts  26.6 us (15%)
  other arithmetic  3.74 us (2%)
    pallas_call x13, Pallas kernels, whole(): pl.pallas_call(kernel, out_shape=out_shape, in_specs=[vmem for _ in opera...  40.2 us
    ppermute x21, waiting for transfers between devices, node_swap(): return lax.ppermute(block, 'node', [(i, i ^ step) for i in range(count)])  31.2 us
    unnamed x68, local copies, waits for them, and re-layouts  25.7 us
    ppermute x21, starting transfers between devices, node_swap(): return lax.ppermute(block, 'node', [(i, i ^ step) for i in range(count)])  25.6 us
    ppermute x9, starting transfers between devices, chip_sum(): lax.ppermute(block, 'rows', route)  20.6 us
    ppermute x9, waiting for transfers between devices, chip_sum(): lax.ppermute(block, 'rows', route)  8.92 us
    pallas_call x1, Pallas kernels, start(): pl.pallas_call(start_kernel, in_specs=[vmem, pl.BlockSpec(memory_space=pl...  3.67 us
    ppermute x5, waiting for transfers between devices, core_swap(): return lax.ppermute(block, 'rows', [(i, i ^ 1) for i in range(count)])  3.65 us
  transfers between devices with their start and end apart: 39, of which 24 were waited for; matrix products, arithmetic and copies ran while one was open for 0% of the time, Pallas kernels for 10%

profile of v4, /device:TPU:0, one launch (start us, length us, event | category | flops | bytes accessed | tf_op | source)
XLA Modules:
  0.0 171.1 jit_solution(7636999748301043044)
XLA Ops:
  3.1 3.7 %start.1 = (f32[768,256]{1,0:T(8,128)}, bf16[128,512]{1,0:T(8,128)(2,1)}, bf16[128,512]{1,0:T(8,128)(2,1)}, bf16[1,2,768,768]{3,2,1,0:T(8,128)(2,1)}) custom-call(f32[1,2]{1,0:T(1,128)S(1)} %copy-done.23, bf16[1,2,768,768]{3,2,1,0:T(8,128)(2,1)} %source.1, bf16[768,256]{1,0:T(8,128)(2,1)S(1)} %copy-done.13, f32[128,128]{1,0:T(8,128)S(1)} %slice.3.coupling), custom_call_target="tpu_custom_call" | custom-call | flops 603979776 | bytes 2359296 | tf_op jit(solution)/shard_map/start/pallas_call | solution.py:186
  9.9 1.7 copy-done
  14.5 2.1 %shard_map.68 = (f32[192,256]{1,0:T(8,128)}, f32[192,256]{1,0:T(8,128)}, f32[192,256]{1,0:T(8,128)}, f32[192,256]{1,0:T(8,128)}) custom-call(f32[1,2]{1,0:T(1,128)S(1)} %copy-done.23, f32[768,256]{1,0:T(8,128)S(1)} %copy-done.12, bf16[128,512]{1,0:T(8,128)(2,1)S(1)} %copy-done.18, bf16[128,512]{1,0:T(8,128)(2,1)S(1)} %copy-done.22, ...), custom_call_target="tpu_custom_call" | custom-call | flops 402653184 | bytes 3473416 | tf_op jit(solution)/shard_map/pallas_call | solution.py:87
  16.6 2.8 %collective-permute-start.2 = (f32[192,256]{1,0:T(8,128)}, f32[192,256]{1,0:T(8,128)S(1)}, u32[]{:S(2)}, u32[]{:S(2)}) collective-permute-start(f32[192,256]{1,0:T(8,128)} %get-tuple-element.43), channel_id=1, source_target_pairs={{0,8},{8,0},{16,24},{24,16},{1,9},{9,1},{17,25},{25,17},{2,10},{10... | collective-permute-start | bytes 589832 | tf_op jit(solution)/shard_map/ppermute | solution.py:99
  19.4 1.5 collective-permute-start.3
  21.0 2.3 %collective-permute-done.2 = f32[192,256]{1,0:T(8,128)S(1)} collective-permute-done((f32[192,256]{1,0:T(8,128)}, f32[192,256]{1,0:T(8,128)S(1)}, u32[]{:S(2)}, u32[]{:S(2)}) %collective-permute-start.2) | collective-permute-done | bytes 196640 | tf_op jit(solution)/shard_map/ppermute | solution.py:99
  23.3 2.4 %collective-permute-done.3 = f32[192,256]{1,0:T(8,128)S(1)} collective-permute-done((f32[192,256]{1,0:T(8,128)}, f32[192,256]{1,0:T(8,128)S(1)}, u32[]{:S(2)}, u32[]{:S(2)}) %collective-permute-start.3) | collective-permute-done | bytes 196640 | tf_op jit(solution)/shard_map/ppermute | solution.py:99
  25.7 3.4 %collective-permute-done.4 = f32[192,256]{1,0:T(8,128)S(1)} collective-permute-done((f32[192,256]{1,0:T(8,128)}, f32[192,256]{1,0:T(8,128)S(1)}, u32[]{:S(2)}, u32[]{:S(2)}) %collective-permute-start.4) | collective-permute-done | bytes 196640 | tf_op jit(solution)/shard_map/ppermute | solution.py:99
  31.3 2.2 %collective-permute-start.5 = (f32[192,256]{1,0:T(8,128)S(1)}, f32[192,256]{1,0:T(8,128)S(1)}, u32[]{:S(2)}, u32[]{:S(2)}) collective-permute-start(f32[192,256]{1,0:T(8,128)S(1)} %add_add_fusion.refs_0_), channel_id=1, source_target_pairs={{0,8},{8,0},{16,24},{24,16},{1,9},{9,1},{17,25},{25,17},{2,10},{10... | collective-permute-start | bytes 589832 | tf_op jit(solution)/shard_map/ppermute | solution.py:99
  33.6 3.4 %collective-permute-done.7.refs_3_ = f32[192,256]{1,0:T(8,128)S(1)} collective-permute-done((f32[192,256]{1,0:T(8,128)S(1)}, f32[192,256]{1,0:T(8,128)S(1)}, u32[]{:S(2)}, u32[]{:S(2)}) %collective-permute-start.7) | collective-permute-done | bytes 196640 | tf_op jit(solution)/shard_map/ppermute | solution.py:99
  37.0 4.7 %collective-permute-done.6.refs_2_ = f32[192,256]{1,0:T(8,128)S(1)} collective-permute-done((f32[192,256]{1,0:T(8,128)S(1)}, f32[192,256]{1,0:T(8,128)S(1)}, u32[]{:S(2)}, u32[]{:S(2)}) %collective-permute-start.6) | collective-permute-done | bytes 196640 | tf_op jit(solution)/shard_map/ppermute | solution.py:99
  41.7 1.6 shard_map.69
  45.8 6.1 %collective-permute-start.11 = (f32[64,256]{1,0:T(8,128)S(1)}, f32[64,256]{1,0:T(8,128)S(1)}, u32[]{:S(2)}, u32[]{:S(2)}) collective-permute-start(f32[64,256]{1,0:T(8,128)S(1)} %add.57), channel_id=1, source_target_pairs={{0,6},{1,7},{2,4},{3,5},{4,2},{5,3},{6,0},{7,1},{8,14},{9,15},{10,... | collective-permute-start | bytes 196616 | tf_op jit(solution)/shard_map/ppermute | solution.py:130
  51.9 2.8 %collective-permute-start.10 = (f32[64,256]{1,0:T(8,128)S(1)}, f32[64,256]{1,0:T(8,128)S(1)}, u32[]{:S(2)}, u32[]{:S(2)}) collective-permute-start(f32[64,256]{1,0:T(8,128)S(1)} %add.57), channel_id=1, source_target_pairs={{0,4},{1,5},{2,6},{3,7},{4,0},{5,1},{6,2},{7,3},{8,12},{9,13},{10,... | collective-permute-start | bytes 196616 | tf_op jit(solution)/shard_map/ppermute | solution.py:130
  54.8 4.3 %collective-permute-done.10 = f32[64,256]{1,0:T(8,128)S(1)} collective-permute-done((f32[64,256]{1,0:T(8,128)S(1)}, f32[64,256]{1,0:T(8,128)S(1)}, u32[]{:S(2)}, u32[]{:S(2)}) %collective-permute-start.10) | collective-permute-done | bytes 65568 | tf_op jit(solution)/shard_map/ppermute | solution.py:130
  59.4 1.5 collective-permute-start.14
  61.0 1.4 collective-permute-start.13
  63.0 1.7 collective-permute-done.14.refs_3_
  66.6 6.4 %shard_map.70 = (f32[128,128]{1,0:T(8,128)}, f32[128,128]{1,0:T(8,128)}, f32[128,128]{1,0:T(8,128)}, f32[1,256]{1,0:T(1,128)}) custom-call(f32[64,256]{1,0:T(8,128)S(1)} %add_add_fusion.3.refs_0_, f32[64,256]{1,0:T(8,128)S(1)} %collective-permute-done.12.refs_1_, f32[64,256]{1,0:T(8,128)S(1)} %collective-permute-done.13.refs_2_, ...), custom_call_target="tpu_custom_call" | custom-call | flops 6000000000 | bytes 262144 | tf_op jit(solution)/shard_map/pallas_call | solution.py:87
  76.2 5.7 %shard_map.71.factor.refs_4_ = f32[256,256]{1,0:T(8,128)} custom-call(f32[128,128]{1,0:T(8,128)S(1)} %copy-done.28, f32[128,128]{1,0:T(8,128)S(1)} %copy-done.29, f32[128,128]{1,0:T(8,128)S(1)} %copy-done.30, f32[1,256]{1,0:T(1,128)S(1)} %copy-done.32), custom_call_target="tpu_custom_call" | custom-call | flops 6000000000 | bytes 197632 | tf_op jit(solution)/shard_map/pallas_call | solution.py:87
  81.9 1.7 copy-done.1
  84.5 2.8 %shard_map.72 = (f32[768,256]{1,0:T(8,128)}, bf16[128,512]{1,0:T(8,128)(2,1)}, bf16[128,512]{1,0:T(8,128)(2,1)}) custom-call(f32[1,2]{1,0:T(1,128)S(1)} %copy-done.24, f32[768,256]{1,0:T(8,128)S(1)} %copy-done.2, f32[256,256]{1,0:T(8,128)S(1)} %copy-done.8, f32[128,128]{1,0:T(8,128)S(1)} %slice.3.coupling, bf16[1,2,768,768]{3,2,1,0:T(8,128)(2,1)S(1)} %copy-done.1), custom_call_target="tpu_custom_call" | custom-call | flops 603979776 | bytes 3473416 | tf_op jit(solution)/shard_map/pallas_call | solution.py:87
  93.2 2.0 %shard_map.73 = (f32[192,256]{1,0:T(8,128)}, bf16[192,256]{1,0:T(8,128)(2,1)}, bf16[192,256]{1,0:T(8,128)(2,1)}, bf16[192,256]{1,0:T(8,128)(2,1)}) custom-call(f32[1,2]{1,0:T(1,128)S(1)} %copy-done.24, f32[768,256]{1,0:T(8,128)S(1)} %copy-done.11, bf16[128,512]{1,0:T(8,128)(2,1)S(1)} %copy-done.16, bf16[128,512]{1,0:T(8,128)(2,1)S(1)} %copy-done.20, ...), custom_call_target="tpu_custom_call" | custom-call | flops 402653184 | bytes 3473416 | tf_op jit(solution)/shard_map/pallas_call | solution.py:87
  95.8 1.4 collective-permute-start.18
  97.2 1.4 collective-permute-start.19
  98.7 1.3 collective-permute-done.17
  100.6 2.5 %collective-permute-done.19 = bf16[192,256]{1,0:T(8,128)(2,1)S(1)} collective-permute-done((bf16[192,256]{1,0:T(8,128)(2,1)}, bf16[192,256]{1,0:T(8,128)(2,1)S(1)}, u32[]{:S(2)}, u32[]{:S(2)}) %collective-permute-start.19) | collective-permute-done | bytes 98336 | tf_op jit(solution)/shard_map/ppermute | solution.py:99
  104.1 1.5 collective-permute-start.22
  106.0 1.6 collective-permute-start.20
  107.6 2.1 %collective-permute-done.22.refs_3_ = bf16[192,256]{1,0:T(8,128)(2,1)S(1)} collective-permute-done((bf16[192,256]{1,0:T(8,128)(2,1)S(1)}, bf16[192,256]{1,0:T(8,128)(2,1)S(1)}, u32[]{:S(2)}, u32[]{:S(2)}) %collective-permute-start.22) | collective-permute-done | bytes 98336 | tf_op jit(solution)/shard_map/ppermute | solution.py:99
  115.6 6.5 %collective-permute-start.26 = (f32[64,256]{1,0:T(8,128)S(1)}, f32[64,256]{1,0:T(8,128)S(1)}, u32[]{:S(2)}, u32[]{:S(2)}) collective-permute-start(f32[64,256]{1,0:T(8,128)S(1)} %add.64), channel_id=1, source_target_pairs={{0,6},{1,7},{2,4},{3,5},{4,2},{5,3},{6,0},{7,1},{8,14},{9,15},{10,... | collective-permute-start | bytes 196616 | tf_op jit(solution)/shard_map/ppermute | solution.py:130
  122.8 1.3 collective-permute-start.31
  124.0 1.3 collective-permute-start.30
  125.4 2.6 %collective-permute-done.25 = f32[64,256]{1,0:T(8,128)S(1)} collective-permute-done((f32[64,256]{1,0:T(8,128)S(1)}, f32[64,256]{1,0:T(8,128)S(1)}, u32[]{:S(2)}, u32[]{:S(2)}) %collective-permute-start.25) | collective-permute-done | bytes 65568 | tf_op jit(solution)/shard_map/ppermute | solution.py:130
  128.0 1.5 collective-permute-start.29
  134.7 1.8 %shard_map.78.refs_0_ = f32[64,256]{1,0:T(8,128)} custom-call(f32[768,256]{1,0:T(8,128)S(1)} %copy-done.3, f32[128,256]{1,0:T(8,128)S(1)} %collective-permute-done.31.after, f32[768,128]{1,0:T(8,128)S(1)} %copy-done.5, f32[768,128]{1,0:T(8,128)S(1)} %copy-done.4), custom_call_target="tpu_custom_call" | custom-call | flops 100000000 | bytes 1703936 | tf_op jit(solution)/shard_map/pallas_call | solution.py:87
  137.4 1.6 shard_map.79
  139.1 6.4 %shard_map.75 = (f32[128,128]{1,0:T(8,128)}, f32[128,128]{1,0:T(8,128)}, f32[128,128]{1,0:T(8,128)}, f32[1,256]{1,0:T(1,128)}) custom-call(f32[64,256]{1,0:T(8,128)S(1)} %add_add_fusion.2.refs_0_, f32[64,256]{1,0:T(8,128)S(1)} %collective-permute-done.27.refs_1_, f32[64,256]{1,0:T(8,128)S(1)} %collective-permute-done.28.refs_2_, ...), custom_call_target="tpu_custom_call" | custom-call | flops 6000000000 | bytes 262144 | tf_op jit(solution)/shard_map/pallas_call | solution.py:87
  145.6 2.6 %collective-permute-start.35 = (f32[128,256]{1,0:T(8,128)S(1)}, f32[128,256]{1,0:T(8,128)S(1)}, u32[]{:S(2)}, u32[]{:S(2)}) collective-permute-start(f32[128,256]{1,0:T(8,128)S(1)} %add.68), channel_id=1, source_target_pairs={{0,6},{1,7},{2,4},{3,5},{4,2},{5,3},{6,0},{7,1},{8,14},{9,15},{10,... | collective-permute-start | bytes 393224 | tf_op jit(solution)/shard_map/ppermute | solution.py:130
  148.3 1.8 %collective-permute-start.33 = (f32[128,256]{1,0:T(8,128)S(1)}, f32[128,256]{1,0:T(8,128)S(1)}, u32[]{:S(2)}, u32[]{:S(2)}) collective-permute-start(f32[128,256]{1,0:T(8,128)S(1)} %add.68), channel_id=1, source_target_pairs={{0,2},{1,3},{2,0},{3,1},{4,6},{5,7},{6,4},{7,5},{8,10},{9,11},{10,... | collective-permute-start | bytes 393224 | tf_op jit(solution)/shard_map/ppermute | solution.py:130
  153.2 5.7 %shard_map.76.factor.refs_5_ = f32[256,256]{1,0:T(8,128)} custom-call(f32[128,128]{1,0:T(8,128)S(1)} %copy-done.25, f32[128,128]{1,0:T(8,128)S(1)} %copy-done.26, f32[128,128]{1,0:T(8,128)S(1)} %copy-done.27, f32[1,256]{1,0:T(1,128)S(1)} %copy-done.31), custom_call_target="tpu_custom_call" | custom-call | flops 6000000000 | bytes 197632 | tf_op jit(solution)/shard_map/pallas_call | solution.py:87
  158.9 1.7 collective-permute-done.34
  160.6 1.7 collective-permute-start.38
  162.3 1.3 collective-permute-start.37
  165.1 1.3 shard_map.77
  166.4 1.4 collective-permute-done.38.refs_3_
  167.8 1.6 collective-permute-done.37.refs_2_
  169.4 1.7 %shard_map.80 = f32[2,256,256]{2,1,0:T(8,128)} custom-call(f32[128,256]{1,0:T(8,128)S(1)} %add_add_fusion.1.refs_0_, f32[128,256]{1,0:T(8,128)S(1)} %collective-permute-done.36.refs_1_, f32[128,256]{1,0:T(8,128)S(1)} %collective-permute-done.37.refs_2_, f32[128,256]{1,0:T(8,128)S(1)} %collective-permute-done.38.refs_3_, f32[256,256]{1,0:T(8,128)S(1)} %copy-done.9, ...), custom_call_target="tpu_custom_call" | custom-call | flops 100000000 | bytes 1048576 | tf_op jit(solution)/shard_map/pallas_call | solution.py:87
  (121 shorter events, 46.4 us)
Async XLA Ops:
  6.8 1.8 %collective-permute-start = (bf16[128,512]{1,0:T(8,128)(2,1)}, bf16[128,512]{1,0:T(8,128)(2,1)S(1)}, u32[]{:S(2)}, u32[]{:S(2)}) collective-permute-start(bf16[128,512]{1,0:T(8,128)(2,1)} %get-tuple-element.39), channel_id=1, source_target_pairs={{0,1},{1,0},{2,3},{3,2},{4,5},{5,4},{6,7},{7,6},{8,9},{9,8},{10,11... | collective-permute-start | bytes 393224 | tf_op jit(solution)/shard_map/ppermute | solution.py:104
  7.4 1.9 %collective-permute-start.1 = (bf16[128,512]{1,0:T(8,128)(2,1)}, bf16[128,512]{1,0:T(8,128)(2,1)S(1)}, u32[]{:S(2)}, u32[]{:S(2)}) collective-permute-start(bf16[128,512]{1,0:T(8,128)(2,1)} %get-tuple-element.40), channel_id=1, source_target_pairs={{1,2},{3,4},{5,6},{2,1},{4,3},{6,5},{9,10},{11,12},{13,14},{10,9},... | collective-permute-start | bytes 393224 | tf_op jit(solution)/shard_map/ppermute | solution.py:110
  9.9 1.7 copy-start
  16.6 6.7 %collective-permute-start.2 = (f32[192,256]{1,0:T(8,128)}, f32[192,256]{1,0:T(8,128)S(1)}, u32[]{:S(2)}, u32[]{:S(2)}) collective-permute-start(f32[192,256]{1,0:T(8,128)} %get-tuple-element.43), channel_id=1, source_target_pairs={{0,8},{8,0},{16,24},{24,16},{1,9},{9,1},{17,25},{25,17},{2,10},{10... | collective-permute-start | bytes 589832 | tf_op jit(solution)/shard_map/ppermute | solution.py:99
  19.4 6.2 %collective-permute-start.3 = (f32[192,256]{1,0:T(8,128)}, f32[192,256]{1,0:T(8,128)S(1)}, u32[]{:S(2)}, u32[]{:S(2)}) collective-permute-start(f32[192,256]{1,0:T(8,128)} %get-tuple-element.44), channel_id=1, source_target_pairs={{0,16},{8,24},{16,0},{24,8},{1,17},{9,25},{17,1},{25,9},{2,18},{10... | collective-permute-start | bytes 589832 | tf_op jit(solution)/shard_map/ppermute | solution.py:99
  21.0 8.0 %collective-permute-start.4 = (f32[192,256]{1,0:T(8,128)}, f32[192,256]{1,0:T(8,128)S(1)}, u32[]{:S(2)}, u32[]{:S(2)}) collective-permute-start(f32[192,256]{1,0:T(8,128)} %get-tuple-element.45), channel_id=1, source_target_pairs={{0,24},{8,16},{16,8},{24,0},{1,25},{9,17},{17,9},{25,1},{2,26},{10... | collective-permute-start | bytes 589832 | tf_op jit(solution)/shard_map/ppermute | solution.py:99
  30.0 7.0 %collective-permute-start.7 = (f32[192,256]{1,0:T(8,128)S(1)}, f32[192,256]{1,0:T(8,128)S(1)}, u32[]{:S(2)}, u32[]{:S(2)}) collective-permute-start(f32[192,256]{1,0:T(8,128)S(1)} %add_add_fusion.refs_0_), channel_id=1, source_target_pairs={{0,24},{8,16},{16,8},{24,0},{1,25},{9,17},{17,9},{25,1},{2,26},{10... | collective-permute-start | bytes 589832 | tf_op jit(solution)/shard_map/ppermute | solution.py:99
  30.4 11.3 %collective-permute-start.6 = (f32[192,256]{1,0:T(8,128)S(1)}, f32[192,256]{1,0:T(8,128)S(1)}, u32[]{:S(2)}, u32[]{:S(2)}) collective-permute-start(f32[192,256]{1,0:T(8,128)S(1)} %add_add_fusion.refs_0_), channel_id=1, source_target_pairs={{0,16},{8,24},{16,0},{24,8},{1,17},{9,25},{17,1},{25,9},{2,18},{10... | collective-permute-start | bytes 589832 | tf_op jit(solution)/shard_map/ppermute | solution.py:99
  31.3 10.3 %collective-permute-start.5 = (f32[192,256]{1,0:T(8,128)S(1)}, f32[192,256]{1,0:T(8,128)S(1)}, u32[]{:S(2)}, u32[]{:S(2)}) collective-permute-start(f32[192,256]{1,0:T(8,128)S(1)} %add_add_fusion.refs_0_), channel_id=1, source_target_pairs={{0,8},{8,0},{16,24},{24,16},{1,9},{9,1},{17,25},{25,17},{2,10},{10... | collective-permute-start | bytes 589832 | tf_op jit(solution)/shard_map/ppermute | solution.py:99
  43.3 1.6 collective-permute-start.8
  45.8 9.0 %collective-permute-start.11 = (f32[64,256]{1,0:T(8,128)S(1)}, f32[64,256]{1,0:T(8,128)S(1)}, u32[]{:S(2)}, u32[]{:S(2)}) collective-permute-start(f32[64,256]{1,0:T(8,128)S(1)} %add.57), channel_id=1, source_target_pairs={{0,6},{1,7},{2,4},{3,5},{4,2},{5,3},{6,0},{7,1},{8,14},{9,15},{10,... | collective-permute-start | bytes 196616 | tf_op jit(solution)/shard_map/ppermute | solution.py:130
  51.9 7.2 %collective-permute-start.10 = (f32[64,256]{1,0:T(8,128)S(1)}, f32[64,256]{1,0:T(8,128)S(1)}, u32[]{:S(2)}, u32[]{:S(2)}) collective-permute-start(f32[64,256]{1,0:T(8,128)S(1)} %add.57), channel_id=1, source_target_pairs={{0,4},{1,5},{2,6},{3,7},{4,0},{5,1},{6,2},{7,3},{8,12},{9,13},{10,... | collective-permute-start | bytes 196616 | tf_op jit(solution)/shard_map/ppermute | solution.py:130
  54.6 4.8 %collective-permute-start.9 = (f32[64,256]{1,0:T(8,128)S(1)}, f32[64,256]{1,0:T(8,128)S(1)}, u32[]{:S(2)}, u32[]{:S(2)}) collective-permute-start(f32[64,256]{1,0:T(8,128)S(1)} %add.57), channel_id=1, source_target_pairs={{0,2},{1,3},{2,0},{3,1},{4,6},{5,7},{6,4},{7,5},{8,10},{9,11},{10,... | collective-permute-start | bytes 196616 | tf_op jit(solution)/shard_map/ppermute | solution.py:130
  59.4 5.2 %collective-permute-start.14 = (f32[64,256]{1,0:T(8,128)S(1)}, f32[64,256]{1,0:T(8,128)S(1)}, u32[]{:S(2)}, u32[]{:S(2)}) collective-permute-start(f32[64,256]{1,0:T(8,128)S(1)} %add_add_fusion.3.refs_0_), channel_id=1, source_target_pairs={{0,24},{8,16},{16,8},{24,0},{1,25},{9,17},{17,9},{25,1},{2,26},{10... | collective-permute-start | bytes 196616 | tf_op jit(solution)/shard_map/ppermute | solution.py:99
  61.0 4.4 %collective-permute-start.13 = (f32[64,256]{1,0:T(8,128)S(1)}, f32[64,256]{1,0:T(8,128)S(1)}, u32[]{:S(2)}, u32[]{:S(2)}) collective-permute-start(f32[64,256]{1,0:T(8,128)S(1)} %add_add_fusion.3.refs_0_), channel_id=1, source_target_pairs={{0,16},{8,24},{16,0},{24,8},{1,17},{9,25},{17,1},{25,9},{2,18},{10... | collective-permute-start | bytes 196616 | tf_op jit(solution)/shard_map/ppermute | solution.py:99
  62.4 4.3 %collective-permute-start.12 = (f32[64,256]{1,0:T(8,128)S(1)}, f32[64,256]{1,0:T(8,128)S(1)}, u32[]{:S(2)}, u32[]{:S(2)}) collective-permute-start(f32[64,256]{1,0:T(8,128)S(1)} %add_add_fusion.3.refs_0_), channel_id=1, source_target_pairs={{0,8},{8,0},{16,24},{24,16},{1,9},{9,1},{17,25},{25,17},{2,10},{10... | collective-permute-start | bytes 196616 | tf_op jit(solution)/shard_map/ppermute | solution.py:99
  76.2 5.7 %copy-start.2 = (f32[768,256]{1,0:T(8,128)S(1)}, f32[768,256]{1,0:T(8,128)}, u32[]{:S(2)}) copy-start(f32[768,256]{1,0:T(8,128)} %get-tuple-element.46.field) | copy-start | bytes 2359300
  76.2 5.7 %copy-start.24 = (f32[1,2]{1,0:T(1,128)S(1)}, f32[1,2]{1,0:T(1,128)}, u32[]{:S(2)}) copy-start(f32[1,2]{1,0:T(1,128)} %weights.7) | copy-start | bytes 28
  81.9 1.7 copy-start.1
  87.3 1.6 collective-permute-start.15
  87.3 2.2 %collective-permute-start.16 = (bf16[128,512]{1,0:T(8,128)(2,1)}, bf16[128,512]{1,0:T(8,128)(2,1)S(1)}, u32[]{:S(2)}, u32[]{:S(2)}) collective-permute-start(bf16[128,512]{1,0:T(8,128)(2,1)} %get-tuple-element.54), channel_id=1, source_target_pairs={{1,2},{3,4},{5,6},{2,1},{4,3},{6,5},{9,10},{11,12},{13,14},{10,9},... | collective-permute-start | bytes 393224 | tf_op jit(solution)/shard_map/ppermute | solution.py:110
  95.2 41.4 %copy-start.6 = (f32[768,128]{1,0:T(8,128)S(1)}, f32[768,128]{1,0:T(8,128)}, u32[]{:S(2)}) copy-start(f32[768,128]{1,0:T(8,128)} %diag_tiles.3) | copy-start | bytes 1179652
  95.2 4.8 %collective-permute-start.17 = (bf16[192,256]{1,0:T(8,128)(2,1)}, bf16[192,256]{1,0:T(8,128)(2,1)S(1)}, u32[]{:S(2)}, u32[]{:S(2)}) collective-permute-start(bf16[192,256]{1,0:T(8,128)(2,1)} %get-tuple-element.56), channel_id=1, source_target_pairs={{0,8},{8,0},{16,24},{24,16},{1,9},{9,1},{17,25},{25,17},{2,10},{10... | collective-permute-start | bytes 294920 | tf_op jit(solution)/shard_map/ppermute | solution.py:99
  95.8 4.8 %collective-permute-start.18 = (bf16[192,256]{1,0:T(8,128)(2,1)}, bf16[192,256]{1,0:T(8,128)(2,1)S(1)}, u32[]{:S(2)}, u32[]{:S(2)}) collective-permute-start(bf16[192,256]{1,0:T(8,128)(2,1)} %get-tuple-element.57), channel_id=1, source_target_pairs={{0,16},{8,24},{16,0},{24,8},{1,17},{9,25},{17,1},{25,9},{2,18},{10... | collective-permute-start | bytes 294920 | tf_op jit(solution)/shard_map/ppermute | solution.py:99
  97.2 5.9 %collective-permute-start.19 = (bf16[192,256]{1,0:T(8,128)(2,1)}, bf16[192,256]{1,0:T(8,128)(2,1)S(1)}, u32[]{:S(2)}, u32[]{:S(2)}) collective-permute-start(bf16[192,256]{1,0:T(8,128)(2,1)} %get-tuple-element.58), channel_id=1, source_target_pairs={{0,24},{8,16},{16,8},{24,0},{1,25},{9,17},{17,9},{25,1},{2,26},{10... | collective-permute-start | bytes 294920 | tf_op jit(solution)/shard_map/ppermute | solution.py:99
  104.1 5.6 %collective-permute-start.22 = (bf16[192,256]{1,0:T(8,128)(2,1)S(1)}, bf16[192,256]{1,0:T(8,128)(2,1)S(1)}, u32[]{:S(2)}, u32[]{:S(2)}) collective-permute-start(bf16[192,256]{1,0:T(8,128)(2,1)S(1)} %add_convert_fusion.refs_0_), channel_id=1, source_target_pairs={{0,24},{8,16},{16,8},{24,0},{1,25},{9,17},{17,9},{25,1},{2,26},{10... | collective-permute-start | bytes 294920 | tf_op jit(solution)/shard_map/ppermute | solution.py:99
  105.5 5.4 %collective-permute-start.21 = (bf16[192,256]{1,0:T(8,128)(2,1)S(1)}, bf16[192,256]{1,0:T(8,128)(2,1)S(1)}, u32[]{:S(2)}, u32[]{:S(2)}) collective-permute-start(bf16[192,256]{1,0:T(8,128)(2,1)S(1)} %add_convert_fusion.refs_0_), channel_id=1, source_target_pairs={{0,16},{8,24},{16,0},{24,8},{1,17},{9,25},{17,1},{25,9},{2,18},{10... | collective-permute-start | bytes 294920 | tf_op jit(solution)/shard_map/ppermute | solution.py:99
  106.0 5.6 %collective-permute-start.20 = (bf16[192,256]{1,0:T(8,128)(2,1)S(1)}, bf16[192,256]{1,0:T(8,128)(2,1)S(1)}, u32[]{:S(2)}, u32[]{:S(2)}) collective-permute-start(bf16[192,256]{1,0:T(8,128)(2,1)S(1)} %add_convert_fusion.refs_0_), channel_id=1, source_target_pairs={{0,8},{8,0},{16,24},{24,16},{1,9},{9,1},{17,25},{25,17},{2,10},{10... | collective-permute-start | bytes 294920 | tf_op jit(solution)/shard_map/ppermute | solution.py:99
  112.6 23.9 %copy-start.7 = (bf16[768,256]{1,0:T(8,128)(2,1)S(1)}, bf16[768,256]{1,0:T(8,128)(2,1)}, u32[]{:S(2)}) copy-start(bf16[768,256]{1,0:T(8,128)(2,1)} %get-tuple-element.59.field) | copy-start | bytes 1179652
  112.6 2.1 %collective-permute-start.23 = (f32[64,256]{1,0:T(8,128)}, f32[64,256]{1,0:T(8,128)S(1)}, u32[]{:S(2)}, u32[]{:S(2)}) collective-permute-start(f32[64,256]{1,0:T(8,128)} %get-tuple-element.60), channel_id=1, source_target_pairs={{0,1},{1,0},{2,3},{3,2},{4,5},{5,4},{6,7},{7,6},{8,9},{9,8},{10,11... | collective-permute-start | bytes 196616 | tf_op jit(solution)/shard_map/ppermute | solution.py:104
  115.6 9.8 %collective-permute-start.26 = (f32[64,256]{1,0:T(8,128)S(1)}, f32[64,256]{1,0:T(8,128)S(1)}, u32[]{:S(2)}, u32[]{:S(2)}) collective-permute-start(f32[64,256]{1,0:T(8,128)S(1)} %add.64), channel_id=1, source_target_pairs={{0,6},{1,7},{2,4},{3,5},{4,2},{5,3},{6,0},{7,1},{8,14},{9,15},{10,... | collective-permute-start | bytes 196616 | tf_op jit(solution)/shard_map/ppermute | solution.py:130
  122.1 5.8 %collective-permute-start.25 = (f32[64,256]{1,0:T(8,128)S(1)}, f32[64,256]{1,0:T(8,128)S(1)}, u32[]{:S(2)}, u32[]{:S(2)}) collective-permute-start(f32[64,256]{1,0:T(8,128)S(1)} %add.64), channel_id=1, source_target_pairs={{0,4},{1,5},{2,6},{3,7},{4,0},{5,1},{6,2},{7,3},{8,12},{9,13},{10,... | collective-permute-start | bytes 196616 | tf_op jit(solution)/shard_map/ppermute | solution.py:130
  122.1 5.8 %collective-permute-start.24 = (f32[64,256]{1,0:T(8,128)S(1)}, f32[64,256]{1,0:T(8,128)S(1)}, u32[]{:S(2)}, u32[]{:S(2)}) collective-permute-start(f32[64,256]{1,0:T(8,128)S(1)} %add.64), channel_id=1, source_target_pairs={{0,2},{1,3},{2,0},{3,1},{4,6},{5,7},{6,4},{7,5},{8,10},{9,11},{10,... | collective-permute-start | bytes 196616 | tf_op jit(solution)/shard_map/ppermute | solution.py:130
  122.8 8.8 %collective-permute-start.31 = (f32[128,256]{1,0:T(8,128)}, f32[128,256]{1,0:T(8,128)S(1)}, u32[]{:S(2)}, u32[]{:S(2)}) collective-permute-start(f32[128,256]{1,0:T(8,128)} %get-tuple-element.69), channel_id=1, source_target_pairs={{1,0},{2,1},{3,2},{4,3},{5,4},{6,5},{7,6},{9,8},{10,9},{11,10},{12... | collective-permute-start | bytes 393224 | tf_op jit(solution)/shard_map/ppermute | solution.py:408
  124.0 12.5 %collective-permute-start.30 = (bf16[128,256]{1,0:T(8,128)(2,1)}, bf16[128,256]{1,0:T(8,128)(2,1)S(1)}, u32[]{:S(2)}, u32[]{:S(2)}) collective-permute-start(bf16[128,256]{1,0:T(8,128)(2,1)} %get-tuple-element.66), channel_id=1, source_target_pairs={{1,0},{2,1},{3,2},{4,3},{5,4},{6,5},{7,6},{9,8},{10,9},{11,10},{12... | collective-permute-start | bytes 196616 | tf_op jit(solution)/shard_map/ppermute | solution.py:408
  128.0 11.0 %collective-permute-start.29 = (f32[64,256]{1,0:T(8,128)S(1)}, f32[64,256]{1,0:T(8,128)S(1)}, u32[]{:S(2)}, u32[]{:S(2)}) collective-permute-start(f32[64,256]{1,0:T(8,128)S(1)} %add_add_fusion.2.refs_0_), channel_id=1, source_target_pairs={{0,24},{8,16},{16,8},{24,0},{1,25},{9,17},{17,9},{25,1},{2,26},{10... | collective-permute-start | bytes 196616 | tf_op jit(solution)/shard_map/ppermute | solution.py:99
  129.5 9.5 %collective-permute-start.28 = (f32[64,256]{1,0:T(8,128)S(1)}, f32[64,256]{1,0:T(8,128)S(1)}, u32[]{:S(2)}, u32[]{:S(2)}) collective-permute-start(f32[64,256]{1,0:T(8,128)S(1)} %add_add_fusion.2.refs_0_), channel_id=1, source_target_pairs={{0,16},{8,24},{16,0},{24,8},{1,17},{9,25},{17,1},{25,9},{2,18},{10... | collective-permute-start | bytes 196616 | tf_op jit(solution)/shard_map/ppermute | solution.py:99
  130.8 8.2 %collective-permute-start.27 = (f32[64,256]{1,0:T(8,128)S(1)}, f32[64,256]{1,0:T(8,128)S(1)}, u32[]{:S(2)}, u32[]{:S(2)}) collective-permute-start(f32[64,256]{1,0:T(8,128)S(1)} %add_add_fusion.2.refs_0_), channel_id=1, source_target_pairs={{0,8},{8,0},{16,24},{24,16},{1,9},{9,1},{17,25},{25,17},{2,10},{10... | collective-permute-start | bytes 196616 | tf_op jit(solution)/shard_map/ppermute | solution.py:99
  131.5 1.1 copy-start.3
  139.0 6.5 %copy-start.33 = (f32[128,256]{1,0:T(8,128)S(1)}, f32[128,256]{1,0:T(8,128)}, u32[]{:S(2)}) copy-start(f32[128,256]{1,0:T(8,128)} %shard_map.79) | copy-start | bytes 393220
  139.0 6.5 %collective-permute-start.32 = (f32[128,256]{1,0:T(8,128)}, f32[128,256]{1,0:T(8,128)S(1)}, u32[]{:S(2)}, u32[]{:S(2)}) collective-permute-start(f32[128,256]{1,0:T(8,128)} %shard_map.79), channel_id=1, source_target_pairs={{0,1},{1,0},{2,3},{3,2},{4,5},{5,4},{6,7},{7,6},{8,9},{9,8},{10,11... | collective-permute-start | bytes 393224 | tf_op jit(solution)/shard_map/ppermute | solution.py:104
  145.6 23.8 %copy-start.9 = (f32[256,256]{1,0:T(8,128)S(1)}, f32[256,256]{1,0:T(8,128)}, u32[]{:S(2)}) copy-start(f32[256,256]{1,0:T(8,128)} %shard_map.71.factor.refs_4_) | copy-start | bytes 786436
  145.6 13.3 %collective-permute-start.35 = (f32[128,256]{1,0:T(8,128)S(1)}, f32[128,256]{1,0:T(8,128)S(1)}, u32[]{:S(2)}, u32[]{:S(2)}) collective-permute-start(f32[128,256]{1,0:T(8,128)S(1)} %add.68), channel_id=1, source_target_pairs={{0,6},{1,7},{2,4},{3,5},{4,2},{5,3},{6,0},{7,1},{8,14},{9,15},{10,... | collective-permute-start | bytes 393224 | tf_op jit(solution)/shard_map/ppermute | solution.py:130
  148.1 12.4 %collective-permute-start.34 = (f32[128,256]{1,0:T(8,128)S(1)}, f32[128,256]{1,0:T(8,128)S(1)}, u32[]{:S(2)}, u32[]{:S(2)}) collective-permute-start(f32[128,256]{1,0:T(8,128)S(1)} %add.68), channel_id=1, source_target_pairs={{0,4},{1,5},{2,6},{3,7},{4,0},{5,1},{6,2},{7,3},{8,12},{9,13},{10,... | collective-permute-start | bytes 393224 | tf_op jit(solution)/shard_map/ppermute | solution.py:130
  148.3 12.3 %collective-permute-start.33 = (f32[128,256]{1,0:T(8,128)S(1)}, f32[128,256]{1,0:T(8,128)S(1)}, u32[]{:S(2)}, u32[]{:S(2)}) collective-permute-start(f32[128,256]{1,0:T(8,128)S(1)} %add.68), channel_id=1, source_target_pairs={{0,2},{1,3},{2,0},{3,1},{4,6},{5,7},{6,4},{7,5},{8,10},{9,11},{10,... | collective-permute-start | bytes 393224 | tf_op jit(solution)/shard_map/ppermute | solution.py:130
  160.6 7.2 %collective-permute-start.38 = (f32[128,256]{1,0:T(8,128)S(1)}, f32[128,256]{1,0:T(8,128)S(1)}, u32[]{:S(2)}, u32[]{:S(2)}) collective-permute-start(f32[128,256]{1,0:T(8,128)S(1)} %add_add_fusion.1.refs_0_), channel_id=1, source_target_pairs={{0,24},{8,16},{16,8},{24,0},{1,25},{9,17},{17,9},{25,1},{2,26},{10... | collective-permute-start | bytes 393224 | tf_op jit(solution)/shard_map/ppermute | solution.py:99
  162.3 7.1 %collective-permute-start.37 = (f32[128,256]{1,0:T(8,128)S(1)}, f32[128,256]{1,0:T(8,128)S(1)}, u32[]{:S(2)}, u32[]{:S(2)}) collective-permute-start(f32[128,256]{1,0:T(8,128)S(1)} %add_add_fusion.1.refs_0_), channel_id=1, source_target_pairs={{0,16},{8,24},{16,0},{24,8},{1,17},{9,25},{17,1},{25,9},{2,18},{10... | collective-permute-start | bytes 393224 | tf_op jit(solution)/shard_map/ppermute | solution.py:99
  163.6 5.8 %collective-permute-start.36 = (f32[128,256]{1,0:T(8,128)S(1)}, f32[128,256]{1,0:T(8,128)S(1)}, u32[]{:S(2)}, u32[]{:S(2)}) collective-permute-start(f32[128,256]{1,0:T(8,128)S(1)} %add_add_fusion.1.refs_0_), channel_id=1, source_target_pairs={{0,8},{8,0},{16,24},{24,16},{1,9},{9,1},{17,25},{25,17},{2,10},{10... | collective-permute-start | bytes 393224 | tf_op jit(solution)/shard_map/ppermute | solution.py:99
  (25 other events, 21.2 us)

commit v5 on v4

--- a/solution.py
+++ b/solution.py
@@ -10,6 +10,7 @@
 
 ITERS = 2
 GROUP = 8
+GRANT = 16 * 2**20
 TERM_TYPES = (jnp.float32, jnp.bfloat16)
 FIELD_TYPES = (jnp.float32, jnp.bfloat16)
 
@@ -71,10 +72,6 @@
 
 NT = (((1,), (1,)), ((), ()))
 TN = (((0,), (0,)), ((), ()))
-
-
-def like(shape, dtype=F32):
-    return jax.ShapeDtypeStruct(shape, dtype)
 
 
 def local(value):
@@ -91,6 +88,7 @@
         out_specs=jax.tree.map(lambda _: vmem, out_shape),
         scratch_shapes=list(scratch),
         cost_estimate=pl.CostEstimate(flops=flops, bytes_accessed=size, transcendentals=0),
+        compiler_params=pltpu.CompilerParams(vmem_limit_bytes=GRANT),
     )(*[local(x) for x in operands])
 
 
@@ -195,8 +193,9 @@
         cost_estimate=pl.CostEstimate(
             flops=4 * rows * rows * columns, bytes_accessed=inverse.size * 2, transcendentals=0
         ),
+        compiler_params=pltpu.CompilerParams(vmem_limit_bytes=GRANT),
         name="start",
-    )(local(weights), inverse, local(vectors), local(coupling))
+    )(local(weights), pltpu.with_memory_space_constraint(inverse, pltpu.HBM), local(vectors), local(coupling))
 
 
 def solve_kernel(weights, field, factor, coupling, inverse, base, out_a, out_b, tip, current):

time: 172 us -> 142 us (0.83)
  local copies, waits for them, and re-layouts: 26.6 us -> 2.51 us
  Pallas kernels: 43.9 us -> 35.5 us
  starting transfers between devices: 52.3 us -> 56.1 us
  other arithmetic: 3.74 us -> 0.22 us
  waiting for transfers between devices: 43.8 us -> 46.4 us
    unnamed x68 -> x10, local copies, waits for them, and re-layouts: 25.7 us -> 1.66 us
    pallas_call x13, Pallas kernels: 40.2 us -> 32.8 us  [whole(): pl.pallas_call(kernel, out_shape=out_shape, in_specs=[vmem for _ in opera...]
    ppermute x9, waiting for transfers between devices: 8.92 us -> 12.8 us  [chip_sum(): lax.ppermute(block, 'rows', route)]
    ppermute x5, starting transfers between devices: 2.17 us -> 4.24 us  [core_swap(): return lax.ppermute(block, 'rows', [(i, i ^ 1) for i in range(count)])]
  transfers between devices with their start and end apart: 39 -> 39, of which waited for: 24 -> 28; matrix products, arithmetic and copies ran while one was open for 0% -> 0% of each run, Pallas kernels for 10% -> 10%
where the time goes in v5:
time: 142 us
  starting transfers between devices  56.1 us (40%)
  waiting for transfers between devices  46.4 us (33%)
  Pallas kernels  35.5 us (25%)
  local copies, waits for them, and re-layouts  2.51 us (2%)
    pallas_call x13, Pallas kernels, whole(): pl.pallas_call(kernel, out_shape=out_shape, in_specs=[vmem for _ in opera...  32.8 us
    ppermute x21, waiting for transfers between devices, node_swap(): return lax.ppermute(block, 'node', [(i, i ^ step) for i in range(count)])  31 us
    ppermute x21, starting transfers between devices, node_swap(): return lax.ppermute(block, 'node', [(i, i ^ step) for i in range(count)])  25.8 us
    ppermute x9, starting transfers between devices, chip_sum(): lax.ppermute(block, 'rows', route)  22 us
    ppermute x9, waiting for transfers between devices, chip_sum(): lax.ppermute(block, 'rows', route)  12.8 us
    ppermute x5, starting transfers between devices, core_swap(): return lax.ppermute(block, 'rows', [(i, i ^ 1) for i in range(count)])  4.24 us
  transfers between devices with their start and end apart: 39, of which 28 were waited for; matrix products, arithmetic and copies ran while one was open for 0% of the time, Pallas kernels for 10%

profile of v5, /device:TPU:0, one launch (start us, length us, event | category | flops | bytes accessed | tf_op | source)
XLA Modules:
  0.0 141.6 jit_solution(11515174544712700320)
XLA Ops:
  3.1 2.7 %start.1 = (f32[768,256]{1,0:T(8,128)S(1)}, bf16[128,512]{1,0:T(8,128)(2,1)S(1)}, bf16[128,512]{1,0:T(8,128)(2,1)S(1)}, bf16[1,2,768,768]{3,2,1,0:T(8,128)(2,1)S(1)}) custom-call(f32[1,2]{1,0:T(1,128)S(1)} %copy-done.3, bf16[1,2,768,768]{3,2,1,0:T(8,128)(2,1)} %source.1, bf16[768,256]{1,0:T(8,128)(2,1)S(1)} %copy-done.2, f32[128,128]{1,0:T(8,128)S(1)} %slice.3.coupling), custom_call_target="tpu_custom_call" | custom-call | flops 603979776 | bytes 2359296 | tf_op jit(solution)/shard_map/start/pallas_call | solution.py:184
  7.4 1.3 shard_map.68
  8.6 2.9 %collective-permute-start.2 = (f32[192,256]{1,0:T(8,128)S(1)}, f32[192,256]{1,0:T(8,128)S(1)}, u32[]{:S(2)}, u32[]{:S(2)}) collective-permute-start(f32[192,256]{1,0:T(8,128)S(1)} %get-tuple-element.43), channel_id=1, source_target_pairs={{0,8},{8,0},{16,24},{24,16},{1,9},{9,1},{17,25},{25,17},{2,10},{10... | collective-permute-start | bytes 589832 | tf_op jit(solution)/shard_map/ppermute | solution.py:97
  11.5 1.5 %collective-permute-start.3 = (f32[192,256]{1,0:T(8,128)S(1)}, f32[192,256]{1,0:T(8,128)S(1)}, u32[]{:S(2)}, u32[]{:S(2)}) collective-permute-start(f32[192,256]{1,0:T(8,128)S(1)} %get-tuple-element.44), channel_id=1, source_target_pairs={{0,16},{8,24},{16,0},{24,8},{1,17},{9,25},{17,1},{25,9},{2,18},{10... | collective-permute-start | bytes 589832 | tf_op jit(solution)/shard_map/ppermute | solution.py:97
  13.1 2.1 %collective-permute-done.2 = f32[192,256]{1,0:T(8,128)S(1)} collective-permute-done((f32[192,256]{1,0:T(8,128)S(1)}, f32[192,256]{1,0:T(8,128)S(1)}, u32[]{:S(2)}, u32[]{:S(2)}) %collective-permute-start.2) | collective-permute-done | bytes 196640 | tf_op jit(solution)/shard_map/ppermute | solution.py:97
  15.2 3.1 %collective-permute-done.3 = f32[192,256]{1,0:T(8,128)S(1)} collective-permute-done((f32[192,256]{1,0:T(8,128)S(1)}, f32[192,256]{1,0:T(8,128)S(1)}, u32[]{:S(2)}, u32[]{:S(2)}) %collective-permute-start.3) | collective-permute-done | bytes 196640 | tf_op jit(solution)/shard_map/ppermute | solution.py:97
  18.3 1.7 %collective-permute-done.4 = f32[192,256]{1,0:T(8,128)S(1)} collective-permute-done((f32[192,256]{1,0:T(8,128)S(1)}, f32[192,256]{1,0:T(8,128)S(1)}, u32[]{:S(2)}, u32[]{:S(2)}) %collective-permute-start.4) | collective-permute-done | bytes 196640 | tf_op jit(solution)/shard_map/ppermute | solution.py:97
  21.9 1.7 %collective-permute-start.5 = (f32[192,256]{1,0:T(8,128)S(1)}, f32[192,256]{1,0:T(8,128)S(1)}, u32[]{:S(2)}, u32[]{:S(2)}) collective-permute-start(f32[192,256]{1,0:T(8,128)S(1)} %add_add_fusion.refs_0_), channel_id=1, source_target_pairs={{0,8},{8,0},{16,24},{24,16},{1,9},{9,1},{17,25},{25,17},{2,10},{10... | collective-permute-start | bytes 589832 | tf_op jit(solution)/shard_map/ppermute | solution.py:97
  23.6 3.2 %collective-permute-done.7.refs_3_ = f32[192,256]{1,0:T(8,128)S(1)} collective-permute-done((f32[192,256]{1,0:T(8,128)S(1)}, f32[192,256]{1,0:T(8,128)S(1)}, u32[]{:S(2)}, u32[]{:S(2)}) %collective-permute-start.7) | collective-permute-done | bytes 196640 | tf_op jit(solution)/shard_map/ppermute | solution.py:97
  26.8 5.3 %collective-permute-done.6.refs_2_ = f32[192,256]{1,0:T(8,128)S(1)} collective-permute-done((f32[192,256]{1,0:T(8,128)S(1)}, f32[192,256]{1,0:T(8,128)S(1)}, u32[]{:S(2)}, u32[]{:S(2)}) %collective-permute-start.6) | collective-permute-done | bytes 196640 | tf_op jit(solution)/shard_map/ppermute | solution.py:97
  34.7 7.2 %collective-permute-start.11 = (f32[64,256]{1,0:T(8,128)S(1)}, f32[64,256]{1,0:T(8,128)S(1)}, u32[]{:S(2)}, u32[]{:S(2)}) collective-permute-start(f32[64,256]{1,0:T(8,128)S(1)} %add.57), channel_id=1, source_target_pairs={{0,6},{1,7},{2,4},{3,5},{4,2},{5,3},{6,0},{7,1},{8,14},{9,15},{10,... | collective-permute-start | bytes 196616 | tf_op jit(solution)/shard_map/ppermute | solution.py:128
  42.0 2.7 %collective-permute-start.10 = (f32[64,256]{1,0:T(8,128)S(1)}, f32[64,256]{1,0:T(8,128)S(1)}, u32[]{:S(2)}, u32[]{:S(2)}) collective-permute-start(f32[64,256]{1,0:T(8,128)S(1)} %add.57), channel_id=1, source_target_pairs={{0,4},{1,5},{2,6},{3,7},{4,0},{5,1},{6,2},{7,3},{8,12},{9,13},{10,... | collective-permute-start | bytes 196616 | tf_op jit(solution)/shard_map/ppermute | solution.py:128
  44.8 4.3 %collective-permute-done.10 = f32[64,256]{1,0:T(8,128)S(1)} collective-permute-done((f32[64,256]{1,0:T(8,128)S(1)}, f32[64,256]{1,0:T(8,128)S(1)}, u32[]{:S(2)}, u32[]{:S(2)}) %collective-permute-start.10) | collective-permute-done | bytes 65568 | tf_op jit(solution)/shard_map/ppermute | solution.py:128
  49.5 1.5 %collective-permute-start.14 = (f32[64,256]{1,0:T(8,128)S(1)}, f32[64,256]{1,0:T(8,128)S(1)}, u32[]{:S(2)}, u32[]{:S(2)}) collective-permute-start(f32[64,256]{1,0:T(8,128)S(1)} %add_add_fusion.3.refs_0_), channel_id=1, source_target_pairs={{0,24},{8,16},{16,8},{24,0},{1,25},{9,17},{17,9},{25,1},{2,26},{10... | collective-permute-start | bytes 196616 | tf_op jit(solution)/shard_map/ppermute | solution.py:97
  51.0 1.4 %collective-permute-start.13 = (f32[64,256]{1,0:T(8,128)S(1)}, f32[64,256]{1,0:T(8,128)S(1)}, u32[]{:S(2)}, u32[]{:S(2)}) collective-permute-start(f32[64,256]{1,0:T(8,128)S(1)} %add_add_fusion.3.refs_0_), channel_id=1, source_target_pairs={{0,16},{8,24},{16,0},{24,8},{1,17},{9,25},{17,1},{25,9},{2,18},{10... | collective-permute-start | bytes 196616 | tf_op jit(solution)/shard_map/ppermute | solution.py:97
  53.0 1.7 %collective-permute-done.14.refs_3_ = f32[64,256]{1,0:T(8,128)S(1)} collective-permute-done((f32[64,256]{1,0:T(8,128)S(1)}, f32[64,256]{1,0:T(8,128)S(1)}, u32[]{:S(2)}, u32[]{:S(2)}) %collective-permute-start.14) | collective-permute-done | bytes 65568 | tf_op jit(solution)/shard_map/ppermute | solution.py:97
  55.4 1.3 collective-permute-done.12.refs_1_
  56.7 5.8 %shard_map.70 = (f32[128,128]{1,0:T(8,128)S(1)}, f32[128,128]{1,0:T(8,128)S(1)}, f32[128,128]{1,0:T(8,128)S(1)}, f32[1,256]{1,0:T(1,128)S(1)}) custom-call(f32[64,256]{1,0:T(8,128)S(1)} %add_add_fusion.3.refs_0_, f32[64,256]{1,0:T(8,128)S(1)} %collective-permute-done.12.refs_1_, f32[64,256]{1,0:T(8,128)S(1)} %collective-permute-done.13.refs_2_, ...), custom_call_target="tpu_custom_call" | custom-call | flops 6000000000 | bytes 262144 | tf_op jit(solution)/shard_map/pallas_call | solution.py:84
  62.5 4.9 %shard_map.71.factor.refs_4_ = f32[256,256]{1,0:T(8,128)S(1)} custom-call(f32[128,128]{1,0:T(8,128)S(1)} %get-tuple-element.48.top, f32[128,128]{1,0:T(8,128)S(1)} %get-tuple-element.49.corner, f32[128,128]{1,0:T(8,128)S(1)} %get-tuple-element.50.rest, f32[1,256]{1,0:T(1,128)S(1)} %get-tuple-element.51.across), custom_call_target="tpu_custom_call" | custom-call | flops 6000000000 | bytes 197632 | tf_op jit(solution)/shard_map/pallas_call | solution.py:84
  67.5 2.1 %shard_map.72 = (f32[768,256]{1,0:T(8,128)S(1)}, bf16[128,512]{1,0:T(8,128)(2,1)S(1)}, bf16[128,512]{1,0:T(8,128)(2,1)S(1)}) custom-call(f32[1,2]{1,0:T(1,128)S(1)} %copy-done.4, f32[768,256]{1,0:T(8,128)S(1)} %get-tuple-element.46.field, f32[256,256]{1,0:T(8,128)S(1)} %shard_map.71.factor.refs_4_, f32[128,128]{1,0:T(8,128)S(1)} %slice.3.coupling, ...), custom_call_target="tpu_custom_call" | custom-call | flops 603979776 | bytes 3473416 | tf_op jit(solution)/shard_map/pallas_call | solution.py:84
  71.0 1.3 shard_map.73
  73.0 1.5 %collective-permute-start.18 = (bf16[192,256]{1,0:T(8,128)(2,1)S(1)}, bf16[192,256]{1,0:T(8,128)(2,1)S(1)}, u32[]{:S(2)}, u32[]{:S(2)}) collective-permute-start(bf16[192,256]{1,0:T(8,128)(2,1)S(1)} %get-tuple-element.57), channel_id=1, source_target_pairs={{0,16},{8,24},{16,0},{24,8},{1,17},{9,25},{17,1},{25,9},{2,18},{10... | collective-permute-start | bytes 294920 | tf_op jit(solution)/shard_map/ppermute | solution.py:97
  74.5 1.4 %collective-permute-start.19 = (bf16[192,256]{1,0:T(8,128)(2,1)S(1)}, bf16[192,256]{1,0:T(8,128)(2,1)S(1)}, u32[]{:S(2)}, u32[]{:S(2)}) collective-permute-start(bf16[192,256]{1,0:T(8,128)(2,1)S(1)} %get-tuple-element.58), channel_id=1, source_target_pairs={{0,24},{8,16},{16,8},{24,0},{1,25},{9,17},{17,9},{25,1},{2,26},{10... | collective-permute-start | bytes 294920 | tf_op jit(solution)/shard_map/ppermute | solution.py:97
  75.9 1.1 collective-permute-done.17
  77.6 2.4 %collective-permute-done.19 = bf16[192,256]{1,0:T(8,128)(2,1)S(1)} collective-permute-done((bf16[192,256]{1,0:T(8,128)(2,1)S(1)}, bf16[192,256]{1,0:T(8,128)(2,1)S(1)}, u32[]{:S(2)}, u32[]{:S(2)}) %collective-permute-start.19) | collective-permute-done | bytes 98336 | tf_op jit(solution)/shard_map/ppermute | solution.py:97
  80.0 1.5 %collective-permute-start.22 = (bf16[192,256]{1,0:T(8,128)(2,1)S(1)}, bf16[192,256]{1,0:T(8,128)(2,1)S(1)}, u32[]{:S(2)}, u32[]{:S(2)}) collective-permute-start(bf16[192,256]{1,0:T(8,128)(2,1)S(1)} %add_convert_fusion.refs_0_), channel_id=1, source_target_pairs={{0,24},{8,16},{16,8},{24,0},{1,25},{9,17},{17,9},{25,1},{2,26},{10... | collective-permute-start | bytes 294920 | tf_op jit(solution)/shard_map/ppermute | solution.py:97
  82.1 1.5 %collective-permute-start.20 = (bf16[192,256]{1,0:T(8,128)(2,1)S(1)}, bf16[192,256]{1,0:T(8,128)(2,1)S(1)}, u32[]{:S(2)}, u32[]{:S(2)}) collective-permute-start(bf16[192,256]{1,0:T(8,128)(2,1)S(1)} %add_convert_fusion.refs_0_), channel_id=1, source_target_pairs={{0,8},{8,0},{16,24},{24,16},{1,9},{9,1},{17,25},{25,17},{2,10},{10... | collective-permute-start | bytes 294920 | tf_op jit(solution)/shard_map/ppermute | solution.py:97
  83.6 2.1 %collective-permute-done.22.refs_3_ = bf16[192,256]{1,0:T(8,128)(2,1)S(1)} collective-permute-done((bf16[192,256]{1,0:T(8,128)(2,1)S(1)}, bf16[192,256]{1,0:T(8,128)(2,1)S(1)}, u32[]{:S(2)}, u32[]{:S(2)}) %collective-permute-start.22) | collective-permute-done | bytes 98336 | tf_op jit(solution)/shard_map/ppermute | solution.py:97
  85.7 1.0 collective-permute-done.21.refs_2_
  87.1 2.8 %collective-permute-start.23 = (f32[64,256]{1,0:T(8,128)S(1)}, f32[64,256]{1,0:T(8,128)S(1)}, u32[]{:S(2)}, u32[]{:S(2)}) collective-permute-start(f32[64,256]{1,0:T(8,128)S(1)} %get-tuple-element.60), channel_id=1, source_target_pairs={{0,1},{1,0},{2,3},{3,2},{4,5},{5,4},{6,7},{7,6},{8,9},{9,8},{10,11... | collective-permute-start | bytes 196616 | tf_op jit(solution)/shard_map/ppermute | solution.py:102
  90.9 6.8 %collective-permute-start.26 = (f32[64,256]{1,0:T(8,128)S(1)}, f32[64,256]{1,0:T(8,128)S(1)}, u32[]{:S(2)}, u32[]{:S(2)}) collective-permute-start(f32[64,256]{1,0:T(8,128)S(1)} %add.64), channel_id=1, source_target_pairs={{0,6},{1,7},{2,4},{3,5},{4,2},{5,3},{6,0},{7,1},{8,14},{9,15},{10,... | collective-permute-start | bytes 196616 | tf_op jit(solution)/shard_map/ppermute | solution.py:128
  98.4 1.3 collective-permute-start.31
  99.6 1.3 collective-permute-start.30
  101.0 2.3 %collective-permute-done.25 = f32[64,256]{1,0:T(8,128)S(1)} collective-permute-done((f32[64,256]{1,0:T(8,128)S(1)}, f32[64,256]{1,0:T(8,128)S(1)}, u32[]{:S(2)}, u32[]{:S(2)}) %collective-permute-start.25) | collective-permute-done | bytes 65568 | tf_op jit(solution)/shard_map/ppermute | solution.py:128
  103.4 1.6 %collective-permute-start.29 = (f32[64,256]{1,0:T(8,128)S(1)}, f32[64,256]{1,0:T(8,128)S(1)}, u32[]{:S(2)}, u32[]{:S(2)}) collective-permute-start(f32[64,256]{1,0:T(8,128)S(1)} %add_add_fusion.2.refs_0_), channel_id=1, source_target_pairs={{0,24},{8,16},{16,8},{24,0},{1,25},{9,17},{17,9},{25,1},{2,26},{10... | collective-permute-start | bytes 196616 | tf_op jit(solution)/shard_map/ppermute | solution.py:97
  105.7 1.2 collective-permute-start.27
  107.0 1.2 shard_map.78.refs_0_
  110.0 5.9 %shard_map.75 = (f32[128,128]{1,0:T(8,128)S(1)}, f32[128,128]{1,0:T(8,128)S(1)}, f32[128,128]{1,0:T(8,128)S(1)}, f32[1,256]{1,0:T(1,128)S(1)}) custom-call(f32[64,256]{1,0:T(8,128)S(1)} %add_add_fusion.2.refs_0_, f32[64,256]{1,0:T(8,128)S(1)} %collective-permute-done.27.refs_1_, f32[64,256]{1,0:T(8,128)S(1)} %collective-permute-done.28.refs_2_, ...), custom_call_target="tpu_custom_call" | custom-call | flops 6000000000 | bytes 262144 | tf_op jit(solution)/shard_map/pallas_call | solution.py:84
  115.9 3.0 %collective-permute-start.35 = (f32[128,256]{1,0:T(8,128)S(1)}, f32[128,256]{1,0:T(8,128)S(1)}, u32[]{:S(2)}, u32[]{:S(2)}) collective-permute-start(f32[128,256]{1,0:T(8,128)S(1)} %add.68), channel_id=1, source_target_pairs={{0,6},{1,7},{2,4},{3,5},{4,2},{5,3},{6,0},{7,1},{8,14},{9,15},{10,... | collective-permute-start | bytes 393224 | tf_op jit(solution)/shard_map/ppermute | solution.py:128
  118.9 1.5 %collective-permute-start.33 = (f32[128,256]{1,0:T(8,128)S(1)}, f32[128,256]{1,0:T(8,128)S(1)}, u32[]{:S(2)}, u32[]{:S(2)}) collective-permute-start(f32[128,256]{1,0:T(8,128)S(1)} %add.68), channel_id=1, source_target_pairs={{0,2},{1,3},{2,0},{3,1},{4,6},{5,7},{6,4},{7,5},{8,10},{9,11},{10,... | collective-permute-start | bytes 393224 | tf_op jit(solution)/shard_map/ppermute | solution.py:128
  120.4 4.9 %shard_map.76.factor.refs_5_ = f32[256,256]{1,0:T(8,128)S(1)} custom-call(f32[128,128]{1,0:T(8,128)S(1)} %get-tuple-element.61.top, f32[128,128]{1,0:T(8,128)S(1)} %get-tuple-element.62.corner, f32[128,128]{1,0:T(8,128)S(1)} %get-tuple-element.63.rest, f32[1,256]{1,0:T(1,128)S(1)} %get-tuple-element.64.across), custom_call_target="tpu_custom_call" | custom-call | flops 6000000000 | bytes 197632 | tf_op jit(solution)/shard_map/pallas_call | solution.py:84
  125.3 5.7 %collective-permute-done.34 = f32[128,256]{1,0:T(8,128)S(1)} collective-permute-done((f32[128,256]{1,0:T(8,128)S(1)}, f32[128,256]{1,0:T(8,128)S(1)}, u32[]{:S(2)}, u32[]{:S(2)}) %collective-permute-start.34) | collective-permute-done | bytes 131104 | tf_op jit(solution)/shard_map/ppermute | solution.py:128
  131.1 1.6 %collective-permute-start.38 = (f32[128,256]{1,0:T(8,128)S(1)}, f32[128,256]{1,0:T(8,128)S(1)}, u32[]{:S(2)}, u32[]{:S(2)}) collective-permute-start(f32[128,256]{1,0:T(8,128)S(1)} %add_add_fusion.1.refs_0_), channel_id=1, source_target_pairs={{0,24},{8,16},{16,8},{24,0},{1,25},{9,17},{17,9},{25,1},{2,26},{10... | collective-permute-start | bytes 393224 | tf_op jit(solution)/shard_map/ppermute | solution.py:97
  132.6 1.2 collective-permute-start.37
  134.6 1.3 shard_map.77
  135.9 2.5 %collective-permute-done.38.refs_3_ = f32[128,256]{1,0:T(8,128)S(1)} collective-permute-done((f32[128,256]{1,0:T(8,128)S(1)}, f32[128,256]{1,0:T(8,128)S(1)}, u32[]{:S(2)}, u32[]{:S(2)}) %collective-permute-start.38) | collective-permute-done | bytes 131104 | tf_op jit(solution)/shard_map/ppermute | solution.py:97
  138.4 1.5 %collective-permute-done.37.refs_2_ = f32[128,256]{1,0:T(8,128)S(1)} collective-permute-done((f32[128,256]{1,0:T(8,128)S(1)}, f32[128,256]{1,0:T(8,128)S(1)}, u32[]{:S(2)}, u32[]{:S(2)}) %collective-permute-start.37) | collective-permute-done | bytes 131104 | tf_op jit(solution)/shard_map/ppermute | solution.py:97
  139.9 1.7 %shard_map.80 = f32[2,256,256]{2,1,0:T(8,128)} custom-call(f32[128,256]{1,0:T(8,128)S(1)} %add_add_fusion.1.refs_0_, f32[128,256]{1,0:T(8,128)S(1)} %collective-permute-done.36.refs_1_, f32[128,256]{1,0:T(8,128)S(1)} %collective-permute-done.37.refs_2_, f32[128,256]{1,0:T(8,128)S(1)} %collective-permute-done.38.refs_3_, ...), custom_call_target="tpu_custom_call" | custom-call | flops 100000000 | bytes 1048576 | tf_op jit(solution)/shard_map/pallas_call | solution.py:84
  (63 shorter events, 19.3 us)
Async XLA Ops:
  1.5 1.0 copy-start.2
  2.5 0.7 copy-start.3
  5.8 1.5 %collective-permute-start = (bf16[128,512]{1,0:T(8,128)(2,1)S(1)}, bf16[128,512]{1,0:T(8,128)(2,1)S(1)}, u32[]{:S(2)}, u32[]{:S(2)}) collective-permute-start(bf16[128,512]{1,0:T(8,128)(2,1)S(1)} %get-tuple-element.39), channel_id=1, source_target_pairs={{0,1},{1,0},{2,3},{3,2},{4,5},{5,4},{6,7},{7,6},{8,9},{9,8},{10,11... | collective-permute-start | bytes 393224 | tf_op jit(solution)/shard_map/ppermute | solution.py:102
  6.4 1.0 collective-permute-start.1
  8.6 6.6 %collective-permute-start.2 = (f32[192,256]{1,0:T(8,128)S(1)}, f32[192,256]{1,0:T(8,128)S(1)}, u32[]{:S(2)}, u32[]{:S(2)}) collective-permute-start(f32[192,256]{1,0:T(8,128)S(1)} %get-tuple-element.43), channel_id=1, source_target_pairs={{0,8},{8,0},{16,24},{24,16},{1,9},{9,1},{17,25},{25,17},{2,10},{10... | collective-permute-start | bytes 589832 | tf_op jit(solution)/shard_map/ppermute | solution.py:97
  11.5 6.8 %collective-permute-start.3 = (f32[192,256]{1,0:T(8,128)S(1)}, f32[192,256]{1,0:T(8,128)S(1)}, u32[]{:S(2)}, u32[]{:S(2)}) collective-permute-start(f32[192,256]{1,0:T(8,128)S(1)} %get-tuple-element.44), channel_id=1, source_target_pairs={{0,16},{8,24},{16,0},{24,8},{1,17},{9,25},{17,1},{25,9},{2,18},{10... | collective-permute-start | bytes 589832 | tf_op jit(solution)/shard_map/ppermute | solution.py:97
  13.1 6.9 %collective-permute-start.4 = (f32[192,256]{1,0:T(8,128)S(1)}, f32[192,256]{1,0:T(8,128)S(1)}, u32[]{:S(2)}, u32[]{:S(2)}) collective-permute-start(f32[192,256]{1,0:T(8,128)S(1)} %get-tuple-element.45), channel_id=1, source_target_pairs={{0,24},{8,16},{16,8},{24,0},{1,25},{9,17},{17,9},{25,1},{2,26},{10... | collective-permute-start | bytes 589832 | tf_op jit(solution)/shard_map/ppermute | solution.py:97
  20.0 6.7 %collective-permute-start.7 = (f32[192,256]{1,0:T(8,128)S(1)}, f32[192,256]{1,0:T(8,128)S(1)}, u32[]{:S(2)}, u32[]{:S(2)}) collective-permute-start(f32[192,256]{1,0:T(8,128)S(1)} %add_add_fusion.refs_0_), channel_id=1, source_target_pairs={{0,24},{8,16},{16,8},{24,0},{1,25},{9,17},{17,9},{25,1},{2,26},{10... | collective-permute-start | bytes 589832 | tf_op jit(solution)/shard_map/ppermute | solution.py:97
  20.9 11.1 %collective-permute-start.6 = (f32[192,256]{1,0:T(8,128)S(1)}, f32[192,256]{1,0:T(8,128)S(1)}, u32[]{:S(2)}, u32[]{:S(2)}) collective-permute-start(f32[192,256]{1,0:T(8,128)S(1)} %add_add_fusion.refs_0_), channel_id=1, source_target_pairs={{0,16},{8,24},{16,0},{24,8},{1,17},{9,25},{17,1},{25,9},{2,18},{10... | collective-permute-start | bytes 589832 | tf_op jit(solution)/shard_map/ppermute | solution.py:97
  21.9 10.1 %collective-permute-start.5 = (f32[192,256]{1,0:T(8,128)S(1)}, f32[192,256]{1,0:T(8,128)S(1)}, u32[]{:S(2)}, u32[]{:S(2)}) collective-permute-start(f32[192,256]{1,0:T(8,128)S(1)} %add_add_fusion.refs_0_), channel_id=1, source_target_pairs={{0,8},{8,0},{16,24},{24,16},{1,9},{9,1},{17,25},{25,17},{2,10},{10... | collective-permute-start | bytes 589832 | tf_op jit(solution)/shard_map/ppermute | solution.py:97
  33.1 1.7 %collective-permute-start.8 = (f32[64,256]{1,0:T(8,128)S(1)}, f32[64,256]{1,0:T(8,128)S(1)}, u32[]{:S(2)}, u32[]{:S(2)}) collective-permute-start(f32[64,256]{1,0:T(8,128)S(1)} %get-tuple-element.47), channel_id=1, source_target_pairs={{0,1},{1,0},{2,3},{3,2},{4,5},{5,4},{6,7},{7,6},{8,9},{9,8},{10,11... | collective-permute-start | bytes 196616 | tf_op jit(solution)/shard_map/ppermute | solution.py:102
  34.7 10.1 %collective-permute-start.11 = (f32[64,256]{1,0:T(8,128)S(1)}, f32[64,256]{1,0:T(8,128)S(1)}, u32[]{:S(2)}, u32[]{:S(2)}) collective-permute-start(f32[64,256]{1,0:T(8,128)S(1)} %add.57), channel_id=1, source_target_pairs={{0,6},{1,7},{2,4},{3,5},{4,2},{5,3},{6,0},{7,1},{8,14},{9,15},{10,... | collective-permute-start | bytes 196616 | tf_op jit(solution)/shard_map/ppermute | solution.py:128
  42.0 7.2 %collective-permute-start.10 = (f32[64,256]{1,0:T(8,128)S(1)}, f32[64,256]{1,0:T(8,128)S(1)}, u32[]{:S(2)}, u32[]{:S(2)}) collective-permute-start(f32[64,256]{1,0:T(8,128)S(1)} %add.57), channel_id=1, source_target_pairs={{0,4},{1,5},{2,6},{3,7},{4,0},{5,1},{6,2},{7,3},{8,12},{9,13},{10,... | collective-permute-start | bytes 196616 | tf_op jit(solution)/shard_map/ppermute | solution.py:128
  44.7 4.8 %collective-permute-start.9 = (f32[64,256]{1,0:T(8,128)S(1)}, f32[64,256]{1,0:T(8,128)S(1)}, u32[]{:S(2)}, u32[]{:S(2)}) collective-permute-start(f32[64,256]{1,0:T(8,128)S(1)} %add.57), channel_id=1, source_target_pairs={{0,2},{1,3},{2,0},{3,1},{4,6},{5,7},{6,4},{7,5},{8,10},{9,11},{10,... | collective-permute-start | bytes 196616 | tf_op jit(solution)/shard_map/ppermute | solution.py:128
  49.5 5.2 %collective-permute-start.14 = (f32[64,256]{1,0:T(8,128)S(1)}, f32[64,256]{1,0:T(8,128)S(1)}, u32[]{:S(2)}, u32[]{:S(2)}) collective-permute-start(f32[64,256]{1,0:T(8,128)S(1)} %add_add_fusion.3.refs_0_), channel_id=1, source_target_pairs={{0,24},{8,16},{16,8},{24,0},{1,25},{9,17},{17,9},{25,1},{2,26},{10... | collective-permute-start | bytes 196616 | tf_op jit(solution)/shard_map/ppermute | solution.py:97
  51.0 4.4 %collective-permute-start.13 = (f32[64,256]{1,0:T(8,128)S(1)}, f32[64,256]{1,0:T(8,128)S(1)}, u32[]{:S(2)}, u32[]{:S(2)}) collective-permute-start(f32[64,256]{1,0:T(8,128)S(1)} %add_add_fusion.3.refs_0_), channel_id=1, source_target_pairs={{0,16},{8,24},{16,0},{24,8},{1,17},{9,25},{17,1},{25,9},{2,18},{10... | collective-permute-start | bytes 196616 | tf_op jit(solution)/shard_map/ppermute | solution.py:97
  52.4 4.3 %collective-permute-start.12 = (f32[64,256]{1,0:T(8,128)S(1)}, f32[64,256]{1,0:T(8,128)S(1)}, u32[]{:S(2)}, u32[]{:S(2)}) collective-permute-start(f32[64,256]{1,0:T(8,128)S(1)} %add_add_fusion.3.refs_0_), channel_id=1, source_target_pairs={{0,8},{8,0},{16,24},{24,16},{1,9},{9,1},{17,25},{25,17},{2,10},{10... | collective-permute-start | bytes 196616 | tf_op jit(solution)/shard_map/ppermute | solution.py:97
  62.5 5.0 %copy-start.4 = (f32[1,2]{1,0:T(1,128)S(1)}, f32[1,2]{1,0:T(1,128)}, u32[]{:S(2)}) copy-start(f32[1,2]{1,0:T(1,128)} %weights.7) | copy-start | bytes 28
  69.6 1.4 collective-permute-start.15
  69.7 1.3 collective-permute-start.16
  71.0 35.9 %copy-start = (f32[768,128]{1,0:T(8,128)S(1)}, f32[768,128]{1,0:T(8,128)}, u32[]{:S(2)}) copy-start(f32[768,128]{1,0:T(8,128)} %upper_tiles.3) | copy-start | bytes 1179652
  71.0 35.9 %copy-start.1 = (f32[768,128]{1,0:T(8,128)S(1)}, f32[768,128]{1,0:T(8,128)}, u32[]{:S(2)}) copy-start(f32[768,128]{1,0:T(8,128)} %diag_tiles.3) | copy-start | bytes 1179652
  72.3 4.7 %collective-permute-start.17 = (bf16[192,256]{1,0:T(8,128)(2,1)S(1)}, bf16[192,256]{1,0:T(8,128)(2,1)S(1)}, u32[]{:S(2)}, u32[]{:S(2)}) collective-permute-start(bf16[192,256]{1,0:T(8,128)(2,1)S(1)} %get-tuple-element.56), channel_id=1, source_target_pairs={{0,8},{8,0},{16,24},{24,16},{1,9},{9,1},{17,25},{25,17},{2,10},{10... | collective-permute-start | bytes 294920 | tf_op jit(solution)/shard_map/ppermute | solution.py:97
  73.0 4.6 %collective-permute-start.18 = (bf16[192,256]{1,0:T(8,128)(2,1)S(1)}, bf16[192,256]{1,0:T(8,128)(2,1)S(1)}, u32[]{:S(2)}, u32[]{:S(2)}) collective-permute-start(bf16[192,256]{1,0:T(8,128)(2,1)S(1)} %get-tuple-element.57), channel_id=1, source_target_pairs={{0,16},{8,24},{16,0},{24,8},{1,17},{9,25},{17,1},{25,9},{2,18},{10... | collective-permute-start | bytes 294920 | tf_op jit(solution)/shard_map/ppermute | solution.py:97
  74.5 5.5 %collective-permute-start.19 = (bf16[192,256]{1,0:T(8,128)(2,1)S(1)}, bf16[192,256]{1,0:T(8,128)(2,1)S(1)}, u32[]{:S(2)}, u32[]{:S(2)}) collective-permute-start(bf16[192,256]{1,0:T(8,128)(2,1)S(1)} %get-tuple-element.58), channel_id=1, source_target_pairs={{0,24},{8,16},{16,8},{24,0},{1,25},{9,17},{17,9},{25,1},{2,26},{10... | collective-permute-start | bytes 294920 | tf_op jit(solution)/shard_map/ppermute | solution.py:97
  80.0 5.6 %collective-permute-start.22 = (bf16[192,256]{1,0:T(8,128)(2,1)S(1)}, bf16[192,256]{1,0:T(8,128)(2,1)S(1)}, u32[]{:S(2)}, u32[]{:S(2)}) collective-permute-start(bf16[192,256]{1,0:T(8,128)(2,1)S(1)} %add_convert_fusion.refs_0_), channel_id=1, source_target_pairs={{0,24},{8,16},{16,8},{24,0},{1,25},{9,17},{17,9},{25,1},{2,26},{10... | collective-permute-start | bytes 294920 | tf_op jit(solution)/shard_map/ppermute | solution.py:97
  81.5 5.1 %collective-permute-start.21 = (bf16[192,256]{1,0:T(8,128)(2,1)S(1)}, bf16[192,256]{1,0:T(8,128)(2,1)S(1)}, u32[]{:S(2)}, u32[]{:S(2)}) collective-permute-start(bf16[192,256]{1,0:T(8,128)(2,1)S(1)} %add_convert_fusion.refs_0_), channel_id=1, source_target_pairs={{0,16},{8,24},{16,0},{24,8},{1,17},{9,25},{17,1},{25,9},{2,18},{10... | collective-permute-start | bytes 294920 | tf_op jit(solution)/shard_map/ppermute | solution.py:97
  82.1 4.6 %collective-permute-start.20 = (bf16[192,256]{1,0:T(8,128)(2,1)S(1)}, bf16[192,256]{1,0:T(8,128)(2,1)S(1)}, u32[]{:S(2)}, u32[]{:S(2)}) collective-permute-start(bf16[192,256]{1,0:T(8,128)(2,1)S(1)} %add_convert_fusion.refs_0_), channel_id=1, source_target_pairs={{0,8},{8,0},{16,24},{24,16},{1,9},{9,1},{17,25},{25,17},{2,10},{10... | collective-permute-start | bytes 294920 | tf_op jit(solution)/shard_map/ppermute | solution.py:97
  87.1 3.8 %collective-permute-start.23 = (f32[64,256]{1,0:T(8,128)S(1)}, f32[64,256]{1,0:T(8,128)S(1)}, u32[]{:S(2)}, u32[]{:S(2)}) collective-permute-start(f32[64,256]{1,0:T(8,128)S(1)} %get-tuple-element.60), channel_id=1, source_target_pairs={{0,1},{1,0},{2,3},{3,2},{4,5},{5,4},{6,7},{7,6},{8,9},{9,8},{10,11... | collective-permute-start | bytes 196616 | tf_op jit(solution)/shard_map/ppermute | solution.py:102
  90.9 10.1 %collective-permute-start.26 = (f32[64,256]{1,0:T(8,128)S(1)}, f32[64,256]{1,0:T(8,128)S(1)}, u32[]{:S(2)}, u32[]{:S(2)}) collective-permute-start(f32[64,256]{1,0:T(8,128)S(1)} %add.64), channel_id=1, source_target_pairs={{0,6},{1,7},{2,4},{3,5},{4,2},{5,3},{6,0},{7,1},{8,14},{9,15},{10,... | collective-permute-start | bytes 196616 | tf_op jit(solution)/shard_map/ppermute | solution.py:128
  97.7 5.5 %collective-permute-start.25 = (f32[64,256]{1,0:T(8,128)S(1)}, f32[64,256]{1,0:T(8,128)S(1)}, u32[]{:S(2)}, u32[]{:S(2)}) collective-permute-start(f32[64,256]{1,0:T(8,128)S(1)} %add.64), channel_id=1, source_target_pairs={{0,4},{1,5},{2,6},{3,7},{4,0},{5,1},{6,2},{7,3},{8,12},{9,13},{10,... | collective-permute-start | bytes 196616 | tf_op jit(solution)/shard_map/ppermute | solution.py:128
  97.7 5.7 %collective-permute-start.24 = (f32[64,256]{1,0:T(8,128)S(1)}, f32[64,256]{1,0:T(8,128)S(1)}, u32[]{:S(2)}, u32[]{:S(2)}) collective-permute-start(f32[64,256]{1,0:T(8,128)S(1)} %add.64), channel_id=1, source_target_pairs={{0,2},{1,3},{2,0},{3,1},{4,6},{5,7},{6,4},{7,5},{8,10},{9,11},{10,... | collective-permute-start | bytes 196616 | tf_op jit(solution)/shard_map/ppermute | solution.py:128
  98.4 8.6 %collective-permute-start.31 = (f32[128,256]{1,0:T(8,128)S(1)}, f32[128,256]{1,0:T(8,128)S(1)}, u32[]{:S(2)}, u32[]{:S(2)}) collective-permute-start(f32[128,256]{1,0:T(8,128)S(1)} %get-tuple-element.69), channel_id=1, source_target_pairs={{1,0},{2,1},{3,2},{4,3},{5,4},{6,5},{7,6},{9,8},{10,9},{11,10},{12... | collective-permute-start | bytes 393224 | tf_op jit(solution)/shard_map/ppermute | solution.py:407
  99.6 8.6 %collective-permute-start.30 = (bf16[128,256]{1,0:T(8,128)(2,1)S(1)}, bf16[128,256]{1,0:T(8,128)(2,1)S(1)}, u32[]{:S(2)}, u32[]{:S(2)}) collective-permute-start(bf16[128,256]{1,0:T(8,128)(2,1)S(1)} %get-tuple-element.66), channel_id=1, source_target_pairs={{1,0},{2,1},{3,2},{4,3},{5,4},{6,5},{7,6},{9,8},{10,9},{11,10},{12... | collective-permute-start | bytes 196616 | tf_op jit(solution)/shard_map/ppermute | solution.py:407
  103.4 6.0 %collective-permute-start.29 = (f32[64,256]{1,0:T(8,128)S(1)}, f32[64,256]{1,0:T(8,128)S(1)}, u32[]{:S(2)}, u32[]{:S(2)}) collective-permute-start(f32[64,256]{1,0:T(8,128)S(1)} %add_add_fusion.2.refs_0_), channel_id=1, source_target_pairs={{0,24},{8,16},{16,8},{24,0},{1,25},{9,17},{17,9},{25,1},{2,26},{10... | collective-permute-start | bytes 196616 | tf_op jit(solution)/shard_map/ppermute | solution.py:97
  105.0 4.6 %collective-permute-start.28 = (f32[64,256]{1,0:T(8,128)S(1)}, f32[64,256]{1,0:T(8,128)S(1)}, u32[]{:S(2)}, u32[]{:S(2)}) collective-permute-start(f32[64,256]{1,0:T(8,128)S(1)} %add_add_fusion.2.refs_0_), channel_id=1, source_target_pairs={{0,16},{8,24},{16,0},{24,8},{1,17},{9,25},{17,1},{25,9},{2,18},{10... | collective-permute-start | bytes 196616 | tf_op jit(solution)/shard_map/ppermute | solution.py:97
  105.7 4.3 %collective-permute-start.27 = (f32[64,256]{1,0:T(8,128)S(1)}, f32[64,256]{1,0:T(8,128)S(1)}, u32[]{:S(2)}, u32[]{:S(2)}) collective-permute-start(f32[64,256]{1,0:T(8,128)S(1)} %add_add_fusion.2.refs_0_), channel_id=1, source_target_pairs={{0,8},{8,0},{16,24},{24,16},{1,9},{9,1},{17,25},{25,17},{2,10},{10... | collective-permute-start | bytes 196616 | tf_op jit(solution)/shard_map/ppermute | solution.py:97
  110.0 5.9 %collective-permute-start.32 = (f32[128,256]{1,0:T(8,128)S(1)}, f32[128,256]{1,0:T(8,128)S(1)}, u32[]{:S(2)}, u32[]{:S(2)}) collective-permute-start(f32[128,256]{1,0:T(8,128)S(1)} %shard_map.79), channel_id=1, source_target_pairs={{0,1},{1,0},{2,3},{3,2},{4,5},{5,4},{6,7},{7,6},{8,9},{9,8},{10,11... | collective-permute-start | bytes 393224 | tf_op jit(solution)/shard_map/ppermute | solution.py:102
  115.9 9.4 %collective-permute-start.35 = (f32[128,256]{1,0:T(8,128)S(1)}, f32[128,256]{1,0:T(8,128)S(1)}, u32[]{:S(2)}, u32[]{:S(2)}) collective-permute-start(f32[128,256]{1,0:T(8,128)S(1)} %add.68), channel_id=1, source_target_pairs={{0,6},{1,7},{2,4},{3,5},{4,2},{5,3},{6,0},{7,1},{8,14},{9,15},{10,... | collective-permute-start | bytes 393224 | tf_op jit(solution)/shard_map/ppermute | solution.py:128
  118.9 12.2 %collective-permute-start.34 = (f32[128,256]{1,0:T(8,128)S(1)}, f32[128,256]{1,0:T(8,128)S(1)}, u32[]{:S(2)}, u32[]{:S(2)}) collective-permute-start(f32[128,256]{1,0:T(8,128)S(1)} %add.68), channel_id=1, source_target_pairs={{0,4},{1,5},{2,6},{3,7},{4,0},{5,1},{6,2},{7,3},{8,12},{9,13},{10,... | collective-permute-start | bytes 393224 | tf_op jit(solution)/shard_map/ppermute | solution.py:128
  118.9 12.2 %collective-permute-start.33 = (f32[128,256]{1,0:T(8,128)S(1)}, f32[128,256]{1,0:T(8,128)S(1)}, u32[]{:S(2)}, u32[]{:S(2)}) collective-permute-start(f32[128,256]{1,0:T(8,128)S(1)} %add.68), channel_id=1, source_target_pairs={{0,2},{1,3},{2,0},{3,1},{4,6},{5,7},{6,4},{7,5},{8,10},{9,11},{10,... | collective-permute-start | bytes 393224 | tf_op jit(solution)/shard_map/ppermute | solution.py:128
  131.1 7.3 %collective-permute-start.38 = (f32[128,256]{1,0:T(8,128)S(1)}, f32[128,256]{1,0:T(8,128)S(1)}, u32[]{:S(2)}, u32[]{:S(2)}) collective-permute-start(f32[128,256]{1,0:T(8,128)S(1)} %add_add_fusion.1.refs_0_), channel_id=1, source_target_pairs={{0,24},{8,16},{16,8},{24,0},{1,25},{9,17},{17,9},{25,1},{2,26},{10... | collective-permute-start | bytes 393224 | tf_op jit(solution)/shard_map/ppermute | solution.py:97
  132.6 7.3 %collective-permute-start.37 = (f32[128,256]{1,0:T(8,128)S(1)}, f32[128,256]{1,0:T(8,128)S(1)}, u32[]{:S(2)}, u32[]{:S(2)}) collective-permute-start(f32[128,256]{1,0:T(8,128)S(1)} %add_add_fusion.1.refs_0_), channel_id=1, source_target_pairs={{0,16},{8,24},{16,0},{24,8},{1,17},{9,25},{17,1},{25,9},{2,18},{10... | collective-permute-start | bytes 393224 | tf_op jit(solution)/shard_map/ppermute | solution.py:97
  133.9 6.0 %collective-permute-start.36 = (f32[128,256]{1,0:T(8,128)S(1)}, f32[128,256]{1,0:T(8,128)S(1)}, u32[]{:S(2)}, u32[]{:S(2)}) collective-permute-start(f32[128,256]{1,0:T(8,128)S(1)} %add_add_fusion.1.refs_0_), channel_id=1, source_target_pairs={{0,8},{8,0},{16,24},{24,16},{1,9},{9,1},{17,25},{25,17},{2,10},{10... | collective-permute-start | bytes 393224 | tf_op jit(solution)/shard_map/ppermute | solution.py:97

commit v6 on v5

--- a/solution.py
+++ b/solution.py
@@ -11,8 +11,6 @@
 ITERS = 2
 GROUP = 8
 GRANT = 16 * 2**20
-TERM_TYPES = (jnp.float32, jnp.bfloat16)
-FIELD_TYPES = (jnp.float32, jnp.bfloat16)
 
 precise = lax.Precision.HIGHEST
 F32 = jnp.float32
@@ -155,53 +153,63 @@
     return weights[:, 0:1] * real - weights[:, 1:2] * imag
 
 
-def start_kernel(weights, source, vectors, coupling, base, out_a, out_b, inverse, tip, arrived):
+def start_kernel(weights_at, source, vectors_at, upper_at, *refs):
+    base, out_a, out_b, inverse, coupling, weights, vectors, tip, arrived = refs
     rows = vectors.shape[0]
     band = coupling.shape[0]
     tile = 2 * band if rows % (2 * band) == 0 else band
     spans = [pl.ds(at, tile) for at in range(0, rows, tile)]
-    copies = [
-        pltpu.make_async_copy(source.at[:, :, span], inverse.at[:, :, span], arrived.at[i])
-        for i, span in enumerate(spans)
-    ]
+    pairs = [(vectors_at, vectors), (weights_at, weights)]
+    pairs += [(source.at[:, :, span], inverse.at[:, :, span]) for span in spans]
+    pairs += [(upper_at.at[pl.ds(rows - band, band)], coupling)]
+    copies = [pltpu.make_async_copy(*pair, arrived.at[i]) for i, pair in enumerate(pairs)]
     for copy in copies:
         copy.start()
+    for copy in copies[:2]:
+        copy.wait()
     for i, span in enumerate(spans):
-        copies[i].wait()
+        copies[2 + i].wait()
         real = jnp.dot(inverse[0, 0, span], vectors[...], preferred_element_type=F32)
         imag = jnp.dot(inverse[0, 1, span], vectors[...], preferred_element_type=F32)
         base[span] = combine(weights, real, imag)
         if i == 0:
             tip[...] = tip_of(real, imag, band)
+    copies[-1].wait()
     emit_messages(real, imag, coupling[...], tip[...], out_a, out_b)
 
 
-def start(vectors, weights, coupling, inverse):
+def start(vectors, weights, upper_tiles, inverse):
     rows, columns = vectors.shape
-    band = coupling.shape[1]
+    band = upper_tiles.shape[1]
     message = like((band, 2 * columns), BF16)
-    vmem = pl.BlockSpec(memory_space=pltpu.VMEM)
+    outs = [like((rows, columns)), message, message]
+    outs += [like(inverse.shape, BF16), like((band, band)), like(weights.shape)]
+    far = lambda x: pltpu.with_memory_space_constraint(x, pltpu.HBM)
     return pl.pallas_call(
         start_kernel,
-        in_specs=[vmem, pl.BlockSpec(memory_space=pltpu.HBM), vmem, vmem],
-        out_specs=[vmem] * 4,
-        out_shape=[like((rows, columns)), message, message, like(inverse.shape, BF16)],
+        in_specs=[pl.BlockSpec(memory_space=pltpu.HBM)] * 4,
+        out_specs=[pl.BlockSpec(memory_space=pltpu.VMEM)] * len(outs),
+        out_shape=outs,
         scratch_shapes=[
+            pltpu.VMEM(vectors.shape, BF16),
             pltpu.VMEM((band, 2 * columns), BF16),
-            pltpu.SemaphoreType.DMA((rows // band,)),
+            pltpu.SemaphoreType.DMA((rows // band + 3,)),
         ],
         cost_estimate=pl.CostEstimate(
             flops=4 * rows * rows * columns, bytes_accessed=inverse.size * 2, transcendentals=0
         ),
         compiler_params=pltpu.CompilerParams(vmem_limit_bytes=GRANT),
         name="start",
-    )(local(weights), pltpu.with_memory_space_constraint(inverse, pltpu.HBM), local(vectors), local(coupling))
-
-
-def solve_kernel(weights, field, factor, coupling, inverse, base, out_a, out_b, tip, current):
+    )(far(weights), far(inverse), far(vectors), far(upper_tiles))
+
+
+def solve_kernel(weights, field, low, factor, coupling, inverse, base, out_a, out_b, tip, current):
     band = coupling.shape[0]
     rows = field.shape[0]
-    current[...] = dot_three(field[...], factor[...], NT).astype(BF16)
+    high, rest = halves_of(factor[...])
+    times = lambda a, b: lax.dot_general(a, b, NT, preferred_element_type=F32)
+    result = times(field[...], high) + (times(field[...], rest) + times(low[...], high))
+    current[...] = result.astype(BF16)
     tile = 2 * band if rows % (2 * band) == 0 else band
     for at in range(0, rows, tile):
         real = jnp.dot(inverse[0, 0, at : at + tile], current[...], preferred_element_type=F32)
@@ -212,7 +220,7 @@
     emit_messages(real, imag, coupling[...], tip[...], out_a, out_b)
 
 
-def solve(field, factor, weights, coupling, inverse):
+def solve(field, low, factor, weights, coupling, inverse):
     rows, columns = field.shape
     band = coupling.shape[1]
     message = like((band, 2 * columns), BF16)
@@ -221,6 +229,7 @@
         [like((rows, columns)), message, message],
         weights,
         field,
+        low,
         factor,
         coupling,
         inverse,
@@ -246,17 +255,21 @@
         total = total - dot_two(inverse[0, 1, :, part], weights[:, 0:1] * imag + weights[:, 1:2] * real)
     term[...] = total
     size = own.shape[0]
+    steps = lax.axis_size("node")
     for s, out in enumerate((own,) + sends):
-        where = pl.multiple_of((node ^ s) * size, 8)
-        out[...] = term[pl.ds(where, size), :].astype(out.dtype)
-
-
-def correct(weights, base, got_a, got_b, coupling, inverse, kind):
+        where = pl.multiple_of((node ^ (s if s < steps else s - steps + 1)) * size, 8)
+        value = term[pl.ds(where, size), :]
+        if s >= steps:
+            value = value - value.astype(BF16).astype(F32)
+        out[...] = value.astype(out.dtype)
+
+
+def correct(weights, base, got_a, got_b, coupling, inverse, parts):
     rows, columns = base.shape
     band = coupling.shape[1]
     count = lax.axis_size("node")
     size = rows // count
-    outs = [like((size, columns))] + [like((size, columns), kind)] * (count - 1)
+    outs = [like((size, columns))] + [like((size, columns), BF16)] * (parts * (count - 1))
     return whole(
         correct_kernel,
         outs,
@@ -282,10 +295,7 @@
     *blocks, field, head, part, matrix = refs
     place(blocks, field)
     head[...] = field[: head.shape[0]]
-    if field.dtype == BF16:
-        matrix[...] = lax.dot_general(field[...], field[...], TN, preferred_element_type=F32)
-    else:
-        matrix[...] = dot_tn(field[...], field[...])
+    matrix[...] = lax.dot_general(field[...], field[...], TN, preferred_element_type=F32)
     size = part.shape[0]
     part[...] = matrix[pl.ds(pl.multiple_of(lax.axis_index("node") * size, 8), size), :]
 
@@ -293,14 +303,22 @@
 def gram_slice(blocks, band):
     rows, columns = blocks[0].shape
     count = len(blocks)
-    kind = blocks[0].dtype
     outs = [
-        like((rows * count, columns), kind),
-        like((band, columns), kind),
+        like((rows * count, columns), BF16),
+        like((band, columns), BF16),
         like((columns // count, columns)),
     ]
     scratch = [pltpu.VMEM((columns, columns), F32)]
     return whole(gram_kernel, outs, *blocks, scratch=scratch)
+
+
+def join_kernel(*refs):
+    place(refs[:-1], refs[-1])
+
+
+def join(blocks):
+    rows, columns = blocks[0].shape
+    return whole(join_kernel, like((rows * len(blocks), columns), BF16), *blocks)
 
 
 def eliminate(block, out, base):
@@ -407,47 +425,49 @@
     return lax.ppermute(head, "rows", [(i + 1, i) for i in range(count - 1)])
 
 
-def band_kernel(field, after, diag_tiles, upper_tiles, *refs):
-    earlier, (part, image, matrix) = refs[:-3], refs[-3:]
+def band_kernel(extra, field, after, diag_tiles, upper_tiles, *refs):
+    low, earlier, (part, image, matrix) = refs[:extra], refs[extra:-3], refs[-3:]
     band = after.shape[0]
     tiles = field.shape[0] // band
-    values = lambda x: x.astype(F32)
+
+    def values(at):
+        total = field[at].astype(F32)
+        return total + low[0][at].astype(F32) if low else total
+
     for t in range(tiles):
         at = slice(t * band, (t + 1) * band)
-        following = after[...] if t == tiles - 1 else field[(t + 1) * band : (t + 2) * band]
-        image[at] = 0.5 * dot_three(diag_tiles[at], values(field[at])) + dot_three(
-            upper_tiles[at], values(following)
+        following = slice((t + 1) * band, (t + 2) * band)
+        following = after[...].astype(F32) if t == tiles - 1 else values(following)
+        image[at] = 0.5 * dot_three(diag_tiles[at], values(at)) + dot_three(upper_tiles[at], following)
+    matrix[...] = dot_two(field[...], image[...], TN)
+    if low:
+        matrix[...] += lax.dot_general(
+            low[0][...], image[...].astype(BF16), TN, preferred_element_type=F32
         )
-    if field.dtype == BF16:
-        matrix[...] = dot_two(field[...], image[...], TN)
-    else:
-        matrix[...] = dot_three(field[...], image[...], TN)
     size = matrix.shape[0] // lax.axis_size("node")
     for ref in earlier:
         part[:-size] = ref[...]
     part[-size:] = matrix[pl.ds(pl.multiple_of(lax.axis_index("node") * size, 8), size), :]
 
 
-def band_slice(field, after, diag_tiles, upper_tiles, *earlier):
+def band_slice(field, low, after, diag_tiles, upper_tiles, earlier):
     rows, columns = field.shape
     size = columns // lax.axis_size("node")
     return whole(
-        band_kernel,
+        functools.partial(band_kernel, len(low)),
         like((size * (1 + sum(x.shape[0] // size for x in earlier)), columns)),
         field,
         after,
         diag_tiles,
         upper_tiles,
+        *low,
         *earlier,
         scratch=[pltpu.VMEM((rows, columns), F32), pltpu.VMEM((columns, columns), F32)],
     )
 
 
 def last_kernel(field, factor, out):
-    if field.dtype == BF16:
-        out[...] = dot_two(field[...], factor[...], NT)
-    else:
-        out[...] = dot_three(field[...], factor[...], NT)
+    out[...] = dot_two(field[...], factor[...], NT)
 
 
 def projected_kernel(order, *refs):
@@ -469,37 +489,48 @@
 def per_device(subspace, inverse, weights, diag_tiles, upper_tiles):
     order = float(subspace.shape[0] * lax.axis_size("rows"))
     band = upper_tiles.shape[1]
-    coupling = upper_tiles[-band:]
     partners = lax.axis_size("node") - 1
     columns = subspace.shape[1]
-    factors, parts = [], ()
+    factors, earlier = [], ()
     for iteration in range(ITERS):
+        final = iteration == ITERS - 1
         if iteration == 0:
-            base, out_a, out_b, inverse = start(subspace, weights, coupling, inverse)
+            base, out_a, out_b, inverse, coupling, weights = start(
+                subspace, weights, upper_tiles, inverse
+            )
         else:
-            base, out_a, out_b = solve(field, factor, weights, coupling, inverse)
+            base, out_a, out_b = solve(field, low[0], factor, weights, coupling, inverse)
         got_a, got_b = core_swap(out_a), link_swap(out_b)
-        own, *others = correct(
-            weights, base, got_a, got_b, coupling, inverse, TERM_TYPES[iteration]
+        own, *terms = correct(
+            weights, base, got_a, got_b, coupling, inverse, 1 if final else 2
         )
-        piece = tree_sum([own] + [x.astype(F32) for x in node_spread(others)])
-        piece = piece.astype(FIELD_TYPES[iteration])
-        field, head, part = gram_slice([piece] + node_spread([piece] * partners), band)
+        got = node_spread(terms[:partners])
+        if not final:
+            low_got = node_spread(terms[partners:])
+        total = tree_sum([own] + [x.astype(F32) for x in got])
+        piece = total.astype(BF16)
+        blocks = [piece] + node_spread([piece] * partners)
+        low = ()
+        if not final:
+            total, sent = lax.optimization_barrier((total, piece))
+            total = total + tree_sum([x.astype(F32) for x in low_got])
+            low_piece = (total - sent.astype(F32)).astype(BF16)
+            low = (join([low_piece] + node_spread([low_piece] * partners)),)
+        field, head, part = gram_slice(blocks, band)
         part = part + core_swap(part)
         following = next_head(after(head, part))
         total = chip_sum(part)
         gathered = [total] + node_spread([total] * partners)
-        pair = band_slice(field, after(following, total), diag_tiles, upper_tiles, *parts)
-        parts = (pair,)
+        pair = band_slice(field, low, after(following, total), diag_tiles, upper_tiles, earlier)
+        earlier = (pair,)
         halves = first_factor(gathered, order)
-        if iteration == ITERS - 1:
-            pair = pair + core_swap(after(pair, *gathered))
+        if final:
+            pair = pair + core_swap(pair)
+            pair = chip_sum(after(pair, *gathered))
             pair = after(pair, *halves)
-            pair = chip_sum(pair)
+            spread = [pair] + node_spread([pair] * partners)
         factor = second_factor(halves)
         factors.append(factor)
-    pair = after(pair, factor)
-    spread = [pair] + node_spread([pair] * partners)
     orthonormal = whole(last_kernel, jax.ShapeDtypeStruct(subspace.shape, F32), field, factor)
     projected = whole(
         functools.partial(projected_kernel, order),

time: 142 us -> 132 us (0.930)
  waiting for transfers between devices: 46.4 us -> 32.1 us
  starting transfers between devices: 56.1 us -> 62.8 us
  local copies, waits for them, and re-layouts: 2.51 us -> 0.01 us
    ppermute x21 -> x27, waiting for transfers between devices: 31 us -> 20.8 us  [node_swap(): return lax.ppermute(block, 'node', [(i, i ^ step) for i in range(count)])]
    ppermute x21 -> x27, starting transfers between devices: 25.8 us -> 31.4 us  [node_swap(): return lax.ppermute(block, 'node', [(i, i ^ step) for i in range(count)])]
    ppermute x5, starting transfers between devices: 4.24 us -> 7.66 us  [core_swap(): return lax.ppermute(block, 'rows', [(i, i ^ 1) for i in range(count)])]
    ppermute x9, waiting for transfers between devices: 12.8 us -> 9.75 us  [chip_sum(): lax.ppermute(block, 'rows', route)]
    ppermute x9, starting transfers between devices: 22 us -> 19.6 us  [chip_sum(): lax.ppermute(block, 'rows', route)]
    unnamed x10 -> x4, local copies, waits for them, and re-layouts: 1.66 us -> 0.01 us
    pallas_call x13 -> x14, Pallas kernels: 32.8 us -> 32.3 us  [whole(): pl.pallas_call(kernel, out_shape=out_shape, in_specs=[vmem for _ in opera...]
  transfers between devices with their start and end apart: 39 -> 45, of which waited for: 28 -> 23; matrix products, arithmetic and copies ran while one was open for 0% -> 0% of each run, Pallas kernels for 10% -> 10%
where the time goes in v6:
time: 132 us; the launch traced here: 131 us
  starting transfers between devices  62.8 us (48%)
  Pallas kernels  35.2 us (27%)
  waiting for transfers between devices  32.1 us (24%)
    pallas_call x14, Pallas kernels, whole(): pl.pallas_call(kernel, out_shape=out_shape, in_specs=[vmem for _ in opera...  32.3 us
    ppermute x27, starting transfers between devices, node_swap(): return lax.ppermute(block, 'node', [(i, i ^ step) for i in range(count)])  31.4 us
    ppermute x27, waiting for transfers between devices, node_swap(): return lax.ppermute(block, 'node', [(i, i ^ step) for i in range(count)])  20.8 us
    ppermute x9, starting transfers between devices, chip_sum(): lax.ppermute(block, 'rows', route)  19.6 us
    ppermute x9, waiting for transfers between devices, chip_sum(): lax.ppermute(block, 'rows', route)  9.75 us
    ppermute x5, starting transfers between devices, core_swap(): return lax.ppermute(block, 'rows', [(i, i ^ 1) for i in range(count)])  7.66 us
    pallas_call x1, Pallas kernels, start(): pl.pallas_call(start_kernel, in_specs=[pl.BlockSpec(memory_space=pltpu.HB...  2.89 us
  transfers between devices with their start and end apart: 45, of which 23 were waited for; matrix products, arithmetic and copies ran while one was open for 0% of the time, Pallas kernels for 10%

profile of v6, /device:TPU:0, one launch (start us, length us, event | category | flops | bytes accessed | tf_op | source)
XLA Modules:
  0.0 131.3 jit_solution(4093167709582593562)
XLA Ops:
  0.6 2.9 %start.1 = (f32[768,256]{1,0:T(8,128)S(1)}, bf16[128,512]{1,0:T(8,128)(2,1)S(1)}, bf16[128,512]{1,0:T(8,128)(2,1)S(1)}, bf16[1,2,768,768]{3,2,1,0:T(8,128)(2,1)S...) custom-call(f32[1,2]{1,0:T(1,128)} %weights_at.1, bf16[1,2,768,768]{3,2,1,0:T(8,128)(2,1)} %source.1, ...), custom_call_target="tpu_custom_call" | custom-call | flops 603979776 | bytes 2359296 | tf_op jit(solution)/shard_map/start/pallas_call | solution.py:188
  5.1 1.3 %shard_map.68 = (f32[192,256]{1,0:T(8,128)S(1)}, bf16[192,256]{1,0:T(8,128)(2,1)S(1)}, bf16[192,256]{1,0:T(8,128)(2,1)S(1)}, bf16[192,256]{1,0:T(8,128)(2,1)S(1)...) custom-call(f32[1,2]{1,0:T(1,128)S(1)} %get-tuple-element.44.weights, ...), custom_call_target="tpu_custom_call" | custom-call | flops 402653184 | bytes 3473416 | tf_op jit(solution)/shard_map/pallas_call | solution.py:82
  6.4 2.9 %collective-permute-start.2 = (bf16[192,256]{1,0:T(8,128)(2,1)S(1)}, bf16[192,256]{1,0:T(8,128)(2,1)S(1)}, u32[]{:S(2)}, u32[]{:S(2)}) collective-permute-start(bf16[192,256]{1,0:T(8,128)(2,1)S(1)} %get-tuple-element.51), channel_id=1, source_target_pairs={{0,8},{8,0},{16,24},{24,16},{1,9},{9,1},{17,25},{25,17},{2,10},{10... | collective-permute-start | bytes 294920 | tf_op jit(solution)/shard_map/ppermute | solution.py:95
  9.3 1.5 %collective-permute-start.3 = (bf16[192,256]{1,0:T(8,128)(2,1)S(1)}, bf16[192,256]{1,0:T(8,128)(2,1)S(1)}, u32[]{:S(2)}, u32[]{:S(2)}) collective-permute-start(bf16[192,256]{1,0:T(8,128)(2,1)S(1)} %get-tuple-element.52), channel_id=1, source_target_pairs={{0,16},{8,24},{16,0},{24,8},{1,17},{9,25},{17,1},{25,9},{2,18},{10... | collective-permute-start | bytes 294920 | tf_op jit(solution)/shard_map/ppermute | solution.py:95
  11.9 2.0 %collective-permute-done.3 = bf16[192,256]{1,0:T(8,128)(2,1)S(1)} collective-permute-done((bf16[192,256]{1,0:T(8,128)(2,1)S(1)}, bf16[192,256]{1,0:T(8,128)(2,1)S(1)}, u32[]{:S(2)}, u32[]{:S(2)}) %collective-permute-start.3) | collective-permute-done | bytes 98336 | tf_op jit(solution)/shard_map/ppermute | solution.py:95
  14.0 2.4 %collective-permute-done.4 = bf16[192,256]{1,0:T(8,128)(2,1)S(1)} collective-permute-done((bf16[192,256]{1,0:T(8,128)(2,1)S(1)}, bf16[192,256]{1,0:T(8,128)(2,1)S(1)}, u32[]{:S(2)}, u32[]{:S(2)}) %collective-permute-start.4) | collective-permute-done | bytes 98336 | tf_op jit(solution)/shard_map/ppermute | solution.py:95
  16.6 1.9 %collective-permute-start.6 = (bf16[192,256]{1,0:T(8,128)(2,1)S(1)}, bf16[192,256]{1,0:T(8,128)(2,1)S(1)}, u32[]{:S(2)}, u32[]{:S(2)}) collective-permute-start(bf16[192,256]{1,0:T(8,128)(2,1)S(1)} %get-tuple-element.59.refs_0_), channel_id=1, source_target_pairs={{0,16},{8,24},{16,0},{24,8},{1,17},{9,25},{17,1},{25,9},{2,18},{10... | collective-permute-start | bytes 294920 | tf_op jit(solution)/shard_map/ppermute | solution.py:95
  18.5 1.5 %collective-permute-start.5 = (bf16[192,256]{1,0:T(8,128)(2,1)S(1)}, bf16[192,256]{1,0:T(8,128)(2,1)S(1)}, u32[]{:S(2)}, u32[]{:S(2)}) collective-permute-start(bf16[192,256]{1,0:T(8,128)(2,1)S(1)} %get-tuple-element.59.refs_0_), channel_id=1, source_target_pairs={{0,8},{8,0},{16,24},{24,16},{1,9},{9,1},{17,25},{25,17},{2,10},{10... | collective-permute-start | bytes 294920 | tf_op jit(solution)/shard_map/ppermute | solution.py:95
  20.7 1.4 %collective-permute-done.7.refs_3_ = bf16[192,256]{1,0:T(8,128)(2,1)S(1)} collective-permute-done((bf16[192,256]{1,0:T(8,128)(2,1)S(1)}, bf16[192,256]{1,0:T(8,128)(2,1)S(1)}, u32[]{:S(2)}, u32[]{:S(2)}) %collective-permute-start.7) | collective-permute-done | bytes 98336 | tf_op jit(solution)/shard_map/ppermute | solution.py:95
  22.0 1.5 %collective-permute-start.10 = (bf16[192,256]{1,0:T(8,128)(2,1)S(1)}, bf16[192,256]{1,0:T(8,128)(2,1)S(1)}, u32[]{:S(2)}, u32[]{:S(2)}) collective-permute-start(bf16[192,256]{1,0:T(8,128)(2,1)S(1)} %get-tuple-element.58), channel_id=1, source_target_pairs={{0,24},{8,16},{16,8},{24,0},{1,25},{9,17},{17,9},{25,1},{2,26},{10... | collective-permute-start | bytes 294920 | tf_op jit(solution)/shard_map/ppermute | solution.py:95
  23.9 3.5 %collective-permute-start.14 = (f32[64,256]{1,0:T(8,128)S(1)}, f32[64,256]{1,0:T(8,128)S(1)}, u32[]{:S(2)}, u32[]{:S(2)}) collective-permute-start(f32[64,256]{1,0:T(8,128)S(1)} %get-tuple-element.60), channel_id=1, source_target_pairs={{0,1},{1,0},{2,3},{3,2},{4,5},{5,4},{6,7},{7,6},{8,9},{9,8},{10,11... | collective-permute-start | bytes 196616 | tf_op jit(solution)/shard_map/ppermute | solution.py:100
  28.3 6.6 %collective-permute-start.17 = (f32[64,256]{1,0:T(8,128)S(1)}, f32[64,256]{1,0:T(8,128)S(1)}, u32[]{:S(2)}, u32[]{:S(2)}) collective-permute-start(f32[64,256]{1,0:T(8,128)S(1)} %add.69), channel_id=1, source_target_pairs={{0,6},{1,7},{2,4},{3,5},{4,2},{5,3},{6,0},{7,1},{8,14},{9,15},{10,... | collective-permute-start | bytes 196616 | tf_op jit(solution)/shard_map/ppermute | solution.py:126
  35.6 1.6 %collective-permute-start.13 = (bf16[192,256]{1,0:T(8,128)(2,1)S(1)}, bf16[192,256]{1,0:T(8,128)(2,1)S(1)}, u32[]{:S(2)}, u32[]{:S(2)}) collective-permute-start(bf16[192,256]{1,0:T(8,128)(2,1)S(1)} %subtract_convert_fusion.refs_0_), channel_id=1, source_target_pairs={{0,24},{8,16},{16,8},{24,0},{1,25},{9,17},{17,9},{25,1},{2,26},{10... | collective-permute-start | bytes 294920 | tf_op jit(solution)/shard_map/ppermute | solution.py:95
  39.1 2.2 %collective-permute-done.16 = f32[64,256]{1,0:T(8,128)S(1)} collective-permute-done((f32[64,256]{1,0:T(8,128)S(1)}, f32[64,256]{1,0:T(8,128)S(1)}, u32[]{:S(2)}, u32[]{:S(2)}) %collective-permute-start.16) | collective-permute-done | bytes 65568 | tf_op jit(solution)/shard_map/ppermute | solution.py:126
  41.3 1.5 %collective-permute-start.20 = (f32[64,256]{1,0:T(8,128)S(1)}, f32[64,256]{1,0:T(8,128)S(1)}, u32[]{:S(2)}, u32[]{:S(2)}) collective-permute-start(f32[64,256]{1,0:T(8,128)S(1)} %add_add_fusion.3.refs_0_), channel_id=1, source_target_pairs={{0,24},{8,16},{16,8},{24,0},{1,25},{9,17},{17,9},{25,1},{2,26},{10... | collective-permute-start | bytes 196616 | tf_op jit(solution)/shard_map/ppermute | solution.py:95
  43.7 1.2 collective-permute-start.18
  45.0 2.2 %collective-permute-done.20.refs_3_ = f32[64,256]{1,0:T(8,128)S(1)} collective-permute-done((f32[64,256]{1,0:T(8,128)S(1)}, f32[64,256]{1,0:T(8,128)S(1)}, u32[]{:S(2)}, u32[]{:S(2)}) %collective-permute-start.20) | collective-permute-done | bytes 65568 | tf_op jit(solution)/shard_map/ppermute | solution.py:95
  48.0 5.9 %shard_map.71 = (f32[128,128]{1,0:T(8,128)S(1)}, f32[128,128]{1,0:T(8,128)S(1)}, f32[128,128]{1,0:T(8,128)S(1)}, f32[1,256]{1,0:T(1,128)S(1)}) custom-call(f32[64,256]{1,0:T(8,128)S(1)} %add_add_fusion.3.refs_0_, f32[64,256]{1,0:T(8,128)S(1)} %collective-permute-done.18.refs_1_, f32[64,256]{1,0:T(8,128)S(1)} %collective-permute-done.19.refs_2_, ...), custom_call_target="tpu_custom_call" | custom-call | flops 6000000000 | bytes 262144 | tf_op jit(solution)/shard_map/pallas_call | solution.py:82
  53.8 4.9 %shard_map.72.factor.refs_4_ = f32[256,256]{1,0:T(8,128)S(1)} custom-call(f32[128,128]{1,0:T(8,128)S(1)} %get-tuple-element.61.top, f32[128,128]{1,0:T(8,128)S(1)} %get-tuple-element.62.corner, f32[128,128]{1,0:T(8,128)S(1)} %get-tuple-element.63.rest, f32[1,256]{1,0:T(1,128)S(1)} %get-tuple-element.64.across), custom_call_target="tpu_custom_call" | custom-call | flops 6000000000 | bytes 197632 | tf_op jit(solution)/shard_map/pallas_call | solution.py:82
  58.8 2.1 %shard_map.73 = (f32[768,256]{1,0:T(8,128)S(1)}, bf16[128,512]{1,0:T(8,128)(2,1)S(1)}, bf16[128,512]{1,0:T(8,128)(2,1)S(1)}) custom-call(f32[1,2]{1,0:T(1,128)S(1)} %get-tuple-element.44.weights, bf16[768,256]{1,0:T(8,128)(2,1)S(1)} %get-tuple-element.54.field, bf16[768,256]{1,0:T(8,128)(2,1)S(1)} %shard_map.70.low.refs_0_, ...), custom_call_target="tpu_custom_call" | custom-call | flops 603979776 | bytes 3473416 | tf_op jit(solution)/shard_map/pallas_call | solution.py:82
  62.4 1.3 shard_map.74
  63.6 1.3 collective-permute-start.23
  65.5 1.7 %collective-permute-start.25 = (bf16[192,256]{1,0:T(8,128)(2,1)S(1)}, bf16[192,256]{1,0:T(8,128)(2,1)S(1)}, u32[]{:S(2)}, u32[]{:S(2)}) collective-permute-start(bf16[192,256]{1,0:T(8,128)(2,1)S(1)} %get-tuple-element.71), channel_id=1, source_target_pairs={{0,24},{8,16},{16,8},{24,0},{1,25},{9,17},{17,9},{25,1},{2,26},{10... | collective-permute-start | bytes 294920 | tf_op jit(solution)/shard_map/ppermute | solution.py:95
  67.2 1.1 collective-permute-done.23
  68.3 1.2 collective-permute-done.24
  69.5 1.5 %collective-permute-done.25 = bf16[192,256]{1,0:T(8,128)(2,1)S(1)} collective-permute-done((bf16[192,256]{1,0:T(8,128)(2,1)S(1)}, bf16[192,256]{1,0:T(8,128)(2,1)S(1)}, u32[]{:S(2)}, u32[]{:S(2)}) %collective-permute-start.25) | collective-permute-done | bytes 98336 | tf_op jit(solution)/shard_map/ppermute | solution.py:95
  71.1 1.8 %collective-permute-start.28 = (bf16[192,256]{1,0:T(8,128)(2,1)S(1)}, bf16[192,256]{1,0:T(8,128)(2,1)S(1)}, u32[]{:S(2)}, u32[]{:S(2)}) collective-permute-start(bf16[192,256]{1,0:T(8,128)(2,1)S(1)} %add_convert_fusion.refs_0_), channel_id=1, source_target_pairs={{0,24},{8,16},{16,8},{24,0},{1,25},{9,17},{17,9},{25,1},{2,26},{10... | collective-permute-start | bytes 294920 | tf_op jit(solution)/shard_map/ppermute | solution.py:95
  72.8 1.1 collective-permute-start.27
  74.6 2.0 %collective-permute-done.28.refs_3_ = bf16[192,256]{1,0:T(8,128)(2,1)S(1)} collective-permute-done((bf16[192,256]{1,0:T(8,128)(2,1)S(1)}, bf16[192,256]{1,0:T(8,128)(2,1)S(1)}, u32[]{:S(2)}, u32[]{:S(2)}) %collective-permute-start.28) | collective-permute-done | bytes 98336 | tf_op jit(solution)/shard_map/ppermute | solution.py:95
  78.9 2.4 %collective-permute-start.29 = (f32[64,256]{1,0:T(8,128)S(1)}, f32[64,256]{1,0:T(8,128)S(1)}, u32[]{:S(2)}, u32[]{:S(2)}) collective-permute-start(f32[64,256]{1,0:T(8,128)S(1)} %get-tuple-element.73), channel_id=1, source_target_pairs={{0,1},{1,0},{2,3},{3,2},{4,5},{5,4},{6,7},{7,6},{8,9},{9,8},{10,11... | collective-permute-start | bytes 196616 | tf_op jit(solution)/shard_map/ppermute | solution.py:100
  81.3 1.3 collective-permute-start.37
  82.6 7.3 %collective-permute-start.32 = (f32[64,256]{1,0:T(8,128)S(1)}, f32[64,256]{1,0:T(8,128)S(1)}, u32[]{:S(2)}, u32[]{:S(2)}) collective-permute-start(f32[64,256]{1,0:T(8,128)S(1)} %add.76), channel_id=1, source_target_pairs={{0,6},{1,7},{2,4},{3,5},{4,2},{5,3},{6,0},{7,1},{8,14},{9,15},{10,... | collective-permute-start | bytes 196616 | tf_op jit(solution)/shard_map/ppermute | solution.py:126
  90.6 1.2 shard_map.79.refs_0_
  91.9 1.3 collective-permute-start.36
  93.8 2.3 %collective-permute-done.31 = f32[64,256]{1,0:T(8,128)S(1)} collective-permute-done((f32[64,256]{1,0:T(8,128)S(1)}, f32[64,256]{1,0:T(8,128)S(1)}, u32[]{:S(2)}, u32[]{:S(2)}) %collective-permute-start.31) | collective-permute-done | bytes 65568 | tf_op jit(solution)/shard_map/ppermute | solution.py:126
  97.1 1.1 collective-permute-start.38
  98.3 1.3 collective-permute-start.35
  100.6 1.2 collective-permute-start.33
  101.8 2.0 %collective-permute-done.35.refs_3_ = f32[64,256]{1,0:T(8,128)S(1)} collective-permute-done((f32[64,256]{1,0:T(8,128)S(1)}, f32[64,256]{1,0:T(8,128)S(1)}, u32[]{:S(2)}, u32[]{:S(2)}) %collective-permute-start.35) | collective-permute-done | bytes 65568 | tf_op jit(solution)/shard_map/ppermute | solution.py:95
  104.9 2.4 %collective-permute-start.41 = (f32[128,256]{1,0:T(8,128)S(1)}, f32[128,256]{1,0:T(8,128)S(1)}, u32[]{:S(2)}, u32[]{:S(2)}) collective-permute-start(f32[128,256]{1,0:T(8,128)S(1)} %add.80), channel_id=1, source_target_pairs={{0,6},{1,7},{2,4},{3,5},{4,2},{5,3},{6,0},{7,1},{8,14},{9,15},{10,... | collective-permute-start | bytes 393224 | tf_op jit(solution)/shard_map/ppermute | solution.py:126
  108.0 1.2 collective-permute-start.39
  109.2 5.9 %shard_map.76 = (f32[128,128]{1,0:T(8,128)S(1)}, f32[128,128]{1,0:T(8,128)S(1)}, f32[128,128]{1,0:T(8,128)S(1)}, f32[1,256]{1,0:T(1,128)S(1)}) custom-call(f32[64,256]{1,0:T(8,128)S(1)} %add_add_fusion.2.refs_0_, f32[64,256]{1,0:T(8,128)S(1)} %collective-permute-done.33.refs_1_, f32[64,256]{1,0:T(8,128)S(1)} %collective-permute-done.34.refs_2_, ...), custom_call_target="tpu_custom_call" | custom-call | flops 6000000000 | bytes 262144 | tf_op jit(solution)/shard_map/pallas_call | solution.py:82
  115.1 4.6 %collective-permute-done.40 = f32[128,256]{1,0:T(8,128)S(1)} collective-permute-done((f32[128,256]{1,0:T(8,128)S(1)}, f32[128,256]{1,0:T(8,128)S(1)}, u32[]{:S(2)}, u32[]{:S(2)}) %collective-permute-start.40) | collective-permute-done | bytes 131104 | tf_op jit(solution)/shard_map/ppermute | solution.py:126
  119.8 1.4 %collective-permute-start.44 = (f32[128,256]{1,0:T(8,128)S(1)}, f32[128,256]{1,0:T(8,128)S(1)}, u32[]{:S(2)}, u32[]{:S(2)}) collective-permute-start(f32[128,256]{1,0:T(8,128)S(1)} %add_add_fusion.1.refs_0_), channel_id=1, source_target_pairs={{0,24},{8,16},{16,8},{24,0},{1,25},{9,17},{17,9},{25,1},{2,26},{10... | collective-permute-start | bytes 393224 | tf_op jit(solution)/shard_map/ppermute | solution.py:95
  122.0 1.4 %collective-permute-start.42 = (f32[128,256]{1,0:T(8,128)S(1)}, f32[128,256]{1,0:T(8,128)S(1)}, u32[]{:S(2)}, u32[]{:S(2)}) collective-permute-start(f32[128,256]{1,0:T(8,128)S(1)} %add_add_fusion.1.refs_0_), channel_id=1, source_target_pairs={{0,8},{8,0},{16,24},{24,16},{1,9},{9,1},{17,25},{25,17},{2,10},{10... | collective-permute-start | bytes 393224 | tf_op jit(solution)/shard_map/ppermute | solution.py:95
  123.3 4.9 %shard_map.77.factor.refs_5_ = f32[256,256]{1,0:T(8,128)S(1)} custom-call(f32[128,128]{1,0:T(8,128)S(1)} %get-tuple-element.74.top, f32[128,128]{1,0:T(8,128)S(1)} %get-tuple-element.75.corner, f32[128,128]{1,0:T(8,128)S(1)} %get-tuple-element.76.rest, f32[1,256]{1,0:T(1,128)S(1)} %get-tuple-element.77.across), custom_call_target="tpu_custom_call" | custom-call | flops 6000000000 | bytes 197632 | tf_op jit(solution)/shard_map/pallas_call | solution.py:82
  128.3 1.3 shard_map.78
  129.6 1.7 %shard_map.81 = f32[2,256,256]{2,1,0:T(8,128)} custom-call(f32[128,256]{1,0:T(8,128)S(1)} %add_add_fusion.1.refs_0_, f32[128,256]{1,0:T(8,128)S(1)} %collective-permute-done.42.refs_1_, f32[128,256]{1,0:T(8,128)S(1)} %collective-permute-done.43.refs_2_, f32[128,256]{1,0:T(8,128)S(1)} %collective-permute-done.44.refs_3_, ...), custom_call_target="tpu_custom_call" | custom-call | flops 100000000 | bytes 1048576 | tf_op jit(solution)/shard_map/pallas_call | solution.py:82
  (70 shorter events, 20.1 us)
Async XLA Ops:
  3.5 1.5 %collective-permute-start = (bf16[128,512]{1,0:T(8,128)(2,1)S(1)}, bf16[128,512]{1,0:T(8,128)(2,1)S(1)}, u32[]{:S(2)}, u32[]{:S(2)}) collective-permute-start(bf16[128,512]{1,0:T(8,128)(2,1)S(1)} %get-tuple-element.46), channel_id=1, source_target_pairs={{0,1},{1,0},{2,3},{3,2},{4,5},{5,4},{6,7},{7,6},{8,9},{9,8},{10,11... | collective-permute-start | bytes 393224 | tf_op jit(solution)/shard_map/ppermute | solution.py:100
  4.1 1.0 collective-permute-start.1
  6.4 5.5 %collective-permute-start.2 = (bf16[192,256]{1,0:T(8,128)(2,1)S(1)}, bf16[192,256]{1,0:T(8,128)(2,1)S(1)}, u32[]{:S(2)}, u32[]{:S(2)}) collective-permute-start(bf16[192,256]{1,0:T(8,128)(2,1)S(1)} %get-tuple-element.51), channel_id=1, source_target_pairs={{0,8},{8,0},{16,24},{24,16},{1,9},{9,1},{17,25},{25,17},{2,10},{10... | collective-permute-start | bytes 294920 | tf_op jit(solution)/shard_map/ppermute | solution.py:95
  9.3 4.6 %collective-permute-start.3 = (bf16[192,256]{1,0:T(8,128)(2,1)S(1)}, bf16[192,256]{1,0:T(8,128)(2,1)S(1)}, u32[]{:S(2)}, u32[]{:S(2)}) collective-permute-start(bf16[192,256]{1,0:T(8,128)(2,1)S(1)} %get-tuple-element.52), channel_id=1, source_target_pairs={{0,16},{8,24},{16,0},{24,8},{1,17},{9,25},{17,1},{25,9},{2,18},{10... | collective-permute-start | bytes 294920 | tf_op jit(solution)/shard_map/ppermute | solution.py:95
  10.9 5.5 %collective-permute-start.4 = (bf16[192,256]{1,0:T(8,128)(2,1)S(1)}, bf16[192,256]{1,0:T(8,128)(2,1)S(1)}, u32[]{:S(2)}, u32[]{:S(2)}) collective-permute-start(bf16[192,256]{1,0:T(8,128)(2,1)S(1)} %get-tuple-element.53), channel_id=1, source_target_pairs={{0,24},{8,16},{16,8},{24,0},{1,25},{9,17},{17,9},{25,1},{2,26},{10... | collective-permute-start | bytes 294920 | tf_op jit(solution)/shard_map/ppermute | solution.py:95
  16.5 5.6 %collective-permute-start.7 = (bf16[192,256]{1,0:T(8,128)(2,1)S(1)}, bf16[192,256]{1,0:T(8,128)(2,1)S(1)}, u32[]{:S(2)}, u32[]{:S(2)}) collective-permute-start(bf16[192,256]{1,0:T(8,128)(2,1)S(1)} %get-tuple-element.59.refs_0_), channel_id=1, source_target_pairs={{0,24},{8,16},{16,8},{24,0},{1,25},{9,17},{17,9},{25,1},{2,26},{10... | collective-permute-start | bytes 294920 | tf_op jit(solution)/shard_map/ppermute | solution.py:95
  16.6 6.9 %collective-permute-start.6 = (bf16[192,256]{1,0:T(8,128)(2,1)S(1)}, bf16[192,256]{1,0:T(8,128)(2,1)S(1)}, u32[]{:S(2)}, u32[]{:S(2)}) collective-permute-start(bf16[192,256]{1,0:T(8,128)(2,1)S(1)} %get-tuple-element.59.refs_0_), channel_id=1, source_target_pairs={{0,16},{8,24},{16,0},{24,8},{1,17},{9,25},{17,1},{25,9},{2,18},{10... | collective-permute-start | bytes 294920 | tf_op jit(solution)/shard_map/ppermute | solution.py:95
  18.5 5.0 %collective-permute-start.5 = (bf16[192,256]{1,0:T(8,128)(2,1)S(1)}, bf16[192,256]{1,0:T(8,128)(2,1)S(1)}, u32[]{:S(2)}, u32[]{:S(2)}) collective-permute-start(bf16[192,256]{1,0:T(8,128)(2,1)S(1)} %get-tuple-element.59.refs_0_), channel_id=1, source_target_pairs={{0,8},{8,0},{16,24},{24,16},{1,9},{9,1},{17,25},{25,17},{2,10},{10... | collective-permute-start | bytes 294920 | tf_op jit(solution)/shard_map/ppermute | solution.py:95
  20.0 15.0 %collective-permute-start.8 = (bf16[192,256]{1,0:T(8,128)(2,1)S(1)}, bf16[192,256]{1,0:T(8,128)(2,1)S(1)}, u32[]{:S(2)}, u32[]{:S(2)}) collective-permute-start(bf16[192,256]{1,0:T(8,128)(2,1)S(1)} %get-tuple-element.56), channel_id=1, source_target_pairs={{0,8},{8,0},{16,24},{24,16},{1,9},{9,1},{17,25},{25,17},{2,10},{10... | collective-permute-start | bytes 294920 | tf_op jit(solution)/shard_map/ppermute | solution.py:95
  20.5 15.0 %collective-permute-start.9 = (bf16[192,256]{1,0:T(8,128)(2,1)S(1)}, bf16[192,256]{1,0:T(8,128)(2,1)S(1)}, u32[]{:S(2)}, u32[]{:S(2)}) collective-permute-start(bf16[192,256]{1,0:T(8,128)(2,1)S(1)} %get-tuple-element.57), channel_id=1, source_target_pairs={{0,16},{8,24},{16,0},{24,8},{1,17},{9,25},{17,1},{25,9},{2,18},{10... | collective-permute-start | bytes 294920 | tf_op jit(solution)/shard_map/ppermute | solution.py:95
  22.0 13.5 %collective-permute-start.10 = (bf16[192,256]{1,0:T(8,128)(2,1)S(1)}, bf16[192,256]{1,0:T(8,128)(2,1)S(1)}, u32[]{:S(2)}, u32[]{:S(2)}) collective-permute-start(bf16[192,256]{1,0:T(8,128)(2,1)S(1)} %get-tuple-element.58), channel_id=1, source_target_pairs={{0,24},{8,16},{16,8},{24,0},{1,25},{9,17},{17,9},{25,1},{2,26},{10... | collective-permute-start | bytes 294920 | tf_op jit(solution)/shard_map/ppermute | solution.py:95
  23.9 4.4 %collective-permute-start.14 = (f32[64,256]{1,0:T(8,128)S(1)}, f32[64,256]{1,0:T(8,128)S(1)}, u32[]{:S(2)}, u32[]{:S(2)}) collective-permute-start(f32[64,256]{1,0:T(8,128)S(1)} %get-tuple-element.60), channel_id=1, source_target_pairs={{0,1},{1,0},{2,3},{3,2},{4,5},{5,4},{6,7},{7,6},{8,9},{9,8},{10,11... | collective-permute-start | bytes 196616 | tf_op jit(solution)/shard_map/ppermute | solution.py:100
  28.3 9.9 %collective-permute-start.17 = (f32[64,256]{1,0:T(8,128)S(1)}, f32[64,256]{1,0:T(8,128)S(1)}, u32[]{:S(2)}, u32[]{:S(2)}) collective-permute-start(f32[64,256]{1,0:T(8,128)S(1)} %add.69), channel_id=1, source_target_pairs={{0,6},{1,7},{2,4},{3,5},{4,2},{5,3},{6,0},{7,1},{8,14},{9,15},{10,... | collective-permute-start | bytes 196616 | tf_op jit(solution)/shard_map/ppermute | solution.py:126
  34.9 6.5 %collective-permute-start.16 = (f32[64,256]{1,0:T(8,128)S(1)}, f32[64,256]{1,0:T(8,128)S(1)}, u32[]{:S(2)}, u32[]{:S(2)}) collective-permute-start(f32[64,256]{1,0:T(8,128)S(1)} %add.69), channel_id=1, source_target_pairs={{0,4},{1,5},{2,6},{3,7},{4,0},{5,1},{6,2},{7,3},{8,12},{9,13},{10,... | collective-permute-start | bytes 196616 | tf_op jit(solution)/shard_map/ppermute | solution.py:126
  35.0 6.3 %collective-permute-start.15 = (f32[64,256]{1,0:T(8,128)S(1)}, f32[64,256]{1,0:T(8,128)S(1)}, u32[]{:S(2)}, u32[]{:S(2)}) collective-permute-start(f32[64,256]{1,0:T(8,128)S(1)} %add.69), channel_id=1, source_target_pairs={{0,2},{1,3},{2,0},{3,1},{4,6},{5,7},{6,4},{7,5},{8,10},{9,11},{10,... | collective-permute-start | bytes 196616 | tf_op jit(solution)/shard_map/ppermute | solution.py:126
  35.6 8.1 %collective-permute-start.13 = (bf16[192,256]{1,0:T(8,128)(2,1)S(1)}, bf16[192,256]{1,0:T(8,128)(2,1)S(1)}, u32[]{:S(2)}, u32[]{:S(2)}) collective-permute-start(bf16[192,256]{1,0:T(8,128)(2,1)S(1)} %subtract_convert_fusion.refs_0_), channel_id=1, source_target_pairs={{0,24},{8,16},{16,8},{24,0},{1,25},{9,17},{17,9},{25,1},{2,26},{10... | collective-permute-start | bytes 294920 | tf_op jit(solution)/shard_map/ppermute | solution.py:95
  37.2 7.7 %collective-permute-start.12 = (bf16[192,256]{1,0:T(8,128)(2,1)S(1)}, bf16[192,256]{1,0:T(8,128)(2,1)S(1)}, u32[]{:S(2)}, u32[]{:S(2)}) collective-permute-start(bf16[192,256]{1,0:T(8,128)(2,1)S(1)} %subtract_convert_fusion.refs_0_), channel_id=1, source_target_pairs={{0,16},{8,24},{16,0},{24,8},{1,17},{9,25},{17,1},{25,9},{2,18},{10... | collective-permute-start | bytes 294920 | tf_op jit(solution)/shard_map/ppermute | solution.py:95
  38.2 6.7 %collective-permute-start.11 = (bf16[192,256]{1,0:T(8,128)(2,1)S(1)}, bf16[192,256]{1,0:T(8,128)(2,1)S(1)}, u32[]{:S(2)}, u32[]{:S(2)}) collective-permute-start(bf16[192,256]{1,0:T(8,128)(2,1)S(1)} %subtract_convert_fusion.refs_0_), channel_id=1, source_target_pairs={{0,8},{8,0},{16,24},{24,16},{1,9},{9,1},{17,25},{25,17},{2,10},{10... | collective-permute-start | bytes 294920 | tf_op jit(solution)/shard_map/ppermute | solution.py:95
  41.3 5.8 %collective-permute-start.20 = (f32[64,256]{1,0:T(8,128)S(1)}, f32[64,256]{1,0:T(8,128)S(1)}, u32[]{:S(2)}, u32[]{:S(2)}) collective-permute-start(f32[64,256]{1,0:T(8,128)S(1)} %add_add_fusion.3.refs_0_), channel_id=1, source_target_pairs={{0,24},{8,16},{16,8},{24,0},{1,25},{9,17},{17,9},{25,1},{2,26},{10... | collective-permute-start | bytes 196616 | tf_op jit(solution)/shard_map/ppermute | solution.py:95
  42.8 4.8 %collective-permute-start.19 = (f32[64,256]{1,0:T(8,128)S(1)}, f32[64,256]{1,0:T(8,128)S(1)}, u32[]{:S(2)}, u32[]{:S(2)}) collective-permute-start(f32[64,256]{1,0:T(8,128)S(1)} %add_add_fusion.3.refs_0_), channel_id=1, source_target_pairs={{0,16},{8,24},{16,0},{24,8},{1,17},{9,25},{17,1},{25,9},{2,18},{10... | collective-permute-start | bytes 196616 | tf_op jit(solution)/shard_map/ppermute | solution.py:95
  43.7 4.3 %collective-permute-start.18 = (f32[64,256]{1,0:T(8,128)S(1)}, f32[64,256]{1,0:T(8,128)S(1)}, u32[]{:S(2)}, u32[]{:S(2)}) collective-permute-start(f32[64,256]{1,0:T(8,128)S(1)} %add_add_fusion.3.refs_0_), channel_id=1, source_target_pairs={{0,8},{8,0},{16,24},{24,16},{1,9},{9,1},{17,25},{25,17},{2,10},{10... | collective-permute-start | bytes 196616 | tf_op jit(solution)/shard_map/ppermute | solution.py:95
  60.9 29.7 %copy-start = (f32[768,128]{1,0:T(8,128)S(1)}, f32[768,128]{1,0:T(8,128)}, u32[]{:S(2)}) copy-start(f32[768,128]{1,0:T(8,128)} %upper_tiles.3) | copy-start | bytes 1179652
  60.9 29.7 %copy-start.1 = (f32[768,128]{1,0:T(8,128)S(1)}, f32[768,128]{1,0:T(8,128)}, u32[]{:S(2)}) copy-start(f32[768,128]{1,0:T(8,128)} %diag_tiles.3) | copy-start | bytes 1179652
  60.9 1.4 %collective-permute-start.21 = (bf16[128,512]{1,0:T(8,128)(2,1)S(1)}, bf16[128,512]{1,0:T(8,128)(2,1)S(1)}, u32[]{:S(2)}, u32[]{:S(2)}) collective-permute-start(bf16[128,512]{1,0:T(8,128)(2,1)S(1)} %get-tuple-element.66), channel_id=1, source_target_pairs={{0,1},{1,0},{2,3},{3,2},{4,5},{5,4},{6,7},{7,6},{8,9},{9,8},{10,11... | collective-permute-start | bytes 393224 | tf_op jit(solution)/shard_map/ppermute | solution.py:100
  61.0 1.3 %collective-permute-start.22 = (bf16[128,512]{1,0:T(8,128)(2,1)S(1)}, bf16[128,512]{1,0:T(8,128)(2,1)S(1)}, u32[]{:S(2)}, u32[]{:S(2)}) collective-permute-start(bf16[128,512]{1,0:T(8,128)(2,1)S(1)} %get-tuple-element.67), channel_id=1, source_target_pairs={{1,2},{3,4},{5,6},{2,1},{4,3},{6,5},{9,10},{11,12},{13,14},{10,9},... | collective-permute-start | bytes 393224 | tf_op jit(solution)/shard_map/ppermute | solution.py:106
  63.6 4.7 %collective-permute-start.23 = (bf16[192,256]{1,0:T(8,128)(2,1)S(1)}, bf16[192,256]{1,0:T(8,128)(2,1)S(1)}, u32[]{:S(2)}, u32[]{:S(2)}) collective-permute-start(bf16[192,256]{1,0:T(8,128)(2,1)S(1)} %get-tuple-element.69), channel_id=1, source_target_pairs={{0,8},{8,0},{16,24},{24,16},{1,9},{9,1},{17,25},{25,17},{2,10},{10... | collective-permute-start | bytes 294920 | tf_op jit(solution)/shard_map/ppermute | solution.py:95
  64.9 4.6 %collective-permute-start.24 = (bf16[192,256]{1,0:T(8,128)(2,1)S(1)}, bf16[192,256]{1,0:T(8,128)(2,1)S(1)}, u32[]{:S(2)}, u32[]{:S(2)}) collective-permute-start(bf16[192,256]{1,0:T(8,128)(2,1)S(1)} %get-tuple-element.70), channel_id=1, source_target_pairs={{0,16},{8,24},{16,0},{24,8},{1,17},{9,25},{17,1},{25,9},{2,18},{10... | collective-permute-start | bytes 294920 | tf_op jit(solution)/shard_map/ppermute | solution.py:95
  65.5 5.5 %collective-permute-start.25 = (bf16[192,256]{1,0:T(8,128)(2,1)S(1)}, bf16[192,256]{1,0:T(8,128)(2,1)S(1)}, u32[]{:S(2)}, u32[]{:S(2)}) collective-permute-start(bf16[192,256]{1,0:T(8,128)(2,1)S(1)} %get-tuple-element.71), channel_id=1, source_target_pairs={{0,24},{8,16},{16,8},{24,0},{1,25},{9,17},{17,9},{25,1},{2,26},{10... | collective-permute-start | bytes 294920 | tf_op jit(solution)/shard_map/ppermute | solution.py:95
  71.1 5.6 %collective-permute-start.28 = (bf16[192,256]{1,0:T(8,128)(2,1)S(1)}, bf16[192,256]{1,0:T(8,128)(2,1)S(1)}, u32[]{:S(2)}, u32[]{:S(2)}) collective-permute-start(bf16[192,256]{1,0:T(8,128)(2,1)S(1)} %add_convert_fusion.refs_0_), channel_id=1, source_target_pairs={{0,24},{8,16},{16,8},{24,0},{1,25},{9,17},{17,9},{25,1},{2,26},{10... | collective-permute-start | bytes 294920 | tf_op jit(solution)/shard_map/ppermute | solution.py:95
  72.8 4.9 %collective-permute-start.27 = (bf16[192,256]{1,0:T(8,128)(2,1)S(1)}, bf16[192,256]{1,0:T(8,128)(2,1)S(1)}, u32[]{:S(2)}, u32[]{:S(2)}) collective-permute-start(bf16[192,256]{1,0:T(8,128)(2,1)S(1)} %add_convert_fusion.refs_0_), channel_id=1, source_target_pairs={{0,16},{8,24},{16,0},{24,8},{1,17},{9,25},{17,1},{25,9},{2,18},{10... | collective-permute-start | bytes 294920 | tf_op jit(solution)/shard_map/ppermute | solution.py:95
  73.9 4.6 %collective-permute-start.26 = (bf16[192,256]{1,0:T(8,128)(2,1)S(1)}, bf16[192,256]{1,0:T(8,128)(2,1)S(1)}, u32[]{:S(2)}, u32[]{:S(2)}) collective-permute-start(bf16[192,256]{1,0:T(8,128)(2,1)S(1)} %add_convert_fusion.refs_0_), channel_id=1, source_target_pairs={{0,8},{8,0},{16,24},{24,16},{1,9},{9,1},{17,25},{25,17},{2,10},{10... | collective-permute-start | bytes 294920 | tf_op jit(solution)/shard_map/ppermute | solution.py:95
  78.9 3.7 %collective-permute-start.29 = (f32[64,256]{1,0:T(8,128)S(1)}, f32[64,256]{1,0:T(8,128)S(1)}, u32[]{:S(2)}, u32[]{:S(2)}) collective-permute-start(f32[64,256]{1,0:T(8,128)S(1)} %get-tuple-element.73), channel_id=1, source_target_pairs={{0,1},{1,0},{2,3},{3,2},{4,5},{5,4},{6,7},{7,6},{8,9},{9,8},{10,11... | collective-permute-start | bytes 196616 | tf_op jit(solution)/shard_map/ppermute | solution.py:100
  81.3 9.3 %collective-permute-start.37 = (bf16[128,256]{1,0:T(8,128)(2,1)S(1)}, bf16[128,256]{1,0:T(8,128)(2,1)S(1)}, u32[]{:S(2)}, u32[]{:S(2)}) collective-permute-start(bf16[128,256]{1,0:T(8,128)(2,1)S(1)} %get-tuple-element.82), channel_id=1, source_target_pairs={{1,0},{2,1},{3,2},{4,3},{5,4},{6,5},{7,6},{9,8},{10,9},{11,10},{12... | collective-permute-start | bytes 196616 | tf_op jit(solution)/shard_map/ppermute | solution.py:425
  82.6 11.1 %collective-permute-start.32 = (f32[64,256]{1,0:T(8,128)S(1)}, f32[64,256]{1,0:T(8,128)S(1)}, u32[]{:S(2)}, u32[]{:S(2)}) collective-permute-start(f32[64,256]{1,0:T(8,128)S(1)} %add.76), channel_id=1, source_target_pairs={{0,6},{1,7},{2,4},{3,5},{4,2},{5,3},{6,0},{7,1},{8,14},{9,15},{10,... | collective-permute-start | bytes 196616 | tf_op jit(solution)/shard_map/ppermute | solution.py:126
  90.0 6.1 %collective-permute-start.31 = (f32[64,256]{1,0:T(8,128)S(1)}, f32[64,256]{1,0:T(8,128)S(1)}, u32[]{:S(2)}, u32[]{:S(2)}) collective-permute-start(f32[64,256]{1,0:T(8,128)S(1)} %add.76), channel_id=1, source_target_pairs={{0,4},{1,5},{2,6},{3,7},{4,0},{5,1},{6,2},{7,3},{8,12},{9,13},{10,... | collective-permute-start | bytes 196616 | tf_op jit(solution)/shard_map/ppermute | solution.py:126
  90.0 6.1 %collective-permute-start.30 = (f32[64,256]{1,0:T(8,128)S(1)}, f32[64,256]{1,0:T(8,128)S(1)}, u32[]{:S(2)}, u32[]{:S(2)}) collective-permute-start(f32[64,256]{1,0:T(8,128)S(1)} %add.76), channel_id=1, source_target_pairs={{0,2},{1,3},{2,0},{3,1},{4,6},{5,7},{6,4},{7,5},{8,10},{9,11},{10,... | collective-permute-start | bytes 196616 | tf_op jit(solution)/shard_map/ppermute | solution.py:126
  91.9 4.3 %collective-permute-start.36 = (bf16[128,256]{1,0:T(8,128)(2,1)S(1)}, bf16[128,256]{1,0:T(8,128)(2,1)S(1)}, u32[]{:S(2)}, u32[]{:S(2)}) collective-permute-start(bf16[128,256]{1,0:T(8,128)(2,1)S(1)} %get-tuple-element.79), channel_id=1, source_target_pairs={{1,0},{2,1},{3,2},{4,3},{5,4},{6,5},{7,6},{9,8},{10,9},{11,10},{12... | collective-permute-start | bytes 196616 | tf_op jit(solution)/shard_map/ppermute | solution.py:425
  97.1 4.6 %collective-permute-start.38 = (f32[128,256]{1,0:T(8,128)S(1)}, f32[128,256]{1,0:T(8,128)S(1)}, u32[]{:S(2)}, u32[]{:S(2)}) collective-permute-start(f32[128,256]{1,0:T(8,128)S(1)} %shard_map.80), channel_id=1, source_target_pairs={{0,1},{1,0},{2,3},{3,2},{4,5},{5,4},{6,7},{7,6},{8,9},{9,8},{10,11... | collective-permute-start | bytes 393224 | tf_op jit(solution)/shard_map/ppermute | solution.py:100
  98.3 5.5 %collective-permute-start.35 = (f32[64,256]{1,0:T(8,128)S(1)}, f32[64,256]{1,0:T(8,128)S(1)}, u32[]{:S(2)}, u32[]{:S(2)}) collective-permute-start(f32[64,256]{1,0:T(8,128)S(1)} %add_add_fusion.2.refs_0_), channel_id=1, source_target_pairs={{0,24},{8,16},{16,8},{24,0},{1,25},{9,17},{17,9},{25,1},{2,26},{10... | collective-permute-start | bytes 196616 | tf_op jit(solution)/shard_map/ppermute | solution.py:95
  99.5 5.1 %collective-permute-start.34 = (f32[64,256]{1,0:T(8,128)S(1)}, f32[64,256]{1,0:T(8,128)S(1)}, u32[]{:S(2)}, u32[]{:S(2)}) collective-permute-start(f32[64,256]{1,0:T(8,128)S(1)} %add_add_fusion.2.refs_0_), channel_id=1, source_target_pairs={{0,16},{8,24},{16,0},{24,8},{1,17},{9,25},{17,1},{25,9},{2,18},{10... | collective-permute-start | bytes 196616 | tf_op jit(solution)/shard_map/ppermute | solution.py:95
  100.6 4.3 %collective-permute-start.33 = (f32[64,256]{1,0:T(8,128)S(1)}, f32[64,256]{1,0:T(8,128)S(1)}, u32[]{:S(2)}, u32[]{:S(2)}) collective-permute-start(f32[64,256]{1,0:T(8,128)S(1)} %add_add_fusion.2.refs_0_), channel_id=1, source_target_pairs={{0,8},{8,0},{16,24},{24,16},{1,9},{9,1},{17,25},{25,17},{2,10},{10... | collective-permute-start | bytes 196616 | tf_op jit(solution)/shard_map/ppermute | solution.py:95
  104.9 10.3 %collective-permute-start.41 = (f32[128,256]{1,0:T(8,128)S(1)}, f32[128,256]{1,0:T(8,128)S(1)}, u32[]{:S(2)}, u32[]{:S(2)}) collective-permute-start(f32[128,256]{1,0:T(8,128)S(1)} %add.80), channel_id=1, source_target_pairs={{0,6},{1,7},{2,4},{3,5},{4,2},{5,3},{6,0},{7,1},{8,14},{9,15},{10,... | collective-permute-start | bytes 393224 | tf_op jit(solution)/shard_map/ppermute | solution.py:126
  107.3 12.4 %collective-permute-start.40 = (f32[128,256]{1,0:T(8,128)S(1)}, f32[128,256]{1,0:T(8,128)S(1)}, u32[]{:S(2)}, u32[]{:S(2)}) collective-permute-start(f32[128,256]{1,0:T(8,128)S(1)} %add.80), channel_id=1, source_target_pairs={{0,4},{1,5},{2,6},{3,7},{4,0},{5,1},{6,2},{7,3},{8,12},{9,13},{10,... | collective-permute-start | bytes 393224 | tf_op jit(solution)/shard_map/ppermute | solution.py:126
  108.0 11.7 %collective-permute-start.39 = (f32[128,256]{1,0:T(8,128)S(1)}, f32[128,256]{1,0:T(8,128)S(1)}, u32[]{:S(2)}, u32[]{:S(2)}) collective-permute-start(f32[128,256]{1,0:T(8,128)S(1)} %add.80), channel_id=1, source_target_pairs={{0,2},{1,3},{2,0},{3,1},{4,6},{5,7},{6,4},{7,5},{8,10},{9,11},{10,... | collective-permute-start | bytes 393224 | tf_op jit(solution)/shard_map/ppermute | solution.py:126
  119.8 9.8 %collective-permute-start.44 = (f32[128,256]{1,0:T(8,128)S(1)}, f32[128,256]{1,0:T(8,128)S(1)}, u32[]{:S(2)}, u32[]{:S(2)}) collective-permute-start(f32[128,256]{1,0:T(8,128)S(1)} %add_add_fusion.1.refs_0_), channel_id=1, source_target_pairs={{0,24},{8,16},{16,8},{24,0},{1,25},{9,17},{17,9},{25,1},{2,26},{10... | collective-permute-start | bytes 393224 | tf_op jit(solution)/shard_map/ppermute | solution.py:95
  121.2 8.4 %collective-permute-start.43 = (f32[128,256]{1,0:T(8,128)S(1)}, f32[128,256]{1,0:T(8,128)S(1)}, u32[]{:S(2)}, u32[]{:S(2)}) collective-permute-start(f32[128,256]{1,0:T(8,128)S(1)} %add_add_fusion.1.refs_0_), channel_id=1, source_target_pairs={{0,16},{8,24},{16,0},{24,8},{1,17},{9,25},{17,1},{25,9},{2,18},{10... | collective-permute-start | bytes 393224 | tf_op jit(solution)/shard_map/ppermute | solution.py:95
  122.0 7.6 %collective-permute-start.42 = (f32[128,256]{1,0:T(8,128)S(1)}, f32[128,256]{1,0:T(8,128)S(1)}, u32[]{:S(2)}, u32[]{:S(2)}) collective-permute-start(f32[128,256]{1,0:T(8,128)S(1)} %add_add_fusion.1.refs_0_), channel_id=1, source_target_pairs={{0,8},{8,0},{16,24},{24,16},{1,9},{9,1},{17,25},{25,17},{2,10},{10... | collective-permute-start | bytes 393224 | tf_op jit(solution)/shard_map/ppermute | solution.py:95

commit v7 on v6

--- a/solution.py
+++ b/solution.py
@@ -206,10 +206,7 @@
 def solve_kernel(weights, field, low, factor, coupling, inverse, base, out_a, out_b, tip, current):
     band = coupling.shape[0]
     rows = field.shape[0]
-    high, rest = halves_of(factor[...])
-    times = lambda a, b: lax.dot_general(a, b, NT, preferred_element_type=F32)
-    result = times(field[...], high) + (times(field[...], rest) + times(low[...], high))
-    current[...] = result.astype(BF16)
+    current[...] = refined(field[...], low[...], factor[...]).astype(BF16)
     tile = 2 * band if rows % (2 * band) == 0 else band
     for at in range(0, rows, tile):
         real = jnp.dot(inverse[0, 0, at : at + tile], current[...], preferred_element_type=F32)
@@ -321,17 +318,24 @@
     return whole(join_kernel, like((rows * len(blocks), columns), BF16), *blocks)
 
 
-def eliminate(block, out, base):
+def eliminate(block, out, base, spread):
     count = block.shape[0]
     full = (GROUP, count)
     lane = lax.broadcasted_iota(jnp.int32, full, 1)
     span = range(GROUP)
     tiles = [block[t * GROUP : (t + 1) * GROUP] for t in range(count // GROUP)]
-    for t, tile in enumerate(tiles):
+    room = GROUP * (GROUP + 1)
+    for t in range(len(tiles)):
         k = t * GROUP
         tile = tiles[t]
-        rows = [jnp.broadcast_to(tile[i : i + 1], full) for i in span]
-        pivot = [[jnp.broadcast_to(rows[i][:, k + j : k + j + 1], full) for j in range(i + 1)] for i in span]
+        slot = (t % 2) * room
+        spread[slot : slot + GROUP] = tile
+        for j in span:
+            at = slot + GROUP * (j + 1)
+            spread[at : at + GROUP] = jnp.broadcast_to(tile[:, k + j : k + j + 1], full)
+        across = lambda row: spread[pl.ds(slot + row, GROUP, stride=0), :]
+        rows = [across(i) for i in span]
+        pivot = [[across(GROUP * (j + 1) + i) for j in range(i + 1)] for i in span]
         scale = []
         low = [[None] * GROUP for _ in span]
         for j in span:
@@ -375,7 +379,7 @@
 
 
 def first_factor_kernel(order, *refs):
-    *blocks, top, corner, rest, across, matrix = refs
+    *blocks, top, corner, rest, across, matrix, spread = refs
     place(blocks, matrix)
     count = matrix.shape[0]
     half = count // 2
@@ -388,19 +392,23 @@
     down = lax.rsqrt(jnp.sum(diagonal, 1, keepdims=True))
     across[...] = scale
     values = values * scale * down
-    eliminate(values[:half, :half], top, 0)
+    eliminate(values[:half, :half], top, 0, spread)
     beside = dot(top[...], values[:half, half:])
     corner[...] = dot_tn(beside, top[...])
     rest[...] = values[half:, half:] - dot_tn(beside, beside)
 
 
-def second_factor_kernel(top, corner, rest, across, out):
+def second_factor_kernel(top, corner, rest, across, out, spread):
     half = top.shape[0]
     out[:half, :half] = top[...]
     out[:half, half:] = jnp.zeros((half, half), F32)
-    eliminate(rest[...], out, half)
+    eliminate(rest[...], out, half, spread)
     out[half:, :half] = -dot(out[half:, half:], corner[...])
     out[...] = out[...] * across[...]
+
+
+def spread_room(columns):
+    return pltpu.VMEM((2 * GROUP * (GROUP + 1), columns // 2), F32)
 
 
 def first_factor(blocks, order):
@@ -410,14 +418,20 @@
         functools.partial(first_factor_kernel, order),
         [half, half, half, like((1, columns))],
         *blocks,
-        scratch=[pltpu.VMEM((columns, columns), F32)],
+        scratch=[pltpu.VMEM((columns, columns), F32), spread_room(columns)],
         flops=6 * 10**9,
     )
 
 
 def second_factor(halves):
     columns = halves[3].shape[1]
-    return whole(second_factor_kernel, like((columns, columns)), *halves, flops=6 * 10**9)
+    return whole(
+        second_factor_kernel,
+        like((columns, columns)),
+        *halves,
+        scratch=[spread_room(columns)],
+        flops=6 * 10**9,
+    )
 
 
 def next_head(head):
@@ -425,14 +439,12 @@
     return lax.ppermute(head, "rows", [(i + 1, i) for i in range(count - 1)])
 
 
-def band_kernel(extra, field, after, diag_tiles, upper_tiles, *refs):
-    low, earlier, (part, image, matrix) = refs[:extra], refs[extra:-3], refs[-3:]
+def band_kernel(field, low, after, diag_tiles, upper_tiles, part, image, matrix):
     band = after.shape[0]
     tiles = field.shape[0] // band
 
     def values(at):
-        total = field[at].astype(F32)
-        return total + low[0][at].astype(F32) if low else total
+        return field[at].astype(F32) + low[at].astype(F32)
 
     for t in range(tiles):
         at = slice(t * band, (t + 1) * band)
@@ -440,34 +452,35 @@
         following = after[...].astype(F32) if t == tiles - 1 else values(following)
         image[at] = 0.5 * dot_three(diag_tiles[at], values(at)) + dot_three(upper_tiles[at], following)
     matrix[...] = dot_two(field[...], image[...], TN)
-    if low:
-        matrix[...] += lax.dot_general(
-            low[0][...], image[...].astype(BF16), TN, preferred_element_type=F32
-        )
-    size = matrix.shape[0] // lax.axis_size("node")
-    for ref in earlier:
-        part[:-size] = ref[...]
-    part[-size:] = matrix[pl.ds(pl.multiple_of(lax.axis_index("node") * size, 8), size), :]
-
-
-def band_slice(field, low, after, diag_tiles, upper_tiles, earlier):
+    matrix[...] += lax.dot_general(
+        low[...], image[...].astype(BF16), TN, preferred_element_type=F32
+    )
+    size = part.shape[0]
+    part[...] = matrix[pl.ds(pl.multiple_of(lax.axis_index("node") * size, 8), size), :]
+
+
+def band_slice(field, low, after, diag_tiles, upper_tiles):
     rows, columns = field.shape
-    size = columns // lax.axis_size("node")
     return whole(
-        functools.partial(band_kernel, len(low)),
-        like((size * (1 + sum(x.shape[0] // size for x in earlier)), columns)),
+        band_kernel,
+        like((columns // lax.axis_size("node"), columns)),
         field,
+        low,
         after,
         diag_tiles,
         upper_tiles,
-        *low,
-        *earlier,
         scratch=[pltpu.VMEM((rows, columns), F32), pltpu.VMEM((columns, columns), F32)],
     )
 
 
-def last_kernel(field, factor, out):
-    out[...] = dot_two(field[...], factor[...], NT)
+def refined(field, low, factor):
+    high, rest = halves_of(factor)
+    times = lambda a, b: lax.dot_general(a, b, NT, preferred_element_type=F32)
+    return times(field, high) + (times(field, rest) + times(low, high))
+
+
+def last_kernel(field, low, factor, out):
+    out[...] = refined(field[...], low[...], factor[...])
 
 
 def projected_kernel(order, *refs):
@@ -491,7 +504,7 @@
     band = upper_tiles.shape[1]
     partners = lax.axis_size("node") - 1
     columns = subspace.shape[1]
-    factors, earlier = [], ()
+    factors, pairs = [], []
     for iteration in range(ITERS):
         final = iteration == ITERS - 1
         if iteration == 0:
@@ -499,8 +512,9 @@
                 subspace, weights, upper_tiles, inverse
             )
         else:
-            base, out_a, out_b = solve(field, low[0], factor, weights, coupling, inverse)
-        got_a, got_b = core_swap(out_a), link_swap(out_b)
+            base, out_a, out_b = solve(field, low, factor, weights, coupling, inverse)
+        got_b = link_swap(out_b)
+        got_a = core_swap(out_a)
         own, *terms = correct(
             weights, base, got_a, got_b, coupling, inverse, 1 if final else 2
         )
@@ -510,28 +524,26 @@
         total = tree_sum([own] + [x.astype(F32) for x in got])
         piece = total.astype(BF16)
         blocks = [piece] + node_spread([piece] * partners)
-        low = ()
+        total, sent = lax.optimization_barrier((total, piece))
         if not final:
-            total, sent = lax.optimization_barrier((total, piece))
             total = total + tree_sum([x.astype(F32) for x in low_got])
-            low_piece = (total - sent.astype(F32)).astype(BF16)
-            low = (join([low_piece] + node_spread([low_piece] * partners)),)
+        low_piece = (total - sent.astype(F32)).astype(BF16)
+        low = join([low_piece] + node_spread([low_piece] * partners))
         field, head, part = gram_slice(blocks, band)
         part = part + core_swap(part)
         following = next_head(after(head, part))
         total = chip_sum(part)
         gathered = [total] + node_spread([total] * partners)
-        pair = band_slice(field, low, after(following, total), diag_tiles, upper_tiles, earlier)
-        earlier = (pair,)
+        pair = band_slice(field, low, after(following, total), diag_tiles, upper_tiles)
         halves = first_factor(gathered, order)
+        pair = pair + core_swap(pair)
+        pairs.append(chip_sum(after(pair, *gathered)))
         if final:
-            pair = pair + core_swap(pair)
-            pair = chip_sum(after(pair, *gathered))
-            pair = after(pair, *halves)
+            pair = after(jnp.concatenate(pairs, 0), *halves)
             spread = [pair] + node_spread([pair] * partners)
         factor = second_factor(halves)
         factors.append(factor)
-    orthonormal = whole(last_kernel, jax.ShapeDtypeStruct(subspace.shape, F32), field, factor)
+    orthonormal = whole(last_kernel, jax.ShapeDtypeStruct(subspace.shape, F32), field, low, factor)
     projected = whole(
         functools.partial(projected_kernel, order),
         jax.ShapeDtypeStruct((ITERS, columns, columns), F32),

time: 132 us -> 129 us (0.977)
  starting transfers between devices: 62.8 us -> 70.7 us
  waiting for transfers between devices: 32.1 us -> 24.6 us
  Pallas kernels: 35.2 us -> 31.9 us
    ppermute x27 -> x30, waiting for transfers between devices: 20.8 us -> 16.3 us  [node_swap(): return lax.ppermute(block, 'node', [(i, i ^ step) for i in range(count)])]
    ppermute x9 -> x12, waiting for transfers between devices: 9.75 us -> 5.3 us  [chip_sum(): lax.ppermute(block, 'rows', route)]
    ppermute x27 -> x30, starting transfers between devices: 31.4 us -> 35 us  [node_swap(): return lax.ppermute(block, 'node', [(i, i ^ step) for i in range(count)])]
    ppermute x9 -> x12, starting transfers between devices: 19.6 us -> 23 us  [chip_sum(): lax.ppermute(block, 'rows', route)]
    pallas_call x14 -> x15, Pallas kernels: 32.3 us -> 29 us  [whole(): pl.pallas_call(kernel, out_shape=out_shape, in_specs=[vmem for _ in opera...]
    ppermute x5 -> x6, starting transfers between devices: 7.66 us -> 8.66 us  [core_swap(): return lax.ppermute(block, 'rows', [(i, i ^ 1) for i in range(count)])]
  transfers between devices with their start and end apart: 45 -> 52, of which waited for: 23 -> 22; matrix products, arithmetic and copies ran while one was open for 0% -> 0% of each run, Pallas kernels for 10% -> 11%
where the time goes in v7:
time: 129 us; the launch traced here: 128 us
  starting transfers between devices  70.7 us (55%)
  Pallas kernels  31.9 us (25%)
  waiting for transfers between devices  24.6 us (19%)
    ppermute x30, starting transfers between devices, node_swap(): return lax.ppermute(block, 'node', [(i, i ^ step) for i in range(count)])  35 us
    pallas_call x15, Pallas kernels, whole(): pl.pallas_call(kernel, out_shape=out_shape, in_specs=[vmem for _ in opera...  29 us
    ppermute x12, starting transfers between devices, chip_sum(): lax.ppermute(block, 'rows', route)  23 us
    ppermute x30, waiting for transfers between devices, node_swap(): return lax.ppermute(block, 'node', [(i, i ^ step) for i in range(count)])  16.3 us
    ppermute x6, starting transfers between devices, core_swap(): return lax.ppermute(block, 'rows', [(i, i ^ 1) for i in range(count)])  8.66 us
    ppermute x12, waiting for transfers between devices, chip_sum(): lax.ppermute(block, 'rows', route)  5.3 us
    pallas_call x1, Pallas kernels, start(): pl.pallas_call(start_kernel, in_specs=[pl.BlockSpec(memory_space=pltpu.HB...  2.88 us
    ppermute x6, waiting for transfers between devices, core_swap(): return lax.ppermute(block, 'rows', [(i, i ^ 1) for i in range(count)])  2.59 us
  transfers between devices with their start and end apart: 52, of which 22 were waited for; matrix products, arithmetic and copies ran while one was open for 0% of the time, Pallas kernels for 11%

profile of v7, /device:TPU:0, one launch (start us, length us, event | category | flops | bytes accessed | tf_op | source)
XLA Modules:
  0.0 128.4 jit_solution(3981928733820877886)
XLA Ops:
  0.6 2.9 %start.1 = (f32[768,256]{1,0:T(8,128)S(1)}, bf16[128,512]{1,0:T(8,128)(2,1)S(1)}, bf16[128,512]{1,0:T(8,128)(2,1)S(1)}, bf16[1,2,768,768]{3,2,1,0:T(8,128)(2,1)S...) custom-call(f32[1,2]{1,0:T(1,128)} %weights_at.1, bf16[1,2,768,768]{3,2,1,0:T(8,128)(2,1)} %source.1, ...), custom_call_target="tpu_custom_call" | custom-call | flops 603979776 | bytes 2359296 | tf_op jit(solution)/shard_map/start/pallas_call | solution.py:188
  5.1 1.3 %shard_map.68 = (f32[192,256]{1,0:T(8,128)S(1)}, bf16[192,256]{1,0:T(8,128)(2,1)S(1)}, bf16[192,256]{1,0:T(8,128)(2,1)S(1)}, bf16[192,256]{1,0:T(8,128)(2,1)S(1)...) custom-call(f32[1,2]{1,0:T(1,128)S(1)} %get-tuple-element.47.weights, ...), custom_call_target="tpu_custom_call" | custom-call | flops 402653184 | bytes 3473416 | tf_op jit(solution)/shard_map/pallas_call | solution.py:82
  6.4 2.9 %collective-permute-start.2 = (bf16[192,256]{1,0:T(8,128)(2,1)S(1)}, bf16[192,256]{1,0:T(8,128)(2,1)S(1)}, u32[]{:S(2)}, u32[]{:S(2)}) collective-permute-start(bf16[192,256]{1,0:T(8,128)(2,1)S(1)} %get-tuple-element.54), channel_id=1, source_target_pairs={{0,8},{8,0},{16,24},{24,16},{1,9},{9,1},{17,25},{25,17},{2,10},{10... | collective-permute-start | bytes 294920 | tf_op jit(solution)/shard_map/ppermute | solution.py:95
  9.3 1.5 %collective-permute-start.3 = (bf16[192,256]{1,0:T(8,128)(2,1)S(1)}, bf16[192,256]{1,0:T(8,128)(2,1)S(1)}, u32[]{:S(2)}, u32[]{:S(2)}) collective-permute-start(bf16[192,256]{1,0:T(8,128)(2,1)S(1)} %get-tuple-element.55), channel_id=1, source_target_pairs={{0,16},{8,24},{16,0},{24,8},{1,17},{9,25},{17,1},{25,9},{2,18},{10... | collective-permute-start | bytes 294920 | tf_op jit(solution)/shard_map/ppermute | solution.py:95
  10.9 1.0 collective-permute-done.2
  11.9 2.0 %collective-permute-done.3 = bf16[192,256]{1,0:T(8,128)(2,1)S(1)} collective-permute-done((bf16[192,256]{1,0:T(8,128)(2,1)S(1)}, bf16[192,256]{1,0:T(8,128)(2,1)S(1)}, u32[]{:S(2)}, u32[]{:S(2)}) %collective-permute-start.3) | collective-permute-done | bytes 98336 | tf_op jit(solution)/shard_map/ppermute | solution.py:95
  14.0 2.4 %collective-permute-done.4 = bf16[192,256]{1,0:T(8,128)(2,1)S(1)} collective-permute-done((bf16[192,256]{1,0:T(8,128)(2,1)S(1)}, bf16[192,256]{1,0:T(8,128)(2,1)S(1)}, u32[]{:S(2)}, u32[]{:S(2)}) %collective-permute-start.4) | collective-permute-done | bytes 98336 | tf_op jit(solution)/shard_map/ppermute | solution.py:95
  16.6 1.9 %collective-permute-start.6 = (bf16[192,256]{1,0:T(8,128)(2,1)S(1)}, bf16[192,256]{1,0:T(8,128)(2,1)S(1)}, u32[]{:S(2)}, u32[]{:S(2)}) collective-permute-start(bf16[192,256]{1,0:T(8,128)(2,1)S(1)} %get-tuple-element.62.refs_0_), channel_id=1, source_target_pairs={{0,16},{8,24},{16,0},{24,8},{1,17},{9,25},{17,1},{25,9},{2,18},{10... | collective-permute-start | bytes 294920 | tf_op jit(solution)/shard_map/ppermute | solution.py:95
  18.5 1.5 %collective-permute-start.5 = (bf16[192,256]{1,0:T(8,128)(2,1)S(1)}, bf16[192,256]{1,0:T(8,128)(2,1)S(1)}, u32[]{:S(2)}, u32[]{:S(2)}) collective-permute-start(bf16[192,256]{1,0:T(8,128)(2,1)S(1)} %get-tuple-element.62.refs_0_), channel_id=1, source_target_pairs={{0,8},{8,0},{16,24},{24,16},{1,9},{9,1},{17,25},{25,17},{2,10},{10... | collective-permute-start | bytes 294920 | tf_op jit(solution)/shard_map/ppermute | solution.py:95
  20.7 1.4 %collective-permute-done.7.refs_3_ = bf16[192,256]{1,0:T(8,128)(2,1)S(1)} collective-permute-done((bf16[192,256]{1,0:T(8,128)(2,1)S(1)}, bf16[192,256]{1,0:T(8,128)(2,1)S(1)}, u32[]{:S(2)}, u32[]{:S(2)}) %collective-permute-start.7) | collective-permute-done | bytes 98336 | tf_op jit(solution)/shard_map/ppermute | solution.py:95
  22.0 1.5 %collective-permute-start.10 = (bf16[192,256]{1,0:T(8,128)(2,1)S(1)}, bf16[192,256]{1,0:T(8,128)(2,1)S(1)}, u32[]{:S(2)}, u32[]{:S(2)}) collective-permute-start(bf16[192,256]{1,0:T(8,128)(2,1)S(1)} %get-tuple-element.61), channel_id=1, source_target_pairs={{0,24},{8,16},{16,8},{24,0},{1,25},{9,17},{17,9},{25,1},{2,26},{10... | collective-permute-start | bytes 294920 | tf_op jit(solution)/shard_map/ppermute | solution.py:95
  23.9 3.5 %collective-permute-start.14 = (f32[64,256]{1,0:T(8,128)S(1)}, f32[64,256]{1,0:T(8,128)S(1)}, u32[]{:S(2)}, u32[]{:S(2)}) collective-permute-start(f32[64,256]{1,0:T(8,128)S(1)} %get-tuple-element.63), channel_id=1, source_target_pairs={{0,1},{1,0},{2,3},{3,2},{4,5},{5,4},{6,7},{7,6},{8,9},{9,8},{10,11... | collective-permute-start | bytes 196616 | tf_op jit(solution)/shard_map/ppermute | solution.py:100
  28.3 6.6 %collective-permute-start.17 = (f32[64,256]{1,0:T(8,128)S(1)}, f32[64,256]{1,0:T(8,128)S(1)}, u32[]{:S(2)}, u32[]{:S(2)}) collective-permute-start(f32[64,256]{1,0:T(8,128)S(1)} %add.81), channel_id=1, source_target_pairs={{0,6},{1,7},{2,4},{3,5},{4,2},{5,3},{6,0},{7,1},{8,14},{9,15},{10,... | collective-permute-start | bytes 196616 | tf_op jit(solution)/shard_map/ppermute | solution.py:126
  35.6 1.6 %collective-permute-start.13 = (bf16[192,256]{1,0:T(8,128)(2,1)S(1)}, bf16[192,256]{1,0:T(8,128)(2,1)S(1)}, u32[]{:S(2)}, u32[]{:S(2)}) collective-permute-start(bf16[192,256]{1,0:T(8,128)(2,1)S(1)} %subtract_convert_fusion.1.refs_0_), channel_id=1, source_target_pairs={{0,24},{8,16},{16,8},{24,0},{1,25},{9,17},{17,9},{25,1},{2,26},{10... | collective-permute-start | bytes 294920 | tf_op jit(solution)/shard_map/ppermute | solution.py:95
  39.2 2.2 %collective-permute-done.16 = f32[64,256]{1,0:T(8,128)S(1)} collective-permute-done((f32[64,256]{1,0:T(8,128)S(1)}, f32[64,256]{1,0:T(8,128)S(1)}, u32[]{:S(2)}, u32[]{:S(2)}) %collective-permute-start.16) | collective-permute-done | bytes 65568 | tf_op jit(solution)/shard_map/ppermute | solution.py:126
  41.3 1.5 %collective-permute-start.20 = (f32[64,256]{1,0:T(8,128)S(1)}, f32[64,256]{1,0:T(8,128)S(1)}, u32[]{:S(2)}, u32[]{:S(2)}) collective-permute-start(f32[64,256]{1,0:T(8,128)S(1)} %add_add_fusion.5.refs_0_), channel_id=1, source_target_pairs={{0,24},{8,16},{16,8},{24,0},{1,25},{9,17},{17,9},{25,1},{2,26},{10... | collective-permute-start | bytes 196616 | tf_op jit(solution)/shard_map/ppermute | solution.py:95
  43.7 1.2 collective-permute-start.18
  45.0 2.2 %collective-permute-done.20.refs_3_ = f32[64,256]{1,0:T(8,128)S(1)} collective-permute-done((f32[64,256]{1,0:T(8,128)S(1)}, f32[64,256]{1,0:T(8,128)S(1)}, u32[]{:S(2)}, u32[]{:S(2)}) %collective-permute-start.20) | collective-permute-done | bytes 65568 | tf_op jit(solution)/shard_map/ppermute | solution.py:95
  48.0 4.8 %shard_map.71 = (f32[128,128]{1,0:T(8,128)S(1)}, f32[128,128]{1,0:T(8,128)S(1)}, f32[128,128]{1,0:T(8,128)S(1)}, f32[1,256]{1,0:T(1,128)S(1)}) custom-call(f32[64,256]{1,0:T(8,128)S(1)} %add_add_fusion.5.refs_0_, f32[64,256]{1,0:T(8,128)S(1)} %collective-permute-done.18.refs_1_, f32[64,256]{1,0:T(8,128)S(1)} %collective-permute-done.19.refs_2_, ...), custom_call_target="tpu_custom_call" | custom-call | flops 6000000000 | bytes 262144 | tf_op jit(solution)/shard_map/pallas_call | solution.py:82
  52.8 4.1 %shard_map.72.factor.refs_4_ = f32[256,256]{1,0:T(8,128)S(1)} custom-call(f32[128,128]{1,0:T(8,128)S(1)} %get-tuple-element.64.top, f32[128,128]{1,0:T(8,128)S(1)} %get-tuple-element.65.corner, f32[128,128]{1,0:T(8,128)S(1)} %get-tuple-element.66.rest, f32[1,256]{1,0:T(1,128)S(1)} %get-tuple-element.67.across), custom_call_target="tpu_custom_call" | custom-call | flops 6000000000 | bytes 197632 | tf_op jit(solution)/shard_map/pallas_call | solution.py:82
  56.9 2.1 %shard_map.73 = (f32[768,256]{1,0:T(8,128)S(1)}, bf16[128,512]{1,0:T(8,128)(2,1)S(1)}, bf16[128,512]{1,0:T(8,128)(2,1)S(1)}) custom-call(f32[1,2]{1,0:T(1,128)S(1)} %get-tuple-element.47.weights, bf16[768,256]{1,0:T(8,128)(2,1)S(1)} %get-tuple-element.57.field, bf16[768,256]{1,0:T(8,128)(2,1)S(1)} %shard_map.70.low, ...), custom_call_target="tpu_custom_call" | custom-call | flops 603979776 | bytes 3473416 | tf_op jit(solution)/shard_map/pallas_call | solution.py:82
  60.5 1.3 shard_map.74
  61.8 1.3 collective-permute-start.23
  63.6 1.7 %collective-permute-start.25 = (bf16[192,256]{1,0:T(8,128)(2,1)S(1)}, bf16[192,256]{1,0:T(8,128)(2,1)S(1)}, u32[]{:S(2)}, u32[]{:S(2)}) collective-permute-start(bf16[192,256]{1,0:T(8,128)(2,1)S(1)} %get-tuple-element.74), channel_id=1, source_target_pairs={{0,24},{8,16},{16,8},{24,0},{1,25},{9,17},{17,9},{25,1},{2,26},{10... | collective-permute-start | bytes 294920 | tf_op jit(solution)/shard_map/ppermute | solution.py:95
  65.3 1.3 collective-permute-start.39
  67.6 1.5 %collective-permute-done.25 = bf16[192,256]{1,0:T(8,128)(2,1)S(1)} collective-permute-done((bf16[192,256]{1,0:T(8,128)(2,1)S(1)}, bf16[192,256]{1,0:T(8,128)(2,1)S(1)}, u32[]{:S(2)}, u32[]{:S(2)}) %collective-permute-start.25) | collective-permute-done | bytes 98336 | tf_op jit(solution)/shard_map/ppermute | solution.py:95
  69.2 1.8 %collective-permute-start.28 = (bf16[192,256]{1,0:T(8,128)(2,1)S(1)}, bf16[192,256]{1,0:T(8,128)(2,1)S(1)}, u32[]{:S(2)}, u32[]{:S(2)}) collective-permute-start(bf16[192,256]{1,0:T(8,128)(2,1)S(1)} %get-tuple-element.77.refs_0_), channel_id=1, source_target_pairs={{0,24},{8,16},{16,8},{24,0},{1,25},{9,17},{17,9},{25,1},{2,26},{10... | collective-permute-start | bytes 294920 | tf_op jit(solution)/shard_map/ppermute | solution.py:95
  71.0 1.1 collective-permute-start.27
  72.8 1.8 %collective-permute-start.31 = (bf16[192,256]{1,0:T(8,128)(2,1)S(1)}, bf16[192,256]{1,0:T(8,128)(2,1)S(1)}, u32[]{:S(2)}, u32[]{:S(2)}) collective-permute-start(bf16[192,256]{1,0:T(8,128)(2,1)S(1)} %subtract_convert_fusion.refs_0_), channel_id=1, source_target_pairs={{0,24},{8,16},{16,8},{24,0},{1,25},{9,17},{17,9},{25,1},{2,26},{10... | collective-permute-start | bytes 294920 | tf_op jit(solution)/shard_map/ppermute | solution.py:95
  77.1 3.4 %collective-permute-start.32 = (f32[64,256]{1,0:T(8,128)S(1)}, f32[64,256]{1,0:T(8,128)S(1)}, u32[]{:S(2)}, u32[]{:S(2)}) collective-permute-start(f32[64,256]{1,0:T(8,128)S(1)} %get-tuple-element.78), channel_id=1, source_target_pairs={{0,1},{1,0},{2,3},{3,2},{4,5},{5,4},{6,7},{7,6},{8,9},{9,8},{10,11... | collective-permute-start | bytes 196616 | tf_op jit(solution)/shard_map/ppermute | solution.py:100
  80.4 1.2 shard_map.80
  81.8 1.2 collective-permute-start.30
  83.8 5.0 %collective-permute-start.35 = (f32[64,256]{1,0:T(8,128)S(1)}, f32[64,256]{1,0:T(8,128)S(1)}, u32[]{:S(2)}, u32[]{:S(2)}) collective-permute-start(f32[64,256]{1,0:T(8,128)S(1)} %add.88), channel_id=1, source_target_pairs={{0,6},{1,7},{2,4},{3,5},{4,2},{5,3},{6,0},{7,1},{8,14},{9,15},{10,... | collective-permute-start | bytes 196616 | tf_op jit(solution)/shard_map/ppermute | solution.py:126
  90.1 3.2 %collective-permute-start.43 = (f32[64,256]{1,0:T(8,128)S(1)}, f32[64,256]{1,0:T(8,128)S(1)}, u32[]{:S(2)}, u32[]{:S(2)}) collective-permute-start(f32[64,256]{1,0:T(8,128)S(1)} %add.92), channel_id=1, source_target_pairs={{0,6},{1,7},{2,4},{3,5},{4,2},{5,3},{6,0},{7,1},{8,14},{9,15},{10,... | collective-permute-start | bytes 196616 | tf_op jit(solution)/shard_map/ppermute | solution.py:126
  93.4 1.3 collective-permute-start.41
  94.7 2.8 %collective-permute-done.34 = f32[64,256]{1,0:T(8,128)S(1)} collective-permute-done((f32[64,256]{1,0:T(8,128)S(1)}, f32[64,256]{1,0:T(8,128)S(1)}, u32[]{:S(2)}, u32[]{:S(2)}) %collective-permute-start.34) | collective-permute-done | bytes 65568 | tf_op jit(solution)/shard_map/ppermute | solution.py:126
  97.5 1.3 collective-permute-start.44
  98.8 1.4 %collective-permute-start.38 = (f32[64,256]{1,0:T(8,128)S(1)}, f32[64,256]{1,0:T(8,128)S(1)}, u32[]{:S(2)}, u32[]{:S(2)}) collective-permute-start(f32[64,256]{1,0:T(8,128)S(1)} %add_add_fusion.4.refs_0_), channel_id=1, source_target_pairs={{0,24},{8,16},{16,8},{24,0},{1,25},{9,17},{17,9},{25,1},{2,26},{10... | collective-permute-start | bytes 196616 | tf_op jit(solution)/shard_map/ppermute | solution.py:95
  101.7 1.2 shard_map.81
  103.8 1.0 collective-permute-start.45
  106.0 1.4 %collective-permute-done.36.refs_1_ = f32[64,256]{1,0:T(8,128)S(1)} collective-permute-done((f32[64,256]{1,0:T(8,128)S(1)}, f32[64,256]{1,0:T(8,128)S(1)}, u32[]{:S(2)}, u32[]{:S(2)}) %collective-permute-start.36) | collective-permute-done | bytes 65568 | tf_op jit(solution)/shard_map/ppermute | solution.py:95
  107.4 4.5 %collective-permute-start.48 = (f32[64,256]{1,0:T(8,128)S(1)}, f32[64,256]{1,0:T(8,128)S(1)}, u32[]{:S(2)}, u32[]{:S(2)}) collective-permute-start(f32[64,256]{1,0:T(8,128)S(1)} %add.96), channel_id=1, source_target_pairs={{0,6},{1,7},{2,4},{3,5},{4,2},{5,3},{6,0},{7,1},{8,14},{9,15},{10,... | collective-permute-start | bytes 196616 | tf_op jit(solution)/shard_map/ppermute | solution.py:126
  112.4 4.8 %shard_map.77 = (f32[128,128]{1,0:T(8,128)S(1)}, f32[128,128]{1,0:T(8,128)S(1)}, f32[128,128]{1,0:T(8,128)S(1)}, f32[1,256]{1,0:T(1,128)S(1)}) custom-call(f32[64,256]{1,0:T(8,128)S(1)} %add_add_fusion.4.refs_0_, f32[64,256]{1,0:T(8,128)S(1)} %collective-permute-done.36.refs_1_, f32[64,256]{1,0:T(8,128)S(1)} %collective-permute-done.37.refs_2_, ...), custom_call_target="tpu_custom_call" | custom-call | flops 6000000000 | bytes 262144 | tf_op jit(solution)/shard_map/pallas_call | solution.py:82
  117.6 1.5 %collective-permute-start.51 = (f32[128,256]{1,0:T(8,128)S(1)}, f32[128,256]{1,0:T(8,128)S(1)}, u32[]{:S(2)}, u32[]{:S(2)}) collective-permute-start(f32[128,256]{1,0:T(8,128)S(1)} %pad_maximum_fusion.refs_0_), channel_id=1, source_target_pairs={{0,24},{8,16},{16,8},{24,0},{1,25},{9,17},{17,9},{25,1},{2,26},{10... | collective-permute-start | bytes 393224 | tf_op jit(solution)/shard_map/ppermute | solution.py:95
  119.7 1.4 %collective-permute-start.49 = (f32[128,256]{1,0:T(8,128)S(1)}, f32[128,256]{1,0:T(8,128)S(1)}, u32[]{:S(2)}, u32[]{:S(2)}) collective-permute-start(f32[128,256]{1,0:T(8,128)S(1)} %pad_maximum_fusion.refs_0_), channel_id=1, source_target_pairs={{0,8},{8,0},{16,24},{24,16},{1,9},{9,1},{17,25},{25,17},{2,10},{10... | collective-permute-start | bytes 393224 | tf_op jit(solution)/shard_map/ppermute | solution.py:95
  121.2 4.1 %shard_map.78.factor.refs_5_ = f32[256,256]{1,0:T(8,128)S(1)} custom-call(f32[128,128]{1,0:T(8,128)S(1)} %get-tuple-element.79.top, f32[128,128]{1,0:T(8,128)S(1)} %get-tuple-element.80.corner, f32[128,128]{1,0:T(8,128)S(1)} %get-tuple-element.81.rest, f32[1,256]{1,0:T(1,128)S(1)} %get-tuple-element.82.across), custom_call_target="tpu_custom_call" | custom-call | flops 6000000000 | bytes 197632 | tf_op jit(solution)/shard_map/pallas_call | solution.py:82
  125.3 1.4 %shard_map.79 = f32[768,256]{1,0:T(8,128)} custom-call(bf16[768,256]{1,0:T(8,128)(2,1)S(1)} %get-tuple-element.75.field, bf16[768,256]{1,0:T(8,128)(2,1)S(1)} %shard_map.76.low, f32[256,256]{1,0:T(8,128)S(1)} %shard_map.78.factor.refs_5_), custom_call_target="tpu_custom_call" | custom-call | flops 100000000 | bytes 1048576 | tf_op jit(solution)/shard_map/pallas_call | solution.py:82
  126.7 1.7 %shard_map.82 = f32[2,256,256]{2,1,0:T(8,128)} custom-call(f32[128,256]{1,0:T(8,128)S(1)} %pad_maximum_fusion.refs_0_, f32[128,256]{1,0:T(8,128)S(1)} %collective-permute-done.49.refs_1_, f32[128,256]{1,0:T(8,128)S(1)} %collective-permute-done.50.refs_2_, f32[128,256]{1,0:T(8,128)S(1)} %collective-permute-done.51.refs_3_, ...), custom_call_target="tpu_custom_call" | custom-call | flops 100000000 | bytes 1048576 | tf_op jit(solution)/shard_map/pallas_call | solution.py:82
  (89 shorter events, 21.6 us)
Async XLA Ops:
  6.4 5.5 %collective-permute-start.2 = (bf16[192,256]{1,0:T(8,128)(2,1)S(1)}, bf16[192,256]{1,0:T(8,128)(2,1)S(1)}, u32[]{:S(2)}, u32[]{:S(2)}) collective-permute-start(bf16[192,256]{1,0:T(8,128)(2,1)S(1)} %get-tuple-element.54), channel_id=1, source_target_pairs={{0,8},{8,0},{16,24},{24,16},{1,9},{9,1},{17,25},{25,17},{2,10},{10... | collective-permute-start | bytes 294920 | tf_op jit(solution)/shard_map/ppermute | solution.py:95
  9.3 4.6 %collective-permute-start.3 = (bf16[192,256]{1,0:T(8,128)(2,1)S(1)}, bf16[192,256]{1,0:T(8,128)(2,1)S(1)}, u32[]{:S(2)}, u32[]{:S(2)}) collective-permute-start(bf16[192,256]{1,0:T(8,128)(2,1)S(1)} %get-tuple-element.55), channel_id=1, source_target_pairs={{0,16},{8,24},{16,0},{24,8},{1,17},{9,25},{17,1},{25,9},{2,18},{10... | collective-permute-start | bytes 294920 | tf_op jit(solution)/shard_map/ppermute | solution.py:95
  10.9 5.5 %collective-permute-start.4 = (bf16[192,256]{1,0:T(8,128)(2,1)S(1)}, bf16[192,256]{1,0:T(8,128)(2,1)S(1)}, u32[]{:S(2)}, u32[]{:S(2)}) collective-permute-start(bf16[192,256]{1,0:T(8,128)(2,1)S(1)} %get-tuple-element.56), channel_id=1, source_target_pairs={{0,24},{8,16},{16,8},{24,0},{1,25},{9,17},{17,9},{25,1},{2,26},{10... | collective-permute-start | bytes 294920 | tf_op jit(solution)/shard_map/ppermute | solution.py:95
  16.5 5.6 %collective-permute-start.7 = (bf16[192,256]{1,0:T(8,128)(2,1)S(1)}, bf16[192,256]{1,0:T(8,128)(2,1)S(1)}, u32[]{:S(2)}, u32[]{:S(2)}) collective-permute-start(bf16[192,256]{1,0:T(8,128)(2,1)S(1)} %get-tuple-element.62.refs_0_), channel_id=1, source_target_pairs={{0,24},{8,16},{16,8},{24,0},{1,25},{9,17},{17,9},{25,1},{2,26},{10... | collective-permute-start | bytes 294920 | tf_op jit(solution)/shard_map/ppermute | solution.py:95
  16.6 6.9 %collective-permute-start.6 = (bf16[192,256]{1,0:T(8,128)(2,1)S(1)}, bf16[192,256]{1,0:T(8,128)(2,1)S(1)}, u32[]{:S(2)}, u32[]{:S(2)}) collective-permute-start(bf16[192,256]{1,0:T(8,128)(2,1)S(1)} %get-tuple-element.62.refs_0_), channel_id=1, source_target_pairs={{0,16},{8,24},{16,0},{24,8},{1,17},{9,25},{17,1},{25,9},{2,18},{10... | collective-permute-start | bytes 294920 | tf_op jit(solution)/shard_map/ppermute | solution.py:95
  18.5 5.0 %collective-permute-start.5 = (bf16[192,256]{1,0:T(8,128)(2,1)S(1)}, bf16[192,256]{1,0:T(8,128)(2,1)S(1)}, u32[]{:S(2)}, u32[]{:S(2)}) collective-permute-start(bf16[192,256]{1,0:T(8,128)(2,1)S(1)} %get-tuple-element.62.refs_0_), channel_id=1, source_target_pairs={{0,8},{8,0},{16,24},{24,16},{1,9},{9,1},{17,25},{25,17},{2,10},{10... | collective-permute-start | bytes 294920 | tf_op jit(solution)/shard_map/ppermute | solution.py:95
  20.0 15.0 %collective-permute-start.8 = (bf16[192,256]{1,0:T(8,128)(2,1)S(1)}, bf16[192,256]{1,0:T(8,128)(2,1)S(1)}, u32[]{:S(2)}, u32[]{:S(2)}) collective-permute-start(bf16[192,256]{1,0:T(8,128)(2,1)S(1)} %get-tuple-element.59), channel_id=1, source_target_pairs={{0,8},{8,0},{16,24},{24,16},{1,9},{9,1},{17,25},{25,17},{2,10},{10... | collective-permute-start | bytes 294920 | tf_op jit(solution)/shard_map/ppermute | solution.py:95
  20.5 15.0 %collective-permute-start.9 = (bf16[192,256]{1,0:T(8,128)(2,1)S(1)}, bf16[192,256]{1,0:T(8,128)(2,1)S(1)}, u32[]{:S(2)}, u32[]{:S(2)}) collective-permute-start(bf16[192,256]{1,0:T(8,128)(2,1)S(1)} %get-tuple-element.60), channel_id=1, source_target_pairs={{0,16},{8,24},{16,0},{24,8},{1,17},{9,25},{17,1},{25,9},{2,18},{10... | collective-permute-start | bytes 294920 | tf_op jit(solution)/shard_map/ppermute | solution.py:95
  22.0 13.5 %collective-permute-start.10 = (bf16[192,256]{1,0:T(8,128)(2,1)S(1)}, bf16[192,256]{1,0:T(8,128)(2,1)S(1)}, u32[]{:S(2)}, u32[]{:S(2)}) collective-permute-start(bf16[192,256]{1,0:T(8,128)(2,1)S(1)} %get-tuple-element.61), channel_id=1, source_target_pairs={{0,24},{8,16},{16,8},{24,0},{1,25},{9,17},{17,9},{25,1},{2,26},{10... | collective-permute-start | bytes 294920 | tf_op jit(solution)/shard_map/ppermute | solution.py:95
  23.9 4.4 %collective-permute-start.14 = (f32[64,256]{1,0:T(8,128)S(1)}, f32[64,256]{1,0:T(8,128)S(1)}, u32[]{:S(2)}, u32[]{:S(2)}) collective-permute-start(f32[64,256]{1,0:T(8,128)S(1)} %get-tuple-element.63), channel_id=1, source_target_pairs={{0,1},{1,0},{2,3},{3,2},{4,5},{5,4},{6,7},{7,6},{8,9},{9,8},{10,11... | collective-permute-start | bytes 196616 | tf_op jit(solution)/shard_map/ppermute | solution.py:100
  28.3 9.9 %collective-permute-start.17 = (f32[64,256]{1,0:T(8,128)S(1)}, f32[64,256]{1,0:T(8,128)S(1)}, u32[]{:S(2)}, u32[]{:S(2)}) collective-permute-start(f32[64,256]{1,0:T(8,128)S(1)} %add.81), channel_id=1, source_target_pairs={{0,6},{1,7},{2,4},{3,5},{4,2},{5,3},{6,0},{7,1},{8,14},{9,15},{10,... | collective-permute-start | bytes 196616 | tf_op jit(solution)/shard_map/ppermute | solution.py:126
  34.9 6.5 %collective-permute-start.16 = (f32[64,256]{1,0:T(8,128)S(1)}, f32[64,256]{1,0:T(8,128)S(1)}, u32[]{:S(2)}, u32[]{:S(2)}) collective-permute-start(f32[64,256]{1,0:T(8,128)S(1)} %add.81), channel_id=1, source_target_pairs={{0,4},{1,5},{2,6},{3,7},{4,0},{5,1},{6,2},{7,3},{8,12},{9,13},{10,... | collective-permute-start | bytes 196616 | tf_op jit(solution)/shard_map/ppermute | solution.py:126
  35.0 6.3 %collective-permute-start.15 = (f32[64,256]{1,0:T(8,128)S(1)}, f32[64,256]{1,0:T(8,128)S(1)}, u32[]{:S(2)}, u32[]{:S(2)}) collective-permute-start(f32[64,256]{1,0:T(8,128)S(1)} %add.81), channel_id=1, source_target_pairs={{0,2},{1,3},{2,0},{3,1},{4,6},{5,7},{6,4},{7,5},{8,10},{9,11},{10,... | collective-permute-start | bytes 196616 | tf_op jit(solution)/shard_map/ppermute | solution.py:126
  35.6 8.1 %collective-permute-start.13 = (bf16[192,256]{1,0:T(8,128)(2,1)S(1)}, bf16[192,256]{1,0:T(8,128)(2,1)S(1)}, u32[]{:S(2)}, u32[]{:S(2)}) collective-permute-start(bf16[192,256]{1,0:T(8,128)(2,1)S(1)} %subtract_convert_fusion.1.refs_0_), channel_id=1, source_target_pairs={{0,24},{8,16},{16,8},{24,0},{1,25},{9,17},{17,9},{25,1},{2,26},{10... | collective-permute-start | bytes 294920 | tf_op jit(solution)/shard_map/ppermute | solution.py:95
  37.2 7.7 %collective-permute-start.12 = (bf16[192,256]{1,0:T(8,128)(2,1)S(1)}, bf16[192,256]{1,0:T(8,128)(2,1)S(1)}, u32[]{:S(2)}, u32[]{:S(2)}) collective-permute-start(bf16[192,256]{1,0:T(8,128)(2,1)S(1)} %subtract_convert_fusion.1.refs_0_), channel_id=1, source_target_pairs={{0,16},{8,24},{16,0},{24,8},{1,17},{9,25},{17,1},{25,9},{2,18},{10... | collective-permute-start | bytes 294920 | tf_op jit(solution)/shard_map/ppermute | solution.py:95
  38.2 6.7 %collective-permute-start.11 = (bf16[192,256]{1,0:T(8,128)(2,1)S(1)}, bf16[192,256]{1,0:T(8,128)(2,1)S(1)}, u32[]{:S(2)}, u32[]{:S(2)}) collective-permute-start(bf16[192,256]{1,0:T(8,128)(2,1)S(1)} %subtract_convert_fusion.1.refs_0_), channel_id=1, source_target_pairs={{0,8},{8,0},{16,24},{24,16},{1,9},{9,1},{17,25},{25,17},{2,10},{10... | collective-permute-start | bytes 294920 | tf_op jit(solution)/shard_map/ppermute | solution.py:95
  41.3 5.8 %collective-permute-start.20 = (f32[64,256]{1,0:T(8,128)S(1)}, f32[64,256]{1,0:T(8,128)S(1)}, u32[]{:S(2)}, u32[]{:S(2)}) collective-permute-start(f32[64,256]{1,0:T(8,128)S(1)} %add_add_fusion.5.refs_0_), channel_id=1, source_target_pairs={{0,24},{8,16},{16,8},{24,0},{1,25},{9,17},{17,9},{25,1},{2,26},{10... | collective-permute-start | bytes 196616 | tf_op jit(solution)/shard_map/ppermute | solution.py:95
  42.8 4.8 %collective-permute-start.19 = (f32[64,256]{1,0:T(8,128)S(1)}, f32[64,256]{1,0:T(8,128)S(1)}, u32[]{:S(2)}, u32[]{:S(2)}) collective-permute-start(f32[64,256]{1,0:T(8,128)S(1)} %add_add_fusion.5.refs_0_), channel_id=1, source_target_pairs={{0,16},{8,24},{16,0},{24,8},{1,17},{9,25},{17,1},{25,9},{2,18},{10... | collective-permute-start | bytes 196616 | tf_op jit(solution)/shard_map/ppermute | solution.py:95
  43.7 4.3 %collective-permute-start.18 = (f32[64,256]{1,0:T(8,128)S(1)}, f32[64,256]{1,0:T(8,128)S(1)}, u32[]{:S(2)}, u32[]{:S(2)}) collective-permute-start(f32[64,256]{1,0:T(8,128)S(1)} %add_add_fusion.5.refs_0_), channel_id=1, source_target_pairs={{0,8},{8,0},{16,24},{24,16},{1,9},{9,1},{17,25},{25,17},{2,10},{10... | collective-permute-start | bytes 196616 | tf_op jit(solution)/shard_map/ppermute | solution.py:95
  61.8 4.8 %collective-permute-start.23 = (bf16[192,256]{1,0:T(8,128)(2,1)S(1)}, bf16[192,256]{1,0:T(8,128)(2,1)S(1)}, u32[]{:S(2)}, u32[]{:S(2)}) collective-permute-start(bf16[192,256]{1,0:T(8,128)(2,1)S(1)} %get-tuple-element.72), channel_id=1, source_target_pairs={{0,8},{8,0},{16,24},{24,16},{1,9},{9,1},{17,25},{25,17},{2,10},{10... | collective-permute-start | bytes 294920 | tf_op jit(solution)/shard_map/ppermute | solution.py:95
  63.0 4.6 %collective-permute-start.24 = (bf16[192,256]{1,0:T(8,128)(2,1)S(1)}, bf16[192,256]{1,0:T(8,128)(2,1)S(1)}, u32[]{:S(2)}, u32[]{:S(2)}) collective-permute-start(bf16[192,256]{1,0:T(8,128)(2,1)S(1)} %get-tuple-element.73), channel_id=1, source_target_pairs={{0,16},{8,24},{16,0},{24,8},{1,17},{9,25},{17,1},{25,9},{2,18},{10... | collective-permute-start | bytes 294920 | tf_op jit(solution)/shard_map/ppermute | solution.py:95
  63.6 5.5 %collective-permute-start.25 = (bf16[192,256]{1,0:T(8,128)(2,1)S(1)}, bf16[192,256]{1,0:T(8,128)(2,1)S(1)}, u32[]{:S(2)}, u32[]{:S(2)}) collective-permute-start(bf16[192,256]{1,0:T(8,128)(2,1)S(1)} %get-tuple-element.74), channel_id=1, source_target_pairs={{0,24},{8,16},{16,8},{24,0},{1,25},{9,17},{17,9},{25,1},{2,26},{10... | collective-permute-start | bytes 294920 | tf_op jit(solution)/shard_map/ppermute | solution.py:95
  65.3 9.2 %collective-permute-start.39 = (bf16[128,256]{1,0:T(8,128)(2,1)S(1)}, bf16[128,256]{1,0:T(8,128)(2,1)S(1)}, u32[]{:S(2)}, u32[]{:S(2)}) collective-permute-start(bf16[128,256]{1,0:T(8,128)(2,1)S(1)} %get-tuple-element.84), channel_id=1, source_target_pairs={{1,0},{2,1},{3,2},{4,3},{5,4},{6,5},{7,6},{9,8},{10,9},{11,10},{12... | collective-permute-start | bytes 196616 | tf_op jit(solution)/shard_map/ppermute | solution.py:439
  69.2 5.6 %collective-permute-start.28 = (bf16[192,256]{1,0:T(8,128)(2,1)S(1)}, bf16[192,256]{1,0:T(8,128)(2,1)S(1)}, u32[]{:S(2)}, u32[]{:S(2)}) collective-permute-start(bf16[192,256]{1,0:T(8,128)(2,1)S(1)} %get-tuple-element.77.refs_0_), channel_id=1, source_target_pairs={{0,24},{8,16},{16,8},{24,0},{1,25},{9,17},{17,9},{25,1},{2,26},{10... | collective-permute-start | bytes 294920 | tf_op jit(solution)/shard_map/ppermute | solution.py:95
  71.0 4.9 %collective-permute-start.27 = (bf16[192,256]{1,0:T(8,128)(2,1)S(1)}, bf16[192,256]{1,0:T(8,128)(2,1)S(1)}, u32[]{:S(2)}, u32[]{:S(2)}) collective-permute-start(bf16[192,256]{1,0:T(8,128)(2,1)S(1)} %get-tuple-element.77.refs_0_), channel_id=1, source_target_pairs={{0,16},{8,24},{16,0},{24,8},{1,17},{9,25},{17,1},{25,9},{2,18},{10... | collective-permute-start | bytes 294920 | tf_op jit(solution)/shard_map/ppermute | solution.py:95
  72.1 4.6 %collective-permute-start.26 = (bf16[192,256]{1,0:T(8,128)(2,1)S(1)}, bf16[192,256]{1,0:T(8,128)(2,1)S(1)}, u32[]{:S(2)}, u32[]{:S(2)}) collective-permute-start(bf16[192,256]{1,0:T(8,128)(2,1)S(1)} %get-tuple-element.77.refs_0_), channel_id=1, source_target_pairs={{0,8},{8,0},{16,24},{24,16},{1,9},{9,1},{17,25},{25,17},{2,10},{10... | collective-permute-start | bytes 294920 | tf_op jit(solution)/shard_map/ppermute | solution.py:95
  72.8 16.8 %collective-permute-start.31 = (bf16[192,256]{1,0:T(8,128)(2,1)S(1)}, bf16[192,256]{1,0:T(8,128)(2,1)S(1)}, u32[]{:S(2)}, u32[]{:S(2)}) collective-permute-start(bf16[192,256]{1,0:T(8,128)(2,1)S(1)} %subtract_convert_fusion.refs_0_), channel_id=1, source_target_pairs={{0,24},{8,16},{16,8},{24,0},{1,25},{9,17},{17,9},{25,1},{2,26},{10... | collective-permute-start | bytes 294920 | tf_op jit(solution)/shard_map/ppermute | solution.py:95
  77.1 6.8 %collective-permute-start.32 = (f32[64,256]{1,0:T(8,128)S(1)}, f32[64,256]{1,0:T(8,128)S(1)}, u32[]{:S(2)}, u32[]{:S(2)}) collective-permute-start(f32[64,256]{1,0:T(8,128)S(1)} %get-tuple-element.78), channel_id=1, source_target_pairs={{0,1},{1,0},{2,3},{3,2},{4,5},{5,4},{6,7},{7,6},{8,9},{9,8},{10,11... | collective-permute-start | bytes 196616 | tf_op jit(solution)/shard_map/ppermute | solution.py:100
  81.7 7.2 %collective-permute-start.40 = (f32[64,256]{1,0:T(8,128)S(1)}, f32[64,256]{1,0:T(8,128)S(1)}, u32[]{:S(2)}, u32[]{:S(2)}) collective-permute-start(f32[64,256]{1,0:T(8,128)S(1)} %shard_map.80), channel_id=1, source_target_pairs={{0,1},{1,0},{2,3},{3,2},{4,5},{5,4},{6,7},{7,6},{8,9},{9,8},{10,11... | collective-permute-start | bytes 196616 | tf_op jit(solution)/shard_map/ppermute | solution.py:100
  81.8 8.3 %collective-permute-start.30 = (bf16[192,256]{1,0:T(8,128)(2,1)S(1)}, bf16[192,256]{1,0:T(8,128)(2,1)S(1)}, u32[]{:S(2)}, u32[]{:S(2)}) collective-permute-start(bf16[192,256]{1,0:T(8,128)(2,1)S(1)} %subtract_convert_fusion.refs_0_), channel_id=1, source_target_pairs={{0,16},{8,24},{16,0},{24,8},{1,17},{9,25},{17,1},{25,9},{2,18},{10... | collective-permute-start | bytes 294920 | tf_op jit(solution)/shard_map/ppermute | solution.py:95
  83.0 10.3 %collective-permute-start.29 = (bf16[192,256]{1,0:T(8,128)(2,1)S(1)}, bf16[192,256]{1,0:T(8,128)(2,1)S(1)}, u32[]{:S(2)}, u32[]{:S(2)}) collective-permute-start(bf16[192,256]{1,0:T(8,128)(2,1)S(1)} %subtract_convert_fusion.refs_0_), channel_id=1, source_target_pairs={{0,8},{8,0},{16,24},{24,16},{1,9},{9,1},{17,25},{25,17},{2,10},{10... | collective-permute-start | bytes 294920 | tf_op jit(solution)/shard_map/ppermute | solution.py:95
  83.8 9.5 %collective-permute-start.35 = (f32[64,256]{1,0:T(8,128)S(1)}, f32[64,256]{1,0:T(8,128)S(1)}, u32[]{:S(2)}, u32[]{:S(2)}) collective-permute-start(f32[64,256]{1,0:T(8,128)S(1)} %add.88), channel_id=1, source_target_pairs={{0,6},{1,7},{2,4},{3,5},{4,2},{5,3},{6,0},{7,1},{8,14},{9,15},{10,... | collective-permute-start | bytes 196616 | tf_op jit(solution)/shard_map/ppermute | solution.py:126
  88.8 8.6 %collective-permute-start.34 = (f32[64,256]{1,0:T(8,128)S(1)}, f32[64,256]{1,0:T(8,128)S(1)}, u32[]{:S(2)}, u32[]{:S(2)}) collective-permute-start(f32[64,256]{1,0:T(8,128)S(1)} %add.88), channel_id=1, source_target_pairs={{0,4},{1,5},{2,6},{3,7},{4,0},{5,1},{6,2},{7,3},{8,12},{9,13},{10,... | collective-permute-start | bytes 196616 | tf_op jit(solution)/shard_map/ppermute | solution.py:126
  89.5 9.3 %collective-permute-start.33 = (f32[64,256]{1,0:T(8,128)S(1)}, f32[64,256]{1,0:T(8,128)S(1)}, u32[]{:S(2)}, u32[]{:S(2)}) collective-permute-start(f32[64,256]{1,0:T(8,128)S(1)} %add.88), channel_id=1, source_target_pairs={{0,2},{1,3},{2,0},{3,1},{4,6},{5,7},{6,4},{7,5},{8,10},{9,11},{10,... | collective-permute-start | bytes 196616 | tf_op jit(solution)/shard_map/ppermute | solution.py:126
  90.1 12.8 %collective-permute-start.43 = (f32[64,256]{1,0:T(8,128)S(1)}, f32[64,256]{1,0:T(8,128)S(1)}, u32[]{:S(2)}, u32[]{:S(2)}) collective-permute-start(f32[64,256]{1,0:T(8,128)S(1)} %add.92), channel_id=1, source_target_pairs={{0,6},{1,7},{2,4},{3,5},{4,2},{5,3},{6,0},{7,1},{8,14},{9,15},{10,... | collective-permute-start | bytes 196616 | tf_op jit(solution)/shard_map/ppermute | solution.py:126
  93.3 10.5 %collective-permute-start.42 = (f32[64,256]{1,0:T(8,128)S(1)}, f32[64,256]{1,0:T(8,128)S(1)}, u32[]{:S(2)}, u32[]{:S(2)}) collective-permute-start(f32[64,256]{1,0:T(8,128)S(1)} %add.92), channel_id=1, source_target_pairs={{0,4},{1,5},{2,6},{3,7},{4,0},{5,1},{6,2},{7,3},{8,12},{9,13},{10,... | collective-permute-start | bytes 196616 | tf_op jit(solution)/shard_map/ppermute | solution.py:126
  93.4 11.5 %collective-permute-start.41 = (f32[64,256]{1,0:T(8,128)S(1)}, f32[64,256]{1,0:T(8,128)S(1)}, u32[]{:S(2)}, u32[]{:S(2)}) collective-permute-start(f32[64,256]{1,0:T(8,128)S(1)} %add.92), channel_id=1, source_target_pairs={{0,2},{1,3},{2,0},{3,1},{4,6},{5,7},{6,4},{7,5},{8,10},{9,11},{10,... | collective-permute-start | bytes 196616 | tf_op jit(solution)/shard_map/ppermute | solution.py:126
  97.5 3.1 %collective-permute-start.44 = (bf16[128,256]{1,0:T(8,128)(2,1)S(1)}, bf16[128,256]{1,0:T(8,128)(2,1)S(1)}, u32[]{:S(2)}, u32[]{:S(2)}) collective-permute-start(bf16[128,256]{1,0:T(8,128)(2,1)S(1)} %get-tuple-element.88), channel_id=1, source_target_pairs={{1,0},{2,1},{3,2},{4,3},{5,4},{6,5},{7,6},{9,8},{10,9},{11,10},{12... | collective-permute-start | bytes 196616 | tf_op jit(solution)/shard_map/ppermute | solution.py:439
  98.8 7.0 %collective-permute-start.38 = (f32[64,256]{1,0:T(8,128)S(1)}, f32[64,256]{1,0:T(8,128)S(1)}, u32[]{:S(2)}, u32[]{:S(2)}) collective-permute-start(f32[64,256]{1,0:T(8,128)S(1)} %add_add_fusion.4.refs_0_), channel_id=1, source_target_pairs={{0,24},{8,16},{16,8},{24,0},{1,25},{9,17},{17,9},{25,1},{2,26},{10... | collective-permute-start | bytes 196616 | tf_op jit(solution)/shard_map/ppermute | solution.py:95
  100.6 5.4 %collective-permute-start.37 = (f32[64,256]{1,0:T(8,128)S(1)}, f32[64,256]{1,0:T(8,128)S(1)}, u32[]{:S(2)}, u32[]{:S(2)}) collective-permute-start(f32[64,256]{1,0:T(8,128)S(1)} %add_add_fusion.4.refs_0_), channel_id=1, source_target_pairs={{0,16},{8,24},{16,0},{24,8},{1,17},{9,25},{17,1},{25,9},{2,18},{10... | collective-permute-start | bytes 196616 | tf_op jit(solution)/shard_map/ppermute | solution.py:95
  102.9 4.5 %collective-permute-start.36 = (f32[64,256]{1,0:T(8,128)S(1)}, f32[64,256]{1,0:T(8,128)S(1)}, u32[]{:S(2)}, u32[]{:S(2)}) collective-permute-start(f32[64,256]{1,0:T(8,128)S(1)} %add_add_fusion.4.refs_0_), channel_id=1, source_target_pairs={{0,8},{8,0},{16,24},{24,16},{1,9},{9,1},{17,25},{25,17},{2,10},{10... | collective-permute-start | bytes 196616 | tf_op jit(solution)/shard_map/ppermute | solution.py:95
  103.8 1.9 %collective-permute-start.45 = (f32[64,256]{1,0:T(8,128)S(1)}, f32[64,256]{1,0:T(8,128)S(1)}, u32[]{:S(2)}, u32[]{:S(2)}) collective-permute-start(f32[64,256]{1,0:T(8,128)S(1)} %shard_map.81), channel_id=1, source_target_pairs={{0,1},{1,0},{2,3},{3,2},{4,5},{5,4},{6,7},{7,6},{8,9},{9,8},{10,11... | collective-permute-start | bytes 196616 | tf_op jit(solution)/shard_map/ppermute | solution.py:100
  107.4 9.9 %collective-permute-start.48 = (f32[64,256]{1,0:T(8,128)S(1)}, f32[64,256]{1,0:T(8,128)S(1)}, u32[]{:S(2)}, u32[]{:S(2)}) collective-permute-start(f32[64,256]{1,0:T(8,128)S(1)} %add.96), channel_id=1, source_target_pairs={{0,6},{1,7},{2,4},{3,5},{4,2},{5,3},{6,0},{7,1},{8,14},{9,15},{10,... | collective-permute-start | bytes 196616 | tf_op jit(solution)/shard_map/ppermute | solution.py:126
  111.9 5.7 %collective-permute-start.47 = (f32[64,256]{1,0:T(8,128)S(1)}, f32[64,256]{1,0:T(8,128)S(1)}, u32[]{:S(2)}, u32[]{:S(2)}) collective-permute-start(f32[64,256]{1,0:T(8,128)S(1)} %add.96), channel_id=1, source_target_pairs={{0,4},{1,5},{2,6},{3,7},{4,0},{5,1},{6,2},{7,3},{8,12},{9,13},{10,... | collective-permute-start | bytes 196616 | tf_op jit(solution)/shard_map/ppermute | solution.py:126
  111.9 5.7 %collective-permute-start.46 = (f32[64,256]{1,0:T(8,128)S(1)}, f32[64,256]{1,0:T(8,128)S(1)}, u32[]{:S(2)}, u32[]{:S(2)}) collective-permute-start(f32[64,256]{1,0:T(8,128)S(1)} %add.96), channel_id=1, source_target_pairs={{0,2},{1,3},{2,0},{3,1},{4,6},{5,7},{6,4},{7,5},{8,10},{9,11},{10,... | collective-permute-start | bytes 196616 | tf_op jit(solution)/shard_map/ppermute | solution.py:126
  117.6 9.1 %collective-permute-start.51 = (f32[128,256]{1,0:T(8,128)S(1)}, f32[128,256]{1,0:T(8,128)S(1)}, u32[]{:S(2)}, u32[]{:S(2)}) collective-permute-start(f32[128,256]{1,0:T(8,128)S(1)} %pad_maximum_fusion.refs_0_), channel_id=1, source_target_pairs={{0,24},{8,16},{16,8},{24,0},{1,25},{9,17},{17,9},{25,1},{2,26},{10... | collective-permute-start | bytes 393224 | tf_op jit(solution)/shard_map/ppermute | solution.py:95
  119.1 7.6 %collective-permute-start.50 = (f32[128,256]{1,0:T(8,128)S(1)}, f32[128,256]{1,0:T(8,128)S(1)}, u32[]{:S(2)}, u32[]{:S(2)}) collective-permute-start(f32[128,256]{1,0:T(8,128)S(1)} %pad_maximum_fusion.refs_0_), channel_id=1, source_target_pairs={{0,16},{8,24},{16,0},{24,8},{1,17},{9,25},{17,1},{25,9},{2,18},{10... | collective-permute-start | bytes 393224 | tf_op jit(solution)/shard_map/ppermute | solution.py:95
  119.7 7.0 %collective-permute-start.49 = (f32[128,256]{1,0:T(8,128)S(1)}, f32[128,256]{1,0:T(8,128)S(1)}, u32[]{:S(2)}, u32[]{:S(2)}) collective-permute-start(f32[128,256]{1,0:T(8,128)S(1)} %pad_maximum_fusion.refs_0_), channel_id=1, source_target_pairs={{0,8},{8,0},{16,24},{24,16},{1,9},{9,1},{17,25},{25,17},{2,10},{10... | collective-permute-start | bytes 393224 | tf_op jit(solution)/shard_map/ppermute | solution.py:95
  (6 other events, 45.2 us)

commit v8 on v7

--- a/solution.py
+++ b/solution.py
@@ -131,126 +131,146 @@
     return block
 
 
-def emit_messages(is_even, first, last, out_a, out_b):
+def combine(weights, real, imag):
+    return weights[:, 0:1] * real - weights[:, 1:2] * imag
+
+
+def emit_messages(vectors, top, bottom, coupling, out_a, out_b):
+    is_even = lax.rem(lax.axis_index("rows"), 2) == 0
+    times = lambda block: jnp.dot(block, vectors, preferred_element_type=F32)
+    both = lambda rows: jnp.concatenate([times(rows[0]), times(rows[1])], 1).astype(BF16)
+    first, last = both(top), both(bottom)
+    last = dot_tn(coupling, last.astype(F32)).astype(BF16)
     out_a[...] = jnp.where(is_even, last, first)
     out_b[...] = jnp.where(is_even, first, last)
 
 
-def emit_messages(real, imag, coupling, tip, out_a, out_b):
-    band = coupling.shape[0]
-    is_even = lax.rem(lax.axis_index("rows"), 2) == 0
-    last = jnp.concatenate([real[-band:], imag[-band:]], 1).astype(BF16)
-    last = dot_tn(coupling, last.astype(F32)).astype(BF16)
-    out_a[...] = jnp.where(is_even, last, tip)
-    out_b[...] = jnp.where(is_even, tip, last)
-
-
-def tip_of(real, imag, band):
-    return jnp.concatenate([real[:band], imag[:band]], 1).astype(BF16)
-
-
-def combine(weights, real, imag):
-    return weights[:, 0:1] * real - weights[:, 1:2] * imag
-
-
-def start_kernel(weights_at, source, vectors_at, upper_at, *refs):
-    base, out_a, out_b, inverse, coupling, weights, vectors, tip, arrived = refs
+def start_kernel(source, vectors_at, upper_at, *refs):
+    out_a, out_b, coupling, vectors, ends, arrived = refs
     rows = vectors.shape[0]
     band = coupling.shape[0]
-    tile = 2 * band if rows % (2 * band) == 0 else band
-    spans = [pl.ds(at, tile) for at in range(0, rows, tile)]
-    pairs = [(vectors_at, vectors), (weights_at, weights)]
-    pairs += [(source.at[:, :, span], inverse.at[:, :, span]) for span in spans]
-    pairs += [(upper_at.at[pl.ds(rows - band, band)], coupling)]
+    pairs = [
+        (vectors_at, vectors),
+        (source.at[0, :, pl.ds(0, band)], ends.at[0]),
+        (source.at[0, :, pl.ds(rows - band, band)], ends.at[1]),
+        (upper_at.at[pl.ds(rows - band, band)], coupling),
+    ]
     copies = [pltpu.make_async_copy(*pair, arrived.at[i]) for i, pair in enumerate(pairs)]
     for copy in copies:
         copy.start()
-    for copy in copies[:2]:
+    for copy in copies:
         copy.wait()
-    for i, span in enumerate(spans):
-        copies[2 + i].wait()
-        real = jnp.dot(inverse[0, 0, span], vectors[...], preferred_element_type=F32)
-        imag = jnp.dot(inverse[0, 1, span], vectors[...], preferred_element_type=F32)
-        base[span] = combine(weights, real, imag)
-        if i == 0:
-            tip[...] = tip_of(real, imag, band)
-    copies[-1].wait()
-    emit_messages(real, imag, coupling[...], tip[...], out_a, out_b)
-
-
-def start(vectors, weights, upper_tiles, inverse):
+    emit_messages(vectors[...], ends.at[0], ends.at[1], coupling[...], out_a, out_b)
+
+
+def from_hbm(kernel, outs, scratch, copies, *operands):
+    far = lambda x: pltpu.with_memory_space_constraint(x, pltpu.HBM)
+    kinds = [pltpu.HBM if is_far else pltpu.VMEM for _, is_far in operands]
+    return pl.pallas_call(
+        kernel,
+        in_specs=[pl.BlockSpec(memory_space=kind) for kind in kinds],
+        out_specs=[pl.BlockSpec(memory_space=pltpu.VMEM)] * len(outs),
+        out_shape=outs,
+        scratch_shapes=scratch + [pltpu.SemaphoreType.DMA((copies,))],
+        cost_estimate=pl.CostEstimate(flops=10**8, bytes_accessed=10**6, transcendentals=0),
+        compiler_params=pltpu.CompilerParams(vmem_limit_bytes=GRANT),
+    )(*[far(x) if is_far else local(x) for x, is_far in operands])
+
+
+def start(vectors, upper_tiles, inverse):
     rows, columns = vectors.shape
     band = upper_tiles.shape[1]
     message = like((band, 2 * columns), BF16)
-    outs = [like((rows, columns)), message, message]
-    outs += [like(inverse.shape, BF16), like((band, band)), like(weights.shape)]
-    far = lambda x: pltpu.with_memory_space_constraint(x, pltpu.HBM)
-    return pl.pallas_call(
-        start_kernel,
-        in_specs=[pl.BlockSpec(memory_space=pltpu.HBM)] * 4,
-        out_specs=[pl.BlockSpec(memory_space=pltpu.VMEM)] * len(outs),
-        out_shape=outs,
-        scratch_shapes=[
-            pltpu.VMEM(vectors.shape, BF16),
-            pltpu.VMEM((band, 2 * columns), BF16),
-            pltpu.SemaphoreType.DMA((rows // band + 3,)),
-        ],
-        cost_estimate=pl.CostEstimate(
-            flops=4 * rows * rows * columns, bytes_accessed=inverse.size * 2, transcendentals=0
-        ),
-        compiler_params=pltpu.CompilerParams(vmem_limit_bytes=GRANT),
-        name="start",
-    )(far(weights), far(inverse), far(vectors), far(upper_tiles))
-
-
-def solve_kernel(weights, field, low, factor, coupling, inverse, base, out_a, out_b, tip, current):
+    outs = [message, message, like((band, band)), like(vectors.shape, BF16)]
+    scratch = [pltpu.VMEM((2, 2, band, rows), BF16)]
+    operands = [(inverse, True), (vectors, True), (upper_tiles, True)]
+    return from_hbm(start_kernel, outs, scratch, 4, *operands)
+
+
+def tile_of(rows, band):
+    return 2 * band if rows % (2 * band) == 0 else band
+
+
+def near_edge(weights, got, coupling, inverse, on_chip):
+    rows, columns = inverse.shape[2], got.shape[1] // 2
     band = coupling.shape[0]
-    rows = field.shape[0]
+    is_even = lax.rem(lax.axis_index("rows"), 2) == 0
+    is_next = is_even if on_chip else jnp.logical_not(is_even)
+    below = dot(coupling[...], got[...].astype(F32)).astype(BF16)
+    edge = jnp.where(is_next, below, got[...]).astype(F32)
+    real, imag = edge[:, :columns], edge[:, columns:]
+    at = pl.multiple_of(jnp.where(is_next, rows - band, 0), band)
+    left = dot_two(inverse[0, 0, :, pl.ds(at, band)], combine(weights, real, imag))
+    right = weights[:, 0:1] * imag + weights[:, 1:2] * real
+    return left - dot_two(inverse[0, 1, :, pl.ds(at, band)], right)
+
+
+def products(weights, vectors, inverse, span):
+    real = jnp.dot(inverse[0, 0, span], vectors[...], preferred_element_type=F32)
+    imag = jnp.dot(inverse[0, 1, span], vectors[...], preferred_element_type=F32)
+    return combine(weights, real, imag)
+
+
+def start_base_kernel(weights_at, source, vectors, coupling, got, base, inverse, weights, arrived):
+    rows = vectors.shape[0]
+    tile = tile_of(rows, coupling.shape[0])
+    spans = [pl.ds(at, tile) for at in range(0, rows, tile)]
+    pairs = [(weights_at, weights)]
+    pairs += [(source.at[:, :, span], inverse.at[:, :, span]) for span in spans]
+    copies = [pltpu.make_async_copy(*pair, arrived.at[i]) for i, pair in enumerate(pairs)]
+    for copy in copies:
+        copy.start()
+    copies[0].wait()
+    for copy, span in zip(copies[1:], spans):
+        copy.wait()
+        base[span] = products(weights, vectors, inverse, span)
+    base[...] += near_edge(weights, got, coupling, inverse, True)
+
+
+def start_base(weights, inverse, vectors, coupling, got):
+    rows, columns = vectors.shape
+    outs = [like((rows, columns)), like(inverse.shape, BF16), like(weights.shape)]
+    operands = [(weights, True), (inverse, True), (vectors, False), (coupling, False), (got, False)]
+    return from_hbm(start_base_kernel, outs, [], rows // coupling.shape[0] + 1, *operands)
+
+
+def refined(field, low, factor):
+    high, rest = halves_of(factor)
+    times = lambda a, b: lax.dot_general(a, b, NT, preferred_element_type=F32)
+    return times(field, high) + (times(field, rest) + times(low, high))
+
+
+def solve_kernel(field, low, factor, coupling, inverse, out_a, out_b, current):
+    band = coupling.shape[0]
     current[...] = refined(field[...], low[...], factor[...]).astype(BF16)
-    tile = 2 * band if rows % (2 * band) == 0 else band
+    top, bottom = inverse.at[0, :, :band], inverse.at[0, :, -band:]
+    emit_messages(current[...], top, bottom, coupling[...], out_a, out_b)
+
+
+def solve(field, low, factor, coupling, inverse):
+    rows, columns = field.shape
+    message = like((coupling.shape[0], 2 * columns), BF16)
+    outs = [message, message, like((rows, columns), BF16)]
+    return whole(solve_kernel, outs, field, low, factor, coupling, inverse)
+
+
+def base_kernel(weights, vectors, coupling, inverse, got, base):
+    rows = vectors.shape[0]
+    tile = tile_of(rows, coupling.shape[0])
     for at in range(0, rows, tile):
-        real = jnp.dot(inverse[0, 0, at : at + tile], current[...], preferred_element_type=F32)
-        imag = jnp.dot(inverse[0, 1, at : at + tile], current[...], preferred_element_type=F32)
-        base[at : at + tile] = combine(weights, real, imag)
-        if at == 0:
-            tip[...] = tip_of(real, imag, band)
-    emit_messages(real, imag, coupling[...], tip[...], out_a, out_b)
-
-
-def solve(field, low, factor, weights, coupling, inverse):
-    rows, columns = field.shape
-    band = coupling.shape[1]
-    message = like((band, 2 * columns), BF16)
-    return whole(
-        solve_kernel,
-        [like((rows, columns)), message, message],
-        weights,
-        field,
-        low,
-        factor,
-        coupling,
-        inverse,
-        scratch=[pltpu.VMEM((band, 2 * columns), BF16), pltpu.VMEM((rows, columns), BF16)],
-        flops=4 * rows * rows * columns,
-    )
-
-
-def correct_kernel(weights, base, got_a, got_b, coupling, inverse, own, *refs):
+        span = pl.ds(at, tile)
+        base[span] = products(weights, vectors, inverse, span)
+    base[...] += near_edge(weights, got, coupling, inverse, True)
+
+
+def solve_base(weights, vectors, coupling, inverse, got):
+    return whole(base_kernel, like(vectors.shape), weights, vectors, coupling, inverse, got)
+
+
+def correct_kernel(weights, base, got, coupling, inverse, own, *refs):
     sends, term = refs[:-1], refs[-1]
-    band = coupling.shape[1]
-    rows, columns = base.shape
     node = lax.axis_index("node")
-    is_even = lax.rem(lax.axis_index("rows"), 2) == 0
-    above = jnp.where(is_even, got_b[...], got_a[...])
-    from_next = jnp.where(is_even, got_a[...], got_b[...])
-    below = dot(coupling[...], from_next.astype(F32)).astype(BF16)
-    total = base[...]
-    for edge, columns_at in ((above, 0), (below, rows - band)):
-        real, imag = edge[:, :columns].astype(F32), edge[:, columns:].astype(F32)
-        part = slice(columns_at, columns_at + band)
-        total = total + dot_two(inverse[0, 0, :, part], combine(weights, real, imag))
-        total = total - dot_two(inverse[0, 1, :, part], weights[:, 0:1] * imag + weights[:, 1:2] * real)
-    term[...] = total
+    term[...] = base[...] + near_edge(weights, got, coupling, inverse, False)
     size = own.shape[0]
     steps = lax.axis_size("node")
     for s, out in enumerate((own,) + sends):
@@ -261,24 +281,13 @@
         out[...] = value.astype(out.dtype)
 
 
-def correct(weights, base, got_a, got_b, coupling, inverse, parts):
+def correct(weights, base, got, coupling, inverse, parts):
     rows, columns = base.shape
-    band = coupling.shape[1]
     count = lax.axis_size("node")
     size = rows // count
     outs = [like((size, columns))] + [like((size, columns), BF16)] * (parts * (count - 1))
-    return whole(
-        correct_kernel,
-        outs,
-        weights,
-        base,
-        got_a,
-        got_b,
-        coupling,
-        inverse,
-        scratch=[pltpu.VMEM((rows, columns), F32)],
-        flops=16 * rows * band * columns,
-    )
+    scratch = [pltpu.VMEM((rows, columns), F32)]
+    return whole(correct_kernel, outs, weights, base, got, coupling, inverse, scratch=scratch)
 
 
 def place(blocks, out):
@@ -473,12 +482,6 @@
     )
 
 
-def refined(field, low, factor):
-    high, rest = halves_of(factor)
-    times = lambda a, b: lax.dot_general(a, b, NT, preferred_element_type=F32)
-    return times(field, high) + (times(field, rest) + times(low, high))
-
-
 def last_kernel(field, low, factor, out):
     out[...] = refined(field[...], low[...], factor[...])
 
@@ -508,16 +511,16 @@
     for iteration in range(ITERS):
         final = iteration == ITERS - 1
         if iteration == 0:
-            base, out_a, out_b, inverse, coupling, weights = start(
-                subspace, weights, upper_tiles, inverse
-            )
+            out_a, out_b, coupling, vectors = start(subspace, upper_tiles, inverse)
         else:
-            base, out_a, out_b = solve(field, low, factor, weights, coupling, inverse)
+            out_a, out_b, vectors = solve(field, low, factor, coupling, inverse)
         got_b = link_swap(out_b)
         got_a = core_swap(out_a)
-        own, *terms = correct(
-            weights, base, got_a, got_b, coupling, inverse, 1 if final else 2
-        )
+        if iteration == 0:
+            base, inverse, weights = start_base(weights, inverse, vectors, coupling, got_a)
+        else:
+            base = solve_base(weights, vectors, coupling, inverse, got_a)
+        own, *terms = correct(weights, base, got_b, coupling, inverse, 1 if final else 2)
         got = node_spread(terms[:partners])
         if not final:
             low_got = node_spread(terms[partners:])

time: 129 us -> 127 us (0.984)
  starting transfers between devices: 70.7 us -> 61.7 us
  waiting for transfers between devices: 24.6 us -> 28.9 us
  Pallas kernels: 31.9 us -> 34.7 us
    ppermute x6, starting transfers between devices: 8.66 us -> 2.45 us  [core_swap(): return lax.ppermute(block, 'rows', [(i, i ^ 1) for i in range(count)])]
    ppermute x30, waiting for transfers between devices: 16.3 us -> 20.5 us  [node_swap(): return lax.ppermute(block, 'node', [(i, i ^ step) for i in range(count)])]
    ppermute x12, starting transfers between devices: 23 us -> 19.6 us  [chip_sum(): lax.ppermute(block, 'rows', route)]
    pallas_call x1 -> x2, Pallas kernels: 2.88 us -> 5.12 us  [from_hbm(): pl.pallas_call(kernel, in_specs=[pl.BlockSpec(memory_space=kind) for kind...]
    pallas_call x15 -> x16, Pallas kernels: 29 us -> 29.6 us  [whole(): pl.pallas_call(kernel, out_shape=out_shape, in_specs=[vmem for _ in opera...]
  transfers between devices with their start and end apart: 52 -> 52, of which waited for: 22 -> 22; matrix products, arithmetic and copies ran while one was open for 0% -> 0% of each run, Pallas kernels for 11% -> 14%
where the time goes in v8:
time: 127 us
  starting transfers between devices  61.7 us (49%)
  Pallas kernels  34.7 us (27%)
  waiting for transfers between devices  28.9 us (23%)
    ppermute x30, starting transfers between devices, node_swap(): return lax.ppermute(block, 'node', [(i, i ^ step) for i in range(count)])  35.6 us
    pallas_call x16, Pallas kernels, whole(): pl.pallas_call(kernel, out_shape=out_shape, in_specs=[vmem for _ in opera...  29.6 us
    ppermute x30, waiting for transfers between devices, node_swap(): return lax.ppermute(block, 'node', [(i, i ^ step) for i in range(count)])  20.5 us
    ppermute x12, starting transfers between devices, chip_sum(): lax.ppermute(block, 'rows', route)  19.6 us
    pallas_call x2, Pallas kernels, from_hbm(): pl.pallas_call(kernel, in_specs=[pl.BlockSpec(memory_space=kind) for kind...  5.12 us
    ppermute x12, waiting for transfers between devices, chip_sum(): lax.ppermute(block, 'rows', route)  5.01 us
    ppermute x6, waiting for transfers between devices, core_swap(): return lax.ppermute(block, 'rows', [(i, i ^ 1) for i in range(count)])  2.92 us
    ppermute x2, starting transfers between devices, next_head(): return lax.ppermute(head, 'rows', [(i + 1, i) for i in range(count - 1)])  2.56 us
  transfers between devices with their start and end apart: 52, of which 22 were waited for; matrix products, arithmetic and copies ran while one was open for 0% of the time, Pallas kernels for 14%

profile of v8, /device:TPU:0, one launch (start us, length us, event | category | flops | bytes accessed | tf_op | source)
XLA Modules:
  0.0 126.6 jit_solution(13374142948562490346)
XLA Ops:
  0.6 2.0 %shard_map.68 = (bf16[128,512]{1,0:T(8,128)(2,1)S(1)}, bf16[128,512]{1,0:T(8,128)(2,1)S(1)}, f32[128,128]{1,0:T(8,128)S(1)}, bf16[768,256]{1,0:T(8,128)(2,1)S(1)}) custom-call(bf16[1,2,768,768]{3,2,1,0:T(8,128)(2,1)} %source.3, bf16[768,256]{1,0:T(8,128)(2,1)} %vectors_at.1, f32[768,128]{1,0:T(8,128)} %upper_tiles.3), custom_call_target="tpu_custom_call" | custom-call | flops 100000000 | bytes 1000000 | tf_op jit(solution)/shard_map/pallas_call | solution.py:169
  4.2 3.1 %shard_map.69 = (f32[768,256]{1,0:T(8,128)S(1)}, bf16[1,2,768,768]{3,2,1,0:T(8,128)(2,1)S(1)}, f32[1,2]{1,0:T(1,128)S(1)}) custom-call(f32[1,2]{1,0:T(1,128)} %weights_at.1, bf16[1,2,768,768]{3,2,1,0:T(8,128)(2,1)} %source.3, bf16[768,256]{1,0:T(8,128)(2,1)S(1)} %get-tuple-element.48.vectors, f32[128,128]{1,0:T(8,128)S(1)} %get-tuple-element.49.coupling, ...), custom_call_target="tpu_custom_call" | custom-call | flops 100000000 | bytes 1000000 | tf_op jit(solution)/shard_map/pallas_call | solution.py:169
  8.4 2.9 %collective-permute-start.2 = (bf16[192,256]{1,0:T(8,128)(2,1)S(1)}, bf16[192,256]{1,0:T(8,128)(2,1)S(1)}, u32[]{:S(2)}, u32[]{:S(2)}) collective-permute-start(bf16[192,256]{1,0:T(8,128)(2,1)S(1)} %get-tuple-element.56), channel_id=1, source_target_pairs={{0,8},{8,0},{16,24},{24,16},{1,9},{9,1},{17,25},{25,17},{2,10},{10... | collective-permute-start | bytes 294920 | tf_op jit(solution)/shard_map/ppermute | solution.py:95
  11.3 1.5 %collective-permute-start.3 = (bf16[192,256]{1,0:T(8,128)(2,1)S(1)}, bf16[192,256]{1,0:T(8,128)(2,1)S(1)}, u32[]{:S(2)}, u32[]{:S(2)}) collective-permute-start(bf16[192,256]{1,0:T(8,128)(2,1)S(1)} %get-tuple-element.57), channel_id=1, source_target_pairs={{0,16},{8,24},{16,0},{24,8},{1,17},{9,25},{17,1},{25,9},{2,18},{10... | collective-permute-start | bytes 294920 | tf_op jit(solution)/shard_map/ppermute | solution.py:95
  13.9 2.0 %collective-permute-done.3 = bf16[192,256]{1,0:T(8,128)(2,1)S(1)} collective-permute-done((bf16[192,256]{1,0:T(8,128)(2,1)S(1)}, bf16[192,256]{1,0:T(8,128)(2,1)S(1)}, u32[]{:S(2)}, u32[]{:S(2)}) %collective-permute-start.3) | collective-permute-done | bytes 98336 | tf_op jit(solution)/shard_map/ppermute | solution.py:95
  15.9 2.7 %collective-permute-done.4 = bf16[192,256]{1,0:T(8,128)(2,1)S(1)} collective-permute-done((bf16[192,256]{1,0:T(8,128)(2,1)S(1)}, bf16[192,256]{1,0:T(8,128)(2,1)S(1)}, u32[]{:S(2)}, u32[]{:S(2)}) %collective-permute-start.4) | collective-permute-done | bytes 98336 | tf_op jit(solution)/shard_map/ppermute | solution.py:95
  19.6 1.9 %collective-permute-start.6 = (bf16[192,256]{1,0:T(8,128)(2,1)S(1)}, bf16[192,256]{1,0:T(8,128)(2,1)S(1)}, u32[]{:S(2)}, u32[]{:S(2)}) collective-permute-start(bf16[192,256]{1,0:T(8,128)(2,1)S(1)} %get-tuple-element.64.refs_0_), channel_id=1, source_target_pairs={{0,16},{8,24},{16,0},{24,8},{1,17},{9,25},{17,1},{25,9},{2,18},{10... | collective-permute-start | bytes 294920 | tf_op jit(solution)/shard_map/ppermute | solution.py:95
  22.3 1.3 %collective-permute-start.8 = (bf16[192,256]{1,0:T(8,128)(2,1)S(1)}, bf16[192,256]{1,0:T(8,128)(2,1)S(1)}, u32[]{:S(2)}, u32[]{:S(2)}) collective-permute-start(bf16[192,256]{1,0:T(8,128)(2,1)S(1)} %get-tuple-element.61), channel_id=1, source_target_pairs={{0,8},{8,0},{16,24},{24,16},{1,9},{9,1},{17,25},{25,17},{2,10},{10... | collective-permute-start | bytes 294920 | tf_op jit(solution)/shard_map/ppermute | solution.py:95
  23.7 1.7 %collective-permute-done.7.refs_3_ = bf16[192,256]{1,0:T(8,128)(2,1)S(1)} collective-permute-done((bf16[192,256]{1,0:T(8,128)(2,1)S(1)}, bf16[192,256]{1,0:T(8,128)(2,1)S(1)}, u32[]{:S(2)}, u32[]{:S(2)}) %collective-permute-start.7) | collective-permute-done | bytes 98336 | tf_op jit(solution)/shard_map/ppermute | solution.py:95
  27.6 1.2 collective-permute-done.14
  28.9 3.8 %collective-permute-start.17 = (f32[64,256]{1,0:T(8,128)S(1)}, f32[64,256]{1,0:T(8,128)S(1)}, u32[]{:S(2)}, u32[]{:S(2)}) collective-permute-start(f32[64,256]{1,0:T(8,128)S(1)} %add.81), channel_id=1, source_target_pairs={{0,6},{1,7},{2,4},{3,5},{4,2},{5,3},{6,0},{7,1},{8,14},{9,15},{10,... | collective-permute-start | bytes 196616 | tf_op jit(solution)/shard_map/ppermute | solution.py:126
  32.7 1.1 collective-permute-start.16
  34.0 1.5 %collective-permute-start.13 = (bf16[192,256]{1,0:T(8,128)(2,1)S(1)}, bf16[192,256]{1,0:T(8,128)(2,1)S(1)}, u32[]{:S(2)}, u32[]{:S(2)}) collective-permute-start(bf16[192,256]{1,0:T(8,128)(2,1)S(1)} %subtract_convert_fusion.1.refs_0_), channel_id=1, source_target_pairs={{0,24},{8,16},{16,8},{24,0},{1,25},{9,17},{17,9},{25,1},{2,26},{10... | collective-permute-start | bytes 294920 | tf_op jit(solution)/shard_map/ppermute | solution.py:95
  35.5 1.1 collective-permute-start.12
  37.6 1.7 %collective-permute-done.16 = f32[64,256]{1,0:T(8,128)S(1)} collective-permute-done((f32[64,256]{1,0:T(8,128)S(1)}, f32[64,256]{1,0:T(8,128)S(1)}, u32[]{:S(2)}, u32[]{:S(2)}) %collective-permute-start.16) | collective-permute-done | bytes 65568 | tf_op jit(solution)/shard_map/ppermute | solution.py:126
  39.4 1.9 %collective-permute-start.20 = (f32[64,256]{1,0:T(8,128)S(1)}, f32[64,256]{1,0:T(8,128)S(1)}, u32[]{:S(2)}, u32[]{:S(2)}) collective-permute-start(f32[64,256]{1,0:T(8,128)S(1)} %add_add_fusion.5.refs_0_), channel_id=1, source_target_pairs={{0,24},{8,16},{16,8},{24,0},{1,25},{9,17},{17,9},{25,1},{2,26},{10... | collective-permute-start | bytes 196616 | tf_op jit(solution)/shard_map/ppermute | solution.py:95
  41.3 1.2 collective-permute-start.19
  43.0 1.7 %collective-permute-done.20.refs_3_ = f32[64,256]{1,0:T(8,128)S(1)} collective-permute-done((f32[64,256]{1,0:T(8,128)S(1)}, f32[64,256]{1,0:T(8,128)S(1)}, u32[]{:S(2)}, u32[]{:S(2)}) %collective-permute-start.20) | collective-permute-done | bytes 65568 | tf_op jit(solution)/shard_map/ppermute | solution.py:95
  46.8 4.8 %shard_map.73 = (f32[128,128]{1,0:T(8,128)S(1)}, f32[128,128]{1,0:T(8,128)S(1)}, f32[128,128]{1,0:T(8,128)S(1)}, f32[1,256]{1,0:T(1,128)S(1)}) custom-call(f32[64,256]{1,0:T(8,128)S(1)} %add_add_fusion.5.refs_0_, f32[64,256]{1,0:T(8,128)S(1)} %collective-permute-done.18.refs_1_, f32[64,256]{1,0:T(8,128)S(1)} %collective-permute-done.19.refs_2_, ...), custom_call_target="tpu_custom_call" | custom-call | flops 6000000000 | bytes 262144 | tf_op jit(solution)/shard_map/pallas_call | solution.py:82
  51.6 4.1 %shard_map.74.factor.refs_4_ = f32[256,256]{1,0:T(8,128)S(1)} custom-call(f32[128,128]{1,0:T(8,128)S(1)} %get-tuple-element.66.top, f32[128,128]{1,0:T(8,128)S(1)} %get-tuple-element.67.corner, f32[128,128]{1,0:T(8,128)S(1)} %get-tuple-element.68.rest, f32[1,256]{1,0:T(1,128)S(1)} %get-tuple-element.69.across), custom_call_target="tpu_custom_call" | custom-call | flops 6000000000 | bytes 197632 | tf_op jit(solution)/shard_map/pallas_call | solution.py:82
  55.7 1.7 %shard_map.75 = (bf16[128,512]{1,0:T(8,128)(2,1)S(1)}, bf16[128,512]{1,0:T(8,128)(2,1)S(1)}, bf16[768,256]{1,0:T(8,128)(2,1)S(1)}) custom-call(bf16[768,256]{1,0:T(8,128)(2,1)S(1)} %get-tuple-element.59.field, bf16[768,256]{1,0:T(8,128)(2,1)S(1)} %shard_map.72.low, f32[256,256]{1,0:T(8,128)S(1)} %shard_map.74.factor.refs_4_, ...), custom_call_target="tpu_custom_call" | custom-call | flops 100000000 | bytes 3473408 | tf_op jit(solution)/shard_map/pallas_call | solution.py:82
  58.8 1.6 %shard_map.76.base = f32[768,256]{1,0:T(8,128)S(1)} custom-call(f32[1,2]{1,0:T(1,128)S(1)} %get-tuple-element.51.weights, bf16[768,256]{1,0:T(8,128)(2,1)S(1)} %get-tuple-element.70.vectors, f32[128,128]{1,0:T(8,128)S(1)} %get-tuple-element.49.coupling, bf16[1,2,768,768]{3,2,1,0:T(8,128)(2,1)S(1)} %get-tuple-element.54.inverse, ...), custom_call_target="tpu_custom_call" | custom-call | flops 100000000 | bytes 2949128 | tf_op jit(solution)/shard_map/pallas_call | solution.py:82
  62.1 1.2 collective-permute-start.24
  63.3 1.7 %collective-permute-start.25 = (bf16[192,256]{1,0:T(8,128)(2,1)S(1)}, bf16[192,256]{1,0:T(8,128)(2,1)S(1)}, u32[]{:S(2)}, u32[]{:S(2)}) collective-permute-start(bf16[192,256]{1,0:T(8,128)(2,1)S(1)} %get-tuple-element.76), channel_id=1, source_target_pairs={{0,24},{8,16},{16,8},{24,0},{1,25},{9,17},{17,9},{25,1},{2,26},{10... | collective-permute-start | bytes 294920 | tf_op jit(solution)/shard_map/ppermute | solution.py:95
  65.0 1.3 %collective-permute-start.39 = (bf16[128,256]{1,0:T(8,128)(2,1)S(1)}, bf16[128,256]{1,0:T(8,128)(2,1)S(1)}, u32[]{:S(2)}, u32[]{:S(2)}) collective-permute-start(bf16[128,256]{1,0:T(8,128)(2,1)S(1)} %get-tuple-element.86), channel_id=1, source_target_pairs={{1,0},{2,1},{3,2},{4,3},{5,4},{6,5},{7,6},{9,8},{10,9},{11,10},{12... | collective-permute-start | bytes 196616 | tf_op jit(solution)/shard_map/ppermute | solution.py:448
  66.7 2.7 %collective-permute-done.25 = bf16[192,256]{1,0:T(8,128)(2,1)S(1)} collective-permute-done((bf16[192,256]{1,0:T(8,128)(2,1)S(1)}, bf16[192,256]{1,0:T(8,128)(2,1)S(1)}, u32[]{:S(2)}, u32[]{:S(2)}) %collective-permute-start.25) | collective-permute-done | bytes 98336 | tf_op jit(solution)/shard_map/ppermute | solution.py:95
  69.5 2.3 %collective-permute-start.28 = (bf16[192,256]{1,0:T(8,128)(2,1)S(1)}, bf16[192,256]{1,0:T(8,128)(2,1)S(1)}, u32[]{:S(2)}, u32[]{:S(2)}) collective-permute-start(bf16[192,256]{1,0:T(8,128)(2,1)S(1)} %get-tuple-element.79.refs_0_), channel_id=1, source_target_pairs={{0,24},{8,16},{16,8},{24,0},{1,25},{9,17},{17,9},{25,1},{2,26},{10... | collective-permute-start | bytes 294920 | tf_op jit(solution)/shard_map/ppermute | solution.py:95
  73.1 2.3 %collective-permute-start.31 = (bf16[192,256]{1,0:T(8,128)(2,1)S(1)}, bf16[192,256]{1,0:T(8,128)(2,1)S(1)}, u32[]{:S(2)}, u32[]{:S(2)}) collective-permute-start(bf16[192,256]{1,0:T(8,128)(2,1)S(1)} %subtract_convert_fusion.refs_0_), channel_id=1, source_target_pairs={{0,24},{8,16},{16,8},{24,0},{1,25},{9,17},{17,9},{25,1},{2,26},{10... | collective-permute-start | bytes 294920 | tf_op jit(solution)/shard_map/ppermute | solution.py:95
  75.6 2.9 %collective-permute-done.27.refs_2_ = bf16[192,256]{1,0:T(8,128)(2,1)S(1)} collective-permute-done((bf16[192,256]{1,0:T(8,128)(2,1)S(1)}, bf16[192,256]{1,0:T(8,128)(2,1)S(1)}, u32[]{:S(2)}, u32[]{:S(2)}) %collective-permute-start.27) | collective-permute-done | bytes 98336 | tf_op jit(solution)/shard_map/ppermute | solution.py:95
  79.1 1.2 shard_map.83
  81.7 1.1 collective-permute-start.29
  82.8 4.1 %collective-permute-start.35 = (f32[64,256]{1,0:T(8,128)S(1)}, f32[64,256]{1,0:T(8,128)S(1)}, u32[]{:S(2)}, u32[]{:S(2)}) collective-permute-start(f32[64,256]{1,0:T(8,128)S(1)} %add.88), channel_id=1, source_target_pairs={{0,6},{1,7},{2,4},{3,5},{4,2},{5,3},{6,0},{7,1},{8,14},{9,15},{10,... | collective-permute-start | bytes 196616 | tf_op jit(solution)/shard_map/ppermute | solution.py:126
  87.8 3.6 %collective-permute-start.43 = (f32[64,256]{1,0:T(8,128)S(1)}, f32[64,256]{1,0:T(8,128)S(1)}, u32[]{:S(2)}, u32[]{:S(2)}) collective-permute-start(f32[64,256]{1,0:T(8,128)S(1)} %add.92), channel_id=1, source_target_pairs={{0,6},{1,7},{2,4},{3,5},{4,2},{5,3},{6,0},{7,1},{8,14},{9,15},{10,... | collective-permute-start | bytes 196616 | tf_op jit(solution)/shard_map/ppermute | solution.py:126
  91.5 1.2 collective-permute-start.41
  92.7 3.0 %collective-permute-done.34 = f32[64,256]{1,0:T(8,128)S(1)} collective-permute-done((f32[64,256]{1,0:T(8,128)S(1)}, f32[64,256]{1,0:T(8,128)S(1)}, u32[]{:S(2)}, u32[]{:S(2)}) %collective-permute-start.34) | collective-permute-done | bytes 65568 | tf_op jit(solution)/shard_map/ppermute | solution.py:126
  95.6 1.3 %collective-permute-start.44 = (bf16[128,256]{1,0:T(8,128)(2,1)S(1)}, bf16[128,256]{1,0:T(8,128)(2,1)S(1)}, u32[]{:S(2)}, u32[]{:S(2)}) collective-permute-start(bf16[128,256]{1,0:T(8,128)(2,1)S(1)} %get-tuple-element.90), channel_id=1, source_target_pairs={{1,0},{2,1},{3,2},{4,3},{5,4},{6,5},{7,6},{9,8},{10,9},{11,10},{12... | collective-permute-start | bytes 196616 | tf_op jit(solution)/shard_map/ppermute | solution.py:448
  97.0 1.3 %collective-permute-start.38 = (f32[64,256]{1,0:T(8,128)S(1)}, f32[64,256]{1,0:T(8,128)S(1)}, u32[]{:S(2)}, u32[]{:S(2)}) collective-permute-start(f32[64,256]{1,0:T(8,128)S(1)} %add_add_fusion.4.refs_0_), channel_id=1, source_target_pairs={{0,24},{8,16},{16,8},{24,0},{1,25},{9,17},{17,9},{25,1},{2,26},{10... | collective-permute-start | bytes 196616 | tf_op jit(solution)/shard_map/ppermute | solution.py:95
  98.8 1.2 collective-permute-start.37
  99.9 1.2 shard_map.84
  101.9 1.1 collective-permute-start.45
  104.2 1.6 %collective-permute-done.36.refs_1_ = f32[64,256]{1,0:T(8,128)S(1)} collective-permute-done((f32[64,256]{1,0:T(8,128)S(1)}, f32[64,256]{1,0:T(8,128)S(1)}, u32[]{:S(2)}, u32[]{:S(2)}) %collective-permute-start.36) | collective-permute-done | bytes 65568 | tf_op jit(solution)/shard_map/ppermute | solution.py:95
  105.8 4.2 %collective-permute-start.48 = (f32[64,256]{1,0:T(8,128)S(1)}, f32[64,256]{1,0:T(8,128)S(1)}, u32[]{:S(2)}, u32[]{:S(2)}) collective-permute-start(f32[64,256]{1,0:T(8,128)S(1)} %add.96), channel_id=1, source_target_pairs={{0,6},{1,7},{2,4},{3,5},{4,2},{5,3},{6,0},{7,1},{8,14},{9,15},{10,... | collective-permute-start | bytes 196616 | tf_op jit(solution)/shard_map/ppermute | solution.py:126
  110.6 4.8 %shard_map.80 = (f32[128,128]{1,0:T(8,128)S(1)}, f32[128,128]{1,0:T(8,128)S(1)}, f32[128,128]{1,0:T(8,128)S(1)}, f32[1,256]{1,0:T(1,128)S(1)}) custom-call(f32[64,256]{1,0:T(8,128)S(1)} %add_add_fusion.4.refs_0_, f32[64,256]{1,0:T(8,128)S(1)} %collective-permute-done.36.refs_1_, f32[64,256]{1,0:T(8,128)S(1)} %collective-permute-done.37.refs_2_, ...), custom_call_target="tpu_custom_call" | custom-call | flops 6000000000 | bytes 262144 | tf_op jit(solution)/shard_map/pallas_call | solution.py:82
  115.8 1.6 %collective-permute-start.51 = (f32[128,256]{1,0:T(8,128)S(1)}, f32[128,256]{1,0:T(8,128)S(1)}, u32[]{:S(2)}, u32[]{:S(2)}) collective-permute-start(f32[128,256]{1,0:T(8,128)S(1)} %pad_maximum_fusion.refs_0_), channel_id=1, source_target_pairs={{0,24},{8,16},{16,8},{24,0},{1,25},{9,17},{17,9},{25,1},{2,26},{10... | collective-permute-start | bytes 393224 | tf_op jit(solution)/shard_map/ppermute | solution.py:95
  117.9 1.4 %collective-permute-start.49 = (f32[128,256]{1,0:T(8,128)S(1)}, f32[128,256]{1,0:T(8,128)S(1)}, u32[]{:S(2)}, u32[]{:S(2)}) collective-permute-start(f32[128,256]{1,0:T(8,128)S(1)} %pad_maximum_fusion.refs_0_), channel_id=1, source_target_pairs={{0,8},{8,0},{16,24},{24,16},{1,9},{9,1},{17,25},{25,17},{2,10},{10... | collective-permute-start | bytes 393224 | tf_op jit(solution)/shard_map/ppermute | solution.py:95
  119.3 4.1 %shard_map.81.factor.refs_5_ = f32[256,256]{1,0:T(8,128)S(1)} custom-call(f32[128,128]{1,0:T(8,128)S(1)} %get-tuple-element.81.top, f32[128,128]{1,0:T(8,128)S(1)} %get-tuple-element.82.corner, f32[128,128]{1,0:T(8,128)S(1)} %get-tuple-element.83.rest, f32[1,256]{1,0:T(1,128)S(1)} %get-tuple-element.84.across), custom_call_target="tpu_custom_call" | custom-call | flops 6000000000 | bytes 197632 | tf_op jit(solution)/shard_map/pallas_call | solution.py:82
  123.5 1.4 %shard_map.82 = f32[768,256]{1,0:T(8,128)} custom-call(bf16[768,256]{1,0:T(8,128)(2,1)S(1)} %get-tuple-element.77.field, bf16[768,256]{1,0:T(8,128)(2,1)S(1)} %shard_map.79.low, f32[256,256]{1,0:T(8,128)S(1)} %shard_map.81.factor.refs_5_), custom_call_target="tpu_custom_call" | custom-call | flops 100000000 | bytes 1048576 | tf_op jit(solution)/shard_map/pallas_call | solution.py:82
  124.9 1.7 %shard_map.85 = f32[2,256,256]{2,1,0:T(8,128)} custom-call(f32[128,256]{1,0:T(8,128)S(1)} %pad_maximum_fusion.refs_0_, f32[128,256]{1,0:T(8,128)S(1)} %collective-permute-done.49.refs_1_, f32[128,256]{1,0:T(8,128)S(1)} %collective-permute-done.50.refs_2_, f32[128,256]{1,0:T(8,128)S(1)} %collective-permute-done.51.refs_3_, ...), custom_call_target="tpu_custom_call" | custom-call | flops 100000000 | bytes 1048576 | tf_op jit(solution)/shard_map/pallas_call | solution.py:82
  (91 shorter events, 23.4 us)
Async XLA Ops:
  3.2 4.1 %collective-permute-start.1 = (bf16[128,512]{1,0:T(8,128)(2,1)S(1)}, bf16[128,512]{1,0:T(8,128)(2,1)S(1)}, u32[]{:S(2)}, u32[]{:S(2)}) collective-permute-start(bf16[128,512]{1,0:T(8,128)(2,1)S(1)} %get-tuple-element.53), channel_id=1, source_target_pairs={{1,2},{3,4},{5,6},{2,1},{4,3},{6,5},{9,10},{11,12},{13,14},{10,9},... | collective-permute-start | bytes 393224 | tf_op jit(solution)/shard_map/ppermute | solution.py:106
  8.4 5.5 %collective-permute-start.2 = (bf16[192,256]{1,0:T(8,128)(2,1)S(1)}, bf16[192,256]{1,0:T(8,128)(2,1)S(1)}, u32[]{:S(2)}, u32[]{:S(2)}) collective-permute-start(bf16[192,256]{1,0:T(8,128)(2,1)S(1)} %get-tuple-element.56), channel_id=1, source_target_pairs={{0,8},{8,0},{16,24},{24,16},{1,9},{9,1},{17,25},{25,17},{2,10},{10... | collective-permute-start | bytes 294920 | tf_op jit(solution)/shard_map/ppermute | solution.py:95
  11.3 4.6 %collective-permute-start.3 = (bf16[192,256]{1,0:T(8,128)(2,1)S(1)}, bf16[192,256]{1,0:T(8,128)(2,1)S(1)}, u32[]{:S(2)}, u32[]{:S(2)}) collective-permute-start(bf16[192,256]{1,0:T(8,128)(2,1)S(1)} %get-tuple-element.57), channel_id=1, source_target_pairs={{0,16},{8,24},{16,0},{24,8},{1,17},{9,25},{17,1},{25,9},{2,18},{10... | collective-permute-start | bytes 294920 | tf_op jit(solution)/shard_map/ppermute | solution.py:95
  12.8 5.8 %collective-permute-start.4 = (bf16[192,256]{1,0:T(8,128)(2,1)S(1)}, bf16[192,256]{1,0:T(8,128)(2,1)S(1)}, u32[]{:S(2)}, u32[]{:S(2)}) collective-permute-start(bf16[192,256]{1,0:T(8,128)(2,1)S(1)} %get-tuple-element.58), channel_id=1, source_target_pairs={{0,24},{8,16},{16,8},{24,0},{1,25},{9,17},{17,9},{25,1},{2,26},{10... | collective-permute-start | bytes 294920 | tf_op jit(solution)/shard_map/ppermute | solution.py:95
  18.7 6.7 %collective-permute-start.7 = (bf16[192,256]{1,0:T(8,128)(2,1)S(1)}, bf16[192,256]{1,0:T(8,128)(2,1)S(1)}, u32[]{:S(2)}, u32[]{:S(2)}) collective-permute-start(bf16[192,256]{1,0:T(8,128)(2,1)S(1)} %get-tuple-element.64.refs_0_), channel_id=1, source_target_pairs={{0,24},{8,16},{16,8},{24,0},{1,25},{9,17},{17,9},{25,1},{2,26},{10... | collective-permute-start | bytes 294920 | tf_op jit(solution)/shard_map/ppermute | solution.py:95
  19.6 7.5 %collective-permute-start.6 = (bf16[192,256]{1,0:T(8,128)(2,1)S(1)}, bf16[192,256]{1,0:T(8,128)(2,1)S(1)}, u32[]{:S(2)}, u32[]{:S(2)}) collective-permute-start(bf16[192,256]{1,0:T(8,128)(2,1)S(1)} %get-tuple-element.64.refs_0_), channel_id=1, source_target_pairs={{0,16},{8,24},{16,0},{24,8},{1,17},{9,25},{17,1},{25,9},{2,18},{10... | collective-permute-start | bytes 294920 | tf_op jit(solution)/shard_map/ppermute | solution.py:95
  21.5 5.7 %collective-permute-start.5 = (bf16[192,256]{1,0:T(8,128)(2,1)S(1)}, bf16[192,256]{1,0:T(8,128)(2,1)S(1)}, u32[]{:S(2)}, u32[]{:S(2)}) collective-permute-start(bf16[192,256]{1,0:T(8,128)(2,1)S(1)} %get-tuple-element.64.refs_0_), channel_id=1, source_target_pairs={{0,8},{8,0},{16,24},{24,16},{1,9},{9,1},{17,25},{25,17},{2,10},{10... | collective-permute-start | bytes 294920 | tf_op jit(solution)/shard_map/ppermute | solution.py:95
  22.3 11.6 %collective-permute-start.8 = (bf16[192,256]{1,0:T(8,128)(2,1)S(1)}, bf16[192,256]{1,0:T(8,128)(2,1)S(1)}, u32[]{:S(2)}, u32[]{:S(2)}) collective-permute-start(bf16[192,256]{1,0:T(8,128)(2,1)S(1)} %get-tuple-element.61), channel_id=1, source_target_pairs={{0,8},{8,0},{16,24},{24,16},{1,9},{9,1},{17,25},{25,17},{2,10},{10... | collective-permute-start | bytes 294920 | tf_op jit(solution)/shard_map/ppermute | solution.py:95
  23.6 10.4 %collective-permute-start.9 = (bf16[192,256]{1,0:T(8,128)(2,1)S(1)}, bf16[192,256]{1,0:T(8,128)(2,1)S(1)}, u32[]{:S(2)}, u32[]{:S(2)}) collective-permute-start(bf16[192,256]{1,0:T(8,128)(2,1)S(1)} %get-tuple-element.62), channel_id=1, source_target_pairs={{0,16},{8,24},{16,0},{24,8},{1,17},{9,25},{17,1},{25,9},{2,18},{10... | collective-permute-start | bytes 294920 | tf_op jit(solution)/shard_map/ppermute | solution.py:95
  25.4 8.6 %collective-permute-start.10 = (bf16[192,256]{1,0:T(8,128)(2,1)S(1)}, bf16[192,256]{1,0:T(8,128)(2,1)S(1)}, u32[]{:S(2)}, u32[]{:S(2)}) collective-permute-start(bf16[192,256]{1,0:T(8,128)(2,1)S(1)} %get-tuple-element.63), channel_id=1, source_target_pairs={{0,24},{8,16},{16,8},{24,0},{1,25},{9,17},{17,9},{25,1},{2,26},{10... | collective-permute-start | bytes 294920 | tf_op jit(solution)/shard_map/ppermute | solution.py:95
  28.9 7.7 %collective-permute-start.17 = (f32[64,256]{1,0:T(8,128)S(1)}, f32[64,256]{1,0:T(8,128)S(1)}, u32[]{:S(2)}, u32[]{:S(2)}) collective-permute-start(f32[64,256]{1,0:T(8,128)S(1)} %add.81), channel_id=1, source_target_pairs={{0,6},{1,7},{2,4},{3,5},{4,2},{5,3},{6,0},{7,1},{8,14},{9,15},{10,... | collective-permute-start | bytes 196616 | tf_op jit(solution)/shard_map/ppermute | solution.py:126
  32.7 6.6 %collective-permute-start.16 = (f32[64,256]{1,0:T(8,128)S(1)}, f32[64,256]{1,0:T(8,128)S(1)}, u32[]{:S(2)}, u32[]{:S(2)}) collective-permute-start(f32[64,256]{1,0:T(8,128)S(1)} %add.81), channel_id=1, source_target_pairs={{0,4},{1,5},{2,6},{3,7},{4,0},{5,1},{6,2},{7,3},{8,12},{9,13},{10,... | collective-permute-start | bytes 196616 | tf_op jit(solution)/shard_map/ppermute | solution.py:126
  33.8 5.5 %collective-permute-start.15 = (f32[64,256]{1,0:T(8,128)S(1)}, f32[64,256]{1,0:T(8,128)S(1)}, u32[]{:S(2)}, u32[]{:S(2)}) collective-permute-start(f32[64,256]{1,0:T(8,128)S(1)} %add.81), channel_id=1, source_target_pairs={{0,2},{1,3},{2,0},{3,1},{4,6},{5,7},{6,4},{7,5},{8,10},{9,11},{10,... | collective-permute-start | bytes 196616 | tf_op jit(solution)/shard_map/ppermute | solution.py:126
  34.0 8.5 %collective-permute-start.13 = (bf16[192,256]{1,0:T(8,128)(2,1)S(1)}, bf16[192,256]{1,0:T(8,128)(2,1)S(1)}, u32[]{:S(2)}, u32[]{:S(2)}) collective-permute-start(bf16[192,256]{1,0:T(8,128)(2,1)S(1)} %subtract_convert_fusion.1.refs_0_), channel_id=1, source_target_pairs={{0,24},{8,16},{16,8},{24,0},{1,25},{9,17},{17,9},{25,1},{2,26},{10... | collective-permute-start | bytes 294920 | tf_op jit(solution)/shard_map/ppermute | solution.py:95
  35.5 7.4 %collective-permute-start.12 = (bf16[192,256]{1,0:T(8,128)(2,1)S(1)}, bf16[192,256]{1,0:T(8,128)(2,1)S(1)}, u32[]{:S(2)}, u32[]{:S(2)}) collective-permute-start(bf16[192,256]{1,0:T(8,128)(2,1)S(1)} %subtract_convert_fusion.1.refs_0_), channel_id=1, source_target_pairs={{0,16},{8,24},{16,0},{24,8},{1,17},{9,25},{17,1},{25,9},{2,18},{10... | collective-permute-start | bytes 294920 | tf_op jit(solution)/shard_map/ppermute | solution.py:95
  36.6 6.3 %collective-permute-start.11 = (bf16[192,256]{1,0:T(8,128)(2,1)S(1)}, bf16[192,256]{1,0:T(8,128)(2,1)S(1)}, u32[]{:S(2)}, u32[]{:S(2)}) collective-permute-start(bf16[192,256]{1,0:T(8,128)(2,1)S(1)} %subtract_convert_fusion.1.refs_0_), channel_id=1, source_target_pairs={{0,8},{8,0},{16,24},{24,16},{1,9},{9,1},{17,25},{25,17},{2,10},{10... | collective-permute-start | bytes 294920 | tf_op jit(solution)/shard_map/ppermute | solution.py:95
  39.4 5.3 %collective-permute-start.20 = (f32[64,256]{1,0:T(8,128)S(1)}, f32[64,256]{1,0:T(8,128)S(1)}, u32[]{:S(2)}, u32[]{:S(2)}) collective-permute-start(f32[64,256]{1,0:T(8,128)S(1)} %add_add_fusion.5.refs_0_), channel_id=1, source_target_pairs={{0,24},{8,16},{16,8},{24,0},{1,25},{9,17},{17,9},{25,1},{2,26},{10... | collective-permute-start | bytes 196616 | tf_op jit(solution)/shard_map/ppermute | solution.py:95
  41.3 4.5 %collective-permute-start.19 = (f32[64,256]{1,0:T(8,128)S(1)}, f32[64,256]{1,0:T(8,128)S(1)}, u32[]{:S(2)}, u32[]{:S(2)}) collective-permute-start(f32[64,256]{1,0:T(8,128)S(1)} %add_add_fusion.5.refs_0_), channel_id=1, source_target_pairs={{0,16},{8,24},{16,0},{24,8},{1,17},{9,25},{17,1},{25,9},{2,18},{10... | collective-permute-start | bytes 196616 | tf_op jit(solution)/shard_map/ppermute | solution.py:95
  42.5 4.3 %collective-permute-start.18 = (f32[64,256]{1,0:T(8,128)S(1)}, f32[64,256]{1,0:T(8,128)S(1)}, u32[]{:S(2)}, u32[]{:S(2)}) collective-permute-start(f32[64,256]{1,0:T(8,128)S(1)} %add_add_fusion.5.refs_0_), channel_id=1, source_target_pairs={{0,8},{8,0},{16,24},{24,16},{1,9},{9,1},{17,25},{25,17},{2,10},{10... | collective-permute-start | bytes 196616 | tf_op jit(solution)/shard_map/ppermute | solution.py:95
  57.5 2.9 %collective-permute-start.22 = (bf16[128,512]{1,0:T(8,128)(2,1)S(1)}, bf16[128,512]{1,0:T(8,128)(2,1)S(1)}, u32[]{:S(2)}, u32[]{:S(2)}) collective-permute-start(bf16[128,512]{1,0:T(8,128)(2,1)S(1)} %get-tuple-element.72), channel_id=1, source_target_pairs={{1,2},{3,4},{5,6},{2,1},{4,3},{6,5},{9,10},{11,12},{13,14},{10,9},... | collective-permute-start | bytes 393224 | tf_op jit(solution)/shard_map/ppermute | solution.py:106
  61.5 4.8 %collective-permute-start.23 = (bf16[192,256]{1,0:T(8,128)(2,1)S(1)}, bf16[192,256]{1,0:T(8,128)(2,1)S(1)}, u32[]{:S(2)}, u32[]{:S(2)}) collective-permute-start(bf16[192,256]{1,0:T(8,128)(2,1)S(1)} %get-tuple-element.74), channel_id=1, source_target_pairs={{0,8},{8,0},{16,24},{24,16},{1,9},{9,1},{17,25},{25,17},{2,10},{10... | collective-permute-start | bytes 294920 | tf_op jit(solution)/shard_map/ppermute | solution.py:95
  62.1 4.6 %collective-permute-start.24 = (bf16[192,256]{1,0:T(8,128)(2,1)S(1)}, bf16[192,256]{1,0:T(8,128)(2,1)S(1)}, u32[]{:S(2)}, u32[]{:S(2)}) collective-permute-start(bf16[192,256]{1,0:T(8,128)(2,1)S(1)} %get-tuple-element.75), channel_id=1, source_target_pairs={{0,16},{8,24},{16,0},{24,8},{1,17},{9,25},{17,1},{25,9},{2,18},{10... | collective-permute-start | bytes 294920 | tf_op jit(solution)/shard_map/ppermute | solution.py:95
  63.3 6.1 %collective-permute-start.25 = (bf16[192,256]{1,0:T(8,128)(2,1)S(1)}, bf16[192,256]{1,0:T(8,128)(2,1)S(1)}, u32[]{:S(2)}, u32[]{:S(2)}) collective-permute-start(bf16[192,256]{1,0:T(8,128)(2,1)S(1)} %get-tuple-element.76), channel_id=1, source_target_pairs={{0,24},{8,16},{16,8},{24,0},{1,25},{9,17},{17,9},{25,1},{2,26},{10... | collective-permute-start | bytes 294920 | tf_op jit(solution)/shard_map/ppermute | solution.py:95
  65.0 10.4 %collective-permute-start.39 = (bf16[128,256]{1,0:T(8,128)(2,1)S(1)}, bf16[128,256]{1,0:T(8,128)(2,1)S(1)}, u32[]{:S(2)}, u32[]{:S(2)}) collective-permute-start(bf16[128,256]{1,0:T(8,128)(2,1)S(1)} %get-tuple-element.86), channel_id=1, source_target_pairs={{1,0},{2,1},{3,2},{4,3},{5,4},{6,5},{7,6},{9,8},{10,9},{11,10},{12... | collective-permute-start | bytes 196616 | tf_op jit(solution)/shard_map/ppermute | solution.py:448
  69.5 6.2 %collective-permute-start.28 = (bf16[192,256]{1,0:T(8,128)(2,1)S(1)}, bf16[192,256]{1,0:T(8,128)(2,1)S(1)}, u32[]{:S(2)}, u32[]{:S(2)}) collective-permute-start(bf16[192,256]{1,0:T(8,128)(2,1)S(1)} %get-tuple-element.79.refs_0_), channel_id=1, source_target_pairs={{0,24},{8,16},{16,8},{24,0},{1,25},{9,17},{17,9},{25,1},{2,26},{10... | collective-permute-start | bytes 294920 | tf_op jit(solution)/shard_map/ppermute | solution.py:95
  71.8 6.8 %collective-permute-start.27 = (bf16[192,256]{1,0:T(8,128)(2,1)S(1)}, bf16[192,256]{1,0:T(8,128)(2,1)S(1)}, u32[]{:S(2)}, u32[]{:S(2)}) collective-permute-start(bf16[192,256]{1,0:T(8,128)(2,1)S(1)} %get-tuple-element.79.refs_0_), channel_id=1, source_target_pairs={{0,16},{8,24},{16,0},{24,8},{1,17},{9,25},{17,1},{25,9},{2,18},{10... | collective-permute-start | bytes 294920 | tf_op jit(solution)/shard_map/ppermute | solution.py:95
  72.1 6.4 %collective-permute-start.26 = (bf16[192,256]{1,0:T(8,128)(2,1)S(1)}, bf16[192,256]{1,0:T(8,128)(2,1)S(1)}, u32[]{:S(2)}, u32[]{:S(2)}) collective-permute-start(bf16[192,256]{1,0:T(8,128)(2,1)S(1)} %get-tuple-element.79.refs_0_), channel_id=1, source_target_pairs={{0,8},{8,0},{16,24},{24,16},{1,9},{9,1},{17,25},{25,17},{2,10},{10... | collective-permute-start | bytes 294920 | tf_op jit(solution)/shard_map/ppermute | solution.py:95
  73.1 14.4 %collective-permute-start.31 = (bf16[192,256]{1,0:T(8,128)(2,1)S(1)}, bf16[192,256]{1,0:T(8,128)(2,1)S(1)}, u32[]{:S(2)}, u32[]{:S(2)}) collective-permute-start(bf16[192,256]{1,0:T(8,128)(2,1)S(1)} %subtract_convert_fusion.refs_0_), channel_id=1, source_target_pairs={{0,24},{8,16},{16,8},{24,0},{1,25},{9,17},{17,9},{25,1},{2,26},{10... | collective-permute-start | bytes 294920 | tf_op jit(solution)/shard_map/ppermute | solution.py:95
  78.9 3.9 %collective-permute-start.32 = (f32[64,256]{1,0:T(8,128)S(1)}, f32[64,256]{1,0:T(8,128)S(1)}, u32[]{:S(2)}, u32[]{:S(2)}) collective-permute-start(f32[64,256]{1,0:T(8,128)S(1)} %get-tuple-element.80), channel_id=1, source_target_pairs={{0,1},{1,0},{2,3},{3,2},{4,5},{5,4},{6,7},{7,6},{8,9},{9,8},{10,11... | collective-permute-start | bytes 196616 | tf_op jit(solution)/shard_map/ppermute | solution.py:100
  80.3 6.7 %collective-permute-start.40 = (f32[64,256]{1,0:T(8,128)S(1)}, f32[64,256]{1,0:T(8,128)S(1)}, u32[]{:S(2)}, u32[]{:S(2)}) collective-permute-start(f32[64,256]{1,0:T(8,128)S(1)} %shard_map.83), channel_id=1, source_target_pairs={{0,1},{1,0},{2,3},{3,2},{4,5},{5,4},{6,7},{7,6},{8,9},{9,8},{10,11... | collective-permute-start | bytes 196616 | tf_op jit(solution)/shard_map/ppermute | solution.py:100
  80.8 7.0 %collective-permute-start.30 = (bf16[192,256]{1,0:T(8,128)(2,1)S(1)}, bf16[192,256]{1,0:T(8,128)(2,1)S(1)}, u32[]{:S(2)}, u32[]{:S(2)}) collective-permute-start(bf16[192,256]{1,0:T(8,128)(2,1)S(1)} %subtract_convert_fusion.refs_0_), channel_id=1, source_target_pairs={{0,16},{8,24},{16,0},{24,8},{1,17},{9,25},{17,1},{25,9},{2,18},{10... | collective-permute-start | bytes 294920 | tf_op jit(solution)/shard_map/ppermute | solution.py:95
  81.7 9.7 %collective-permute-start.29 = (bf16[192,256]{1,0:T(8,128)(2,1)S(1)}, bf16[192,256]{1,0:T(8,128)(2,1)S(1)}, u32[]{:S(2)}, u32[]{:S(2)}) collective-permute-start(bf16[192,256]{1,0:T(8,128)(2,1)S(1)} %subtract_convert_fusion.refs_0_), channel_id=1, source_target_pairs={{0,8},{8,0},{16,24},{24,16},{1,9},{9,1},{17,25},{25,17},{2,10},{10... | collective-permute-start | bytes 294920 | tf_op jit(solution)/shard_map/ppermute | solution.py:95
  82.8 8.7 %collective-permute-start.35 = (f32[64,256]{1,0:T(8,128)S(1)}, f32[64,256]{1,0:T(8,128)S(1)}, u32[]{:S(2)}, u32[]{:S(2)}) collective-permute-start(f32[64,256]{1,0:T(8,128)S(1)} %add.88), channel_id=1, source_target_pairs={{0,6},{1,7},{2,4},{3,5},{4,2},{5,3},{6,0},{7,1},{8,14},{9,15},{10,... | collective-permute-start | bytes 196616 | tf_op jit(solution)/shard_map/ppermute | solution.py:126
  87.0 8.7 %collective-permute-start.34 = (f32[64,256]{1,0:T(8,128)S(1)}, f32[64,256]{1,0:T(8,128)S(1)}, u32[]{:S(2)}, u32[]{:S(2)}) collective-permute-start(f32[64,256]{1,0:T(8,128)S(1)} %add.88), channel_id=1, source_target_pairs={{0,4},{1,5},{2,6},{3,7},{4,0},{5,1},{6,2},{7,3},{8,12},{9,13},{10,... | collective-permute-start | bytes 196616 | tf_op jit(solution)/shard_map/ppermute | solution.py:126
  87.5 9.5 %collective-permute-start.33 = (f32[64,256]{1,0:T(8,128)S(1)}, f32[64,256]{1,0:T(8,128)S(1)}, u32[]{:S(2)}, u32[]{:S(2)}) collective-permute-start(f32[64,256]{1,0:T(8,128)S(1)} %add.88), channel_id=1, source_target_pairs={{0,2},{1,3},{2,0},{3,1},{4,6},{5,7},{6,4},{7,5},{8,10},{9,11},{10,... | collective-permute-start | bytes 196616 | tf_op jit(solution)/shard_map/ppermute | solution.py:126
  87.8 13.3 %collective-permute-start.43 = (f32[64,256]{1,0:T(8,128)S(1)}, f32[64,256]{1,0:T(8,128)S(1)}, u32[]{:S(2)}, u32[]{:S(2)}) collective-permute-start(f32[64,256]{1,0:T(8,128)S(1)} %add.92), channel_id=1, source_target_pairs={{0,6},{1,7},{2,4},{3,5},{4,2},{5,3},{6,0},{7,1},{8,14},{9,15},{10,... | collective-permute-start | bytes 196616 | tf_op jit(solution)/shard_map/ppermute | solution.py:126
  91.5 10.5 %collective-permute-start.42 = (f32[64,256]{1,0:T(8,128)S(1)}, f32[64,256]{1,0:T(8,128)S(1)}, u32[]{:S(2)}, u32[]{:S(2)}) collective-permute-start(f32[64,256]{1,0:T(8,128)S(1)} %add.92), channel_id=1, source_target_pairs={{0,4},{1,5},{2,6},{3,7},{4,0},{5,1},{6,2},{7,3},{8,12},{9,13},{10,... | collective-permute-start | bytes 196616 | tf_op jit(solution)/shard_map/ppermute | solution.py:126
  91.5 11.5 %collective-permute-start.41 = (f32[64,256]{1,0:T(8,128)S(1)}, f32[64,256]{1,0:T(8,128)S(1)}, u32[]{:S(2)}, u32[]{:S(2)}) collective-permute-start(f32[64,256]{1,0:T(8,128)S(1)} %add.92), channel_id=1, source_target_pairs={{0,2},{1,3},{2,0},{3,1},{4,6},{5,7},{6,4},{7,5},{8,10},{9,11},{10,... | collective-permute-start | bytes 196616 | tf_op jit(solution)/shard_map/ppermute | solution.py:126
  95.6 3.1 %collective-permute-start.44 = (bf16[128,256]{1,0:T(8,128)(2,1)S(1)}, bf16[128,256]{1,0:T(8,128)(2,1)S(1)}, u32[]{:S(2)}, u32[]{:S(2)}) collective-permute-start(bf16[128,256]{1,0:T(8,128)(2,1)S(1)} %get-tuple-element.90), channel_id=1, source_target_pairs={{1,0},{2,1},{3,2},{4,3},{5,4},{6,5},{7,6},{9,8},{10,9},{11,10},{12... | collective-permute-start | bytes 196616 | tf_op jit(solution)/shard_map/ppermute | solution.py:448
  97.0 7.0 %collective-permute-start.38 = (f32[64,256]{1,0:T(8,128)S(1)}, f32[64,256]{1,0:T(8,128)S(1)}, u32[]{:S(2)}, u32[]{:S(2)}) collective-permute-start(f32[64,256]{1,0:T(8,128)S(1)} %add_add_fusion.4.refs_0_), channel_id=1, source_target_pairs={{0,24},{8,16},{16,8},{24,0},{1,25},{9,17},{17,9},{25,1},{2,26},{10... | collective-permute-start | bytes 196616 | tf_op jit(solution)/shard_map/ppermute | solution.py:95
  98.8 5.4 %collective-permute-start.37 = (f32[64,256]{1,0:T(8,128)S(1)}, f32[64,256]{1,0:T(8,128)S(1)}, u32[]{:S(2)}, u32[]{:S(2)}) collective-permute-start(f32[64,256]{1,0:T(8,128)S(1)} %add_add_fusion.4.refs_0_), channel_id=1, source_target_pairs={{0,16},{8,24},{16,0},{24,8},{1,17},{9,25},{17,1},{25,9},{2,18},{10... | collective-permute-start | bytes 196616 | tf_op jit(solution)/shard_map/ppermute | solution.py:95
  101.2 4.7 %collective-permute-start.36 = (f32[64,256]{1,0:T(8,128)S(1)}, f32[64,256]{1,0:T(8,128)S(1)}, u32[]{:S(2)}, u32[]{:S(2)}) collective-permute-start(f32[64,256]{1,0:T(8,128)S(1)} %add_add_fusion.4.refs_0_), channel_id=1, source_target_pairs={{0,8},{8,0},{16,24},{24,16},{1,9},{9,1},{17,25},{25,17},{2,10},{10... | collective-permute-start | bytes 196616 | tf_op jit(solution)/shard_map/ppermute | solution.py:95
  105.8 9.6 %collective-permute-start.48 = (f32[64,256]{1,0:T(8,128)S(1)}, f32[64,256]{1,0:T(8,128)S(1)}, u32[]{:S(2)}, u32[]{:S(2)}) collective-permute-start(f32[64,256]{1,0:T(8,128)S(1)} %add.96), channel_id=1, source_target_pairs={{0,6},{1,7},{2,4},{3,5},{4,2},{5,3},{6,0},{7,1},{8,14},{9,15},{10,... | collective-permute-start | bytes 196616 | tf_op jit(solution)/shard_map/ppermute | solution.py:126
  110.0 5.7 %collective-permute-start.47 = (f32[64,256]{1,0:T(8,128)S(1)}, f32[64,256]{1,0:T(8,128)S(1)}, u32[]{:S(2)}, u32[]{:S(2)}) collective-permute-start(f32[64,256]{1,0:T(8,128)S(1)} %add.96), channel_id=1, source_target_pairs={{0,4},{1,5},{2,6},{3,7},{4,0},{5,1},{6,2},{7,3},{8,12},{9,13},{10,... | collective-permute-start | bytes 196616 | tf_op jit(solution)/shard_map/ppermute | solution.py:126
  110.0 5.7 %collective-permute-start.46 = (f32[64,256]{1,0:T(8,128)S(1)}, f32[64,256]{1,0:T(8,128)S(1)}, u32[]{:S(2)}, u32[]{:S(2)}) collective-permute-start(f32[64,256]{1,0:T(8,128)S(1)} %add.96), channel_id=1, source_target_pairs={{0,2},{1,3},{2,0},{3,1},{4,6},{5,7},{6,4},{7,5},{8,10},{9,11},{10,... | collective-permute-start | bytes 196616 | tf_op jit(solution)/shard_map/ppermute | solution.py:126
  115.8 9.1 %collective-permute-start.51 = (f32[128,256]{1,0:T(8,128)S(1)}, f32[128,256]{1,0:T(8,128)S(1)}, u32[]{:S(2)}, u32[]{:S(2)}) collective-permute-start(f32[128,256]{1,0:T(8,128)S(1)} %pad_maximum_fusion.refs_0_), channel_id=1, source_target_pairs={{0,24},{8,16},{16,8},{24,0},{1,25},{9,17},{17,9},{25,1},{2,26},{10... | collective-permute-start | bytes 393224 | tf_op jit(solution)/shard_map/ppermute | solution.py:95
  117.4 7.5 %collective-permute-start.50 = (f32[128,256]{1,0:T(8,128)S(1)}, f32[128,256]{1,0:T(8,128)S(1)}, u32[]{:S(2)}, u32[]{:S(2)}) collective-permute-start(f32[128,256]{1,0:T(8,128)S(1)} %pad_maximum_fusion.refs_0_), channel_id=1, source_target_pairs={{0,16},{8,24},{16,0},{24,8},{1,17},{9,25},{17,1},{25,9},{2,18},{10... | collective-permute-start | bytes 393224 | tf_op jit(solution)/shard_map/ppermute | solution.py:95
  117.9 7.0 %collective-permute-start.49 = (f32[128,256]{1,0:T(8,128)S(1)}, f32[128,256]{1,0:T(8,128)S(1)}, u32[]{:S(2)}, u32[]{:S(2)}) collective-permute-start(f32[128,256]{1,0:T(8,128)S(1)} %pad_maximum_fusion.refs_0_), channel_id=1, source_target_pairs={{0,8},{8,0},{16,24},{24,16},{1,9},{9,1},{17,25},{25,17},{2,10},{10... | collective-permute-start | bytes 393224 | tf_op jit(solution)/shard_map/ppermute | solution.py:95
  (6 other events, 43.6 us)

commit v9 on v8

--- a/solution.py
+++ b/solution.py
@@ -191,14 +191,18 @@
     return 2 * band if rows % (2 * band) == 0 else band
 
 
-def near_edge(weights, got, coupling, inverse, on_chip):
+def near_edge(weights, got, coupling, inverse, on_chip, factor=None):
     rows, columns = inverse.shape[2], got.shape[1] // 2
     band = coupling.shape[0]
     is_even = lax.rem(lax.axis_index("rows"), 2) == 0
     is_next = is_even if on_chip else jnp.logical_not(is_even)
-    below = dot(coupling[...], got[...].astype(F32)).astype(BF16)
-    edge = jnp.where(is_next, below, got[...]).astype(F32)
-    real, imag = edge[:, :columns], edge[:, columns:]
+    if factor is None:
+        below = dot(coupling[...], got[...].astype(F32)).astype(BF16)
+        edge = jnp.where(is_next, below, got[...]).astype(F32)
+        real, imag = edge[:, :columns], edge[:, columns:]
+    else:
+        turned = [dot_three(got[:, at : at + columns], factor, NT) for at in (0, columns)]
+        real, imag = [jnp.where(is_next, dot_three(coupling[...], x), x) for x in turned]
     at = pl.multiple_of(jnp.where(is_next, rows - band, 0), band)
     left = dot_two(inverse[0, 0, :, pl.ds(at, band)], combine(weights, real, imag))
     right = weights[:, 0:1] * imag + weights[:, 1:2] * real
@@ -240,37 +244,30 @@
     return times(field, high) + (times(field, rest) + times(low, high))
 
 
-def solve_kernel(field, low, factor, coupling, inverse, out_a, out_b, current):
+def tips_kernel(field, low, coupling, inverse, out_a, out_b):
     band = coupling.shape[0]
-    current[...] = refined(field[...], low[...], factor[...]).astype(BF16)
-    top, bottom = inverse.at[0, :, :band], inverse.at[0, :, -band:]
-    emit_messages(current[...], top, bottom, coupling[...], out_a, out_b)
-
-
-def solve(field, low, factor, coupling, inverse):
-    rows, columns = field.shape
-    message = like((coupling.shape[0], 2 * columns), BF16)
-    outs = [message, message, like((rows, columns), BF16)]
-    return whole(solve_kernel, outs, field, low, factor, coupling, inverse)
-
-
-def base_kernel(weights, vectors, coupling, inverse, got, base):
-    rows = vectors.shape[0]
-    tile = tile_of(rows, coupling.shape[0])
-    for at in range(0, rows, tile):
-        span = pl.ds(at, tile)
-        base[span] = products(weights, vectors, inverse, span)
-    base[...] += near_edge(weights, got, coupling, inverse, True)
-
-
-def solve_base(weights, vectors, coupling, inverse, got):
-    return whole(base_kernel, like(vectors.shape), weights, vectors, coupling, inverse, got)
-
-
-def correct_kernel(weights, base, got, coupling, inverse, own, *refs):
-    sends, term = refs[:-1], refs[-1]
+    is_even = lax.rem(lax.axis_index("rows"), 2) == 0
+
+    def both(at):
+        times = lambda part, x: jnp.dot(
+            inverse[0, part, at : at + band], x, preferred_element_type=F32
+        )
+        of = lambda part: times(part, field[...]) + times(part, low[...])
+        return jnp.concatenate([of(0), of(1)], 1)
+
+    first = both(0)
+    last = dot_tn(coupling[...], both(field.shape[0] - band))
+    out_a[...] = jnp.where(is_even, last, first)
+    out_b[...] = jnp.where(is_even, first, last)
+
+
+def tips(field, low, coupling, inverse):
+    message = like((coupling.shape[0], 2 * field.shape[1]))
+    return whole(tips_kernel, [message, message], field, low, coupling, inverse)
+
+
+def emit_term(term, own, sends):
     node = lax.axis_index("node")
-    term[...] = base[...] + near_edge(weights, got, coupling, inverse, False)
     size = own.shape[0]
     steps = lax.axis_size("node")
     for s, out in enumerate((own,) + sends):
@@ -281,11 +278,51 @@
         out[...] = value.astype(out.dtype)
 
 
+def solve_kernel(weights, field, low, factor, coupling, inverse, got_a, got_b, own, *refs):
+    sends, (current, term) = refs[:-2], refs[-2:]
+    current[...] = refined(field[...], low[...], factor[...]).astype(BF16)
+    rows = field.shape[0]
+    tile = tile_of(rows, coupling.shape[0])
+    for at in range(0, rows, tile):
+        span = pl.ds(at, tile)
+        term[span] = products(weights, current, inverse, span)
+    term[...] += near_edge(weights, got_a, coupling, inverse, True, factor[...])
+    term[...] += near_edge(weights, got_b, coupling, inverse, False, factor[...])
+    emit_term(term, own, sends)
+
+
+def blocks_of(rows, columns, parts):
+    count = lax.axis_size("node")
+    size = rows // count
+    return [like((size, columns))] + [like((size, columns), BF16)] * (parts * (count - 1))
+
+
+def solve(weights, field, low, factor, coupling, inverse, got_a, got_b, parts):
+    rows, columns = field.shape
+    return whole(
+        solve_kernel,
+        blocks_of(rows, columns, parts),
+        weights,
+        field,
+        low,
+        factor,
+        coupling,
+        inverse,
+        got_a,
+        got_b,
+        scratch=[pltpu.VMEM((rows, columns), BF16), pltpu.VMEM((rows, columns), F32)],
+    )
+
+
+def correct_kernel(weights, base, got, coupling, inverse, own, *refs):
+    sends, term = refs[:-1], refs[-1]
+    term[...] = base[...] + near_edge(weights, got, coupling, inverse, False)
+    emit_term(term, own, sends)
+
+
 def correct(weights, base, got, coupling, inverse, parts):
     rows, columns = base.shape
-    count = lax.axis_size("node")
-    size = rows // count
-    outs = [like((size, columns))] + [like((size, columns), BF16)] * (parts * (count - 1))
+    outs = blocks_of(rows, columns, parts)
     scratch = [pltpu.VMEM((rows, columns), F32)]
     return whole(correct_kernel, outs, weights, base, got, coupling, inverse, scratch=scratch)
 
@@ -482,12 +519,21 @@
     )
 
 
-def last_kernel(field, low, factor, out):
-    out[...] = refined(field[...], low[...], factor[...])
-
-
-def projected_kernel(order, *refs):
-    blocks, factors, (out, matrix) = refs[: -2 - ITERS], refs[-2 - ITERS : -2], refs[-2:]
+def finish_kernel(order, field, low, *refs):
+    blocks, factors = refs[: -6 - ITERS], refs[-6 - ITERS : -6]
+    vectors_at, projected_at, vectors, projected, matrix, sent = refs[-6:]
+    rows = field.shape[0]
+    tile = rows // 3 if rows % 48 == 0 else rows
+    copies = []
+
+    def send(source, target):
+        copies.append(pltpu.make_async_copy(source, target, sent.at[len(copies)]))
+        copies[-1].start()
+
+    for at in range(0, rows, tile):
+        span = pl.ds(at, tile)
+        vectors[span] = refined(field[span], low[span], factors[-1][...])
+        send(vectors.at[span], vectors_at.at[span])
     node = lax.axis_index("node")
     size = blocks[0].shape[0] // ITERS
     for k, factor in enumerate(factors):
@@ -495,7 +541,28 @@
             at = pl.multiple_of((node ^ step) * size, 8)
             matrix[pl.ds(at, size), :] = block[k * size : (k + 1) * size]
         value = dot_three(dot_three(factor[...], matrix[...]), factor[...], NT)
-        out[k] = (value + value.T) * (1.0 / order)
+        projected[k] = (value + value.T) * (1.0 / order)
+        send(projected.at[k], projected_at.at[k])
+    for copy in copies:
+        copy.wait()
+
+
+def finish(field, low, blocks, factors, order):
+    rows, columns = field.shape
+    operands = [field, low, *blocks, *factors]
+    vmem = pl.BlockSpec(memory_space=pltpu.VMEM)
+    shapes = [(rows, columns), (ITERS, columns, columns)]
+    return pl.pallas_call(
+        functools.partial(finish_kernel, order),
+        in_specs=[vmem for _ in operands],
+        out_specs=[pl.BlockSpec(memory_space=pltpu.HBM)] * 2,
+        out_shape=[jax.ShapeDtypeStruct(x, F32) for x in shapes],
+        scratch_shapes=[pltpu.VMEM(x, F32) for x in shapes]
+        + [pltpu.VMEM((columns, columns), F32), pltpu.SemaphoreType.DMA((3 + ITERS,))],
+        cost_estimate=pl.CostEstimate(flops=10**9, bytes_accessed=10**6, transcendentals=0),
+        compiler_params=pltpu.CompilerParams(vmem_limit_bytes=GRANT),
+        name="finish",
+    )(*[local(x) for x in operands])
 
 
 def after(value, *others):
@@ -506,21 +573,20 @@
     order = float(subspace.shape[0] * lax.axis_size("rows"))
     band = upper_tiles.shape[1]
     partners = lax.axis_size("node") - 1
-    columns = subspace.shape[1]
     factors, pairs = [], []
     for iteration in range(ITERS):
         final = iteration == ITERS - 1
+        parts = 1 if final else 2
         if iteration == 0:
             out_a, out_b, coupling, vectors = start(subspace, upper_tiles, inverse)
+            got_b = link_swap(out_b)
+            got_a = core_swap(out_a)
+            base, inverse, weights = start_base(weights, inverse, vectors, coupling, got_a)
+            own, *terms = correct(weights, base, got_b, coupling, inverse, parts)
         else:
-            out_a, out_b, vectors = solve(field, low, factor, coupling, inverse)
-        got_b = link_swap(out_b)
-        got_a = core_swap(out_a)
-        if iteration == 0:
-            base, inverse, weights = start_base(weights, inverse, vectors, coupling, got_a)
-        else:
-            base = solve_base(weights, vectors, coupling, inverse, got_a)
-        own, *terms = correct(weights, base, got_b, coupling, inverse, 1 if final else 2)
+            own, *terms = solve(
+                weights, field, low, factor, coupling, inverse, got_a, got_b, parts
+            )
         got = node_spread(terms[:partners])
         if not final:
             low_got = node_spread(terms[partners:])
@@ -538,6 +604,10 @@
         total = chip_sum(part)
         gathered = [total] + node_spread([total] * partners)
         pair = band_slice(field, low, after(following, total), diag_tiles, upper_tiles)
+        if not final:
+            out_a, out_b = tips(field, low, coupling, inverse)
+            got_b = link_swap(out_b)
+            got_a = core_swap(out_a)
         halves = first_factor(gathered, order)
         pair = pair + core_swap(pair)
         pairs.append(chip_sum(after(pair, *gathered)))
@@ -546,14 +616,7 @@
             spread = [pair] + node_spread([pair] * partners)
         factor = second_factor(halves)
         factors.append(factor)
-    orthonormal = whole(last_kernel, jax.ShapeDtypeStruct(subspace.shape, F32), field, low, factor)
-    projected = whole(
-        functools.partial(projected_kernel, order),
-        jax.ShapeDtypeStruct((ITERS, columns, columns), F32),
-        *spread,
-        *factors,
-        scratch=[pltpu.VMEM((columns, columns), F32)],
-    )
+    orthonormal, projected = finish(field, low, spread, factors, order)
     return orthonormal, projected
 
 

time: 127 us -> 124 us (0.976)
  waiting for transfers between devices: 28.9 us -> 26.3 us
    pallas_call x16 -> x13, Pallas kernels: 29.6 us -> 27 us  [whole(): pl.pallas_call(kernel, out_shape=out_shape, in_specs=[vmem for _ in opera...]
    pallas_call x0 -> x1, Pallas kernels: none -> 1.99 us  [finish(): pl.pallas_call(functools.partial(finish_kernel, order), in_specs=[vmem fo...]
  transfers between devices with their start and end apart: 52 -> 52, of which waited for: 22 -> 21; matrix products, arithmetic and copies ran while one was open for 0% -> 0% of each run, Pallas kernels for 14% -> 20%
where the time goes in v9:
time: 124 us; the launch traced here: 123 us
  starting transfers between devices  61.4 us (50%)
  Pallas kernels  34.1 us (28%)
  waiting for transfers between devices  26.3 us (21%)
    ppermute x30, starting transfers between devices, node_swap(): return lax.ppermute(block, 'node', [(i, i ^ step) for i in range(count)])  35 us
    pallas_call x13, Pallas kernels, whole(): pl.pallas_call(kernel, out_shape=out_shape, in_specs=[vmem for _ in opera...  27 us
    ppermute x12, starting transfers between devices, chip_sum(): lax.ppermute(block, 'rows', route)  20.7 us
    ppermute x30, waiting for transfers between devices, node_swap(): return lax.ppermute(block, 'node', [(i, i ^ step) for i in range(count)])  19.7 us
    pallas_call x2, Pallas kernels, from_hbm(): pl.pallas_call(kernel, in_specs=[pl.BlockSpec(memory_space=kind) for kind...  5.12 us
    ppermute x12, waiting for transfers between devices, chip_sum(): lax.ppermute(block, 'rows', route)  3.85 us
    ppermute x2, starting transfers between devices, next_head(): return lax.ppermute(head, 'rows', [(i + 1, i) for i in range(count - 1)])  2.78 us
    ppermute x6, waiting for transfers between devices, core_swap(): return lax.ppermute(block, 'rows', [(i, i ^ 1) for i in range(count)])  2.75 us
  transfers between devices with their start and end apart: 52, of which 21 were waited for; matrix products, arithmetic and copies ran while one was open for 0% of the time, Pallas kernels for 20%

profile of v9, /device:TPU:0, one launch (start us, length us, event | category | flops | bytes accessed | tf_op | source)
XLA Modules:
  0.0 123.3 jit_solution(1612775569251593792)
XLA Ops:
  0.6 2.0 %shard_map.68 = (bf16[128,512]{1,0:T(8,128)(2,1)S(1)}, bf16[128,512]{1,0:T(8,128)(2,1)S(1)}, f32[128,128]{1,0:T(8,128)S(1)}, bf16[768,256]{1,0:T(8,128)(2,1)S(1)}) custom-call(bf16[1,2,768,768]{3,2,1,0:T(8,128)(2,1)} %source.3, bf16[768,256]{1,0:T(8,128)(2,1)} %vectors_at.1, f32[768,128]{1,0:T(8,128)} %upper_tiles.3), custom_call_target="tpu_custom_call" | custom-call | flops 100000000 | bytes 1000000 | tf_op jit(solution)/shard_map/pallas_call | solution.py:169
  4.2 3.1 %shard_map.69 = (f32[768,256]{1,0:T(8,128)S(1)}, bf16[1,2,768,768]{3,2,1,0:T(8,128)(2,1)S(1)}, f32[1,2]{1,0:T(1,128)S(1)}) custom-call(f32[1,2]{1,0:T(1,128)} %weights_at.1, bf16[1,2,768,768]{3,2,1,0:T(8,128)(2,1)} %source.3, bf16[768,256]{1,0:T(8,128)(2,1)S(1)} %get-tuple-element.47.vectors, f32[128,128]{1,0:T(8,128)S(1)} %get-tuple-element.48.coupling, ...), custom_call_target="tpu_custom_call" | custom-call | flops 100000000 | bytes 1000000 | tf_op jit(solution)/shard_map/pallas_call | solution.py:169
  7.3 1.1 shard_map.70
  8.4 2.9 %collective-permute-start.2 = (bf16[192,256]{1,0:T(8,128)(2,1)S(1)}, bf16[192,256]{1,0:T(8,128)(2,1)S(1)}, u32[]{:S(2)}, u32[]{:S(2)}) collective-permute-start(bf16[192,256]{1,0:T(8,128)(2,1)S(1)} %get-tuple-element.55), channel_id=1, source_target_pairs={{0,8},{8,0},{16,24},{24,16},{1,9},{9,1},{17,25},{25,17},{2,10},{10... | collective-permute-start | bytes 294920 | tf_op jit(solution)/shard_map/ppermute | solution.py:95
  11.3 1.5 %collective-permute-start.3 = (bf16[192,256]{1,0:T(8,128)(2,1)S(1)}, bf16[192,256]{1,0:T(8,128)(2,1)S(1)}, u32[]{:S(2)}, u32[]{:S(2)}) collective-permute-start(bf16[192,256]{1,0:T(8,128)(2,1)S(1)} %get-tuple-element.56), channel_id=1, source_target_pairs={{0,16},{8,24},{16,0},{24,8},{1,17},{9,25},{17,1},{25,9},{2,18},{10... | collective-permute-start | bytes 294920 | tf_op jit(solution)/shard_map/ppermute | solution.py:95
  12.9 1.1 collective-permute-done.2
  13.9 2.0 %collective-permute-done.3 = bf16[192,256]{1,0:T(8,128)(2,1)S(1)} collective-permute-done((bf16[192,256]{1,0:T(8,128)(2,1)S(1)}, bf16[192,256]{1,0:T(8,128)(2,1)S(1)}, u32[]{:S(2)}, u32[]{:S(2)}) %collective-permute-start.3) | collective-permute-done | bytes 98336 | tf_op jit(solution)/shard_map/ppermute | solution.py:95
  15.9 2.7 %collective-permute-done.4 = bf16[192,256]{1,0:T(8,128)(2,1)S(1)} collective-permute-done((bf16[192,256]{1,0:T(8,128)(2,1)S(1)}, bf16[192,256]{1,0:T(8,128)(2,1)S(1)}, u32[]{:S(2)}, u32[]{:S(2)}) %collective-permute-start.4) | collective-permute-done | bytes 98336 | tf_op jit(solution)/shard_map/ppermute | solution.py:95
  19.6 1.9 %collective-permute-start.6 = (bf16[192,256]{1,0:T(8,128)(2,1)S(1)}, bf16[192,256]{1,0:T(8,128)(2,1)S(1)}, u32[]{:S(2)}, u32[]{:S(2)}) collective-permute-start(bf16[192,256]{1,0:T(8,128)(2,1)S(1)} %get-tuple-element.63.refs_0_), channel_id=1, source_target_pairs={{0,16},{8,24},{16,0},{24,8},{1,17},{9,25},{17,1},{25,9},{2,18},{10... | collective-permute-start | bytes 294920 | tf_op jit(solution)/shard_map/ppermute | solution.py:95
  22.2 1.3 %collective-permute-start.8 = (bf16[192,256]{1,0:T(8,128)(2,1)S(1)}, bf16[192,256]{1,0:T(8,128)(2,1)S(1)}, u32[]{:S(2)}, u32[]{:S(2)}) collective-permute-start(bf16[192,256]{1,0:T(8,128)(2,1)S(1)} %get-tuple-element.60), channel_id=1, source_target_pairs={{0,8},{8,0},{16,24},{24,16},{1,9},{9,1},{17,25},{25,17},{2,10},{10... | collective-permute-start | bytes 294920 | tf_op jit(solution)/shard_map/ppermute | solution.py:95
  23.7 1.7 %collective-permute-done.7.refs_3_ = bf16[192,256]{1,0:T(8,128)(2,1)S(1)} collective-permute-done((bf16[192,256]{1,0:T(8,128)(2,1)S(1)}, bf16[192,256]{1,0:T(8,128)(2,1)S(1)}, u32[]{:S(2)}, u32[]{:S(2)}) %collective-permute-start.7) | collective-permute-done | bytes 98336 | tf_op jit(solution)/shard_map/ppermute | solution.py:95
  27.6 1.2 %collective-permute-done.14 = f32[64,256]{1,0:T(8,128)S(1)} collective-permute-done((f32[64,256]{1,0:T(8,128)S(1)}, f32[64,256]{1,0:T(8,128)S(1)}, u32[]{:S(2)}, u32[]{:S(2)}) %collective-permute-start.14) | collective-permute-done | bytes 65568 | tf_op jit(solution)/shard_map/ppermute | solution.py:100
  28.9 3.9 %collective-permute-start.17 = (f32[64,256]{1,0:T(8,128)S(1)}, f32[64,256]{1,0:T(8,128)S(1)}, u32[]{:S(2)}, u32[]{:S(2)}) collective-permute-start(f32[64,256]{1,0:T(8,128)S(1)} %add.81), channel_id=1, source_target_pairs={{0,6},{1,7},{2,4},{3,5},{4,2},{5,3},{6,0},{7,1},{8,14},{9,15},{10,... | collective-permute-start | bytes 196616 | tf_op jit(solution)/shard_map/ppermute | solution.py:126
  34.0 1.5 %collective-permute-start.13 = (bf16[192,256]{1,0:T(8,128)(2,1)S(1)}, bf16[192,256]{1,0:T(8,128)(2,1)S(1)}, u32[]{:S(2)}, u32[]{:S(2)}) collective-permute-start(bf16[192,256]{1,0:T(8,128)(2,1)S(1)} %subtract_convert_fusion.1.refs_0_), channel_id=1, source_target_pairs={{0,24},{8,16},{16,8},{24,0},{1,25},{9,17},{17,9},{25,1},{2,26},{10... | collective-permute-start | bytes 294920 | tf_op jit(solution)/shard_map/ppermute | solution.py:95
  35.5 1.1 collective-permute-start.12
  37.6 1.9 %collective-permute-done.16 = f32[64,256]{1,0:T(8,128)S(1)} collective-permute-done((f32[64,256]{1,0:T(8,128)S(1)}, f32[64,256]{1,0:T(8,128)S(1)}, u32[]{:S(2)}, u32[]{:S(2)}) %collective-permute-start.16) | collective-permute-done | bytes 65568 | tf_op jit(solution)/shard_map/ppermute | solution.py:126
  39.5 1.8 %collective-permute-start.20 = (f32[64,256]{1,0:T(8,128)S(1)}, f32[64,256]{1,0:T(8,128)S(1)}, u32[]{:S(2)}, u32[]{:S(2)}) collective-permute-start(f32[64,256]{1,0:T(8,128)S(1)} %add_add_fusion.5.refs_0_), channel_id=1, source_target_pairs={{0,24},{8,16},{16,8},{24,0},{1,25},{9,17},{17,9},{25,1},{2,26},{10... | collective-permute-start | bytes 196616 | tf_op jit(solution)/shard_map/ppermute | solution.py:95
  41.3 1.2 %collective-permute-start.19 = (f32[64,256]{1,0:T(8,128)S(1)}, f32[64,256]{1,0:T(8,128)S(1)}, u32[]{:S(2)}, u32[]{:S(2)}) collective-permute-start(f32[64,256]{1,0:T(8,128)S(1)} %add_add_fusion.5.refs_0_), channel_id=1, source_target_pairs={{0,16},{8,24},{16,0},{24,8},{1,17},{9,25},{17,1},{25,9},{2,18},{10... | collective-permute-start | bytes 196616 | tf_op jit(solution)/shard_map/ppermute | solution.py:95
  46.8 4.8 %shard_map.73 = (f32[128,128]{1,0:T(8,128)S(1)}, f32[128,128]{1,0:T(8,128)S(1)}, f32[128,128]{1,0:T(8,128)S(1)}, f32[1,256]{1,0:T(1,128)S(1)}) custom-call(f32[64,256]{1,0:T(8,128)S(1)} %add_add_fusion.5.refs_0_, f32[64,256]{1,0:T(8,128)S(1)} %collective-permute-done.18.refs_1_, f32[64,256]{1,0:T(8,128)S(1)} %collective-permute-done.19.refs_2_, ...), custom_call_target="tpu_custom_call" | custom-call | flops 6000000000 | bytes 262144 | tf_op jit(solution)/shard_map/pallas_call | solution.py:82
  51.6 4.1 %shard_map.74.factor.refs_4_ = f32[256,256]{1,0:T(8,128)S(1)} custom-call(f32[128,128]{1,0:T(8,128)S(1)} %get-tuple-element.65.top, f32[128,128]{1,0:T(8,128)S(1)} %get-tuple-element.66.corner, f32[128,128]{1,0:T(8,128)S(1)} %get-tuple-element.67.rest, f32[1,256]{1,0:T(1,128)S(1)} %get-tuple-element.68.across), custom_call_target="tpu_custom_call" | custom-call | flops 6000000000 | bytes 197632 | tf_op jit(solution)/shard_map/pallas_call | solution.py:82
  55.8 3.9 %shard_map.76 = (f32[192,256]{1,0:T(8,128)S(1)}, bf16[192,256]{1,0:T(8,128)(2,1)S(1)}, bf16[192,256]{1,0:T(8,128)(2,1)S(1)}, bf16[192,256]{1,0:T(8,128)(2,1)S(1)}) custom-call(f32[1,2]{1,0:T(1,128)S(1)} %get-tuple-element.50.weights, bf16[768,256]{1,0:T(8,128)(2,1)S(1)} %get-tuple-element.58.field, bf16[768,256]{1,0:T(8,128)(2,1)S(1)} %shard_map.72.low, ...), custom_call_target="tpu_custom_call" | custom-call | flops 100000000 | bytes 3997704 | tf_op jit(solution)/shard_map/pallas_call | solution.py:82
  60.3 1.2 collective-permute-start.24
  61.5 1.7 %collective-permute-start.25 = (bf16[192,256]{1,0:T(8,128)(2,1)S(1)}, bf16[192,256]{1,0:T(8,128)(2,1)S(1)}, u32[]{:S(2)}, u32[]{:S(2)}) collective-permute-start(bf16[192,256]{1,0:T(8,128)(2,1)S(1)} %get-tuple-element.74), channel_id=1, source_target_pairs={{0,24},{8,16},{16,8},{24,0},{1,25},{9,17},{17,9},{25,1},{2,26},{10... | collective-permute-start | bytes 294920 | tf_op jit(solution)/shard_map/ppermute | solution.py:95
  63.2 1.3 %collective-permute-start.32 = (bf16[128,256]{1,0:T(8,128)(2,1)S(1)}, bf16[128,256]{1,0:T(8,128)(2,1)S(1)}, u32[]{:S(2)}, u32[]{:S(2)}) collective-permute-start(bf16[128,256]{1,0:T(8,128)(2,1)S(1)} %get-tuple-element.79), channel_id=1, source_target_pairs={{1,0},{2,1},{3,2},{4,3},{5,4},{6,5},{7,6},{9,8},{10,9},{11,10},{12... | collective-permute-start | bytes 196616 | tf_op jit(solution)/shard_map/ppermute | solution.py:485
  65.9 2.2 %collective-permute-done.25 = bf16[192,256]{1,0:T(8,128)(2,1)S(1)} collective-permute-done((bf16[192,256]{1,0:T(8,128)(2,1)S(1)}, bf16[192,256]{1,0:T(8,128)(2,1)S(1)}, u32[]{:S(2)}, u32[]{:S(2)}) %collective-permute-start.25) | collective-permute-done | bytes 98336 | tf_op jit(solution)/shard_map/ppermute | solution.py:95
  68.2 1.3 %collective-permute-start.28 = (bf16[192,256]{1,0:T(8,128)(2,1)S(1)}, bf16[192,256]{1,0:T(8,128)(2,1)S(1)}, u32[]{:S(2)}, u32[]{:S(2)}) collective-permute-start(bf16[192,256]{1,0:T(8,128)(2,1)S(1)} %get-tuple-element.77.refs_0_), channel_id=1, source_target_pairs={{0,24},{8,16},{16,8},{24,0},{1,25},{9,17},{17,9},{25,1},{2,26},{10... | collective-permute-start | bytes 294920 | tf_op jit(solution)/shard_map/ppermute | solution.py:95
  70.4 1.3 %collective-permute-start.26 = (bf16[192,256]{1,0:T(8,128)(2,1)S(1)}, bf16[192,256]{1,0:T(8,128)(2,1)S(1)}, u32[]{:S(2)}, u32[]{:S(2)}) collective-permute-start(bf16[192,256]{1,0:T(8,128)(2,1)S(1)} %get-tuple-element.77.refs_0_), channel_id=1, source_target_pairs={{0,8},{8,0},{16,24},{24,16},{1,9},{9,1},{17,25},{25,17},{2,10},{10... | collective-permute-start | bytes 294920 | tf_op jit(solution)/shard_map/ppermute | solution.py:95
  71.7 1.3 %collective-permute-start.31 = (bf16[192,256]{1,0:T(8,128)(2,1)S(1)}, bf16[192,256]{1,0:T(8,128)(2,1)S(1)}, u32[]{:S(2)}, u32[]{:S(2)}) collective-permute-start(bf16[192,256]{1,0:T(8,128)(2,1)S(1)} %subtract_convert_fusion.refs_0_), channel_id=1, source_target_pairs={{0,24},{8,16},{16,8},{24,0},{1,25},{9,17},{17,9},{25,1},{2,26},{10... | collective-permute-start | bytes 294920 | tf_op jit(solution)/shard_map/ppermute | solution.py:95
  73.0 1.8 %collective-permute-done.28.refs_3_ = bf16[192,256]{1,0:T(8,128)(2,1)S(1)} collective-permute-done((bf16[192,256]{1,0:T(8,128)(2,1)S(1)}, bf16[192,256]{1,0:T(8,128)(2,1)S(1)}, u32[]{:S(2)}, u32[]{:S(2)}) %collective-permute-start.28) | collective-permute-done | bytes 98336 | tf_op jit(solution)/shard_map/ppermute | solution.py:95
  75.2 1.2 collective-permute-done.26.refs_1_
  76.9 1.2 shard_map.79
  78.6 1.1 collective-permute-start.30
  80.5 2.6 %collective-permute-start.41 = (f32[64,256]{1,0:T(8,128)S(1)}, f32[64,256]{1,0:T(8,128)S(1)}, u32[]{:S(2)}, u32[]{:S(2)}) collective-permute-start(f32[64,256]{1,0:T(8,128)S(1)} %add.92), channel_id=1, source_target_pairs={{0,6},{1,7},{2,4},{3,5},{4,2},{5,3},{6,0},{7,1},{8,14},{9,15},{10,... | collective-permute-start | bytes 196616 | tf_op jit(solution)/shard_map/ppermute | solution.py:126
  83.1 2.0 %collective-permute-start.40 = (f32[64,256]{1,0:T(8,128)S(1)}, f32[64,256]{1,0:T(8,128)S(1)}, u32[]{:S(2)}, u32[]{:S(2)}) collective-permute-start(f32[64,256]{1,0:T(8,128)S(1)} %add.92), channel_id=1, source_target_pairs={{0,4},{1,5},{2,6},{3,7},{4,0},{5,1},{6,2},{7,3},{8,12},{9,13},{10,... | collective-permute-start | bytes 196616 | tf_op jit(solution)/shard_map/ppermute | solution.py:126
  85.1 2.5 %collective-permute-start.36 = (f32[64,256]{1,0:T(8,128)S(1)}, f32[64,256]{1,0:T(8,128)S(1)}, u32[]{:S(2)}, u32[]{:S(2)}) collective-permute-start(f32[64,256]{1,0:T(8,128)S(1)} %add.88), channel_id=1, source_target_pairs={{0,6},{1,7},{2,4},{3,5},{4,2},{5,3},{6,0},{7,1},{8,14},{9,15},{10,... | collective-permute-start | bytes 196616 | tf_op jit(solution)/shard_map/ppermute | solution.py:126
  88.7 3.1 %collective-permute-start.34 = (f32[64,256]{1,0:T(8,128)S(1)}, f32[64,256]{1,0:T(8,128)S(1)}, u32[]{:S(2)}, u32[]{:S(2)}) collective-permute-start(f32[64,256]{1,0:T(8,128)S(1)} %add.88), channel_id=1, source_target_pairs={{0,2},{1,3},{2,0},{3,1},{4,6},{5,7},{6,4},{7,5},{8,10},{9,11},{10,... | collective-permute-start | bytes 196616 | tf_op jit(solution)/shard_map/ppermute | solution.py:126
  91.8 2.0 %collective-permute-done.40 = f32[64,256]{1,0:T(8,128)S(1)} collective-permute-done((f32[64,256]{1,0:T(8,128)S(1)}, f32[64,256]{1,0:T(8,128)S(1)}, u32[]{:S(2)}, u32[]{:S(2)}) %collective-permute-start.40) | collective-permute-done | bytes 65568 | tf_op jit(solution)/shard_map/ppermute | solution.py:126
  93.8 1.5 %collective-permute-start.38 = (bf16[128,256]{1,0:T(8,128)(2,1)S(1)}, bf16[128,256]{1,0:T(8,128)(2,1)S(1)}, u32[]{:S(2)}, u32[]{:S(2)}) collective-permute-start(bf16[128,256]{1,0:T(8,128)(2,1)S(1)} %get-tuple-element.84), channel_id=1, source_target_pairs={{1,0},{2,1},{3,2},{4,3},{5,4},{6,5},{7,6},{9,8},{10,9},{11,10},{12... | collective-permute-start | bytes 196616 | tf_op jit(solution)/shard_map/ppermute | solution.py:485
  95.4 1.7 %collective-permute-start.45 = (f32[64,256]{1,0:T(8,128)S(1)}, f32[64,256]{1,0:T(8,128)S(1)}, u32[]{:S(2)}, u32[]{:S(2)}) collective-permute-start(f32[64,256]{1,0:T(8,128)S(1)} %add_add_fusion.3.refs_0_), channel_id=1, source_target_pairs={{0,24},{8,16},{16,8},{24,0},{1,25},{9,17},{17,9},{25,1},{2,26},{10... | collective-permute-start | bytes 196616 | tf_op jit(solution)/shard_map/ppermute | solution.py:95
  97.6 1.2 shard_map.80
  98.9 1.6 %collective-permute-start.43 = (f32[64,256]{1,0:T(8,128)S(1)}, f32[64,256]{1,0:T(8,128)S(1)}, u32[]{:S(2)}, u32[]{:S(2)}) collective-permute-start(f32[64,256]{1,0:T(8,128)S(1)} %add_add_fusion.3.refs_0_), channel_id=1, source_target_pairs={{0,8},{8,0},{16,24},{24,16},{1,9},{9,1},{17,25},{25,17},{2,10},{10... | collective-permute-start | bytes 196616 | tf_op jit(solution)/shard_map/ppermute | solution.py:95
  100.5 1.2 collective-permute-done.42
  103.5 2.6 %collective-permute-start.48 = (f32[64,256]{1,0:T(8,128)S(1)}, f32[64,256]{1,0:T(8,128)S(1)}, u32[]{:S(2)}, u32[]{:S(2)}) collective-permute-start(f32[64,256]{1,0:T(8,128)S(1)} %add.96), channel_id=1, source_target_pairs={{0,6},{1,7},{2,4},{3,5},{4,2},{5,3},{6,0},{7,1},{8,14},{9,15},{10,... | collective-permute-start | bytes 196616 | tf_op jit(solution)/shard_map/ppermute | solution.py:126
  106.1 1.8 %collective-permute-start.46 = (f32[64,256]{1,0:T(8,128)S(1)}, f32[64,256]{1,0:T(8,128)S(1)}, u32[]{:S(2)}, u32[]{:S(2)}) collective-permute-start(f32[64,256]{1,0:T(8,128)S(1)} %add.96), channel_id=1, source_target_pairs={{0,2},{1,3},{2,0},{3,1},{4,6},{5,7},{6,4},{7,5},{8,10},{9,11},{10,... | collective-permute-start | bytes 196616 | tf_op jit(solution)/shard_map/ppermute | solution.py:126
  107.8 4.8 %shard_map.81 = (f32[128,128]{1,0:T(8,128)S(1)}, f32[128,128]{1,0:T(8,128)S(1)}, f32[128,128]{1,0:T(8,128)S(1)}, f32[1,256]{1,0:T(1,128)S(1)}) custom-call(f32[64,256]{1,0:T(8,128)S(1)} %add_add_fusion.3.refs_0_, f32[64,256]{1,0:T(8,128)S(1)} %collective-permute-done.43.refs_1_, f32[64,256]{1,0:T(8,128)S(1)} %collective-permute-done.44.refs_2_, ...), custom_call_target="tpu_custom_call" | custom-call | flops 6000000000 | bytes 262144 | tf_op jit(solution)/shard_map/pallas_call | solution.py:82
  112.7 2.0 %collective-permute-start.51 = (f32[128,256]{1,0:T(8,128)S(1)}, f32[128,256]{1,0:T(8,128)S(1)}, u32[]{:S(2)}, u32[]{:S(2)}) collective-permute-start(f32[128,256]{1,0:T(8,128)S(1)} %pad_maximum_fusion.refs_0_), channel_id=1, source_target_pairs={{0,24},{8,16},{16,8},{24,0},{1,25},{9,17},{17,9},{25,1},{2,26},{10... | collective-permute-start | bytes 393224 | tf_op jit(solution)/shard_map/ppermute | solution.py:95
  116.3 4.1 %shard_map.82.refs_5_ = f32[256,256]{1,0:T(8,128)S(1)} custom-call(f32[128,128]{1,0:T(8,128)S(1)} %get-tuple-element.87.top, f32[128,128]{1,0:T(8,128)S(1)} %get-tuple-element.88.corner, f32[128,128]{1,0:T(8,128)S(1)} %get-tuple-element.89.rest, f32[1,256]{1,0:T(1,128)S(1)} %get-tuple-element.90.across), custom_call_target="tpu_custom_call" | custom-call | flops 6000000000 | bytes 197632 | tf_op jit(solution)/shard_map/pallas_call | solution.py:82
  121.2 2.0 %finish.1 = (f32[768,256]{1,0:T(8,128)}, f32[2,256,256]{2,1,0:T(8,128)}) custom-call(bf16[768,256]{1,0:T(8,128)(2,1)S(1)} %get-tuple-element.75.field, bf16[768,256]{1,0:T(8,128)(2,1)S(1)} %shard_map.78.low, f32[128,256]{1,0:T(8,128)S(1)} %pad_maximum_fusion.refs_0_, f32[128,256]{1,0:T(8,128)S(1)} %collective-permute-done.49.refs_1_, ...), custom_call_target="tpu_custom_call" | custom-call | flops 1000000000 | bytes 1000000 | tf_op jit(solution)/shard_map/finish/pallas_call | solution.py:555
  (89 shorter events, 23.2 us)
Async XLA Ops:
  3.2 4.1 %collective-permute-start.1 = (bf16[128,512]{1,0:T(8,128)(2,1)S(1)}, bf16[128,512]{1,0:T(8,128)(2,1)S(1)}, u32[]{:S(2)}, u32[]{:S(2)}) collective-permute-start(bf16[128,512]{1,0:T(8,128)(2,1)S(1)} %get-tuple-element.52), channel_id=1, source_target_pairs={{1,2},{3,4},{5,6},{2,1},{4,3},{6,5},{9,10},{11,12},{13,14},{10,9},... | collective-permute-start | bytes 393224 | tf_op jit(solution)/shard_map/ppermute | solution.py:106
  8.4 5.5 %collective-permute-start.2 = (bf16[192,256]{1,0:T(8,128)(2,1)S(1)}, bf16[192,256]{1,0:T(8,128)(2,1)S(1)}, u32[]{:S(2)}, u32[]{:S(2)}) collective-permute-start(bf16[192,256]{1,0:T(8,128)(2,1)S(1)} %get-tuple-element.55), channel_id=1, source_target_pairs={{0,8},{8,0},{16,24},{24,16},{1,9},{9,1},{17,25},{25,17},{2,10},{10... | collective-permute-start | bytes 294920 | tf_op jit(solution)/shard_map/ppermute | solution.py:95
  11.3 4.6 %collective-permute-start.3 = (bf16[192,256]{1,0:T(8,128)(2,1)S(1)}, bf16[192,256]{1,0:T(8,128)(2,1)S(1)}, u32[]{:S(2)}, u32[]{:S(2)}) collective-permute-start(bf16[192,256]{1,0:T(8,128)(2,1)S(1)} %get-tuple-element.56), channel_id=1, source_target_pairs={{0,16},{8,24},{16,0},{24,8},{1,17},{9,25},{17,1},{25,9},{2,18},{10... | collective-permute-start | bytes 294920 | tf_op jit(solution)/shard_map/ppermute | solution.py:95
  12.8 5.8 %collective-permute-start.4 = (bf16[192,256]{1,0:T(8,128)(2,1)S(1)}, bf16[192,256]{1,0:T(8,128)(2,1)S(1)}, u32[]{:S(2)}, u32[]{:S(2)}) collective-permute-start(bf16[192,256]{1,0:T(8,128)(2,1)S(1)} %get-tuple-element.57), channel_id=1, source_target_pairs={{0,24},{8,16},{16,8},{24,0},{1,25},{9,17},{17,9},{25,1},{2,26},{10... | collective-permute-start | bytes 294920 | tf_op jit(solution)/shard_map/ppermute | solution.py:95
  18.7 6.7 %collective-permute-start.7 = (bf16[192,256]{1,0:T(8,128)(2,1)S(1)}, bf16[192,256]{1,0:T(8,128)(2,1)S(1)}, u32[]{:S(2)}, u32[]{:S(2)}) collective-permute-start(bf16[192,256]{1,0:T(8,128)(2,1)S(1)} %get-tuple-element.63.refs_0_), channel_id=1, source_target_pairs={{0,24},{8,16},{16,8},{24,0},{1,25},{9,17},{17,9},{25,1},{2,26},{10... | collective-permute-start | bytes 294920 | tf_op jit(solution)/shard_map/ppermute | solution.py:95
  19.6 7.5 %collective-permute-start.6 = (bf16[192,256]{1,0:T(8,128)(2,1)S(1)}, bf16[192,256]{1,0:T(8,128)(2,1)S(1)}, u32[]{:S(2)}, u32[]{:S(2)}) collective-permute-start(bf16[192,256]{1,0:T(8,128)(2,1)S(1)} %get-tuple-element.63.refs_0_), channel_id=1, source_target_pairs={{0,16},{8,24},{16,0},{24,8},{1,17},{9,25},{17,1},{25,9},{2,18},{10... | collective-permute-start | bytes 294920 | tf_op jit(solution)/shard_map/ppermute | solution.py:95
  21.5 5.7 %collective-permute-start.5 = (bf16[192,256]{1,0:T(8,128)(2,1)S(1)}, bf16[192,256]{1,0:T(8,128)(2,1)S(1)}, u32[]{:S(2)}, u32[]{:S(2)}) collective-permute-start(bf16[192,256]{1,0:T(8,128)(2,1)S(1)} %get-tuple-element.63.refs_0_), channel_id=1, source_target_pairs={{0,8},{8,0},{16,24},{24,16},{1,9},{9,1},{17,25},{25,17},{2,10},{10... | collective-permute-start | bytes 294920 | tf_op jit(solution)/shard_map/ppermute | solution.py:95
  22.2 11.6 %collective-permute-start.8 = (bf16[192,256]{1,0:T(8,128)(2,1)S(1)}, bf16[192,256]{1,0:T(8,128)(2,1)S(1)}, u32[]{:S(2)}, u32[]{:S(2)}) collective-permute-start(bf16[192,256]{1,0:T(8,128)(2,1)S(1)} %get-tuple-element.60), channel_id=1, source_target_pairs={{0,8},{8,0},{16,24},{24,16},{1,9},{9,1},{17,25},{25,17},{2,10},{10... | collective-permute-start | bytes 294920 | tf_op jit(solution)/shard_map/ppermute | solution.py:95
  23.5 10.4 %collective-permute-start.9 = (bf16[192,256]{1,0:T(8,128)(2,1)S(1)}, bf16[192,256]{1,0:T(8,128)(2,1)S(1)}, u32[]{:S(2)}, u32[]{:S(2)}) collective-permute-start(bf16[192,256]{1,0:T(8,128)(2,1)S(1)} %get-tuple-element.61), channel_id=1, source_target_pairs={{0,16},{8,24},{16,0},{24,8},{1,17},{9,25},{17,1},{25,9},{2,18},{10... | collective-permute-start | bytes 294920 | tf_op jit(solution)/shard_map/ppermute | solution.py:95
  25.4 8.6 %collective-permute-start.10 = (bf16[192,256]{1,0:T(8,128)(2,1)S(1)}, bf16[192,256]{1,0:T(8,128)(2,1)S(1)}, u32[]{:S(2)}, u32[]{:S(2)}) collective-permute-start(bf16[192,256]{1,0:T(8,128)(2,1)S(1)} %get-tuple-element.62), channel_id=1, source_target_pairs={{0,24},{8,16},{16,8},{24,0},{1,25},{9,17},{17,9},{25,1},{2,26},{10... | collective-permute-start | bytes 294920 | tf_op jit(solution)/shard_map/ppermute | solution.py:95
  28.9 7.7 %collective-permute-start.17 = (f32[64,256]{1,0:T(8,128)S(1)}, f32[64,256]{1,0:T(8,128)S(1)}, u32[]{:S(2)}, u32[]{:S(2)}) collective-permute-start(f32[64,256]{1,0:T(8,128)S(1)} %add.81), channel_id=1, source_target_pairs={{0,6},{1,7},{2,4},{3,5},{4,2},{5,3},{6,0},{7,1},{8,14},{9,15},{10,... | collective-permute-start | bytes 196616 | tf_op jit(solution)/shard_map/ppermute | solution.py:126
  32.8 6.6 %collective-permute-start.16 = (f32[64,256]{1,0:T(8,128)S(1)}, f32[64,256]{1,0:T(8,128)S(1)}, u32[]{:S(2)}, u32[]{:S(2)}) collective-permute-start(f32[64,256]{1,0:T(8,128)S(1)} %add.81), channel_id=1, source_target_pairs={{0,4},{1,5},{2,6},{3,7},{4,0},{5,1},{6,2},{7,3},{8,12},{9,13},{10,... | collective-permute-start | bytes 196616 | tf_op jit(solution)/shard_map/ppermute | solution.py:126
  33.8 5.6 %collective-permute-start.15 = (f32[64,256]{1,0:T(8,128)S(1)}, f32[64,256]{1,0:T(8,128)S(1)}, u32[]{:S(2)}, u32[]{:S(2)}) collective-permute-start(f32[64,256]{1,0:T(8,128)S(1)} %add.81), channel_id=1, source_target_pairs={{0,2},{1,3},{2,0},{3,1},{4,6},{5,7},{6,4},{7,5},{8,10},{9,11},{10,... | collective-permute-start | bytes 196616 | tf_op jit(solution)/shard_map/ppermute | solution.py:126
  34.0 8.5 %collective-permute-start.13 = (bf16[192,256]{1,0:T(8,128)(2,1)S(1)}, bf16[192,256]{1,0:T(8,128)(2,1)S(1)}, u32[]{:S(2)}, u32[]{:S(2)}) collective-permute-start(bf16[192,256]{1,0:T(8,128)(2,1)S(1)} %subtract_convert_fusion.1.refs_0_), channel_id=1, source_target_pairs={{0,24},{8,16},{16,8},{24,0},{1,25},{9,17},{17,9},{25,1},{2,26},{10... | collective-permute-start | bytes 294920 | tf_op jit(solution)/shard_map/ppermute | solution.py:95
  35.5 7.5 %collective-permute-start.12 = (bf16[192,256]{1,0:T(8,128)(2,1)S(1)}, bf16[192,256]{1,0:T(8,128)(2,1)S(1)}, u32[]{:S(2)}, u32[]{:S(2)}) collective-permute-start(bf16[192,256]{1,0:T(8,128)(2,1)S(1)} %subtract_convert_fusion.1.refs_0_), channel_id=1, source_target_pairs={{0,16},{8,24},{16,0},{24,8},{1,17},{9,25},{17,1},{25,9},{2,18},{10... | collective-permute-start | bytes 294920 | tf_op jit(solution)/shard_map/ppermute | solution.py:95
  36.6 6.5 %collective-permute-start.11 = (bf16[192,256]{1,0:T(8,128)(2,1)S(1)}, bf16[192,256]{1,0:T(8,128)(2,1)S(1)}, u32[]{:S(2)}, u32[]{:S(2)}) collective-permute-start(bf16[192,256]{1,0:T(8,128)(2,1)S(1)} %subtract_convert_fusion.1.refs_0_), channel_id=1, source_target_pairs={{0,8},{8,0},{16,24},{24,16},{1,9},{9,1},{17,25},{25,17},{2,10},{10... | collective-permute-start | bytes 294920 | tf_op jit(solution)/shard_map/ppermute | solution.py:95
  39.5 5.5 %collective-permute-start.20 = (f32[64,256]{1,0:T(8,128)S(1)}, f32[64,256]{1,0:T(8,128)S(1)}, u32[]{:S(2)}, u32[]{:S(2)}) collective-permute-start(f32[64,256]{1,0:T(8,128)S(1)} %add_add_fusion.5.refs_0_), channel_id=1, source_target_pairs={{0,24},{8,16},{16,8},{24,0},{1,25},{9,17},{17,9},{25,1},{2,26},{10... | collective-permute-start | bytes 196616 | tf_op jit(solution)/shard_map/ppermute | solution.py:95
  41.3 4.5 %collective-permute-start.19 = (f32[64,256]{1,0:T(8,128)S(1)}, f32[64,256]{1,0:T(8,128)S(1)}, u32[]{:S(2)}, u32[]{:S(2)}) collective-permute-start(f32[64,256]{1,0:T(8,128)S(1)} %add_add_fusion.5.refs_0_), channel_id=1, source_target_pairs={{0,16},{8,24},{16,0},{24,8},{1,17},{9,25},{17,1},{25,9},{2,18},{10... | collective-permute-start | bytes 196616 | tf_op jit(solution)/shard_map/ppermute | solution.py:95
  42.5 4.3 %collective-permute-start.18 = (f32[64,256]{1,0:T(8,128)S(1)}, f32[64,256]{1,0:T(8,128)S(1)}, u32[]{:S(2)}, u32[]{:S(2)}) collective-permute-start(f32[64,256]{1,0:T(8,128)S(1)} %add_add_fusion.5.refs_0_), channel_id=1, source_target_pairs={{0,8},{8,0},{16,24},{24,16},{1,9},{9,1},{17,25},{25,17},{2,10},{10... | collective-permute-start | bytes 196616 | tf_op jit(solution)/shard_map/ppermute | solution.py:95
  44.0 11.8 %collective-permute-start.21 = (f32[128,512]{1,0:T(8,128)S(1)}, f32[128,512]{1,0:T(8,128)S(1)}, u32[]{:S(2)}, u32[]{:S(2)}) collective-permute-start(f32[128,512]{1,0:T(8,128)S(1)} %get-tuple-element.69), channel_id=1, source_target_pairs={{0,1},{1,0},{2,3},{3,2},{4,5},{5,4},{6,7},{7,6},{8,9},{9,8},{10,11... | collective-permute-start | bytes 786440 | tf_op jit(solution)/shard_map/ppermute | solution.py:100
  44.1 11.7 %collective-permute-start.22 = (f32[128,512]{1,0:T(8,128)S(1)}, f32[128,512]{1,0:T(8,128)S(1)}, u32[]{:S(2)}, u32[]{:S(2)}) collective-permute-start(f32[128,512]{1,0:T(8,128)S(1)} %get-tuple-element.70), channel_id=1, source_target_pairs={{1,2},{3,4},{5,6},{2,1},{4,3},{6,5},{9,10},{11,12},{13,14},{10,9},... | collective-permute-start | bytes 786440 | tf_op jit(solution)/shard_map/ppermute | solution.py:106
  59.7 5.3 %collective-permute-start.23 = (bf16[192,256]{1,0:T(8,128)(2,1)S(1)}, bf16[192,256]{1,0:T(8,128)(2,1)S(1)}, u32[]{:S(2)}, u32[]{:S(2)}) collective-permute-start(bf16[192,256]{1,0:T(8,128)(2,1)S(1)} %get-tuple-element.72), channel_id=1, source_target_pairs={{0,8},{8,0},{16,24},{24,16},{1,9},{9,1},{17,25},{25,17},{2,10},{10... | collective-permute-start | bytes 294920 | tf_op jit(solution)/shard_map/ppermute | solution.py:95
  60.3 5.5 %collective-permute-start.24 = (bf16[192,256]{1,0:T(8,128)(2,1)S(1)}, bf16[192,256]{1,0:T(8,128)(2,1)S(1)}, u32[]{:S(2)}, u32[]{:S(2)}) collective-permute-start(bf16[192,256]{1,0:T(8,128)(2,1)S(1)} %get-tuple-element.73), channel_id=1, source_target_pairs={{0,16},{8,24},{16,0},{24,8},{1,17},{9,25},{17,1},{25,9},{2,18},{10... | collective-permute-start | bytes 294920 | tf_op jit(solution)/shard_map/ppermute | solution.py:95
  61.5 6.6 %collective-permute-start.25 = (bf16[192,256]{1,0:T(8,128)(2,1)S(1)}, bf16[192,256]{1,0:T(8,128)(2,1)S(1)}, u32[]{:S(2)}, u32[]{:S(2)}) collective-permute-start(bf16[192,256]{1,0:T(8,128)(2,1)S(1)} %get-tuple-element.74), channel_id=1, source_target_pairs={{0,24},{8,16},{16,8},{24,0},{1,25},{9,17},{17,9},{25,1},{2,26},{10... | collective-permute-start | bytes 294920 | tf_op jit(solution)/shard_map/ppermute | solution.py:95
  63.2 9.8 %collective-permute-start.32 = (bf16[128,256]{1,0:T(8,128)(2,1)S(1)}, bf16[128,256]{1,0:T(8,128)(2,1)S(1)}, u32[]{:S(2)}, u32[]{:S(2)}) collective-permute-start(bf16[128,256]{1,0:T(8,128)(2,1)S(1)} %get-tuple-element.79), channel_id=1, source_target_pairs={{1,0},{2,1},{3,2},{4,3},{5,4},{6,5},{7,6},{9,8},{10,9},{11,10},{12... | collective-permute-start | bytes 196616 | tf_op jit(solution)/shard_map/ppermute | solution.py:485
  68.2 6.7 %collective-permute-start.28 = (bf16[192,256]{1,0:T(8,128)(2,1)S(1)}, bf16[192,256]{1,0:T(8,128)(2,1)S(1)}, u32[]{:S(2)}, u32[]{:S(2)}) collective-permute-start(bf16[192,256]{1,0:T(8,128)(2,1)S(1)} %get-tuple-element.77.refs_0_), channel_id=1, source_target_pairs={{0,24},{8,16},{16,8},{24,0},{1,25},{9,17},{17,9},{25,1},{2,26},{10... | collective-permute-start | bytes 294920 | tf_op jit(solution)/shard_map/ppermute | solution.py:95
  69.4 5.8 %collective-permute-start.27 = (bf16[192,256]{1,0:T(8,128)(2,1)S(1)}, bf16[192,256]{1,0:T(8,128)(2,1)S(1)}, u32[]{:S(2)}, u32[]{:S(2)}) collective-permute-start(bf16[192,256]{1,0:T(8,128)(2,1)S(1)} %get-tuple-element.77.refs_0_), channel_id=1, source_target_pairs={{0,16},{8,24},{16,0},{24,8},{1,17},{9,25},{17,1},{25,9},{2,18},{10... | collective-permute-start | bytes 294920 | tf_op jit(solution)/shard_map/ppermute | solution.py:95
  70.4 6.0 %collective-permute-start.26 = (bf16[192,256]{1,0:T(8,128)(2,1)S(1)}, bf16[192,256]{1,0:T(8,128)(2,1)S(1)}, u32[]{:S(2)}, u32[]{:S(2)}) collective-permute-start(bf16[192,256]{1,0:T(8,128)(2,1)S(1)} %get-tuple-element.77.refs_0_), channel_id=1, source_target_pairs={{0,8},{8,0},{16,24},{24,16},{1,9},{9,1},{17,25},{25,17},{2,10},{10... | collective-permute-start | bytes 294920 | tf_op jit(solution)/shard_map/ppermute | solution.py:95
  71.7 13.3 %collective-permute-start.31 = (bf16[192,256]{1,0:T(8,128)(2,1)S(1)}, bf16[192,256]{1,0:T(8,128)(2,1)S(1)}, u32[]{:S(2)}, u32[]{:S(2)}) collective-permute-start(bf16[192,256]{1,0:T(8,128)(2,1)S(1)} %subtract_convert_fusion.refs_0_), channel_id=1, source_target_pairs={{0,24},{8,16},{16,8},{24,0},{1,25},{9,17},{17,9},{25,1},{2,26},{10... | collective-permute-start | bytes 294920 | tf_op jit(solution)/shard_map/ppermute | solution.py:95
  76.8 3.7 %collective-permute-start.37 = (f32[64,256]{1,0:T(8,128)S(1)}, f32[64,256]{1,0:T(8,128)S(1)}, u32[]{:S(2)}, u32[]{:S(2)}) collective-permute-start(f32[64,256]{1,0:T(8,128)S(1)} %get-tuple-element.83), channel_id=1, source_target_pairs={{0,1},{1,0},{2,3},{3,2},{4,5},{5,4},{6,7},{7,6},{8,9},{9,8},{10,11... | collective-permute-start | bytes 196616 | tf_op jit(solution)/shard_map/ppermute | solution.py:100
  78.1 5.0 %collective-permute-start.33 = (f32[64,256]{1,0:T(8,128)S(1)}, f32[64,256]{1,0:T(8,128)S(1)}, u32[]{:S(2)}, u32[]{:S(2)}) collective-permute-start(f32[64,256]{1,0:T(8,128)S(1)} %shard_map.79), channel_id=1, source_target_pairs={{0,1},{1,0},{2,3},{3,2},{4,5},{5,4},{6,7},{7,6},{8,9},{9,8},{10,11... | collective-permute-start | bytes 196616 | tf_op jit(solution)/shard_map/ppermute | solution.py:100
  78.6 6.4 %collective-permute-start.30 = (bf16[192,256]{1,0:T(8,128)(2,1)S(1)}, bf16[192,256]{1,0:T(8,128)(2,1)S(1)}, u32[]{:S(2)}, u32[]{:S(2)}) collective-permute-start(bf16[192,256]{1,0:T(8,128)(2,1)S(1)} %subtract_convert_fusion.refs_0_), channel_id=1, source_target_pairs={{0,16},{8,24},{16,0},{24,8},{1,17},{9,25},{17,1},{25,9},{2,18},{10... | collective-permute-start | bytes 294920 | tf_op jit(solution)/shard_map/ppermute | solution.py:95
  79.7 7.8 %collective-permute-start.29 = (bf16[192,256]{1,0:T(8,128)(2,1)S(1)}, bf16[192,256]{1,0:T(8,128)(2,1)S(1)}, u32[]{:S(2)}, u32[]{:S(2)}) collective-permute-start(bf16[192,256]{1,0:T(8,128)(2,1)S(1)} %subtract_convert_fusion.refs_0_), channel_id=1, source_target_pairs={{0,8},{8,0},{16,24},{24,16},{1,9},{9,1},{17,25},{25,17},{2,10},{10... | collective-permute-start | bytes 294920 | tf_op jit(solution)/shard_map/ppermute | solution.py:95
  80.5 8.2 %collective-permute-start.41 = (f32[64,256]{1,0:T(8,128)S(1)}, f32[64,256]{1,0:T(8,128)S(1)}, u32[]{:S(2)}, u32[]{:S(2)}) collective-permute-start(f32[64,256]{1,0:T(8,128)S(1)} %add.92), channel_id=1, source_target_pairs={{0,6},{1,7},{2,4},{3,5},{4,2},{5,3},{6,0},{7,1},{8,14},{9,15},{10,... | collective-permute-start | bytes 196616 | tf_op jit(solution)/shard_map/ppermute | solution.py:126
  83.1 10.7 %collective-permute-start.40 = (f32[64,256]{1,0:T(8,128)S(1)}, f32[64,256]{1,0:T(8,128)S(1)}, u32[]{:S(2)}, u32[]{:S(2)}) collective-permute-start(f32[64,256]{1,0:T(8,128)S(1)} %add.92), channel_id=1, source_target_pairs={{0,4},{1,5},{2,6},{3,7},{4,0},{5,1},{6,2},{7,3},{8,12},{9,13},{10,... | collective-permute-start | bytes 196616 | tf_op jit(solution)/shard_map/ppermute | solution.py:126
  85.1 10.3 %collective-permute-start.39 = (f32[64,256]{1,0:T(8,128)S(1)}, f32[64,256]{1,0:T(8,128)S(1)}, u32[]{:S(2)}, u32[]{:S(2)}) collective-permute-start(f32[64,256]{1,0:T(8,128)S(1)} %add.92), channel_id=1, source_target_pairs={{0,2},{1,3},{2,0},{3,1},{4,6},{5,7},{6,4},{7,5},{8,10},{9,11},{10,... | collective-permute-start | bytes 196616 | tf_op jit(solution)/shard_map/ppermute | solution.py:126
  85.1 13.8 %collective-permute-start.36 = (f32[64,256]{1,0:T(8,128)S(1)}, f32[64,256]{1,0:T(8,128)S(1)}, u32[]{:S(2)}, u32[]{:S(2)}) collective-permute-start(f32[64,256]{1,0:T(8,128)S(1)} %add.88), channel_id=1, source_target_pairs={{0,6},{1,7},{2,4},{3,5},{4,2},{5,3},{6,0},{7,1},{8,14},{9,15},{10,... | collective-permute-start | bytes 196616 | tf_op jit(solution)/shard_map/ppermute | solution.py:126
  87.6 12.9 %collective-permute-start.35 = (f32[64,256]{1,0:T(8,128)S(1)}, f32[64,256]{1,0:T(8,128)S(1)}, u32[]{:S(2)}, u32[]{:S(2)}) collective-permute-start(f32[64,256]{1,0:T(8,128)S(1)} %add.88), channel_id=1, source_target_pairs={{0,4},{1,5},{2,6},{3,7},{4,0},{5,1},{6,2},{7,3},{8,12},{9,13},{10,... | collective-permute-start | bytes 196616 | tf_op jit(solution)/shard_map/ppermute | solution.py:126
  88.7 11.8 %collective-permute-start.34 = (f32[64,256]{1,0:T(8,128)S(1)}, f32[64,256]{1,0:T(8,128)S(1)}, u32[]{:S(2)}, u32[]{:S(2)}) collective-permute-start(f32[64,256]{1,0:T(8,128)S(1)} %add.88), channel_id=1, source_target_pairs={{0,2},{1,3},{2,0},{3,1},{4,6},{5,7},{6,4},{7,5},{8,10},{9,11},{10,... | collective-permute-start | bytes 196616 | tf_op jit(solution)/shard_map/ppermute | solution.py:126
  95.4 6.4 %collective-permute-start.45 = (f32[64,256]{1,0:T(8,128)S(1)}, f32[64,256]{1,0:T(8,128)S(1)}, u32[]{:S(2)}, u32[]{:S(2)}) collective-permute-start(f32[64,256]{1,0:T(8,128)S(1)} %add_add_fusion.3.refs_0_), channel_id=1, source_target_pairs={{0,24},{8,16},{16,8},{24,0},{1,25},{9,17},{17,9},{25,1},{2,26},{10... | collective-permute-start | bytes 196616 | tf_op jit(solution)/shard_map/ppermute | solution.py:95
  97.1 5.6 %collective-permute-start.44 = (f32[64,256]{1,0:T(8,128)S(1)}, f32[64,256]{1,0:T(8,128)S(1)}, u32[]{:S(2)}, u32[]{:S(2)}) collective-permute-start(f32[64,256]{1,0:T(8,128)S(1)} %add_add_fusion.3.refs_0_), channel_id=1, source_target_pairs={{0,16},{8,24},{16,0},{24,8},{1,17},{9,25},{17,1},{25,9},{2,18},{10... | collective-permute-start | bytes 196616 | tf_op jit(solution)/shard_map/ppermute | solution.py:95
  98.9 4.6 %collective-permute-start.43 = (f32[64,256]{1,0:T(8,128)S(1)}, f32[64,256]{1,0:T(8,128)S(1)}, u32[]{:S(2)}, u32[]{:S(2)}) collective-permute-start(f32[64,256]{1,0:T(8,128)S(1)} %add_add_fusion.3.refs_0_), channel_id=1, source_target_pairs={{0,8},{8,0},{16,24},{24,16},{1,9},{9,1},{17,25},{25,17},{2,10},{10... | collective-permute-start | bytes 196616 | tf_op jit(solution)/shard_map/ppermute | solution.py:95
  103.5 9.2 %collective-permute-start.48 = (f32[64,256]{1,0:T(8,128)S(1)}, f32[64,256]{1,0:T(8,128)S(1)}, u32[]{:S(2)}, u32[]{:S(2)}) collective-permute-start(f32[64,256]{1,0:T(8,128)S(1)} %add.96), channel_id=1, source_target_pairs={{0,6},{1,7},{2,4},{3,5},{4,2},{5,3},{6,0},{7,1},{8,14},{9,15},{10,... | collective-permute-start | bytes 196616 | tf_op jit(solution)/shard_map/ppermute | solution.py:126
  106.1 6.6 %collective-permute-start.47 = (f32[64,256]{1,0:T(8,128)S(1)}, f32[64,256]{1,0:T(8,128)S(1)}, u32[]{:S(2)}, u32[]{:S(2)}) collective-permute-start(f32[64,256]{1,0:T(8,128)S(1)} %add.96), channel_id=1, source_target_pairs={{0,4},{1,5},{2,6},{3,7},{4,0},{5,1},{6,2},{7,3},{8,12},{9,13},{10,... | collective-permute-start | bytes 196616 | tf_op jit(solution)/shard_map/ppermute | solution.py:126
  106.1 6.6 %collective-permute-start.46 = (f32[64,256]{1,0:T(8,128)S(1)}, f32[64,256]{1,0:T(8,128)S(1)}, u32[]{:S(2)}, u32[]{:S(2)}) collective-permute-start(f32[64,256]{1,0:T(8,128)S(1)} %add.96), channel_id=1, source_target_pairs={{0,2},{1,3},{2,0},{3,1},{4,6},{5,7},{6,4},{7,5},{8,10},{9,11},{10,... | collective-permute-start | bytes 196616 | tf_op jit(solution)/shard_map/ppermute | solution.py:126
  112.7 7.7 %collective-permute-start.51 = (f32[128,256]{1,0:T(8,128)S(1)}, f32[128,256]{1,0:T(8,128)S(1)}, u32[]{:S(2)}, u32[]{:S(2)}) collective-permute-start(f32[128,256]{1,0:T(8,128)S(1)} %pad_maximum_fusion.refs_0_), channel_id=1, source_target_pairs={{0,24},{8,16},{16,8},{24,0},{1,25},{9,17},{17,9},{25,1},{2,26},{10... | collective-permute-start | bytes 393224 | tf_op jit(solution)/shard_map/ppermute | solution.py:95
  114.7 6.5 %collective-permute-start.50 = (f32[128,256]{1,0:T(8,128)S(1)}, f32[128,256]{1,0:T(8,128)S(1)}, u32[]{:S(2)}, u32[]{:S(2)}) collective-permute-start(f32[128,256]{1,0:T(8,128)S(1)} %pad_maximum_fusion.refs_0_), channel_id=1, source_target_pairs={{0,16},{8,24},{16,0},{24,8},{1,17},{9,25},{17,1},{25,9},{2,18},{10... | collective-permute-start | bytes 393224 | tf_op jit(solution)/shard_map/ppermute | solution.py:95
  115.6 5.6 %collective-permute-start.49 = (f32[128,256]{1,0:T(8,128)S(1)}, f32[128,256]{1,0:T(8,128)S(1)}, u32[]{:S(2)}, u32[]{:S(2)}) collective-permute-start(f32[128,256]{1,0:T(8,128)S(1)} %pad_maximum_fusion.refs_0_), channel_id=1, source_target_pairs={{0,8},{8,0},{16,24},{24,16},{1,9},{9,1},{17,25},{25,17},{2,10},{10... | collective-permute-start | bytes 393224 | tf_op jit(solution)/shard_map/ppermute | solution.py:95
  (6 other events, 49.6 us)
